TPU v7x, 32 devices: a whole 2x2x4 slice. The times are simulated.
32 devices in a mesh: section: 2 (over core), dp: 16 (over z, y, x).
Axes of the slice: x: 2, y: 2, z: 4, core: 2. Of those that a mesh axis runs over, the one named last changes fastest.
Arguments:
- inputs: bfloat16 [32, 128, 1024], P('dp'), may hold values from -6 to 6
- cotangent: bfloat16 [32, 128, 1024], P('dp'), may hold values from -6 to 6
- domain: int32 [32], P('dp'), may hold values from 0 to 15, as said below
- lengths: int32 [32], P('dp'), may hold values from 64 to 128
- steps_since_reset: int32 [1], replicated, may hold values from 0 to 49
- frozen_query_weight: bfloat16 [4, 1024, 3072], P('section', 'dp'), may hold values from -0.1875 to 0.1875
- frozen_output_weight: bfloat16 [4, 1024, 1024], P('section', 'dp'), may hold values from -0.75 to 0.75
- frozen_up_weight: bfloat16 [4, 1024, 4096], P('section', 'dp'), may hold values from -0.1875 to 0.1875
- frozen_down_weight: bfloat16 [4, 4096, 1024], P('section', 'dp'), may hold values from -0.09375 to 0.09375
- query_adapter_first: bfloat16 [4, 1024, 128], P('section'), may hold values from -0.1875 to 0.1875
- query_adapter_second: bfloat16 [4, 128, 3072], P('section'), may hold values from -0.5 to 0.5
- output_adapter_first: bfloat16 [4, 1024, 128], P('section'), may hold values from -0.1875 to 0.1875
- output_adapter_second: bfloat16 [4, 128, 1024], P('section'), may hold values from -2 to 2
- up_adapter_first: bfloat16 [4, 1024, 128], P('section'), may hold values from -0.1875 to 0.1875
- up_adapter_second: bfloat16 [4, 128, 4096], P('section'), may hold values from -0.5 to 0.5
- down_adapter_first: bfloat16 [4, 4096, 128], P('section'), may hold values from -0.09375 to 0.09375
- down_adapter_second: bfloat16 [4, 128, 1024], P('section'), may hold values from -0.5 to 0.5
- layer_norm_gain: float32 [4, 2, 1024], P('section'), may hold values from 0.5 to 1.5
- layer_norm_bias: float32 [4, 2, 1024], P('section'), may hold values from -1.5 to 1.5
Outputs:
- section_out: bfloat16 [2, 32, 128, 1024], P('section', 'dp')
- section_grad: float32 [2, 32, 128, 1024], P('section', 'dp')
- gradient_query_first: float32 [4, 1024, 128], P('section')
- gradient_query_second: float32 [4, 128, 3072], P('section')
- gradient_output_first: float32 [4, 1024, 128], P('section')
- gradient_output_second: float32 [4, 128, 1024], P('section')
- gradient_up_first: float32 [4, 1024, 128], P('section')
- gradient_up_second: float32 [4, 128, 4096], P('section')
- gradient_down_first: float32 [4, 4096, 128], P('section')
- gradient_down_second: float32 [4, 128, 1024], P('section')
- grad_norm_gain: float32 [4, 2, 1024], P('section')
- grad_norm_bias: float32 [4, 2, 1024], P('section')
- folded_query_weight: bfloat16 [4, 1024, 3072], P('section', 'dp')
- folded_output_weight: bfloat16 [4, 1024, 1024], P('section', 'dp')
- folded_up_weight: bfloat16 [4, 1024, 4096], P('section', 'dp')
- folded_down_weight: bfloat16 [4, 4096, 1024], P('section', 'dp')
- rms_stats: float32 [4, 3, 17], P('section')
Inputs may be any that keep to these rules, and one draw needn't show every extreme that they name: `domain`: some domains may name no sequence.
All inputs are finite; a program needn't handle non-finite values.
Results may differ from a plain program's by a relative error of at most 0.022.
Values may be sent and summed in bfloat16 or wider, within the bound.
No kernel may reach another device: no remote copies, remote signals or barrier semaphores. Data moves between devices by JAX's collectives and lax.ppermute only.
A program may use at most 256 MiB of HBM per device.

v0:
```python
from functools import partial

import jax
import jax.numpy as jnp
from jax import lax
from jax.sharding import PartitionSpec as P

HEADS = 16
HEAD_DIM = 64
ROT = 16
DOMAINS = 16
MICRO = 2
WARM = 50


adapter_scale = 0.5
norm_eps = 1e-05
peak_rate = 0.0002
masked_score = -1e30


def from_behind(value, axis, steps):
    count = lax.axis_size(axis)
    initial, last = (max(0, -steps), min(count, count - steps))
    return lax.ppermute(value, axis, [(source, source + steps) for source in range(initial, last)])


def layer_norm(value, gain, bias):
    centred = value - jnp.mean(value, axis=-1, keepdims=True)
    spread = jnp.mean(centred * centred, axis=-1, keepdims=True)
    return centred * lax.rsqrt(spread + norm_eps) * gain + bias


def both_norms(value, gain_pair, bias_pair):
    return (
        layer_norm(value, gain_pair[0], bias_pair[0]),
        layer_norm(value, gain_pair[1], bias_pair[1]),
    )


def rotary(field):
    seq_len = field.shape[-3]
    half_rot = ROT // 2
    freqs = 10000.0 ** (-(jnp.arange(half_rot, dtype=jnp.float32) * 2.0 / ROT))
    angles = jnp.arange(seq_len, dtype=jnp.float32)[:, None] * freqs[None, :]
    cosine = jnp.concatenate([jnp.cos(angles), jnp.cos(angles)], -1)[:, None, :]
    sine = jnp.concatenate([jnp.sin(angles), jnp.sin(angles)], -1)[:, None, :]
    turned = field[..., :ROT]
    remain = field[..., ROT:]
    swapped = jnp.concatenate([-turned[..., half_rot:], turned[..., :half_rot]], -1)
    return jnp.concatenate([turned * cosine + swapped * sine, remain], -1)


def flatten_parts(parts):
    return jnp.concatenate([part.reshape(-1) for part in parts])


def unflatten_parts(flat, templates):
    pieces = []
    offset = 0
    for template in templates:
        count = template.size
        pieces.append(flat[offset : offset + count].reshape(template.shape))
        offset = offset + count
    return tuple(pieces)


def adapter_forward(saved_activations, dense_matmul, adapter_first_factor, adapter_second_factor):
    hidden_state = jnp.dot(
        saved_activations, adapter_first_factor, preferred_element_type=jnp.float32
    ).astype(jnp.bfloat16)
    final_result = jnp.dot(saved_activations, dense_matmul, preferred_element_type=jnp.float32)
    final_result = final_result + adapter_scale * jnp.dot(
        hidden_state, adapter_second_factor, preferred_element_type=jnp.float32
    )
    return (final_result, hidden_state)


def adapter_backward(
    gradient_layer_output,
    saved_activations,
    hidden_state,
    dense_matmul,
    adapter_first_factor,
    adapter_second_factor,
):
    gradient_hidden_state = (
        adapter_scale
        * jnp.einsum(
            "hfq,tq->hft",
            gradient_layer_output,
            adapter_second_factor,
            preferred_element_type=jnp.float32,
        )
    ).astype(jnp.bfloat16)
    gradient_feed_normed = adapter_scale * jnp.einsum(
        "rsm,rsn->mn", hidden_state, gradient_layer_output, preferred_element_type=jnp.float32
    )
    gradient_attention_normed = jnp.einsum(
        "rsk,rsm->km", saved_activations, gradient_hidden_state, preferred_element_type=jnp.float32
    )
    grad_inputs = jnp.einsum(
        "rsn,kn->rsk", gradient_layer_output, dense_matmul, preferred_element_type=jnp.float32
    )
    grad_inputs = grad_inputs + jnp.einsum(
        "efj,lj->efl",
        gradient_hidden_state,
        adapter_first_factor,
        preferred_element_type=jnp.float32,
    )
    return (grad_inputs, gradient_attention_normed, gradient_feed_normed)


def attention_mask(valid_boolean_mask):
    seq_len = valid_boolean_mask.shape[-1]
    positions = jnp.arange(seq_len)
    causal = positions[None, :] <= positions[:, None]
    return causal[None, None] & valid_boolean_mask[:, None, None, :]


def layer_forward(residual, weights, valid_boolean_mask):
    (
        frozen_query_weight,
        frozen_output_weight,
        frozen_up_weight,
        frozen_down_weight,
        query_first_factor,
        query_second_factor,
        output_first_factor,
        output_second_factor,
        up_first_factor,
        up_second_factor,
        down_first_factor,
        down_second_factor,
        gain,
        bias,
    ) = weights
    row_count, seq_len, model_width = residual.shape
    attention_normed = layer_norm(residual, gain[0], bias[0]).astype(jnp.bfloat16)
    feed_normed = layer_norm(residual, gain[1], bias[1]).astype(jnp.bfloat16)
    combined_output, hidden_query_rank = adapter_forward(
        attention_normed, frozen_query_weight, query_first_factor, query_second_factor
    )
    combined_output = combined_output.reshape(row_count, seq_len, 3, HEADS, HEAD_DIM)
    queries = rotary(combined_output[:, :, 0]).astype(jnp.bfloat16)
    key_heads = rotary(combined_output[:, :, 1]).astype(jnp.bfloat16)
    values = combined_output[:, :, 2].astype(jnp.bfloat16)
    allowed = attention_mask(valid_boolean_mask)
    scores = jnp.einsum(
        "rqhd,rkhd->rhqk", queries, key_heads, preferred_element_type=jnp.float32
    ) * HEAD_DIM ** (-0.5)
    scores = jnp.where(allowed, scores, masked_score)
    top_score = jnp.max(scores, axis=-1, keepdims=True)
    expo_score = jnp.exp(scores - top_score)
    exp_total = jnp.sum(expo_score, axis=-1, keepdims=True)
    probability = expo_score / exp_total
    log_total = top_score + jnp.log(exp_total)
    merged_head_values = jnp.einsum(
        "rhqk,rkhd->rqhd",
        probability.astype(jnp.bfloat16),
        values,
        preferred_element_type=jnp.float32,
    )
    merged_head_values = merged_head_values.reshape(row_count, seq_len, model_width).astype(
        jnp.bfloat16
    )
    attention_output, hidden_output_rank = adapter_forward(
        merged_head_values, frozen_output_weight, output_first_factor, output_second_factor
    )
    upward_projection, hidden_up_rank = adapter_forward(
        feed_normed, frozen_up_weight, up_first_factor, up_second_factor
    )
    gelu_output = jax.nn.gelu(upward_projection, approximate=False).astype(jnp.bfloat16)
    feedforward_output, hidden_down_rank = adapter_forward(
        gelu_output, frozen_down_weight, down_first_factor, down_second_factor
    )
    output = residual + (attention_output + feedforward_output)
    squared_values = jnp.stack(
        [
            jnp.sum(residual * residual, -1),
            jnp.sum(attention_output * attention_output, -1),
            jnp.sum(feedforward_output * feedforward_output, -1),
        ],
        -1,
    )
    row_sums = jnp.einsum(
        "nx,nxo->no",
        valid_boolean_mask.astype(jnp.float32),
        squared_values,
        precision=lax.Precision.HIGHEST,
    )
    kept_state = (
        residual,
        queries,
        key_heads,
        values,
        log_total,
        merged_head_values,
        upward_projection,
        hidden_query_rank,
        hidden_output_rank,
        hidden_up_rank,
        hidden_down_rank,
    )
    return (output, kept_state, row_sums)


def layer_backward(gradient_layer_output, kept_state, weights, valid_boolean_mask):
    (
        frozen_query_weight,
        frozen_output_weight,
        frozen_up_weight,
        frozen_down_weight,
        query_first_factor,
        query_second_factor,
        output_first_factor,
        output_second_factor,
        up_first_factor,
        up_second_factor,
        down_first_factor,
        down_second_factor,
        gain,
        bias,
    ) = weights
    (
        residual,
        queries,
        key_heads,
        values,
        log_total,
        merged_head_values,
        upward_projection,
        hidden_query_rank,
        hidden_output_rank,
        hidden_up_rank,
        hidden_down_rank,
    ) = kept_state
    row_count, seq_len, model_width = residual.shape
    (attention_normed, feed_normed), norm_back = jax.vjp(both_norms, residual, gain, bias)
    attention_normed = attention_normed.astype(jnp.bfloat16)
    feed_normed = feed_normed.astype(jnp.bfloat16)
    grad_branch = gradient_layer_output.astype(jnp.bfloat16)
    gelu_output, gelu_back = jax.vjp(partial(jax.nn.gelu, approximate=False), upward_projection)
    gelu_output = gelu_output.astype(jnp.bfloat16)
    gradient_gelu_output, gradient_down_first, gradient_down_second = adapter_backward(
        grad_branch,
        gelu_output,
        hidden_down_rank,
        frozen_down_weight,
        down_first_factor,
        down_second_factor,
    )
    rounded_activated = lax.optimization_barrier(gradient_gelu_output.astype(jnp.bfloat16)).astype(
        jnp.float32
    )
    grad_upper = gelu_back(rounded_activated)[0].astype(jnp.bfloat16)
    gradient_feed_normed, gradient_up_first, gradient_up_second = adapter_backward(
        grad_upper, feed_normed, hidden_up_rank, frozen_up_weight, up_first_factor, up_second_factor
    )
    gradient_mixed_heads, gradient_output_first, gradient_output_second = adapter_backward(
        grad_branch,
        merged_head_values,
        hidden_output_rank,
        frozen_output_weight,
        output_first_factor,
        output_second_factor,
    )
    gradient_mixed_heads = gradient_mixed_heads.astype(jnp.bfloat16).reshape(
        row_count, seq_len, HEADS, HEAD_DIM
    )
    allowed = attention_mask(valid_boolean_mask)
    scale_factor = HEAD_DIM ** (-0.5)
    scores = (
        jnp.einsum("rqhd,rkhd->rhqk", queries, key_heads, preferred_element_type=jnp.float32)
        * scale_factor
    )
    probability = jnp.where(allowed, jnp.exp(scores - log_total), 0.0)
    grad_probs = jnp.einsum(
        "rqhd,rkhd->rhqk", gradient_mixed_heads, values, preferred_element_type=jnp.float32
    )
    grad_values = jnp.einsum(
        "rhqk,rqhd->rkhd",
        probability.astype(jnp.bfloat16),
        gradient_mixed_heads,
        preferred_element_type=jnp.float32,
    )
    grad_scores = probability * (
        grad_probs - jnp.sum(probability * grad_probs, axis=-1, keepdims=True)
    )
    grad_scores = grad_scores.astype(jnp.bfloat16)
    grad_queries = (
        jnp.einsum("rhqk,rkhd->rqhd", grad_scores, key_heads, preferred_element_type=jnp.float32)
        * scale_factor
    )
    grad_keys = (
        jnp.einsum("rhqk,rqhd->rkhd", grad_scores, queries, preferred_element_type=jnp.float32)
        * scale_factor
    )
    rotary_back = jax.vjp(rotary, jnp.zeros(grad_queries.shape, jnp.float32))[1]
    grad_joint = jnp.stack(
        [rotary_back(grad_queries)[0], rotary_back(grad_keys)[0], grad_values], 2
    )
    grad_joint = grad_joint.reshape(row_count, seq_len, 3 * model_width).astype(jnp.bfloat16)
    gradient_attention_normed, gradient_query_first, gradient_query_second = adapter_backward(
        grad_joint,
        attention_normed,
        hidden_query_rank,
        frozen_query_weight,
        query_first_factor,
        query_second_factor,
    )
    grad_residual, grad_gain, grad_bias = norm_back(
        (gradient_attention_normed, gradient_feed_normed)
    )
    layer_grads = (
        gradient_query_first,
        gradient_query_second,
        gradient_output_first,
        gradient_output_second,
        gradient_up_first,
        gradient_up_second,
        gradient_down_first,
        gradient_down_second,
        grad_gain,
        grad_bias,
    )
    return (gradient_layer_output + grad_residual, layer_grads)


def shards(
    inputs,
    cotangent,
    domain,
    lengths,
    steps_since_reset,
    frozen_query_weight,
    frozen_output_weight,
    frozen_up_weight,
    frozen_down_weight,
    query_adapter_first,
    query_adapter_second,
    output_adapter_first,
    output_adapter_second,
    up_adapter_first,
    up_adapter_second,
    down_adapter_first,
    down_adapter_second,
    layer_norm_gain,
    layer_norm_bias,
):
    section_index = lax.axis_index("section")
    leading = section_index == 0
    local_layers = frozen_query_weight.shape[0]
    rows_dev, seq_len, model_width = inputs.shape
    rows_micro = rows_dev // MICRO
    trained = (
        query_adapter_first,
        query_adapter_second,
        output_adapter_first,
        output_adapter_second,
        up_adapter_first,
        up_adapter_second,
        down_adapter_first,
        down_adapter_second,
        layer_norm_gain,
        layer_norm_bias,
    )
    layer_templates = tuple((jnp.zeros(parameter.shape[1:], jnp.float32) for parameter in trained))
    dense_full = (
        lax.all_gather(frozen_query_weight, "dp", axis=1, tiled=True),
        lax.all_gather(frozen_output_weight, "dp", axis=1, tiled=True),
        lax.all_gather(frozen_up_weight, "dp", axis=1, tiled=True),
        lax.all_gather(frozen_down_weight, "dp", axis=1, tiled=True),
    )

    def layer_weights(dense_set, layer_index):
        return tuple((matrix[layer_index] for matrix in dense_set)) + tuple(
            (parameter[layer_index] for parameter in trained)
        )

    positions = jnp.arange(seq_len)
    length_blocks = lengths.reshape(MICRO, rows_micro)
    valid_blocks = positions[None, None, :] < length_blocks[:, :, None]
    domain_blocks = (domain.reshape(MICRO, rows_micro)[..., None] == jnp.arange(DOMAINS)).astype(
        jnp.float32
    )
    input_blocks = inputs.reshape(MICRO, rows_micro, seq_len, model_width)
    cot_blocks = cotangent.reshape(MICRO, rows_micro, seq_len, model_width)
    domain_whole = (domain[:, None] == jnp.arange(DOMAINS)[None, :]).astype(jnp.float32)
    domain_counts = jnp.dot(
        lengths.astype(jnp.float32), domain_whole, precision=lax.Precision.HIGHEST
    )
    all_count = jnp.sum(lengths.astype(jnp.float32))
    domain_parts = [jnp.zeros((3, DOMAINS), jnp.float32) for _ in range(local_layers)]
    total_parts = [jnp.zeros((3,), jnp.float32) for _ in range(local_layers)]
    received = jnp.zeros((rows_micro, seq_len, model_width), jnp.float32)
    kept_ticks = []
    output_ticks = []
    for tick_index in range(MICRO + 1):
        micro_index = tick_index - section_index
        active = ((micro_index >= 0) & (micro_index < MICRO)).astype(jnp.float32)
        micro_slot = jnp.clip(micro_index, 0, MICRO - 1)
        valid_boolean_mask = lax.dynamic_index_in_dim(valid_blocks, micro_slot, 0, keepdims=False)
        domain_table = lax.dynamic_index_in_dim(domain_blocks, micro_slot, 0, keepdims=False)
        residual = jnp.where(
            leading, input_blocks[min(tick_index, MICRO - 1)].astype(jnp.float32), received
        )
        kept_layers = []
        for layer_index in range(local_layers):
            residual, kept_state, row_sums = layer_forward(
                residual, layer_weights(dense_full, layer_index), valid_boolean_mask
            )
            kept_layers.append(kept_state)
            domain_parts[layer_index] = domain_parts[layer_index] + active * jnp.einsum(
                "rq,rn->qn", row_sums, domain_table, precision=lax.Precision.HIGHEST
            )
            total_parts[layer_index] = total_parts[layer_index] + active * jnp.sum(row_sums, axis=0)
        kept_ticks.append(tuple(kept_layers))
        output_ticks.append(residual)
        if tick_index < MICRO:
            received = from_behind(residual.astype(jnp.bfloat16), "section", 1).astype(jnp.float32)
    domain_sums = jnp.stack(domain_parts)
    all_sums = jnp.stack(total_parts)
    grad_totals = [layer_templates for _ in range(local_layers)]
    came_back = jnp.zeros((rows_micro, seq_len, model_width), jnp.float32)
    grad_ticks = []
    for tick_index in range(MICRO + 1):
        micro_index = tick_index + section_index - 1
        active = ((micro_index >= 0) & (micro_index < MICRO)).astype(jnp.float32)
        micro_slot = jnp.clip(micro_index, 0, MICRO - 1)
        valid_boolean_mask = lax.dynamic_index_in_dim(valid_blocks, micro_slot, 0, keepdims=False)
        late_slot = min(tick_index, MICRO - 1)
        start_grad = cot_blocks[late_slot].astype(jnp.float32) * valid_blocks[late_slot][
            ..., None
        ].astype(jnp.float32)
        gradient_layer_output = jnp.where(leading, came_back, start_grad) * active
        chosen = jax.tree.map(
            lambda early_value, later_value: jnp.where(leading, early_value, later_value),
            kept_ticks[max(tick_index - 1, 0)],
            kept_ticks[min(tick_index + 1, MICRO)],
        )
        for layer_index in reversed(range(local_layers)):
            gradient_layer_output, layer_grads = layer_backward(
                gradient_layer_output,
                chosen[layer_index],
                layer_weights(dense_full, layer_index),
                valid_boolean_mask,
            )
            grad_totals[layer_index] = tuple(
                (total + extra for total, extra in zip(grad_totals[layer_index], layer_grads))
            )
        sent_grad = gradient_layer_output.astype(jnp.bfloat16)
        grad_ticks.append(jnp.where(leading, gradient_layer_output, sent_grad.astype(jnp.float32)))
        if tick_index < MICRO:
            came_back = from_behind(sent_grad, "section", -1).astype(jnp.float32)
    flat_grads = flatten_parts(
        [grad_part for layer_grads in grad_totals for grad_part in layer_grads]
    )
    flat_grads, domain_sums, all_sums, domain_counts, all_count = lax.psum(
        (flat_grads, domain_sums, all_sums, domain_counts, all_count), "dp"
    )
    all_templates = tuple((template for _ in range(local_layers) for template in layer_templates))
    pieces = unflatten_parts(flat_grads, all_templates)
    each_count = len(trained)
    summed = [
        tuple(pieces[layer_index * each_count : (layer_index + 1) * each_count])
        for layer_index in range(local_layers)
    ]
    stacked_arrays = [
        jnp.stack([summed[layer_index][param_index] for layer_index in range(local_layers)])
        for param_index in range(len(trained))
    ]
    rms_domain = jnp.sqrt(domain_sums / (jnp.maximum(domain_counts, 1.0) * model_width))
    rms_all = jnp.sqrt(all_sums / (all_count * model_width))
    rms_stats = jnp.concatenate([rms_domain, rms_all[..., None]], -1)
    rate = peak_rate * (steps_since_reset[0].astype(jnp.float32) + 1.0) / WARM
    shard_index = lax.axis_index("dp")

    def merge_adapter(
        frozen_branch, first_factor, second_factor, gradient_attention_normed, gradient_feed_normed
    ):
        row_span = frozen_branch.shape[1]
        new_first = first_factor.astype(jnp.float32) - rate * gradient_attention_normed
        new_second = second_factor.astype(jnp.float32) - rate * gradient_feed_normed
        first_rows = lax.dynamic_slice_in_dim(new_first, shard_index * row_span, row_span, 1)
        matrix_product = jnp.einsum(
            "lkr,lrn->lkn", first_rows, new_second, precision=lax.Precision.HIGHEST
        )
        return (frozen_branch.astype(jnp.float32) + adapter_scale * matrix_product).astype(
            jnp.bfloat16
        )

    folded_query_weight = merge_adapter(
        frozen_query_weight,
        query_adapter_first,
        query_adapter_second,
        stacked_arrays[0],
        stacked_arrays[1],
    )
    folded_output_weight = merge_adapter(
        frozen_output_weight,
        output_adapter_first,
        output_adapter_second,
        stacked_arrays[2],
        stacked_arrays[3],
    )
    folded_up_weight = merge_adapter(
        frozen_up_weight, up_adapter_first, up_adapter_second, stacked_arrays[4], stacked_arrays[5]
    )
    folded_down_weight = merge_adapter(
        frozen_down_weight,
        down_adapter_first,
        down_adapter_second,
        stacked_arrays[6],
        stacked_arrays[7],
    )
    out_blocks = [
        jnp.where(leading, output_ticks[block_index], output_ticks[block_index + 1]).astype(
            jnp.bfloat16
        )
        for block_index in range(MICRO)
    ]
    section_out = jnp.stack(out_blocks).reshape(1, rows_dev, seq_len, model_width)
    grad_blocks = [
        jnp.where(leading, grad_ticks[block_index + 1], grad_ticks[block_index])
        for block_index in range(MICRO)
    ]
    section_grad = jnp.stack(grad_blocks).reshape(1, rows_dev, seq_len, model_width)
    return (
        section_out,
        section_grad,
        stacked_arrays[0],
        stacked_arrays[1],
        stacked_arrays[2],
        stacked_arrays[3],
        stacked_arrays[4],
        stacked_arrays[5],
        stacked_arrays[6],
        stacked_arrays[7],
        stacked_arrays[8],
        stacked_arrays[9],
        folded_query_weight,
        folded_output_weight,
        folded_up_weight,
        folded_down_weight,
        rms_stats,
    )


def solution(mesh):
    placed = (
        P("dp", None, None),
        P("dp", None, None),
        P("dp"),
        P("dp"),
        P(),
        P("section", "dp", None),
        P("section", "dp", None),
        P("section", "dp", None),
        P("section", "dp", None),
        P("section", None, None),
        P("section", None, None),
        P("section", None, None),
        P("section", None, None),
        P("section", None, None),
        P("section", None, None),
        P("section", None, None),
        P("section", None, None),
        P("section", None, None),
        P("section", None, None),
    )
    return jax.shard_map(
        shards,
        mesh=mesh,
        in_specs=placed,
        out_specs=(
            P("section", "dp", None, None),
            P("section", "dp", None, None),
            P("section", None, None),
            P("section", None, None),
            P("section", None, None),
            P("section", None, None),
            P("section", None, None),
            P("section", None, None),
            P("section", None, None),
            P("section", None, None),
            P("section", None, None),
            P("section", None, None),
            P("section", "dp", None),
            P("section", "dp", None),
            P("section", "dp", None),
            P("section", "dp", None),
            P("section", None, None),
        ),
        check_vma=False,
    )
```

profile of v0, /device:TPU:26, one launch (start us, length us, event | category | flops | bytes accessed | tf_op | source)
XLA Modules:
  0.0 1692.6 jit_solution(12577641963923932548)
XLA Ops:
  16.8 69.2 %all-gather.7.cloned.1.call-done = bf16[2,1024,1024]{2,1,0:T(8,128)(2,1)} async-done(((bf16[2,64,1024]{2,1,0:T(8,128)(2,1)}), bf16[2,1024,1024]{2,1,0:T(8,128)(2,1)}) %all-gather.7.cloned.1.call-update) | async-done | bytes 4194320 | tf_op jit(solution)/shard_map/all_gather | solution.py:371
  89.6 149.6 %all-gather.5.cloned.1.call-done = bf16[2,1024,3072]{2,1,0:T(8,128)(2,1)} async-done(((bf16[2,64,3072]{2,1,0:T(8,128)(2,1)}), bf16[2,1024,3072]{2,1,0:T(8,128)(2,1)}) %all-gather.5.cloned.1.call-update) | async-done | bytes 12582928 | tf_op jit(solution)/shard_map/all_gather | solution.py:370
  253.4 178.2 %all-gather.9.cloned.1.call-done = bf16[2,1024,4096]{2,1,0:T(8,128)(2,1)} async-done(((bf16[2,64,4096]{2,1,0:T(8,128)(2,1)}), bf16[2,1024,4096]{2,1,0:T(8,128)(2,1)}) %all-gather.9.cloned.1.call-update) | async-done | bytes 16777232 | tf_op jit(solution)/shard_map/all_gather | solution.py:372
  436.5 6.0 fusion.122
  444.0 180.1 %all-gather.11.cloned.1.call-done = bf16[2,4096,1024]{2,1,0:T(8,128)(2,1)} async-done(((bf16[2,256,1024]{2,1,0:T(8,128)(2,1)}), bf16[2,4096,1024]{2,1,0:T(8,128)(2,1)}) %all-gather.11.cloned.1.call-update) | async-done | bytes 16777232 | tf_op jit(solution)/shard_map/all_gather | solution.py:373
  624.1 5.1 fusion.50
  650.3 6.2 fusion.125
  687.8 6.0 fusion.128
  728.5 5.1 fusion.74
  734.5 5.3 fusion.55
  739.9 5.9 fusion.131
  745.8 6.3 fusion.83
  775.0 6.4 fusion.47
  783.6 5.2 fusion.90
  806.7 5.8 fusion.68
  846.1 6.3 fusion.134
  891.0 6.0 fusion.137
  925.0 6.4 fusion.97
  932.0 5.4 fusion.73
  970.3 6.8 fusion.46
  979.3 6.2 fusion.104
  988.9 5.3 fusion.67
  1040.3 5.2 fusion.111
  1046.0 5.1 fusion.72
  1052.0 6.5 fusion.51
  1085.7 6.8 fusion.45
  1132.2 6.1 fusion.5
  1149.1 5.9 fusion.2
  1162.3 6.1 fusion.60
  1171.0 39.0 %all-reduce.72 = (f32[2,3]{1,0:T(2,128)S(1)}, f32[]{:T(128)}, f32[2,3,16]{2,1,0:T(4,128)S(1)}, f32[16]{0:T(128)S(1)}) all-reduce(f32[2,3]{1,0:T(2,128)S(1)} %pad_maximum_fusion.22, f32[]{:T(128)} %convert_reduce_fusion, f32[2,3,16]{2,1,0:T(4,128)S(1)} %pad_maximum_fusion.20, ...), channel_id=1, replica_groups=mesh['section'=2,'dp'=16] {'dp'}, use_global_device_ids=true, to_apply=%region_111.112 | all-reduce | flops 119 | bytes 952 | tf_op jit(solution)/shard_map/psum | solution.py:459
  1215.4 402.8 %all-reduce.75.cloned.1.call-done = f32[4202496]{0:T(1024)} async-done(((f32[4202496]{0:T(1024)}), f32[4202496]{0:T(1024)}) %all-reduce.75.cloned.1.call-update) | async-done | bytes 16810000 | tf_op jit(solution)/shard_map/psum | solution.py:459
  1630.7 6.9 slice_bitcast_fusion.43
  (1777 shorter events, 495.4 us)
Async XLA Ops:
  7.3 78.8 %all-gather.7.cloned.1.call-start = ((), (), s32[]{:S(2)}) async-start(), calls=%async_computation.1 | async-start | bytes 4456448 | tf_op jit(solution)/shard_map/all_gather | solution.py:371
  8.0 231.3 %all-gather.5.cloned.1.call-start = ((), (), s32[]{:S(2)}) async-start(), calls=%async_computation | async-start | bytes 13369344 | tf_op jit(solution)/shard_map/all_gather | solution.py:370
  8.8 422.8 %all-gather.9.cloned.1.call-start = ((), (), s32[]{:S(2)}) async-start(), calls=%async_computation.2 | async-start | bytes 17825792 | tf_op jit(solution)/shard_map/all_gather | solution.py:372
  9.5 614.6 %all-gather.11.cloned.1.call-start = ((), (), s32[]{:S(2)}) async-start(), calls=%async_computation.3 | async-start | bytes 17825792 | tf_op jit(solution)/shard_map/all_gather | solution.py:373
  10.1 1608.1 %all-reduce.75.cloned.1.call-start = ((), (), s32[]{:S(2)}) async-start(), calls=%async_computation.4 | async-start | bytes 33619968 | tf_op jit(solution)/shard_map/psum | solution.py:459
  11.3 74.8 %copy-start.530 = (f32[128]{0:T(128)}, f32[128]{0:T(128)S(1)}, u32[]{:S(2)}) copy-start(f32[128]{0:T(128)S(1)} %get-tuple-element.336) | copy-start | bytes 1540
  14.1 417.5 %copy-start.307 = (f32[1,1,1024]{2,1,0:T(1,128)}, f32[1,1,1024]{2,1,0:T(1,128)S(1)}, u32[]{:S(2)}) copy-start(f32[1,1,1024]{2,1,0:T(1,128)S(1)} %get-tuple-element.292) | copy-start | bytes 12292
  14.1 617.6 %copy-start.339 = (f32[1,1,1024]{2,1,0:T(1,128)}, f32[1,1,1024]{2,1,0:T(1,128)S(1)}, u32[]{:S(2)}) copy-start(f32[1,1,1024]{2,1,0:T(1,128)S(1)} %get-tuple-element.294) | copy-start | bytes 12292
  14.1 631.1 %copy-start.332 = (f32[1,1,1024]{2,1,0:T(1,128)}, f32[1,1,1024]{2,1,0:T(1,128)S(1)}, u32[]{:S(2)}) copy-start(f32[1,1,1024]{2,1,0:T(1,128)S(1)} %get-tuple-element.291) | copy-start | bytes 12292
  14.1 654.8 %copy-start.312 = (f32[1,1,1024]{2,1,0:T(1,128)}, f32[1,1,1024]{2,1,0:T(1,128)S(1)}, u32[]{:S(2)}) copy-start(f32[1,1,1024]{2,1,0:T(1,128)S(1)} %get-tuple-element.293) | copy-start | bytes 12292
  14.2 417.4 %copy-start.461 = (f32[1,1,1024]{2,1,0:T(1,128)}, f32[1,1,1024]{2,1,0:T(1,128)S(1)}, u32[]{:S(2)}) copy-start(f32[1,1,1024]{2,1,0:T(1,128)S(1)} %get-tuple-element.296) | copy-start | bytes 12292
  14.2 617.5 %copy-start.455 = (f32[1,1,1024]{2,1,0:T(1,128)}, f32[1,1,1024]{2,1,0:T(1,128)S(1)}, u32[]{:S(2)}) copy-start(f32[1,1,1024]{2,1,0:T(1,128)S(1)} %get-tuple-element.298) | copy-start | bytes 12292
  14.2 631.1 %copy-start.450 = (f32[1,1,1024]{2,1,0:T(1,128)}, f32[1,1,1024]{2,1,0:T(1,128)S(1)}, u32[]{:S(2)}) copy-start(f32[1,1,1024]{2,1,0:T(1,128)S(1)} %get-tuple-element.295) | copy-start | bytes 12292
  14.2 654.7 %copy-start.466 = (f32[1,1,1024]{2,1,0:T(1,128)}, f32[1,1,1024]{2,1,0:T(1,128)S(1)}, u32[]{:S(2)}) copy-start(f32[1,1,1024]{2,1,0:T(1,128)S(1)} %get-tuple-element.297) | copy-start | bytes 12292
  15.2 650.3 %copy-start.404 = (bf16[128,128]{1,0:T(8,128)(2,1)}, bf16[128,128]{1,0:T(8,128)(2,1)S(1)}, u32[]{:S(2)}) copy-start(bf16[128,128]{1,0:T(8,128)(2,1)S(1)} %fusion.304) | copy-start | bytes 98308
  16.5 420.0 %copy-start.392 = (bf16[128,128]{1,0:T(8,128)(2,1)}, bf16[128,128]{1,0:T(8,128)(2,1)S(1)}, u32[]{:S(2)}) copy-start(bf16[128,128]{1,0:T(8,128)(2,1)S(1)} %convolution_convert_fusion.27) | copy-start | bytes 98308
  16.8 226.4 %copy-start.353 = (bf16[128,128]{1,0:T(8,128)(2,1)}, bf16[128,128]{1,0:T(8,128)(2,1)S(1)}, u32[]{:S(2)}) copy-start(bf16[128,128]{1,0:T(8,128)(2,1)S(1)} %convolution_convert_fusion.29) | copy-start | bytes 98308
  16.8 71.7 %copy-start.21 = (bf16[2,1024,128]{2,1,0:T(8,128)(2,1)S(1)}, bf16[2,1024,128]{2,1,0:T(8,128)(2,1)}, u32[]{:S(2)}) copy-start(bf16[2,1024,128]{2,1,0:T(8,128)(2,1)} %param.30) | copy-start | bytes 1572868
  16.8 71.7 %copy-start.414 = (bf16[128,128]{1,0:T(8,128)(2,1)S(1)}, bf16[128,128]{1,0:T(8,128)(2,1)}, u32[]{:S(2)}) copy-start(bf16[128,128]{1,0:T(8,128)(2,1)} %fusion.305) | copy-start | bytes 98308
  89.6 153.6 %copy-start.10 = (bf16[2,128,3072]{2,1,0:T(8,128)(2,1)S(1)}, bf16[2,128,3072]{2,1,0:T(8,128)(2,1)}, u32[]{:S(2)}) copy-start(bf16[2,128,3072]{2,1,0:T(8,128)(2,1)} %param.29) | copy-start | bytes 4718596
  249.9 181.6 %copy-start.564 = (f32[128]{0:T(128)S(1)}, f32[128]{0:T(128)}, u32[]{:S(2)}) copy-start(f32[128]{0:T(128)} %copy-done.563) | copy-start | bytes 1540
  250.0 181.6 %copy-start.588 = (f32[128]{0:T(128)S(1)}, f32[128]{0:T(128)}, u32[]{:S(2)}) copy-start(f32[128]{0:T(128)} %copy-done.587) | copy-start | bytes 1540
  251.5 378.0 %copy-start.272 = (bf16[16,64,128]{2,1,0:T(8,128)(2,1)}, bf16[16,64,128]{2,1,0:T(8,128)(2,1)S(1)}, u32[]{:S(2)}) copy-start(bf16[16,64,128]{2,1,0:T(8,128)(2,1)S(1)} %convolution_convert_fusion.5) | copy-start | bytes 786436
  443.9 185.3 %copy-start.375 = (bf16[128,128]{1,0:T(8,128)(2,1)}, bf16[128,128]{1,0:T(8,128)(2,1)S(1)}, u32[]{:S(2)}) copy-start(bf16[128,128]{1,0:T(8,128)(2,1)S(1)} %convolution_convert_fusion.11) | copy-start | bytes 98308
  444.0 185.3 %copy-start.52 = (bf16[2,128,1024]{2,1,0:T(8,128)(2,1)S(1)}, bf16[2,128,1024]{2,1,0:T(8,128)(2,1)}, u32[]{:S(2)}) copy-start(bf16[2,128,1024]{2,1,0:T(8,128)(2,1)} %param.35) | copy-start | bytes 1572868
  660.6 6.4 collective-permute-start
  667.0 154.2 %copy-start.142 = (bf16[1,128,1024]{2,1,0:T(8,128)(2,1)}, bf16[1,128,1024]{2,1,0:T(8,128)(2,1)S(1)}, u32[]{:S(2)}) copy-start(bf16[1,128,1024]{2,1,0:T(8,128)(2,1)S(1)} %collective-permute-done) | copy-start | bytes 786436
  679.0 90.3 %copy-start.276 = (bf16[128,16,16]{0,2,1:T(8,128)(2,1)}, bf16[128,16,16]{0,2,1:T(8,128)(2,1)S(1)}, u32[]{:S(2)}) copy-start(bf16[128,16,16]{0,2,1:T(8,128)(2,1)S(1)} %get-tuple-element.289) | copy-start | bytes 196612
  679.0 91.2 %copy-start.274 = (bf16[128,16,16]{0,2,1:T(8,128)(2,1)}, bf16[128,16,16]{0,2,1:T(8,128)(2,1)S(1)}, u32[]{:S(2)}) copy-start(bf16[128,16,16]{0,2,1:T(8,128)(2,1)S(1)} %get-tuple-element.290) | copy-start | bytes 196612
  801.0 18.9 %collective-permute-start.1 = (bf16[1,128,1024]{2,1,0:T(8,128)(2,1)}, bf16[1,128,1024]{2,1,0:T(8,128)(2,1)}, u32[]{:S(2)}, u32[]{:S(2)}) collective-permute-start(bf16[1,128,1024]{2,1,0:T(8,128)(2,1)} %get-tuple-element.173), channel_id=1, source_target_pairs={{0,16},{1,17},{2,18},{3,19},{4,20},{5,21},{6,22},{7,23},{8,24},{9,... | collective-permute-start | bytes 786440 | tf_op jit(solution)/shard_map/ppermute | solution.py:25
  881.1 22.2 %collective-permute-start.2 = (bf16[1,128,1024]{2,1,0:T(8,128)(2,1)}, bf16[1,128,1024]{2,1,0:T(8,128)(2,1)}, u32[]{:S(2)}, u32[]{:S(2)}) collective-permute-start(bf16[1,128,1024]{2,1,0:T(8,128)(2,1)} %get-tuple-element.150), channel_id=1, source_target_pairs={{16,0},{17,1},{18,2},{19,3},{20,4},{21,5},{22,6},{23,7},{24,8},{25... | collective-permute-start | bytes 786440 | tf_op jit(solution)/shard_map/ppermute | solution.py:25
  1009.5 12.6 collective-permute-start.3
  (600 other events, 2797.7 us)
Sparse Core Ops, SparseCore 0:
  10.8 75.1 all-gather.6
  88.7 150.4 all-gather.4
  242.0 189.5 all-gather.8
  434.2 189.8 all-gather.10
  1157.5 460.6 all-reduce.74
where the time goes:
time: 1710 us; the launch traced here: 1690 us
  waiting for transfers between devices  983 us (57%)
  matrix products  394 us (23%)
  local copies, waits for them, and re-layouts  142 us (8%)
  other arithmetic  104 us (6%)
  blocking collectives  39 us (2%)
  between operations  23.8 us (1%)
    psum x1, waiting for transfers between devices, shards(): lax.psum((flat_grads, domain_sums, all_sums, domain_counts, all_count), '...  403 us
    all_gather x1, waiting for transfers between devices, shards(): lax.all_gather(frozen_down_weight, 'dp', axis=1, tiled=True)  180 us
    all_gather x1, waiting for transfers between devices, shards(): lax.all_gather(frozen_up_weight, 'dp', axis=1, tiled=True)  178 us
    all_gather x1, waiting for transfers between devices, shards(): lax.all_gather(frozen_query_weight, 'dp', axis=1, tiled=True)  150 us
    dot_general x24, matrix products, adapter_backward(): jnp.einsum('rsn,kn->rsk', gradient_layer_output, dense_matmul, preferred_...  90.3 us
    dot_general x24, matrix products, adapter_forward(): jnp.dot(saved_activations, dense_matmul, preferred_element_type=jnp.float32)  81.6 us
    all_gather x1, waiting for transfers between devices, shards(): lax.all_gather(frozen_output_weight, 'dp', axis=1, tiled=True)  69.2 us
    unnamed x1270, local copies, waits for them, and re-layouts  68.7 us
  transfers between devices with their start and end apart: 9, of which 5 were waited for; matrix products, arithmetic and copies ran while one was open for 6% of the time, Pallas kernels for 0%

commit v1 on v0

v1 whole, which is shorter than its diff:
```python
from functools import partial

import jax
import jax.numpy as jnp
from jax import lax
from jax.experimental import pallas as pl
from jax.experimental.pallas import tpu as pltpu
from jax.sharding import PartitionSpec as P

HEADS = 16
HEAD_DIM = 64
ROT = 16
DOMAINS = 16
WARM = 50
RANK = 128
WIDE = 1024
UNITS = 12
HALF_UNITS = 6

adapter_scale = 0.5
norm_eps = 1e-05
peak_rate = 0.0002
masked_score = -1e30


def both_axes(value, pairs):
    return lax.ppermute(value, ("section", "dp"), pairs)


def flip_core(value):
    return lax.ppermute(value, "section", [(0, 1), (1, 0)])


def flip_place(value, mask):
    count = lax.axis_size("dp")
    return lax.ppermute(value, "dp", [(place, place ^ mask) for place in range(count)])


def split_units(matrices):
    query, output, upper, down = matrices
    rows = output.shape[0]
    return [
        query[:, :WIDE],
        query[:, WIDE : 2 * WIDE],
        query[:, 2 * WIDE :],
        output,
        upper[:, :WIDE],
        upper[:, WIDE : 2 * WIDE],
        upper[:, 2 * WIDE : 3 * WIDE],
        upper[:, 3 * WIDE :],
        down[:rows],
        down[rows : 2 * rows],
        down[2 * rows : 3 * rows],
        down[3 * rows :],
    ]


def gather_steps(piece, masks):
    held = piece[None]
    found = [0]
    for mask in masks:
        held = jnp.concatenate([held, flip_place(held, mask)], 0)
        found = found + [known ^ mask for known in found]
    return held, found


def assemble_kernel(info_ref, *refs):
    mine, theirs, outs = refs[:3], refs[3:6], refs[-4:]
    query_out, output_out, upper_out, down_out = outs
    rows = output_out.shape[0]

    def write(first, second):
        query_out[:, :WIDE] = first[0][0, 0]
        query_out[:, WIDE : 2 * WIDE] = first[0][0, 1]
        query_out[:, 2 * WIDE :] = first[1][0, 0]
        output_out[...] = first[1][0, 1]
        upper_out[:, :WIDE] = first[2][0, 0]
        upper_out[:, WIDE : 2 * WIDE] = first[2][0, 1]
        upper_out[:, 2 * WIDE : 3 * WIDE] = second[0][0, 0]
        upper_out[:, 3 * WIDE :] = second[0][0, 1]
        down_out[:rows] = second[1][0, 0]
        down_out[rows : 2 * rows] = second[1][0, 1]
        down_out[2 * rows : 3 * rows] = second[2][0, 0]
        down_out[3 * rows :] = second[2][0, 1]

    @pl.when(info_ref[0, 0] == 0)
    def _():
        write(mine, theirs)

    @pl.when(info_ref[0, 0] != 0)
    def _():
        write(theirs, mine)


def assemble(info, mine, theirs, rows, count, into):
    blocks = mine[0].shape[0]

    def source(part):
        return pl.BlockSpec((1, 2, rows, WIDE), lambda step, info_ref: (info_ref[2 + part, step], 0, 0, 0))

    def target(height, width):
        return pl.BlockSpec((height, width), lambda step, info_ref: (info_ref[1, step], 0))

    total = rows * count
    shapes = [(total, 3 * WIDE), (total, WIDE), (total, 4 * WIDE), (4 * total, WIDE)]
    extra = [] if into is None else list(into)
    size = 2 * 2 * UNITS * rows * WIDE * blocks
    return pl.pallas_call(
        assemble_kernel,
        out_shape=[jax.ShapeDtypeStruct(shape, jnp.bfloat16) for shape in shapes],
        grid_spec=pltpu.PrefetchScalarGridSpec(
            num_scalar_prefetch=1,
            grid=(blocks,),
            in_specs=[source(0), source(1), source(2)] * 2
            + [pl.BlockSpec(memory_space=pl.ANY)] * len(extra),
            out_specs=[target(rows, 3 * WIDE), target(rows, WIDE), target(rows, 4 * WIDE), target(4 * rows, WIDE)],
        ),
        input_output_aliases={7 + index: index for index in range(len(extra))},
        cost_estimate=pl.CostEstimate(flops=0, bytes_accessed=size, transcendentals=0),
        name="assemble",
    )(info, *mine, *theirs, *extra)


def rotations(masks):
    return [[masks[(start + index) % len(masks)] for index in range(len(masks))] for start in range(3)]


def gather_layer(matrices, core, stage, low, home, count, masks):
    half = count // 2
    units = split_units(matrices)
    rows = units[0].shape[0]
    first, second = jnp.stack(units[:HALF_UNITS]), jnp.stack(units[HALF_UNITS:])
    same = jnp.where(stage == 0, first, second)
    other = jnp.where(stage == 0, second, first)
    places = [(place // half, place) for place in range(count)]
    near = [(here * count + place, (1 - here) * count + place) for here, place in places]
    far = [((1 - here) * count + place, (1 - here) * count + (place ^ half)) for here, place in places]
    cross = [((1 - here) * count + place, here * count + (place ^ half)) for here, place in places]
    from_first = both_axes(other, near + far)
    from_second = both_axes(same, cross)
    own = jnp.where(home, same, from_first)
    partner = jnp.where(home, from_first, from_second)
    whole = None
    for which, block in enumerate((own, partner)):
        base = jnp.where(stage == which, 0, half)
        mine, theirs, rows_of = [], [], []
        order = None
        for part, turn in enumerate(rotations(masks)):
            held, found = gather_steps(block[2 * part : 2 * part + 2], turn)
            mine.append(held)
            theirs.append(flip_core(held))
            if order is None:
                order = found
            rows_of.append([found.index(mask) for mask in order])
        blocks = jnp.asarray(order, jnp.int32) ^ low
        info = jnp.stack(
            [jnp.full((half,), core, jnp.int32), blocks + base]
            + [jnp.asarray(row, jnp.int32) for row in rows_of]
        )
        whole = assemble(info, mine, theirs, rows, count, whole)
    return whole


def part_rows(total):
    first = (total // 3 + 7) // 8 * 8
    return [(0, first), (first, 2 * first), (2 * first, total)]


def reduce_section(parts, section, core, stage, low, count, masks):
    half = count // 2
    rounded = parts.astype(jnp.bfloat16)
    columns = parts.shape[1] // 2
    send = jnp.where(core == 0, rounded[:, columns:], rounded[:, :columns])
    keep = jnp.where(core == 0, parts[:, :columns], parts[:, columns:])
    held = (keep + flip_core(send).astype(jnp.float32)).astype(jnp.bfloat16)
    whole = []
    for (begin, end), turn in zip(part_rows(parts.shape[0]), rotations(masks)):
        slab = held[begin:end]
        for mask in turn:
            columns = slab.shape[1] // 2
            upper_side = (low & mask) != 0
            left, right = slab[:, :columns], slab[:, columns:]
            send = jnp.where(upper_side, left, right)
            keep = jnp.where(upper_side, right, left)
            slab = (keep.astype(jnp.float32) + flip_place(send, mask).astype(jnp.float32)).astype(jnp.bfloat16)
        across = flip_place(slab, half)
        slab = jnp.where(stage == section, slab, across)
        for mask in reversed(turn):
            upper_side = (low & mask) != 0
            there = flip_place(slab, mask)
            slab = jnp.concatenate(
                [jnp.where(upper_side, there, slab), jnp.where(upper_side, slab, there)], 1
            )
        whole.append(slab)
    here = jnp.concatenate(whole, 0)
    there = lax.ppermute(here, "section", [(1 - section, section)])
    return jnp.concatenate([here, there] if section == 0 else [there, here], 1)


def layer_norm(value, gain, bias):
    centred = value - jnp.mean(value, axis=-1, keepdims=True)
    spread = jnp.mean(centred * centred, axis=-1, keepdims=True)
    return centred * lax.rsqrt(spread + norm_eps) * gain + bias


def both_norms(value, gain_pair, bias_pair):
    return (
        layer_norm(value, gain_pair[0], bias_pair[0]),
        layer_norm(value, gain_pair[1], bias_pair[1]),
    )


def rotary(field):
    seq_len = field.shape[-3]
    half_rot = ROT // 2
    freqs = 10000.0 ** (-(jnp.arange(half_rot, dtype=jnp.float32) * 2.0 / ROT))
    angles = jnp.arange(seq_len, dtype=jnp.float32)[:, None] * freqs[None, :]
    cosine = jnp.concatenate([jnp.cos(angles), jnp.cos(angles)], -1)[:, None, :]
    sine = jnp.concatenate([jnp.sin(angles), jnp.sin(angles)], -1)[:, None, :]
    turned = field[..., :ROT]
    remain = field[..., ROT:]
    swapped = jnp.concatenate([-turned[..., half_rot:], turned[..., :half_rot]], -1)
    return jnp.concatenate([turned * cosine + swapped * sine, remain], -1)


def adapter_forward(saved_activations, dense_matmul, adapter_first_factor, adapter_second_factor):
    hidden_state = jnp.dot(
        saved_activations, adapter_first_factor, preferred_element_type=jnp.float32
    ).astype(jnp.bfloat16)
    final_result = jnp.dot(saved_activations, dense_matmul, preferred_element_type=jnp.float32)
    final_result = final_result + adapter_scale * jnp.dot(
        hidden_state, adapter_second_factor, preferred_element_type=jnp.float32
    )
    return (final_result, hidden_state)


def adapter_backward(
    gradient_layer_output,
    saved_activations,
    hidden_state,
    dense_matmul,
    adapter_first_factor,
    adapter_second_factor,
):
    gradient_hidden_state = (
        adapter_scale
        * jnp.einsum(
            "hfq,tq->hft",
            gradient_layer_output,
            adapter_second_factor,
            preferred_element_type=jnp.float32,
        )
    ).astype(jnp.bfloat16)
    gradient_feed_normed = adapter_scale * jnp.einsum(
        "rsm,rsn->mn", hidden_state, gradient_layer_output, preferred_element_type=jnp.float32
    )
    gradient_attention_normed = jnp.einsum(
        "rsm,rsk->mk", gradient_hidden_state, saved_activations, preferred_element_type=jnp.float32
    )
    grad_inputs = jnp.einsum(
        "rsn,kn->rsk", gradient_layer_output, dense_matmul, preferred_element_type=jnp.float32
    )
    grad_inputs = grad_inputs + jnp.einsum(
        "efj,lj->efl",
        gradient_hidden_state,
        adapter_first_factor,
        preferred_element_type=jnp.float32,
    )
    return (grad_inputs, gradient_attention_normed, gradient_feed_normed)


def attention_mask(valid_boolean_mask):
    seq_len = valid_boolean_mask.shape[-1]
    positions = jnp.arange(seq_len)
    causal = positions[None, :] <= positions[:, None]
    return causal[None, None] & valid_boolean_mask[:, None, None, :]


def layer_forward(residual, weights, valid_boolean_mask):
    (
        frozen_query_weight,
        frozen_output_weight,
        frozen_up_weight,
        frozen_down_weight,
        query_first_factor,
        query_second_factor,
        output_first_factor,
        output_second_factor,
        up_first_factor,
        up_second_factor,
        down_first_factor,
        down_second_factor,
        gain,
        bias,
    ) = weights
    row_count, seq_len, model_width = residual.shape
    attention_normed = layer_norm(residual, gain[0], bias[0]).astype(jnp.bfloat16)
    feed_normed = layer_norm(residual, gain[1], bias[1]).astype(jnp.bfloat16)
    combined_output, hidden_query_rank = adapter_forward(
        attention_normed, frozen_query_weight, query_first_factor, query_second_factor
    )
    combined_output = combined_output.reshape(row_count, seq_len, 3, HEADS, HEAD_DIM)
    queries = rotary(combined_output[:, :, 0]).astype(jnp.bfloat16)
    key_heads = rotary(combined_output[:, :, 1]).astype(jnp.bfloat16)
    values = combined_output[:, :, 2].astype(jnp.bfloat16)
    allowed = attention_mask(valid_boolean_mask)
    scores = jnp.einsum(
        "rqhd,rkhd->rhqk", queries, key_heads, preferred_element_type=jnp.float32
    ) * HEAD_DIM ** (-0.5)
    scores = jnp.where(allowed, scores, masked_score)
    top_score = jnp.max(scores, axis=-1, keepdims=True)
    expo_score = jnp.exp(scores - top_score)
    exp_total = jnp.sum(expo_score, axis=-1, keepdims=True)
    probability = expo_score / exp_total
    log_total = top_score + jnp.log(exp_total)
    merged_head_values = jnp.einsum(
        "rhqk,rkhd->rqhd",
        probability.astype(jnp.bfloat16),
        values,
        preferred_element_type=jnp.float32,
    )
    merged_head_values = merged_head_values.reshape(row_count, seq_len, model_width).astype(
        jnp.bfloat16
    )
    attention_output, hidden_output_rank = adapter_forward(
        merged_head_values, frozen_output_weight, output_first_factor, output_second_factor
    )
    upward_projection, hidden_up_rank = adapter_forward(
        feed_normed, frozen_up_weight, up_first_factor, up_second_factor
    )
    gelu_output = jax.nn.gelu(upward_projection, approximate=False).astype(jnp.bfloat16)
    feedforward_output, hidden_down_rank = adapter_forward(
        gelu_output, frozen_down_weight, down_first_factor, down_second_factor
    )
    output = residual + (attention_output + feedforward_output)
    squared_values = jnp.stack(
        [
            jnp.sum(residual * residual, -1),
            jnp.sum(attention_output * attention_output, -1),
            jnp.sum(feedforward_output * feedforward_output, -1),
        ],
        -1,
    )
    row_sums = jnp.einsum(
        "nx,nxo->no",
        valid_boolean_mask.astype(jnp.float32),
        squared_values,
        precision=lax.Precision.HIGHEST,
    )
    kept_state = (
        residual,
        queries,
        key_heads,
        values,
        log_total,
        merged_head_values,
        upward_projection,
        hidden_query_rank,
        hidden_output_rank,
        hidden_up_rank,
        hidden_down_rank,
    )
    return (output, kept_state, row_sums)


def layer_backward(gradient_layer_output, kept_state, weights, valid_boolean_mask):
    (
        frozen_query_weight,
        frozen_output_weight,
        frozen_up_weight,
        frozen_down_weight,
        query_first_factor,
        query_second_factor,
        output_first_factor,
        output_second_factor,
        up_first_factor,
        up_second_factor,
        down_first_factor,
        down_second_factor,
        gain,
        bias,
    ) = weights
    (
        residual,
        queries,
        key_heads,
        values,
        log_total,
        merged_head_values,
        upward_projection,
        hidden_query_rank,
        hidden_output_rank,
        hidden_up_rank,
        hidden_down_rank,
    ) = kept_state
    row_count, seq_len, model_width = residual.shape
    (attention_normed, feed_normed), norm_back = jax.vjp(both_norms, residual, gain, bias)
    attention_normed = attention_normed.astype(jnp.bfloat16)
    feed_normed = feed_normed.astype(jnp.bfloat16)
    grad_branch = gradient_layer_output.astype(jnp.bfloat16)
    gelu_output, gelu_back = jax.vjp(partial(jax.nn.gelu, approximate=False), upward_projection)
    gelu_output = gelu_output.astype(jnp.bfloat16)
    gradient_gelu_output, gradient_down_first, gradient_down_second = adapter_backward(
        grad_branch,
        gelu_output,
        hidden_down_rank,
        frozen_down_weight,
        down_first_factor,
        down_second_factor,
    )
    rounded_activated = lax.optimization_barrier(gradient_gelu_output.astype(jnp.bfloat16)).astype(
        jnp.float32
    )
    grad_upper = gelu_back(rounded_activated)[0].astype(jnp.bfloat16)
    gradient_feed_normed, gradient_up_first, gradient_up_second = adapter_backward(
        grad_upper, feed_normed, hidden_up_rank, frozen_up_weight, up_first_factor, up_second_factor
    )
    gradient_mixed_heads, gradient_output_first, gradient_output_second = adapter_backward(
        grad_branch,
        merged_head_values,
        hidden_output_rank,
        frozen_output_weight,
        output_first_factor,
        output_second_factor,
    )
    gradient_mixed_heads = gradient_mixed_heads.astype(jnp.bfloat16).reshape(
        row_count, seq_len, HEADS, HEAD_DIM
    )
    allowed = attention_mask(valid_boolean_mask)
    scale_factor = HEAD_DIM ** (-0.5)
    scores = (
        jnp.einsum("rqhd,rkhd->rhqk", queries, key_heads, preferred_element_type=jnp.float32)
        * scale_factor
    )
    probability = jnp.where(allowed, jnp.exp(scores - log_total), 0.0)
    grad_probs = jnp.einsum(
        "rqhd,rkhd->rhqk", gradient_mixed_heads, values, preferred_element_type=jnp.float32
    )
    grad_values = jnp.einsum(
        "rhqk,rqhd->rkhd",
        probability.astype(jnp.bfloat16),
        gradient_mixed_heads,
        preferred_element_type=jnp.float32,
    )
    grad_scores = probability * (
        grad_probs - jnp.sum(probability * grad_probs, axis=-1, keepdims=True)
    )
    grad_scores = grad_scores.astype(jnp.bfloat16)
    grad_queries = (
        jnp.einsum("rhqk,rkhd->rqhd", grad_scores, key_heads, preferred_element_type=jnp.float32)
        * scale_factor
    )
    grad_keys = (
        jnp.einsum("rhqk,rqhd->rkhd", grad_scores, queries, preferred_element_type=jnp.float32)
        * scale_factor
    )
    rotary_back = jax.vjp(rotary, jnp.zeros(grad_queries.shape, jnp.float32))[1]
    grad_joint = jnp.stack(
        [rotary_back(grad_queries)[0], rotary_back(grad_keys)[0], grad_values], 2
    )
    grad_joint = grad_joint.reshape(row_count, seq_len, 3 * model_width).astype(jnp.bfloat16)
    gradient_attention_normed, gradient_query_first, gradient_query_second = adapter_backward(
        grad_joint,
        attention_normed,
        hidden_query_rank,
        frozen_query_weight,
        query_first_factor,
        query_second_factor,
    )
    grad_residual, grad_gain, grad_bias = norm_back(
        (gradient_attention_normed, gradient_feed_normed)
    )
    layer_grads = (
        gradient_query_first,
        gradient_query_second,
        gradient_output_first,
        gradient_output_second,
        gradient_up_first,
        gradient_up_second,
        gradient_down_first,
        gradient_down_second,
        grad_gain,
        grad_bias,
    )
    return (gradient_layer_output + grad_residual, layer_grads)


def gradient_block(layer_grads, table):
    (
        query_first,
        query_second,
        output_first,
        output_second,
        up_first,
        up_second,
        down_first,
        down_second,
        gain,
        bias,
    ) = layer_grads
    main = jnp.concatenate(
        [query_first, output_first, up_first, down_first, query_second, output_second, up_second, down_second],
        1,
    )
    extra = jnp.concatenate([gain.reshape(1, -1), bias.reshape(1, -1), table.reshape(1, -1)], 1)
    extra = jnp.pad(extra, ((0, 7), (0, main.shape[1] - extra.shape[1])))
    return jnp.concatenate([main, extra], 0)


def unpack_gradients(block):
    offset = 0
    firsts = []
    for width in (1, 1, 1, 4):
        firsts.append(block[:RANK, offset : offset + width * WIDE].astype(jnp.float32).T)
        offset = offset + width * WIDE
    seconds = []
    for width in (3, 1, 4, 1):
        seconds.append(block[:RANK, offset : offset + width * WIDE].astype(jnp.float32))
        offset = offset + width * WIDE
    row = block[RANK].astype(jnp.float32)
    gain = row[: 2 * WIDE].reshape(2, WIDE)
    bias = row[2 * WIDE : 4 * WIDE].reshape(2, WIDE)
    table = row[4 * WIDE : 4 * WIDE + 3 * (DOMAINS + 1)].reshape(3, DOMAINS + 1)
    return [part for pair in zip(firsts, seconds) for part in pair] + [gain, bias, table]


def shards(
    inputs,
    cotangent,
    domain,
    lengths,
    steps_since_reset,
    frozen_query_weight,
    frozen_output_weight,
    frozen_up_weight,
    frozen_down_weight,
    query_adapter_first,
    query_adapter_second,
    output_adapter_first,
    output_adapter_second,
    up_adapter_first,
    up_adapter_second,
    down_adapter_first,
    down_adapter_second,
    layer_norm_gain,
    layer_norm_bias,
):
    core = lax.axis_index("section")
    place = lax.axis_index("dp")
    count = lax.axis_size("dp")
    half = count // 2
    stage = place // half
    low = place % half
    home = core == stage
    masks = [1 << bit for bit in range(half.bit_length() - 1)]
    frozen = (frozen_query_weight, frozen_output_weight, frozen_up_weight, frozen_down_weight)
    trained = (
        query_adapter_first,
        query_adapter_second,
        output_adapter_first,
        output_adapter_second,
        up_adapter_first,
        up_adapter_second,
        down_adapter_first,
        down_adapter_second,
        layer_norm_gain,
        layer_norm_bias,
    )
    local_layers = frozen_query_weight.shape[0]
    rows_dev, seq_len, model_width = inputs.shape
    span = frozen_output_weight.shape[1]

    dense = [
        gather_layer([matrix[layer] for matrix in frozen], core, stage, low, home, count, masks)
        for layer in range(local_layers)
    ]
    to_sibling = [
        ((index // half) * count + index, (1 - index // half) * count + index) for index in range(count)
    ]
    weights = []
    for layer in range(local_layers):
        adapters = tuple(
            jnp.where(home, parameter[layer], both_axes(parameter[layer], to_sibling))
            for parameter in trained
        )
        weights.append(tuple(dense[layer]) + adapters)

    away = [
        ((1 - index // half) * count + index, (index // half) * count + (index ^ half))
        for index in range(count)
    ]
    visiting = both_axes(jnp.where(stage == 0, cotangent, inputs), away)
    facts = jnp.stack([lengths, domain])
    facts = jnp.where(home, facts, both_axes(facts, away))
    group_lengths, group_domain = facts[0], facts[1]
    start = jnp.where(home, inputs, visiting).astype(jnp.float32)
    valid = jnp.arange(seq_len)[None, :] < group_lengths[:, None]
    end_grad = jnp.where(home, cotangent, visiting).astype(jnp.float32)
    end_grad = jnp.where(stage == 1, end_grad * valid[..., None].astype(jnp.float32), 0.0)
    table = (group_domain[:, None] == jnp.arange(DOMAINS)[None, :]).astype(jnp.float32)
    table = jnp.concatenate([table, jnp.ones((rows_dev, 1), jnp.float32)], 1)

    own_table = (domain[:, None] == jnp.arange(DOMAINS)[None, :]).astype(jnp.float32)
    own_table = jnp.concatenate([own_table, jnp.ones((rows_dev, 1), jnp.float32)], 1)
    counts = jnp.sum(own_table * lengths.astype(jnp.float32)[:, None], axis=0)
    for mask in masks + [half]:
        counts = counts + flip_place(counts, mask)

    def stage_forward(residual):
        kept, sums = [], []
        for layer in range(local_layers):
            residual, kept_state, row_sums = layer_forward(residual, weights[layer], valid)
            kept.append(kept_state)
            sums.append(row_sums)
        return residual, kept, sums

    def stage_backward(gradient, kept, section):
        blocks = [None] * local_layers
        for layer in reversed(range(local_layers)):
            gradient, layer_grads = layer_backward(gradient, kept[layer], weights[layer], valid)
            block = gradient_block(layer_grads, tables[layer])
            blocks[layer] = reduce_section(block, section, core, stage, low, count, masks)
        return gradient, blocks

    boundary, _, _ = stage_forward(start)
    boundary = boundary.astype(jnp.bfloat16)
    forward_pairs = [(index, index + half) for index in range(half)]
    received = lax.ppermute(boundary, "dp", forward_pairs)
    entry = jnp.where(stage == 0, start, received.astype(jnp.float32))
    final, kept, sums = stage_forward(entry)
    tables = [
        jnp.einsum("rq,rn->qn", row_sums, table, precision=lax.Precision.HIGHEST) for row_sums in sums
    ]
    final = final.astype(jnp.bfloat16)
    out_pairs = [(count + index + half, index + half) for index in range(half)]
    out_pairs = out_pairs + [(index + half, count + index) for index in range(half)]
    visiting = both_axes(jnp.where(core == 0, final, received), out_pairs)
    section_out = jnp.where(home, jnp.where(stage == 0, boundary, final), visiting)[None]

    gradient, late_blocks = stage_backward(end_grad, kept, 1)
    sent = gradient.astype(jnp.bfloat16)
    came_back = lax.ppermute(sent, "dp", [(after, before) for before, after in forward_pairs])
    gradient, early_blocks = stage_backward(
        jnp.where(stage == 0, came_back.astype(jnp.float32), 0.0), kept, 0
    )
    grad_pairs = [(index, count + index) for index in range(half)]
    grad_pairs = grad_pairs + [(count + index, index + half) for index in range(half)]
    visiting = both_axes(
        jnp.where(core == 0, came_back, gradient.astype(jnp.bfloat16)), grad_pairs
    ).astype(jnp.float32)
    section_grad = jnp.where(
        home, jnp.where(stage == 0, gradient, sent.astype(jnp.float32)), visiting
    )[None]

    unpacked = [
        unpack_gradients(jnp.where(core == 0, early, late))
        for early, late in zip(early_blocks, late_blocks)
    ]
    stacked = [jnp.stack([layer[index] for layer in unpacked]) for index in range(11)]
    table_sums = stacked.pop()
    bounded = jnp.concatenate([jnp.maximum(counts[:DOMAINS], 1.0), counts[DOMAINS:]])
    rms_stats = jnp.sqrt(table_sums / (bounded * model_width))
    rate = peak_rate * (steps_since_reset[0].astype(jnp.float32) + 1.0) / WARM

    def merge_adapter(matrix, first_factor, second_factor, first_grad, second_grad):
        row_span = matrix.shape[1]
        first_rows = lax.dynamic_slice_in_dim(
            first_factor, place * row_span, row_span, 1
        ).astype(jnp.float32) - rate * lax.dynamic_slice_in_dim(first_grad, place * row_span, row_span, 1)
        new_second = second_factor.astype(jnp.float32) - rate * second_grad
        product = jnp.einsum("lkr,lrn->lkn", first_rows, new_second, precision=lax.Precision.HIGHEST)
        return (matrix.astype(jnp.float32) + adapter_scale * product).astype(jnp.bfloat16)

    folded = [
        merge_adapter(
            frozen[index],
            trained[2 * index],
            trained[2 * index + 1],
            stacked[2 * index],
            stacked[2 * index + 1],
        )
        for index in range(4)
    ]
    return (section_out, section_grad, *stacked, *folded, rms_stats)


def solution(mesh):
    across = P("dp", None, None)
    copied = P("section", None, None)
    split = P("section", "dp", None)
    wide = P("section", "dp", None, None)
    return jax.shard_map(
        shards,
        mesh=mesh,
        in_specs=(across, across, P("dp"), P("dp"), P()) + (split,) * 4 + (copied,) * 10,
        out_specs=(wide, wide) + (copied,) * 10 + (split,) * 4 + (copied,),
        check_vma=False,
    )
```

time: 1710 us -> 1380 us (0.81)
  waiting for transfers between devices: 983 us -> 282 us
  other arithmetic: 104 us -> 347 us
  starting transfers between devices: 7.05 us -> 250 us
  matrix products: 394 us -> 306 us
  Pallas kernels: 0 us -> 47.7 us
  blocking collectives: 39 us -> 0 us
  local copies, waits for them, and re-layouts: 142 us -> 120 us
    all_gather x4 -> x0, waiting for transfers between devices: 577 us -> none  [the longest x1 180 us: shards(): lax.all_gather(frozen_down_weight, 'dp', axis=1, tiled=True)]
    psum x1 -> x0, waiting for transfers between devices: 403 us -> none  [shards(): lax.psum((flat_grads, domain_sums, all_sums, domain_counts, all_count), '...]
    ppermute x4 -> x174, waiting for transfers between devices: 0.01 us -> 282 us  [the longest x124 251 us: flip_place(): lax.ppermute(value, 'dp', [(place, place ^ mask) for place in range(count)])]
    ppermute x4 -> x174, starting transfers between devices: 6.86 us -> 250 us  [the longest x124 162 us: flip_place(): lax.ppermute(value, 'dp', [(place, place ^ mask) for place in range(count)])]
    select_n x3 -> x104, other arithmetic: 1.31 us -> 108 us  [the longest x2 82.5 us: shards(): jnp.where(core == 0, early, late)]
    concatenate x8 -> x70, other arithmetic: 0.38 us -> 89.3 us  [the longest x4 34.9 us: reduce_section(): here = jnp.concatenate(whole, 0)]
    convert_element_type x8 -> x49, other arithmetic: 1.8 us -> 67.5 us  [the longest x3 33.1 us: layer_forward(): jax.nn.gelu(upward_projection, approximate=False).astype(jnp.bfloat16)]
    pallas_call x0 -> x4, Pallas kernels: none -> 47.7 us  [assemble(): pl.pallas_call(assemble_kernel, out_shape=[jax.ShapeDtypeStruct(shape, jn...]
  transfers between devices with their start and end apart: 9 -> 174, of which waited for: 5 -> 53; matrix products, arithmetic and copies ran while one was open for 6% -> 22% of each run, Pallas kernels for 0% -> 3%
where the time goes in v1:
time: 1380 us; the launch traced here: 1360 us
  other arithmetic  347 us (25%)
  matrix products  306 us (22%)
  waiting for transfers between devices  282 us (20%)
  starting transfers between devices  250 us (18%)
  local copies, waits for them, and re-layouts  120 us (9%)
  Pallas kernels  47.7 us (3%)
    ppermute x124, waiting for transfers between devices, flip_place(): lax.ppermute(value, 'dp', [(place, place ^ mask) for place in range(count)])  251 us
    ppermute x124, starting transfers between devices, flip_place(): lax.ppermute(value, 'dp', [(place, place ^ mask) for place in range(count)])  162 us
    select_n x2, other arithmetic, shards(): jnp.where(core == 0, early, late)  82.5 us
    dot_general x16, matrix products, adapter_forward(): jnp.dot(saved_activations, dense_matmul, preferred_element_type=jnp.float32)  77.4 us
    dot_general x16, matrix products, adapter_backward(): jnp.einsum('rsn,kn->rsk', gradient_layer_output, dense_matmul, preferred_...  67.7 us
    ppermute x28, starting transfers between devices, both_axes(): return lax.ppermute(value, ('section', 'dp'), pairs)  64.8 us
    pallas_call x4, Pallas kernels, assemble(): pl.pallas_call(assemble_kernel, out_shape=[jax.ShapeDtypeStruct(shape, jn...  47.7 us
    unnamed x948, local copies, waits for them, and re-layouts  47.5 us
  transfers between devices with their start and end apart: 174, of which 53 were waited for; matrix products, arithmetic and copies ran while one was open for 22% of the time, Pallas kernels for 3%

profile of v1, /device:TPU:26, one launch (start us, length us, event | category | flops | bytes accessed | tf_op | source)
XLA Modules:
  0.0 1362.9 jit_solution(14423415126888547163)
XLA Ops:
  111.4 15.2 %collective-permute-start.4 = (bf16[6,64,1024]{2,1,0:T(8,128)(2,1)S(1)}, bf16[6,64,1024]{2,1,0:T(8,128)(2,1)S(1)}, u32[]{:S(2)}, u32[]{:S(2)}) collective-permute-start(bf16[6,64,1024]{2,1,0:T(8,128)(2,1)S(1)} %get-tuple-element.175), channel_id=1, source_target_pairs={{16,8},{17,9},{18,10},{19,11},{20,12},{21,13},{22,14},{23,15},{8,1... | collective-permute-start | bytes 2359304 | tf_op jit(solution)/shard_map/ppermute | solution.py:27
  129.1 13.6 collective-permute-start.23
  169.4 13.6 %collective-permute-done.41 = bf16[6,64,1024]{2,1,0:T(8,128)(2,1)S(1)} collective-permute-done((bf16[6,64,1024]{2,1,0:T(8,128)(2,1)S(1)}, bf16[6,64,1024]{2,1,0:T(8,128)(2,1)S(1)}, u32[]{:S(2)}, u32[]{:S(2)}) %collective-permute-start.41) | collective-permute-done | bytes 786464 | tf_op jit(solution)/shard_map/ppermute | solution.py:27
  191.1 8.2 collective-permute-done.8
  211.3 8.9 collective-permute-done.58
  237.2 25.2 %collective-permute-done.46 = bf16[2,2,64,1024]{3,2,1,0:T(8,128)(2,1)S(1)} collective-permute-done((bf16[2,2,64,1024]{3,2,1,0:T(8,128)(2,1)S(1)}, bf16[2,2,64,1024]{3,2,1,0:T(8,128)(2,1)S(1)}, u32[]{:S(2)}, u32[]{:S(2)}) %collective-permute-start.46) | collective-permute-done | bytes 524320 | tf_op jit(solution)/shard_map/ppermute | solution.py:36
  274.7 13.8 %collective-permute-done.56 = bf16[4,2,64,1024]{3,2,1,0:T(8,128)(2,1)S(1)} collective-permute-done((bf16[4,2,64,1024]{3,2,1,0:T(8,128)(2,1)S(1)}, bf16[4,2,64,1024]{3,2,1,0:T(8,128)(2,1)S(1)}, u32[]{:S(2)}, u32[]{:S(2)}) %collective-permute-start.56) | collective-permute-done | bytes 1048608 | tf_op jit(solution)/shard_map/ppermute | solution.py:36
  300.6 10.5 collective-permute-done.7
  313.7 13.6 collective-permute-done.44
  343.5 9.5 collective-permute-done.50
  375.3 12.1 assemble.4
  388.0 11.9 assemble.6
  400.2 11.9 assemble.5
  427.2 10.3 fusion.409
  445.6 10.6 fusion.138
  471.7 11.9 assemble.7
  503.7 8.3 fusion.410
  512.1 10.5 fusion.141
  548.2 8.6 fusion.77
  556.8 14.3 %collective-permute-done.74 = bf16[2,128,1024]{2,1,0:T(8,128)(2,1)S(1)} collective-permute-done((bf16[2,128,1024]{2,1,0:T(8,128)(2,1)}, bf16[2,128,1024]{2,1,0:T(8,128)(2,1)S(1)}, u32[]{:S(2)}, u32[]{:S(2)}) %collective-permute-start.74) | collective-permute-done | bytes 524320 | tf_op jit(solution)/shard_map/ppermute | solution.py:628
  592.6 12.0 multiply_convert_fusion.1
  652.4 11.3 fusion.113
  838.6 7.9 select_maximum_fusion.1
  857.4 7.8 select_maximum_fusion
  1081.9 7.9 collective-permute-done.151
  1098.6 10.0 collective-permute-done.136
  1186.3 8.5 maximum_maximum_fusion.2
  1198.1 8.5 maximum_maximum_fusion.3
  1210.2 8.5 maximum_maximum_fusion
  1220.4 9.5 maximum_maximum_fusion.1
  1234.7 41.0 %maximum_select_fusion.1 = bf16[136,16384]{1,0:T(8,128)(2,1)S(1)} fusion(bf16[136,8192]{1,0:T(8,128)(2,1)S(1)} %collective-permute-done.146, bf16[40,4096]{1,0:T(8,128)(2,1)S(1)} %get-tuple-element.299, bf16[40,4096]{1,0:T(8,128)(2,1)S(1)} %get-tuple-element.298, bf16[48,4096]{1,0:T(8,128)(2,1)S(1)} %get-tuple-element.277, ...), kind=kLoop, calls=%fused_computation.119 | loop fusion | flops 64618496 | bytes 13369345 | tf_op jit(solution)/shard_map/jit(_where)/select_n | solution.py:656
  1276.7 41.5 %maximum_select_fusion = bf16[136,16384]{1,0:T(8,128)(2,1)S(1)} fusion(bf16[136,8192]{1,0:T(8,128)(2,1)S(1)} %collective-permute-done.100, bf16[40,4096]{1,0:T(8,128)(2,1)S(1)} %get-tuple-element.295, bf16[40,4096]{1,0:T(8,128)(2,1)S(1)} %get-tuple-element.294, bf16[48,4096]{1,0:T(8,128)(2,1)S(1)} %get-tuple-element.269, ...), kind=kLoop, calls=%fused_computation.118 | loop fusion | flops 64618496 | bytes 13369345 | tf_op jit(solution)/shard_map/jit(_where)/select_n | solution.py:656
  (1877 shorter events, 936.8 us)
Async XLA Ops:
  2.1 70.9 %collective-permute-start.39 = (f32[2,1024]{1,0:T(2,128)}, f32[2,1024]{1,0:T(2,128)}, u32[]{:S(2)}, u32[]{:S(2)}) collective-permute-start(f32[2,1024]{1,0:T(2,128)} %get-tuple-element.409), channel_id=1, source_target_pairs={{0,16},{1,17},{2,18},{3,19},{4,20},{5,21},{6,22},{7,23},{24,8},{25... | collective-permute-start | bytes 24584 | tf_op jit(solution)/shard_map/ppermute | solution.py:27
  3.4 70.9 %collective-permute-start.2 = (f32[2,1024]{1,0:T(2,128)}, f32[2,1024]{1,0:T(2,128)}, u32[]{:S(2)}, u32[]{:S(2)}) collective-permute-start(f32[2,1024]{1,0:T(2,128)} %get-tuple-element.410), channel_id=1, source_target_pairs={{0,16},{1,17},{2,18},{3,19},{4,20},{5,21},{6,22},{7,23},{24,8},{25... | collective-permute-start | bytes 24584 | tf_op jit(solution)/shard_map/ppermute | solution.py:27
  6.1 69.6 %collective-permute-start.1 = (f32[2,1024]{1,0:T(2,128)}, f32[2,1024]{1,0:T(2,128)}, u32[]{:S(2)}, u32[]{:S(2)}) collective-permute-start(f32[2,1024]{1,0:T(2,128)} %get-tuple-element.406), channel_id=1, source_target_pairs={{0,16},{1,17},{2,18},{3,19},{4,20},{5,21},{6,22},{7,23},{24,8},{25... | collective-permute-start | bytes 24584 | tf_op jit(solution)/shard_map/ppermute | solution.py:27
  7.3 69.6 %collective-permute-start.38 = (f32[2,1024]{1,0:T(2,128)}, f32[2,1024]{1,0:T(2,128)}, u32[]{:S(2)}, u32[]{:S(2)}) collective-permute-start(f32[2,1024]{1,0:T(2,128)} %get-tuple-element.405), channel_id=1, source_target_pairs={{0,16},{1,17},{2,18},{3,19},{4,20},{5,21},{6,22},{7,23},{24,8},{25... | collective-permute-start | bytes 24584 | tf_op jit(solution)/shard_map/ppermute | solution.py:27
  9.9 44.2 %collective-permute-start.31 = (s32[2,2]{1,0:T(2,128)}, s32[2,2]{1,0:T(2,128)}, u32[]{:S(2)}, u32[]{:S(2)}) collective-permute-start(s32[2,2]{1,0:T(2,128)} %pad_add_fusion.8), channel_id=1, source_target_pairs={{16,8},{17,9},{18,10},{19,11},{20,12},{21,13},{22,14},{23,15},{8,1... | collective-permute-start | bytes 56 | tf_op jit(solution)/shard_map/ppermute | solution.py:27
  69.2 38.7 %collective-permute-start = (bf16[2,128,1024]{2,1,0:T(8,128)(2,1)S(1)}, bf16[2,128,1024]{2,1,0:T(8,128)(2,1)S(1)}, u32[]{:S(2)}, u32[]{:S(2)}) collective-permute-start(bf16[2,128,1024]{2,1,0:T(8,128)(2,1)S(1)} %broadcast_select_fusion.15), channel_id=1, source_target_pairs={{16,8},{17,9},{18,10},{19,11},{20,12},{21,13},{22,14},{23,15},{8,1... | collective-permute-start | bytes 1572872 | tf_op jit(solution)/shard_map/ppermute | solution.py:27
  99.2 43.4 %collective-permute-start.30 = (bf16[128,3072]{1,0:T(8,128)(2,1)S(1)}, bf16[128,3072]{1,0:T(8,128)(2,1)S(1)}, u32[]{:S(2)}, u32[]{:S(2)}) collective-permute-start(bf16[128,3072]{1,0:T(8,128)(2,1)S(1)} %copy-done.308), channel_id=1, source_target_pairs={{0,16},{1,17},{2,18},{3,19},{4,20},{5,21},{6,22},{7,23},{24,8},{25... | collective-permute-start | bytes 2359304 | tf_op jit(solution)/shard_map/ppermute | solution.py:27
  111.4 51.5 %collective-permute-start.4 = (bf16[6,64,1024]{2,1,0:T(8,128)(2,1)S(1)}, bf16[6,64,1024]{2,1,0:T(8,128)(2,1)S(1)}, u32[]{:S(2)}, u32[]{:S(2)}) collective-permute-start(bf16[6,64,1024]{2,1,0:T(8,128)(2,1)S(1)} %get-tuple-element.175), channel_id=1, source_target_pairs={{16,8},{17,9},{18,10},{19,11},{20,12},{21,13},{22,14},{23,15},{8,1... | collective-permute-start | bytes 2359304 | tf_op jit(solution)/shard_map/ppermute | solution.py:27
  209.0 54.1 %collective-permute-start.19 = (bf16[4,2,64,1024]{3,2,1,0:T(8,128)(2,1)S(1)}, bf16[4,2,64,1024]{3,2,1,0:T(8,128)(2,1)S(1)}, u32[]{:S(2)}, u32[]{:S(2)}) collective-permute-start(bf16[4,2,64,1024]{3,2,1,0:T(8,128)(2,1)S(1)} %pad_maximum_fusion.19), channel_id=1, source_target_pairs={{0,4},{1,5},{2,6},{3,7},{4,0},{5,1},{6,2},{7,3},{8,12},{9,13},{10,... | collective-permute-start | bytes 3145736 | tf_op jit(solution)/shard_map/ppermute | solution.py:36
  222.3 40.1 %collective-permute-start.46 = (bf16[2,2,64,1024]{3,2,1,0:T(8,128)(2,1)S(1)}, bf16[2,2,64,1024]{3,2,1,0:T(8,128)(2,1)S(1)}, u32[]{:S(2)}, u32[]{:S(2)}) collective-permute-start(bf16[2,2,64,1024]{3,2,1,0:T(8,128)(2,1)S(1)} %pad_maximum_fusion.35), channel_id=1, source_target_pairs={{0,4},{1,5},{2,6},{3,7},{4,0},{5,1},{6,2},{7,3},{8,12},{9,13},{10,... | collective-permute-start | bytes 1572872 | tf_op jit(solution)/shard_map/ppermute | solution.py:36
  235.0 36.5 %collective-permute-start.22 = (bf16[4,2,64,1024]{3,2,1,0:T(8,128)(2,1)S(1)}, bf16[4,2,64,1024]{3,2,1,0:T(8,128)(2,1)S(1)}, u32[]{:S(2)}, u32[]{:S(2)}) collective-permute-start(bf16[4,2,64,1024]{3,2,1,0:T(8,128)(2,1)S(1)} %pad_maximum_fusion.20), channel_id=1, source_target_pairs={{0,1},{1,0},{2,3},{3,2},{4,5},{5,4},{6,7},{7,6},{8,9},{9,8},{10,11... | collective-permute-start | bytes 3145736 | tf_op jit(solution)/shard_map/ppermute | solution.py:36
  235.6 37.8 %collective-permute-start.25 = (bf16[4,2,64,1024]{3,2,1,0:T(8,128)(2,1)S(1)}, bf16[4,2,64,1024]{3,2,1,0:T(8,128)(2,1)S(1)}, u32[]{:S(2)}, u32[]{:S(2)}) collective-permute-start(bf16[4,2,64,1024]{3,2,1,0:T(8,128)(2,1)S(1)} %pad_maximum_fusion.21), channel_id=1, source_target_pairs={{0,2},{1,3},{2,0},{3,1},{4,6},{5,7},{6,4},{7,5},{8,10},{9,11},{10,... | collective-permute-start | bytes 3145736 | tf_op jit(solution)/shard_map/ppermute | solution.py:36
  271.5 39.6 %collective-permute-start.7 = (bf16[4,2,64,1024]{3,2,1,0:T(8,128)(2,1)}, bf16[4,2,64,1024]{3,2,1,0:T(8,128)(2,1)}, u32[]{:S(2)}, u32[]{:S(2)}) collective-permute-start(bf16[4,2,64,1024]{3,2,1,0:T(8,128)(2,1)} %pad_maximum_fusion.16), channel_id=1, source_target_pairs={{0,4},{1,5},{2,6},{3,7},{4,0},{5,1},{6,2},{7,3},{8,12},{9,13},{10,... | collective-permute-start | bytes 3145736 | tf_op jit(solution)/shard_map/ppermute | solution.py:36
  273.4 39.8 %collective-permute-start.10 = (bf16[4,2,64,1024]{3,2,1,0:T(8,128)(2,1)}, bf16[4,2,64,1024]{3,2,1,0:T(8,128)(2,1)}, u32[]{:S(2)}, u32[]{:S(2)}) collective-permute-start(bf16[4,2,64,1024]{3,2,1,0:T(8,128)(2,1)} %pad_maximum_fusion.17), channel_id=1, source_target_pairs={{0,1},{1,0},{2,3},{3,2},{4,5},{5,4},{6,7},{7,6},{8,9},{9,8},{10,11... | collective-permute-start | bytes 3145736 | tf_op jit(solution)/shard_map/ppermute | solution.py:36
  290.6 36.7 %collective-permute-start.44 = (bf16[4,2,64,1024]{3,2,1,0:T(8,128)(2,1)}, bf16[4,2,64,1024]{3,2,1,0:T(8,128)(2,1)}, u32[]{:S(2)}, u32[]{:S(2)}) collective-permute-start(bf16[4,2,64,1024]{3,2,1,0:T(8,128)(2,1)} %pad_maximum_fusion.22), channel_id=1, source_target_pairs={{0,4},{1,5},{2,6},{3,7},{4,0},{5,1},{6,2},{7,3},{8,12},{9,13},{10,... | collective-permute-start | bytes 3145736 | tf_op jit(solution)/shard_map/ppermute | solution.py:36
  291.6 38.6 %collective-permute-start.47 = (bf16[4,2,64,1024]{3,2,1,0:T(8,128)(2,1)}, bf16[4,2,64,1024]{3,2,1,0:T(8,128)(2,1)}, u32[]{:S(2)}, u32[]{:S(2)}) collective-permute-start(bf16[4,2,64,1024]{3,2,1,0:T(8,128)(2,1)} %pad_maximum_fusion.23), channel_id=1, source_target_pairs={{0,1},{1,0},{2,3},{3,2},{4,5},{5,4},{6,7},{7,6},{8,9},{9,8},{10,11... | collective-permute-start | bytes 3145736 | tf_op jit(solution)/shard_map/ppermute | solution.py:36
  311.1 42.0 %collective-permute-start.26 = (bf16[8,2,64,1024]{3,2,1,0:T(8,128)(2,1)S(1)}, bf16[8,2,64,1024]{3,2,1,0:T(8,128)(2,1)S(1)}, u32[]{:S(2)}, u32[]{:S(2)}) collective-permute-start(bf16[8,2,64,1024]{3,2,1,0:T(8,128)(2,1)S(1)} %pad_maximum_fusion.3.refs_0_), channel_id=1, source_target_pairs={{0,16},{16,0},{1,17},{17,1},{2,18},{18,2},{3,19},{19,3},{4,20},{20... | collective-permute-start | bytes 6291464 | tf_op jit(solution)/shard_map/ppermute | solution.py:31
  313.2 44.8 %collective-permute-start.27 = (bf16[8,2,64,1024]{3,2,1,0:T(8,128)(2,1)S(1)}, bf16[8,2,64,1024]{3,2,1,0:T(8,128)(2,1)S(1)}, u32[]{:S(2)}, u32[]{:S(2)}) collective-permute-start(bf16[8,2,64,1024]{3,2,1,0:T(8,128)(2,1)S(1)} %pad_maximum_fusion.4.refs_1_), channel_id=1, source_target_pairs={{0,16},{16,0},{1,17},{17,1},{2,18},{18,2},{3,19},{19,3},{4,20},{20... | collective-permute-start | bytes 6291464 | tf_op jit(solution)/shard_map/ppermute | solution.py:31
  313.2 45.0 %collective-permute-start.28 = (bf16[8,2,64,1024]{3,2,1,0:T(8,128)(2,1)S(1)}, bf16[8,2,64,1024]{3,2,1,0:T(8,128)(2,1)S(1)}, u32[]{:S(2)}, u32[]{:S(2)}) collective-permute-start(bf16[8,2,64,1024]{3,2,1,0:T(8,128)(2,1)S(1)} %pad_maximum_fusion.5.refs_2_), channel_id=1, source_target_pairs={{0,16},{16,0},{1,17},{17,1},{2,18},{18,2},{3,19},{19,3},{4,20},{20... | collective-permute-start | bytes 6291464 | tf_op jit(solution)/shard_map/ppermute | solution.py:31
  358.0 41.8 %collective-permute-start.14 = (bf16[8,2,64,1024]{3,2,1,0:T(8,128)(2,1)}, bf16[8,2,64,1024]{3,2,1,0:T(8,128)(2,1)}, u32[]{:S(2)}, u32[]{:S(2)}) collective-permute-start(bf16[8,2,64,1024]{3,2,1,0:T(8,128)(2,1)} %pad_maximum_fusion.refs_0_), channel_id=1, source_target_pairs={{0,16},{16,0},{1,17},{17,1},{2,18},{18,2},{3,19},{19,3},{4,20},{20... | collective-permute-start | bytes 6291464 | tf_op jit(solution)/shard_map/ppermute | solution.py:31
  358.2 42.1 %collective-permute-start.15 = (bf16[8,2,64,1024]{3,2,1,0:T(8,128)(2,1)}, bf16[8,2,64,1024]{3,2,1,0:T(8,128)(2,1)}, u32[]{:S(2)}, u32[]{:S(2)}) collective-permute-start(bf16[8,2,64,1024]{3,2,1,0:T(8,128)(2,1)} %pad_maximum_fusion.1.refs_1_), channel_id=1, source_target_pairs={{0,16},{16,0},{1,17},{17,1},{2,18},{18,2},{3,19},{19,3},{4,20},{20... | collective-permute-start | bytes 6291464 | tf_op jit(solution)/shard_map/ppermute | solution.py:31
  358.5 41.7 %collective-permute-start.16 = (bf16[8,2,64,1024]{3,2,1,0:T(8,128)(2,1)}, bf16[8,2,64,1024]{3,2,1,0:T(8,128)(2,1)}, u32[]{:S(2)}, u32[]{:S(2)}) collective-permute-start(bf16[8,2,64,1024]{3,2,1,0:T(8,128)(2,1)} %pad_maximum_fusion.2.refs_2_), channel_id=1, source_target_pairs={{0,16},{16,0},{1,17},{17,1},{2,18},{18,2},{3,19},{19,3},{4,20},{20... | collective-permute-start | bytes 6291464 | tf_op jit(solution)/shard_map/ppermute | solution.py:31
  387.4 84.3 %collective-permute-start.51 = (bf16[8,2,64,1024]{3,2,1,0:T(8,128)(2,1)}, bf16[8,2,64,1024]{3,2,1,0:T(8,128)(2,1)}, u32[]{:S(2)}, u32[]{:S(2)}) collective-permute-start(bf16[8,2,64,1024]{3,2,1,0:T(8,128)(2,1)} %pad_maximum_fusion.6.refs_0_), channel_id=1, source_target_pairs={{0,16},{16,0},{1,17},{17,1},{2,18},{18,2},{3,19},{19,3},{4,20},{20... | collective-permute-start | bytes 6291464 | tf_op jit(solution)/shard_map/ppermute | solution.py:31
  387.8 83.9 %collective-permute-start.52 = (bf16[8,2,64,1024]{3,2,1,0:T(8,128)(2,1)}, bf16[8,2,64,1024]{3,2,1,0:T(8,128)(2,1)}, u32[]{:S(2)}, u32[]{:S(2)}) collective-permute-start(bf16[8,2,64,1024]{3,2,1,0:T(8,128)(2,1)} %pad_maximum_fusion.7.refs_1_), channel_id=1, source_target_pairs={{0,16},{16,0},{1,17},{17,1},{2,18},{18,2},{3,19},{19,3},{4,20},{20... | collective-permute-start | bytes 6291464 | tf_op jit(solution)/shard_map/ppermute | solution.py:31
  399.9 71.8 %collective-permute-start.53 = (bf16[8,2,64,1024]{3,2,1,0:T(8,128)(2,1)}, bf16[8,2,64,1024]{3,2,1,0:T(8,128)(2,1)}, u32[]{:S(2)}, u32[]{:S(2)}) collective-permute-start(bf16[8,2,64,1024]{3,2,1,0:T(8,128)(2,1)} %pad_maximum_fusion.8.refs_2_), channel_id=1, source_target_pairs={{0,16},{16,0},{1,17},{17,1},{2,18},{18,2},{3,19},{19,3},{4,20},{20... | collective-permute-start | bytes 6291464 | tf_op jit(solution)/shard_map/ppermute | solution.py:31
  1089.8 52.5 %collective-permute-start.144 = (bf16[40,2048]{1,0:T(8,128)(2,1)S(1)}, bf16[40,2048]{1,0:T(8,128)(2,1)S(1)}, u32[]{:S(2)}, u32[]{:S(2)}) collective-permute-start(bf16[40,2048]{1,0:T(8,128)(2,1)S(1)} %pad_maximum_fusion.66), channel_id=1, source_target_pairs={{0,1},{1,0},{2,3},{3,2},{4,5},{5,4},{6,7},{7,6},{8,9},{9,8},{10,11... | collective-permute-start | bytes 491528 | tf_op jit(solution)/shard_map/ppermute | solution.py:36
  1091.9 52.0 %collective-permute-start.167 = (bf16[40,2048]{1,0:T(8,128)(2,1)S(1)}, bf16[40,2048]{1,0:T(8,128)(2,1)S(1)}, u32[]{:S(2)}, u32[]{:S(2)}) collective-permute-start(bf16[40,2048]{1,0:T(8,128)(2,1)S(1)} %pad_maximum_fusion.67), channel_id=1, source_target_pairs={{0,1},{1,0},{2,3},{3,2},{4,5},{5,4},{6,7},{7,6},{8,9},{9,8},{10,11... | collective-permute-start | bytes 491528 | tf_op jit(solution)/shard_map/ppermute | solution.py:36
  1094.0 52.1 %collective-permute-start.98 = (bf16[40,2048]{1,0:T(8,128)(2,1)S(1)}, bf16[40,2048]{1,0:T(8,128)(2,1)S(1)}, u32[]{:S(2)}, u32[]{:S(2)}) collective-permute-start(bf16[40,2048]{1,0:T(8,128)(2,1)S(1)} %pad_maximum_fusion.64), channel_id=1, source_target_pairs={{0,1},{1,0},{2,3},{3,2},{4,5},{5,4},{6,7},{7,6},{8,9},{9,8},{10,11... | collective-permute-start | bytes 491528 | tf_op jit(solution)/shard_map/ppermute | solution.py:36
  1096.1 50.7 %collective-permute-start.121 = (bf16[40,2048]{1,0:T(8,128)(2,1)S(1)}, bf16[40,2048]{1,0:T(8,128)(2,1)S(1)}, u32[]{:S(2)}, u32[]{:S(2)}) collective-permute-start(bf16[40,2048]{1,0:T(8,128)(2,1)S(1)} %pad_maximum_fusion.65), channel_id=1, source_target_pairs={{0,1},{1,0},{2,3},{3,2},{4,5},{5,4},{6,7},{7,6},{8,9},{9,8},{10,11... | collective-permute-start | bytes 491528 | tf_op jit(solution)/shard_map/ppermute | solution.py:36
  1196.5 38.2 %collective-permute-start.146 = (bf16[136,8192]{1,0:T(8,128)(2,1)S(1)}, bf16[136,8192]{1,0:T(8,128)(2,1)S(1)}, u32[]{:S(2)}, u32[]{:S(2)}) collective-permute-start(bf16[136,8192]{1,0:T(8,128)(2,1)S(1)} %maximum_maximum_fusion.2), channel_id=1, source_target_pairs={{16,0},{17,1},{18,2},{19,3},{20,4},{21,5},{22,6},{23,7},{24,8},{25... | collective-permute-start | bytes 6684680 | tf_op jit(solution)/shard_map/ppermute | solution.py:196
  1218.7 58.0 %collective-permute-start.100 = (bf16[136,8192]{1,0:T(8,128)(2,1)S(1)}, bf16[136,8192]{1,0:T(8,128)(2,1)S(1)}, u32[]{:S(2)}, u32[]{:S(2)}) collective-permute-start(bf16[136,8192]{1,0:T(8,128)(2,1)S(1)} %maximum_maximum_fusion), channel_id=1, source_target_pairs={{16,0},{17,1},{18,2},{19,3},{20,4},{21,5},{22,6},{23,7},{24,8},{25... | collective-permute-start | bytes 6684680 | tf_op jit(solution)/shard_map/ppermute | solution.py:196
  1229.8 46.9 %collective-permute-start.123 = (bf16[136,8192]{1,0:T(8,128)(2,1)}, bf16[136,8192]{1,0:T(8,128)(2,1)}, u32[]{:S(2)}, u32[]{:S(2)}) collective-permute-start(bf16[136,8192]{1,0:T(8,128)(2,1)} %maximum_maximum_fusion.1), channel_id=1, source_target_pairs={{0,16},{1,17},{2,18},{3,19},{4,20},{5,21},{6,22},{7,23},{8,24},{9,... | collective-permute-start | bytes 6684680 | tf_op jit(solution)/shard_map/ppermute | solution.py:196
  (600 other events, 8187.8 us)

commit v2 on v1

v2 whole, which is shorter than its diff:
```python
from functools import partial

import jax
import jax.numpy as jnp
from jax import lax
from jax.experimental import pallas as pl
from jax.experimental.pallas import tpu as pltpu
from jax.sharding import PartitionSpec as P

HEADS = 16
HEAD_DIM = 64
ROT = 16
DOMAINS = 16
WARM = 50
RANK = 128
WIDE = 1024
UNITS = 12
HALF_UNITS = 6

adapter_scale = 0.5
norm_eps = 1e-05
peak_rate = 0.0002
masked_score = -1e30


def both_axes(value, pairs):
    return lax.ppermute(value, ("section", "dp"), pairs)


def tie(value, *others):
    return lax.optimization_barrier((value, others))[0]


def flip_place(value, mask):
    count = lax.axis_size("dp")
    return lax.ppermute(value, "dp", [(place, place ^ mask) for place in range(count)])


def flip_core(value):
    return lax.ppermute(value, "section", [(0, 1), (1, 0)])


def split_units(matrices):
    query, output, upper, down = matrices
    rows = output.shape[0]
    return [
        query[:, :WIDE],
        query[:, WIDE : 2 * WIDE],
        query[:, 2 * WIDE :],
        output,
        upper[:, :WIDE],
        upper[:, WIDE : 2 * WIDE],
        upper[:, 2 * WIDE : 3 * WIDE],
        upper[:, 3 * WIDE :],
        down[:rows],
        down[rows : 2 * rows],
        down[2 * rows : 3 * rows],
        down[3 * rows :],
    ]


def rotations(masks):
    return [[masks[(start + index) % len(masks)] for index in range(len(masks))] for start in range(3)]


def assemble_kernel(info_ref, *refs):
    mine, theirs, outs = refs[:3], refs[3:6], refs[-4:]
    query_out, output_out, upper_out, down_out = outs
    rows = output_out.shape[0]

    def write(first, second):
        query_out[:, :WIDE] = first[0][0, 0]
        query_out[:, WIDE : 2 * WIDE] = first[0][0, 1]
        query_out[:, 2 * WIDE :] = first[1][0, 0]
        output_out[...] = first[1][0, 1]
        upper_out[:, :WIDE] = first[2][0, 0]
        upper_out[:, WIDE : 2 * WIDE] = first[2][0, 1]
        upper_out[:, 2 * WIDE : 3 * WIDE] = second[0][0, 0]
        upper_out[:, 3 * WIDE :] = second[0][0, 1]
        down_out[:rows] = second[1][0, 0]
        down_out[rows : 2 * rows] = second[1][0, 1]
        down_out[2 * rows : 3 * rows] = second[2][0, 0]
        down_out[3 * rows :] = second[2][0, 1]

    @pl.when(info_ref[0, 0] == 0)
    def _():
        write(mine, theirs)

    @pl.when(info_ref[0, 0] != 0)
    def _():
        write(theirs, mine)


def assemble(info, mine, theirs, rows, count, into):
    blocks = mine[0].shape[0]

    def source(part):
        return pl.BlockSpec((1, 2, rows, WIDE), lambda step, info_ref: (info_ref[2 + part, step], 0, 0, 0))

    def target(height, width):
        return pl.BlockSpec((height, width), lambda step, info_ref: (info_ref[1, step], 0))

    total = rows * count
    shapes = [(total, 3 * WIDE), (total, WIDE), (total, 4 * WIDE), (4 * total, WIDE)]
    extra = [] if into is None else list(into)
    size = 2 * 2 * UNITS * rows * WIDE * blocks
    return pl.pallas_call(
        assemble_kernel,
        out_shape=[jax.ShapeDtypeStruct(shape, jnp.bfloat16) for shape in shapes],
        grid_spec=pltpu.PrefetchScalarGridSpec(
            num_scalar_prefetch=1,
            grid=(blocks,),
            in_specs=[source(0), source(1), source(2)] * 2
            + [pl.BlockSpec(memory_space=pl.ANY)] * len(extra),
            out_specs=[target(rows, 3 * WIDE), target(rows, WIDE), target(rows, 4 * WIDE), target(4 * rows, WIDE)],
        ),
        input_output_aliases={7 + index: index for index in range(len(extra))},
        cost_estimate=pl.CostEstimate(flops=0, bytes_accessed=size, transcendentals=0),
        name="assemble",
    )(info, *mine, *theirs, *extra)


class Steps:
    def __init__(self):
        self.ended = ()

    def run(self, *moves):
        values = tuple(value for value, _ in moves)
        if self.ended:
            values = tie(values, *self.ended)
        self.ended = tuple(send(value) for value, (_, send) in zip(values, moves))
        return list(self.ended)


def pick_halves(matrices, stage):
    units = split_units(matrices)
    first, second = jnp.stack(units[:HALF_UNITS]), jnp.stack(units[HALF_UNITS:])
    return jnp.where(stage == 0, first, second), jnp.where(stage == 0, second, first)


class Gather:
    def __init__(self, block, masks):
        self.held = [block[2 * part : 2 * part + 2][None] for part in range(3)]
        self.found = [[0], [0], [0]]
        self.turns = rotations(masks)
        self.step = 0

    def moves(self):
        return [
            (self.held[part], partial(flip_place, mask=self.turns[part][self.step])) for part in range(3)
        ]

    def take(self, there):
        for part in range(3):
            self.held[part] = jnp.concatenate([self.held[part], there[part]], 0)
            mask = self.turns[part][self.step]
            self.found[part] = self.found[part] + [known ^ mask for known in self.found[part]]
        self.step = self.step + 1
        return there[3:]


def part_rows(total):
    first = (total // 3 + 15) // 16 * 16
    return [(0, first), (first, 2 * first), (2 * first, total)]


def side(value, which, axis=1):
    size = value.shape[axis] // 2
    return lax.dynamic_slice_in_dim(value, which * size, size, axis)


def total_of(first, second):
    return (first.astype(jnp.float32) + second.astype(jnp.float32)).astype(jnp.bfloat16)


class Scatter:
    def __init__(self, blocks, section, core, low, count, masks):
        middle = count // 2
        self.inside = [place for place in range(count) if place // middle == section]
        self.swap = [(here * count + place, (1 - here) * count + place) for here in range(2) for place in self.inside]
        self.blocks, self.core, self.low = blocks, core, low
        self.turns = rotations(masks)
        self.step = -1

    def moves(self):
        if self.step < 0:
            return [(side(block, 1 - self.core), partial(both_axes, pairs=self.swap)) for block in self.blocks]
        moves = []
        for slab, turn in zip(self.slabs, self.turns):
            mask = turn[self.step]
            pairs = [(place, place ^ mask) for place in self.inside]
            lower_side = ((self.low & mask) == 0).astype(jnp.int32)
            moves.append((side(slab, lower_side), partial(lax.ppermute, axis_name="dp", perm=pairs)))
        return moves

    def take(self, there):
        if self.step < 0:
            used = len(self.blocks)
            halves = [total_of(side(block, self.core), part) for block, part in zip(self.blocks, there)]
            self.slabs = [
                jnp.concatenate([part[begin:end] for part in halves], 0)
                for begin, end in part_rows(halves[0].shape[0])
            ]
        else:
            used = 3
            for part in range(3):
                upper_side = ((self.low & self.turns[part][self.step]) != 0).astype(jnp.int32)
                self.slabs[part] = total_of(side(self.slabs[part], upper_side), there[part])
        self.step = self.step + 1
        return there[used:]


def scatter_section(blocks, section, core, low, count, masks, steps):
    scatter = Scatter(blocks, section, core, low, count, masks)
    for step in range(len(masks) + 1):
        scatter.take(steps.run(*scatter.moves()))
    return scatter.slabs


class Spread:
    def __init__(self, slabs, section, masks, count, stage):
        middle = count // 2
        self.across = [(place, place ^ middle) for place in range(count) if place // middle == section]
        self.held, self.section, self.here = slabs, section, stage == section
        self.turns = [list(reversed(turn)) for turn in rotations(masks)]
        self.step = -1

    def done(self):
        return self.step > len(self.turns[0])

    def moves(self):
        if self.step < 0:
            return [(slab, partial(lax.ppermute, axis_name="dp", perm=self.across)) for slab in self.held]
        if self.step == len(self.turns[0]):
            pairs = [(1 - self.section, self.section)]
            return [(held, partial(lax.ppermute, axis_name="section", perm=pairs)) for held in self.held]
        return [(held, partial(flip_place, mask=turn[self.step])) for held, turn in zip(self.held, self.turns)]

    def take(self, there):
        if self.step < 0:
            self.held = [jnp.where(self.here, held, part)[None] for held, part in zip(self.held, there)]
        elif self.step == len(self.turns[0]):
            self.theirs = there[:3]
        else:
            self.held = [jnp.concatenate([held, part], 0) for held, part in zip(self.held, there)]
        self.step = self.step + 1
        return there[3:]


def place_kernel(section, layers, info_ref, *refs):
    mine, theirs, olds, outs = refs[:3], refs[3:6], refs[6:-layers], refs[-layers:]

    def write():
        for source, target in ((mine, section), (theirs, 1 - section)):
            begin = 0
            for slab in source:
                rows = slab.shape[1] // layers
                for layer in range(layers):
                    outs[layer][target, begin : begin + rows] = slab[0, layer * rows : (layer + 1) * rows]
                begin = begin + rows

    if not olds:
        write()
    else:
        pl.when(info_ref[0, 0] == section)(write)

        @pl.when(info_ref[0, 0] != section)
        def _():
            for old, out in zip(olds, outs):
                out[...] = old[...]


def place_section(section, core, low, masks, spread, olds, layers):
    mine, theirs = spread.held, spread.theirs
    pieces, _, columns = mine[0].shape
    rows = sum(slab.shape[1] for slab in mine) // layers
    step = jnp.arange(pieces, dtype=jnp.int32)
    info = [jnp.full((pieces,), core, jnp.int32), step]
    for turn in rotations(masks):
        here = sum(((low & mask) != 0).astype(jnp.int32) << (len(masks) - 1 - index) for index, mask in enumerate(turn))
        info.append(step ^ here)
    info = jnp.stack(info)

    def source(part):
        return pl.BlockSpec((1, mine[part].shape[1], columns), lambda step, info_ref: (info_ref[2 + part, step], 0, 0))

    target = pl.BlockSpec((2, rows, columns), lambda step, info_ref: (0, 0, info_ref[1, step]))
    shape = jax.ShapeDtypeStruct((2, rows, pieces * columns), jnp.bfloat16)
    return pl.pallas_call(
        partial(place_kernel, section, layers),
        out_shape=[shape] * layers,
        grid_spec=pltpu.PrefetchScalarGridSpec(
            num_scalar_prefetch=1,
            grid=(pieces,),
            in_specs=[source(0), source(1), source(2)] * 2 + [target] * len(olds or ()),
            out_specs=[target] * layers,
        ),
        cost_estimate=pl.CostEstimate(
            flops=0, bytes_accessed=8 * rows * pieces * columns * layers, transcendentals=0
        ),
        name="place",
    )(info, *mine, *theirs, *(olds or ()))


def finish_kernel(
    info_ref, rate_ref, g0_ref, g1_ref, counts_ref, aq_ref, ao_ref, au_ref, ad_ref, bq_ref, bo_ref, bu_ref, bd_ref,
    wq_ref, wo_ref, wu_ref, wd_ref,
    gaq, gbq, gao, gbo, gau, gbu, gad, gbd, gain_out, bias_out, fq, fo, fu, fd, rms_out,
):
    rate = rate_ref[0]

    def run(g_ref):
        per = g_ref.shape[2] // WIDE

        def columns(index, begin=0, end=RANK):
            return g_ref[index // per, begin:end, (index % per) * WIDE : (index % per + 1) * WIDE].astype(jnp.float32)

        def project(first_at, second_at, a_ref, b_ref, w_ref, ga, gb, folded):
            for index in range(ga.shape[1] // WIDE):
                ga[0, index * WIDE : (index + 1) * WIDE] = columns(first_at + index).T
            span = w_ref.shape[1]
            rows = pl.ds(pl.multiple_of(info_ref[0] * span, span), span)
            new_first = a_ref[0, rows].astype(jnp.float32) - rate * ga[0, rows]
            for index in range(gb.shape[2] // WIDE):
                lanes = slice(index * WIDE, (index + 1) * WIDE)
                grad = columns(second_at + index)
                gb[0, :, lanes] = grad
                new_second = b_ref[0, :, lanes].astype(jnp.float32) - rate * grad
                product = jnp.dot(new_first, new_second, precision=lax.Precision.HIGHEST)
                folded[0, :, lanes] = (
                    w_ref[0, :, lanes].astype(jnp.float32) + adapter_scale * product
                ).astype(jnp.bfloat16)

        project(0, 2, aq_ref, bq_ref, wq_ref, gaq, gbq, fq)
        project(1, 5, ao_ref, bo_ref, wo_ref, gao, gbo, fo)
        project(6, 11, au_ref, bu_ref, wu_ref, gau, gbu, fu)
        project(7, 15, ad_ref, bd_ref, wd_ref, gad, gbd, fd)
        extra = [columns(index, RANK, RANK + 8)[:1] for index in (0, 6, 1, 7)]
        gain_out[0] = jnp.concatenate(extra[:2], 0)
        bias_out[0] = jnp.concatenate(extra[2:], 0)
        sums = columns(8, RANK, RANK + 8)[:1]
        sums = jnp.concatenate([sums[:, 128 * index : 128 * (index + 1)] for index in range(3)], 0)
        rms_out[0] = jnp.sqrt(sums / counts_ref[...])

    @pl.when(pl.program_id(0) == 0)
    def _():
        run(g0_ref)

    @pl.when(pl.program_id(0) != 0)
    def _():
        run(g1_ref)


def finish(place, rate, blocks, counts, trained, frozen):
    firsts, seconds = trained[0:8:2], trained[1:8:2]
    layers = firsts[0].shape[0]

    def layer_block(value):
        return pl.BlockSpec((1,) + value.shape[1:], lambda step, *_: (step, 0, 0))

    shapes = []
    for first, second in zip(firsts, seconds):
        shapes.append(jax.ShapeDtypeStruct(first.shape, jnp.float32))
        shapes.append(jax.ShapeDtypeStruct(second.shape, jnp.float32))
    shapes += [jax.ShapeDtypeStruct((layers, 2, WIDE), jnp.float32)] * 2
    shapes += [jax.ShapeDtypeStruct(matrix.shape, jnp.bfloat16) for matrix in frozen]
    shapes += [jax.ShapeDtypeStruct((layers, 3, 128), jnp.float32)]
    keep = pl.BlockSpec(blocks[0].shape, lambda step, *_: (0, 0, 0))
    return pl.pallas_call(
        finish_kernel,
        out_shape=shapes,
        grid_spec=pltpu.PrefetchScalarGridSpec(
            num_scalar_prefetch=1,
            grid=(layers,),
            in_specs=[pl.BlockSpec(memory_space=pltpu.SMEM), keep, keep, pl.BlockSpec((1, 128), lambda step, *_: (0, 0))]
            + [layer_block(value) for value in firsts + seconds + frozen],
            out_specs=[layer_block(shape) for shape in shapes],
        ),
        compiler_params=pltpu.CompilerParams(vmem_limit_bytes=60 << 20),
        cost_estimate=pl.CostEstimate(flops=1 << 30, bytes_accessed=48 << 20, transcendentals=0),
        name="finish",
    )(place.reshape(1), rate.reshape(1), *blocks, counts, *firsts, *seconds, *frozen)


def mm(left, right):
    return jnp.dot(left, right, preferred_element_type=jnp.float32)


def mm_nt(left, right):
    return lax.dot_general(left, right, (((1,), (1,)), ((), ())), preferred_element_type=jnp.float32)


def mm_tn(left, right):
    return lax.dot_general(left, right, (((0,), (0,)), ((), ())), preferred_element_type=jnp.float32)


def half(value):
    return value.astype(jnp.bfloat16)


def normalize(value):
    centred = value - jnp.mean(value, axis=-1, keepdims=True)
    scale = lax.rsqrt(jnp.mean(centred * centred, axis=-1, keepdims=True) + norm_eps)
    return centred * scale, scale


def norm_gradient(grad, normal, scale, gain):
    pulled = grad * gain
    inner = pulled - jnp.mean(pulled, axis=-1, keepdims=True)
    return scale * (inner - normal * jnp.mean(pulled * normal, axis=-1, keepdims=True))


def rotary_tables(seq_len):
    half_rot = ROT // 2
    lane = jnp.arange(2 * HEAD_DIM) % HEAD_DIM
    freqs = 10000.0 ** (-((lane % half_rot).astype(jnp.float32) * 2.0 / ROT))
    angles = jnp.arange(seq_len, dtype=jnp.float32)[:, None] * freqs[None, :]
    turning = (lane < ROT)[None, :]
    cosine = jnp.where(turning, jnp.cos(angles), 1.0)
    ahead = jnp.where((lane < half_rot)[None, :], -jnp.sin(angles), 0.0)
    behind = jnp.where(turning & (lane >= half_rot)[None, :], jnp.sin(angles), 0.0)
    return jnp.stack([cosine, ahead, behind])


def tile_table(table, rows, columns):
    return jnp.concatenate([jnp.concatenate([table] * (columns // table.shape[1]), 1)] * rows, 0)


def turn(value, cosine, ahead, behind):
    width = value.shape[1]
    step = ROT // 2
    return value * cosine + pltpu.roll(value, width - step, 1) * ahead + pltpu.roll(value, step, 1) * behind


def turn_back(value, cosine, ahead, behind):
    width = value.shape[1]
    step = ROT // 2
    return value * cosine + pltpu.roll(value * ahead, step, 1) + pltpu.roll(value * behind, width - step, 1)


def stack_heads(pair):
    low = lax.broadcasted_iota(jnp.int32, pair.shape, 1) < HEAD_DIM
    zero = jnp.zeros_like(pair)
    return jnp.concatenate([jnp.where(low, pair, zero), jnp.where(low, zero, pair)], 0)


def merge_heads(stacked):
    rows = stacked.shape[0] // 2
    low = lax.broadcasted_iota(jnp.int32, (rows, stacked.shape[1]), 1) < HEAD_DIM
    return jnp.where(low, stacked[:rows], stacked[rows:])


def pair_softmax(query_stack, key_pair, limit):
    scores = mm_nt(query_stack, key_pair) * HEAD_DIM ** (-0.5)
    seq_len = key_pair.shape[0]
    row = lax.broadcasted_iota(jnp.int32, scores.shape, 0) % seq_len
    column = lax.broadcasted_iota(jnp.int32, scores.shape, 1)
    scores = jnp.where((column <= row) & (column < limit), scores, masked_score)
    grown = jnp.exp(scores - jnp.max(scores, axis=-1, keepdims=True))
    return grown / jnp.sum(grown, axis=-1, keepdims=True)


GROUP = 4 * HEAD_DIM
BLOCK = 512


def attention_forward_kernel(
    facts_ref, x_ref, norm_ref, table_ref, first_ref, wq_ref, wk_ref, wv_ref, bq_ref, bk_ref, bv_ref,
    wo_ref, ao_ref, bo_ref,
    q_out, k_out, v_out, mixed_out, midq_out, mido_out, att_out,
    a_scr, mid_scr,
):
    step = pl.program_id(0)
    seqs = x_ref.shape[0] // table_ref.shape[1]
    seq_len = table_ref.shape[1]

    @pl.when(step == 0)
    def _():
        normal, _ = normalize(x_ref[...])
        a_scr[...] = half(normal * norm_ref[0:1] + norm_ref[2:3])
        midq_out[...] = half(mm(a_scr[...], first_ref[...]))
        att_out[...] = jnp.zeros_like(att_out)
        mid_scr[...] = jnp.zeros_like(mid_scr)

    normed = a_scr[...]
    mid = midq_out[...]
    tables = [tile_table(table_ref[index], seqs, GROUP) for index in range(3)]
    query = mm(normed, wq_ref[...]) + adapter_scale * mm(mid, bq_ref[...])
    q_out[...] = half(turn(query, *tables))
    key = mm(normed, wk_ref[...]) + adapter_scale * mm(mid, bk_ref[...])
    k_out[...] = half(turn(key, *tables))
    v_out[...] = half(mm(normed, wv_ref[...]) + adapter_scale * mm(mid, bv_ref[...]))
    for seq in range(seqs):
        rows = slice(seq * seq_len, (seq + 1) * seq_len)
        for pair in range(GROUP // (2 * HEAD_DIM)):
            lanes = slice(pair * 2 * HEAD_DIM, (pair + 1) * 2 * HEAD_DIM)
            probability = pair_softmax(stack_heads(q_out[rows, lanes]), k_out[rows, lanes], facts_ref[0, seq])
            mixed_out[rows, lanes] = half(merge_heads(mm(half(probability), v_out[rows, lanes])))
    mixed = mixed_out[...]
    att_out[...] += mm(mixed, wo_ref[...])
    mid_scr[...] += mm(mixed, ao_ref[...])

    @pl.when(step == pl.num_programs(0) - 1)
    def _():
        mido_out[...] = half(mid_scr[...])
        att_out[...] += adapter_scale * mm(mido_out[...], bo_ref[...])


def whole(*shape):
    return pl.BlockSpec(shape, lambda step, facts_ref: (0,) * len(shape))


def fixed(height, width, down=0, right=0):
    return pl.BlockSpec((height, width), lambda step, facts_ref: (down, right))


def column_block(height, width, offset=0):
    return pl.BlockSpec((height, width), lambda step, facts_ref: (0, step + offset))


def row_block(height, width, offset=0):
    return pl.BlockSpec((height, width), lambda step, facts_ref: (step + offset, 0))


def kernel_call(kernel, name, steps, in_specs, out_specs, out_shape, scratch, flops, size, exps=0, aliases={}):
    return pl.pallas_call(
        kernel,
        out_shape=out_shape,
        grid_spec=pltpu.PrefetchScalarGridSpec(
            num_scalar_prefetch=1, grid=(steps,), in_specs=in_specs, out_specs=out_specs, scratch_shapes=scratch
        ),
        compiler_params=pltpu.CompilerParams(
            dimension_semantics=("arbitrary",), vmem_limit_bytes=48 << 20
        ),
        input_output_aliases=aliases,
        cost_estimate=pl.CostEstimate(flops=flops, bytes_accessed=size, transcendentals=exps),
        name=name,
    )


def shaped(shape, dtype=jnp.bfloat16):
    return jax.ShapeDtypeStruct(shape, dtype)


def attention_forward(residual, weights, norms, tables, facts):
    tokens, width = residual.shape
    groups = width // GROUP
    joint, output = weights[0], weights[1]
    firsts, seconds = weights[4:6]
    seq_len = tables.shape[1]
    return kernel_call(
        attention_forward_kernel,
        "attention_forward",
        groups,
        [
            whole(tokens, width),
            whole(4, width),
            whole(3, seq_len, 2 * HEAD_DIM),
            whole(width, RANK),
            column_block(width, GROUP),
            column_block(width, GROUP, groups),
            column_block(width, GROUP, 2 * groups),
            column_block(RANK, GROUP),
            column_block(RANK, GROUP, groups),
            column_block(RANK, GROUP, 2 * groups),
            row_block(GROUP, width),
            row_block(GROUP, RANK, groups),
            fixed(RANK, width, 0, 3),
        ],
        [column_block(tokens, GROUP)] * 4 + [whole(tokens, RANK), whole(tokens, RANK), whole(tokens, width)],
        [shaped((tokens, width))] * 4
        + [shaped((tokens, RANK)), shaped((tokens, RANK)), shaped((tokens, width), jnp.float32)],
        [pltpu.VMEM((tokens, width), jnp.bfloat16), pltpu.VMEM((tokens, RANK), jnp.float32)],
        2 * tokens * width * width * 4,
        2 * 5 * width * width + 12 * tokens * width,
    )(
        facts, residual, norms, tables, firsts, joint, joint, joint, seconds, seconds, seconds, output,
        firsts, seconds,
    )


def feed_forward_kernel(
    facts_ref, x_ref, norm_ref, att_ref, first_ref, wu_ref, bu_ref, wd_ref, ad_ref, bd_ref,
    act_out, slope_out, midu_out, midd_out, x_out, sums_out,
    a_scr, mid_scr,
):
    step = pl.program_id(0)

    @pl.when(step == 0)
    def _():
        normal, _ = normalize(x_ref[...])
        a_scr[...] = half(normal * norm_ref[1:2] + norm_ref[3:4])
        midu_out[...] = half(mm(a_scr[...], first_ref[...]))
        x_out[...] = jnp.zeros_like(x_out)
        mid_scr[...] = jnp.zeros_like(mid_scr)

    upper = mm(a_scr[...], wu_ref[...]) + adapter_scale * mm(midu_out[...], bu_ref[...])
    spread = 0.5 + 0.5 * lax.erf(upper * 0.5**0.5)
    density = jnp.exp(-0.5 * upper * upper) * (0.5 / jnp.pi) ** 0.5
    act_out[...] = half(upper * spread)
    slope_out[...] = half(spread + upper * density)
    active = act_out[...]
    x_out[...] += mm(active, wd_ref[...])
    mid_scr[...] += mm(active, ad_ref[...])

    @pl.when(step == pl.num_programs(0) - 1)
    def _():
        midd_out[...] = half(mid_scr[...])
        feed = x_out[...] + adapter_scale * mm(midd_out[...], bd_ref[...])
        attended = att_ref[...]
        residual = x_ref[...]
        x_out[...] = residual + (attended + feed)
        lane = lax.broadcasted_iota(jnp.int32, (1, 128), 1)
        seqs = facts_ref.shape[1]
        seq_len = residual.shape[0] // seqs
        row = lax.broadcasted_iota(jnp.int32, (seq_len, 1), 0)
        parts = []
        for part in (residual, attended, feed):
            squares = jnp.sum(part * part, axis=-1, keepdims=True)
            sums = jnp.zeros((1, 128), jnp.float32)
            for seq in range(seqs):
                valid = jnp.where(row < facts_ref[0, seq], squares[seq * seq_len : (seq + 1) * seq_len], 0.0)
                counted = (lane == facts_ref[1, seq]) | (lane == DOMAINS)
                sums = sums + jnp.where(counted, jnp.sum(valid), 0.0)
            parts.append(sums)
        sums_out[...] = jnp.concatenate(parts + [jnp.zeros((5, 128), jnp.float32)], 0)


def feed_forward(residual, attended, weights, norms, facts):
    tokens, width = residual.shape
    upper, down = weights[2], weights[3]
    firsts, seconds = weights[4:6]
    hidden = upper.shape[1]
    return kernel_call(
        feed_forward_kernel,
        "feed_forward",
        hidden // BLOCK,
        [
            whole(tokens, width),
            whole(4, width),
            whole(tokens, width),
            fixed(width, RANK, 2, 0),
            column_block(width, BLOCK),
            column_block(RANK, BLOCK, 4 * width // BLOCK),
            row_block(BLOCK, width),
            row_block(BLOCK, RANK, 3 * width // BLOCK),
            fixed(RANK, width, 0, 8),
        ],
        [column_block(tokens, BLOCK)] * 2
        + [whole(tokens, RANK), whole(tokens, RANK), whole(tokens, width), whole(8, 128)],
        [shaped((tokens, hidden))] * 2
        + [shaped((tokens, RANK))] * 2
        + [shaped((tokens, width), jnp.float32), shaped((8, 128), jnp.float32)],
        [pltpu.VMEM((tokens, width), jnp.bfloat16), pltpu.VMEM((tokens, RANK), jnp.float32)],
        2 * tokens * width * hidden * 2,
        4 * width * hidden + 4 * tokens * hidden + 12 * tokens * width,
        2 * tokens * hidden,
    )(facts, residual, norms, attended, firsts, upper, seconds, down, firsts, seconds)


def write_extra(block_out, grad, normal, sums):
    width = grad.shape[1]
    row = [jnp.sum(grad * normal, axis=0, keepdims=True), jnp.sum(grad, axis=0, keepdims=True)] + sums
    rest = block_out.shape[1] - sum(part.shape[1] for part in row)
    row = jnp.concatenate(row + [jnp.zeros((1, rest), jnp.float32)], 1)
    block_out[RANK:, :] = half(jnp.concatenate([row, jnp.zeros((7, row.shape[1]), jnp.float32)], 0))


def feed_backward_kernel(
    facts_ref, g_ref, x_ref, norm_ref, act_ref, slope_ref, midu_ref, midd_ref, sums_ref, wu_ref, wd_ref, au_ref,
    bu_ref, ad_ref, bd_ref,
    whole_out, gx_out,
    block_out, g_scr, gmd_scr, gmdt_scr, midut_scr, gmu_scr, sem,
):
    step = pl.program_id(0)
    width = x_ref.shape[1]
    hidden = pl.num_programs(0) * BLOCK

    @pl.when(step == 0)
    def _():
        g_scr[...] = half(g_ref[...])
        grad_mid = adapter_scale * mm_nt(g_scr[...], bd_ref[...])
        gmd_scr[...] = half(grad_mid)
        gmdt_scr[...] = half(half(grad_mid).astype(jnp.float32).T)
        midut_scr[...] = half(midu_ref[...].astype(jnp.float32).T)
        gx_out[...] = jnp.zeros_like(gx_out)
        gmu_scr[...] = jnp.zeros_like(gmu_scr)
        middt = half(midd_ref[...].astype(jnp.float32).T)
        block_out[:RANK, pl.ds(width + 2 * hidden, width)] = half(adapter_scale * mm(middt, g_scr[...]))

    grad_act = mm_nt(g_scr[...], wd_ref[...]) + mm_nt(gmd_scr[...], ad_ref[...])
    grad_up = half(half(grad_act).astype(jnp.float32) * slope_ref[...].astype(jnp.float32))
    first_at = pl.multiple_of(width + step * BLOCK, BLOCK)
    second_at = pl.multiple_of(width + hidden + step * BLOCK, BLOCK)
    block_out[:RANK, pl.ds(first_at, BLOCK)] = half(mm(gmdt_scr[...], act_ref[...]))
    block_out[:RANK, pl.ds(second_at, BLOCK)] = half(adapter_scale * mm(midut_scr[...], grad_up))
    gmu_scr[...] += mm_nt(grad_up, bu_ref[...])
    gx_out[...] += mm_nt(grad_up, wu_ref[...])

    @pl.when(step == pl.num_programs(0) - 1)
    def _():
        grad_mid = half(adapter_scale * gmu_scr[...])
        normal, scale = normalize(x_ref[...])
        normed = half(normal * norm_ref[1:2] + norm_ref[3:4])
        block_out[:RANK, :width] = half(mm(half(grad_mid.astype(jnp.float32).T), normed))
        grad = gx_out[...] + mm_nt(grad_mid, au_ref[...])
        write_extra(block_out, grad, normal, [sums_ref[index : index + 1] for index in range(3)])
        gather = pltpu.make_async_copy(
            block_out, whole_out.at[:, pl.ds(6 * width, block_out.shape[1])], sem
        )
        gather.start()
        gx_out[...] = g_ref[...] + norm_gradient(grad, normal, scale, norm_ref[1:2])
        gather.wait()


def feed_backward(gradient, residual, weights, norms, kept, facts):
    tokens, width = residual.shape
    upper, down = weights[2], weights[3]
    firsts, seconds = weights[4:6]
    active, slope, mid_u, mid_d, sums = kept
    hidden = upper.shape[1]
    return kernel_call(
        feed_backward_kernel,
        "feed_backward",
        hidden // BLOCK,
        [
            whole(tokens, width),
            whole(tokens, width),
            whole(4, width),
            column_block(tokens, BLOCK),
            column_block(tokens, BLOCK),
            whole(tokens, RANK),
            whole(tokens, RANK),
            whole(8, 128),
            column_block(width, BLOCK),
            row_block(BLOCK, width),
            fixed(width, RANK, 2, 0),
            column_block(RANK, BLOCK, 4 * width // BLOCK),
            row_block(BLOCK, RANK, 3 * width // BLOCK),
            fixed(RANK, width, 0, 8),
        ],
        [pl.BlockSpec(memory_space=pl.ANY), whole(tokens, width)],
        [shaped((RANK + 8, 16 * width)), shaped((tokens, width), jnp.float32)],
        [
            pltpu.VMEM((RANK + 8, 2 * width + 2 * hidden), jnp.bfloat16),
            pltpu.VMEM((tokens, width), jnp.bfloat16),
            pltpu.VMEM((tokens, RANK), jnp.bfloat16),
            pltpu.VMEM((RANK, tokens), jnp.bfloat16),
            pltpu.VMEM((RANK, tokens), jnp.bfloat16),
            pltpu.VMEM((tokens, RANK), jnp.float32),
            pltpu.SemaphoreType.DMA,
        ],
        2 * tokens * width * hidden * 2,
        4 * width * hidden + 4 * tokens * hidden + 16 * tokens * width,
    )(
        facts, gradient, residual, norms, active, slope, mid_u, mid_d, sums, upper, down, firsts, seconds,
        firsts, seconds,
    )


def attention_backward_kernel(
    facts_ref, g_ref, gx_ref, x_ref, norm_ref, table_ref, q_ref, k_ref, v_ref, mixed_ref, midq_ref, mido_ref,
    wq_ref, wk_ref, wv_ref, aq_ref, bq_ref, bk_ref, bv_ref, wo_ref, ao_ref, bo_ref, feed_block_ref,
    whole_out, gx_out,
    block_out, g_scr, gmo_scr, gmot_scr, midqt_scr, gmq_scr, acc_scr, gq_scr, gk_scr, gv_scr, sem,
):
    step = pl.program_id(0)
    width = x_ref.shape[1]
    seq_len = table_ref.shape[1]
    seqs = x_ref.shape[0] // seq_len
    scale_factor = HEAD_DIM ** (-0.5)

    @pl.when(step == 0)
    def _():
        g_scr[...] = half(g_ref[...])
        grad_mid = half(adapter_scale * mm_nt(g_scr[...], bo_ref[...]))
        gmo_scr[...] = grad_mid
        gmot_scr[...] = half(grad_mid.astype(jnp.float32).T)
        midqt_scr[...] = half(midq_ref[...].astype(jnp.float32).T)
        acc_scr[...] = jnp.zeros_like(acc_scr)
        gmq_scr[...] = jnp.zeros_like(gmq_scr)
        midot = half(mido_ref[...].astype(jnp.float32).T)
        block_out[:RANK, pl.ds(5 * width, width)] = half(adapter_scale * mm(midot, g_scr[...]))

    grad_mixed = half(mm_nt(g_scr[...], wo_ref[...]) + mm_nt(gmo_scr[...], ao_ref[...]))
    first_at = pl.multiple_of(width + step * GROUP, GROUP)
    block_out[:RANK, pl.ds(first_at, GROUP)] = half(mm(gmot_scr[...], mixed_ref[...]))
    for seq in range(seqs):
        rows = slice(seq * seq_len, (seq + 1) * seq_len)
        for pair in range(GROUP // (2 * HEAD_DIM)):
            lanes = slice(pair * 2 * HEAD_DIM, (pair + 1) * 2 * HEAD_DIM)
            query_stack = stack_heads(q_ref[rows, lanes])
            key_pair = k_ref[rows, lanes]
            probability = pair_softmax(query_stack, key_pair, facts_ref[0, seq])
            grad_stack = stack_heads(grad_mixed[rows, lanes])
            grad_prob = mm_nt(grad_stack, v_ref[rows, lanes])
            gv_scr[rows, lanes] = half(mm_tn(half(probability), grad_stack))
            inner = jnp.sum(probability * grad_prob, axis=-1, keepdims=True)
            grad_scores = half(probability * (grad_prob - inner))
            gq_scr[rows, lanes] = merge_heads(mm(grad_scores, key_pair)) * scale_factor
            gk_scr[rows, lanes] = mm_tn(grad_scores, query_stack) * scale_factor
    tables = [tile_table(table_ref[index], seqs, GROUP) for index in range(3)]
    joint = (half(turn_back(gq_scr[...], *tables)), half(turn_back(gk_scr[...], *tables)), gv_scr[...])
    mid = midqt_scr[...]
    for index, (grad, w_ref, b_ref) in enumerate(zip(joint, (wq_ref, wk_ref, wv_ref), (bq_ref, bk_ref, bv_ref))):
        second_at = pl.multiple_of((2 + index) * width + step * GROUP, GROUP)
        block_out[:RANK, pl.ds(second_at, GROUP)] = half(adapter_scale * mm(mid, grad))
        gmq_scr[...] += mm_nt(grad, b_ref[...])
        acc_scr[...] += mm_nt(grad, w_ref[...])

    @pl.when(step == pl.num_programs(0) - 1)
    def _():
        grad_mid = half(adapter_scale * gmq_scr[...])
        normal, scale = normalize(x_ref[...])
        normed = half(normal * norm_ref[0:1] + norm_ref[2:3])
        block_out[:RANK, :width] = half(mm(half(grad_mid.astype(jnp.float32).T), normed))
        grad = acc_scr[...] + mm_nt(grad_mid, aq_ref[...])
        write_extra(block_out, grad, normal, [])
        gather = pltpu.make_async_copy(block_out, whole_out.at[:, pl.ds(0, block_out.shape[1])], sem)
        gather.start()
        gx_out[...] = gx_ref[...] + norm_gradient(grad, normal, scale, norm_ref[0:1])
        gather.wait()


def attention_backward(gradient, grad_feed, feed_block, residual, weights, norms, tables, kept, facts):
    tokens, width = residual.shape
    groups = width // GROUP
    joint, output = weights[0], weights[1]
    firsts, seconds = weights[4:6]
    queries, keys, values, mixed, mid_q, mid_o = kept
    seq_len = tables.shape[1]
    block = column_block(tokens, GROUP)
    return kernel_call(
        attention_backward_kernel,
        "attention_backward",
        groups,
        [
            whole(tokens, width),
            whole(tokens, width),
            whole(tokens, width),
            whole(4, width),
            whole(3, seq_len, 2 * HEAD_DIM),
            block,
            block,
            block,
            block,
            whole(tokens, RANK),
            whole(tokens, RANK),
            column_block(width, GROUP),
            column_block(width, GROUP, groups),
            column_block(width, GROUP, 2 * groups),
            whole(width, RANK),
            column_block(RANK, GROUP),
            column_block(RANK, GROUP, groups),
            column_block(RANK, GROUP, 2 * groups),
            row_block(GROUP, width),
            row_block(GROUP, RANK, groups),
            fixed(RANK, width, 0, 3),
            pl.BlockSpec(memory_space=pl.ANY),
        ],
        [pl.BlockSpec(memory_space=pl.ANY), whole(tokens, width)],
        [shaped((RANK + 8, 16 * width)), shaped((tokens, width), jnp.float32)],
        [
            pltpu.VMEM((RANK + 8, 6 * width), jnp.bfloat16),
            pltpu.VMEM((tokens, width), jnp.bfloat16),
            pltpu.VMEM((tokens, RANK), jnp.bfloat16),
            pltpu.VMEM((RANK, tokens), jnp.bfloat16),
            pltpu.VMEM((RANK, tokens), jnp.bfloat16),
            pltpu.VMEM((tokens, RANK), jnp.float32),
            pltpu.VMEM((tokens, width), jnp.float32),
            pltpu.VMEM((tokens, GROUP), jnp.float32),
            pltpu.VMEM((tokens, GROUP), jnp.float32),
            pltpu.VMEM((tokens, GROUP), jnp.bfloat16),
            pltpu.SemaphoreType.DMA,
        ],
        2 * tokens * width * width * 4,
        2 * 5 * width * width + 24 * tokens * width,
        aliases={22: 0},
    )(
        facts, gradient, grad_feed, residual, norms, tables, queries, keys, values, mixed, mid_q, mid_o, joint,
        joint, joint, firsts, seconds, seconds, seconds, output, firsts, seconds, feed_block,
    )


def layer_forward(residual, weights, tables, facts):
    norms = weights[6]
    *kept_attention, attended = attention_forward(residual, weights, norms, tables, facts)
    *kept_feed, output, sums = feed_forward(residual, attended, weights, norms, facts)
    return output, (residual, kept_attention, kept_feed + [sums])


def layer_backward(gradient, kept, weights, tables, facts):
    residual, kept_attention, kept_feed = kept
    norms = weights[6]
    feed_block, grad_feed = feed_backward(gradient, residual, weights, norms, kept_feed, facts)
    block, grad_input = attention_backward(
        gradient, grad_feed, feed_block, residual, weights, norms, tables, kept_attention, facts
    )
    return grad_input, block


def gather_plan(gathers, turns):
    if (gathers, turns) == (4, 3):
        return [[0, 2], [0], [0, 1], [1, 2], [1, 3], [2, 3], [3], []]
    return [
        [index for index in range(gathers) if index <= step < index + turns] for step in range(gathers + turns)
    ]


def shards(
    inputs,
    cotangent,
    domain,
    lengths,
    steps_since_reset,
    frozen_query_weight,
    frozen_output_weight,
    frozen_up_weight,
    frozen_down_weight,
    query_adapter_first,
    query_adapter_second,
    output_adapter_first,
    output_adapter_second,
    up_adapter_first,
    up_adapter_second,
    down_adapter_first,
    down_adapter_second,
    layer_norm_gain,
    layer_norm_bias,
):
    core = lax.axis_index("section")
    place = lax.axis_index("dp")
    count = lax.axis_size("dp")
    middle = count // 2
    stage = place // middle
    low = place % middle
    home = core == stage
    masks = [1 << bit for bit in range(middle.bit_length() - 1)]
    frozen = (frozen_query_weight, frozen_output_weight, frozen_up_weight, frozen_down_weight)
    trained = (
        query_adapter_first,
        query_adapter_second,
        output_adapter_first,
        output_adapter_second,
        up_adapter_first,
        up_adapter_second,
        down_adapter_first,
        down_adapter_second,
    )
    local_layers = frozen_query_weight.shape[0]
    rows_dev, seq_len, model_width = inputs.shape
    tokens = rows_dev * seq_len
    rows = frozen_output_weight.shape[1]

    places = [(index // middle, index) for index in range(count)]
    to_sibling = [(here * count + index, (1 - here) * count + index) for here, index in places]
    to_far = [((1 - here) * count + index, (1 - here) * count + (index ^ middle)) for here, index in places]
    to_cross = [((1 - here) * count + index, here * count + (index ^ middle)) for here, index in places]
    halves = [pick_halves([matrix[layer] for matrix in frozen], stage) for layer in range(local_layers)]
    packed = [
        (
            jnp.concatenate([factor[layer] for factor in trained[0::2]], 0),
            jnp.concatenate([factor[layer] for factor in trained[1::2]], 1),
            jnp.concatenate([layer_norm_gain[layer], layer_norm_bias[layer]], 0),
        )
        for layer in range(local_layers)
    ]
    sibling, far, cross = [
        partial(both_axes, pairs=pairs) for pairs in (to_sibling, to_far, to_cross)
    ]
    steps = Steps()
    near = steps.run(*[(other, sibling) for _, other in halves])
    apart = []
    for same, other in halves:
        same, other = tie((same, other), *(near + apart[-1:]))
        apart.append((far(other), cross(same)))
    gathers = []
    for layer in range(local_layers):
        gathers.append(Gather(jnp.where(home, halves[layer][0], near[layer]), masks))
        gathers.append(Gather(jnp.where(home, *apart[layer]), masks))
    plan = gather_plan(len(gathers), len(masks))
    visiting = jnp.where(stage == 0, cotangent, inputs)
    facts = jnp.stack([lengths, domain])
    weights = [None] * local_layers
    swapped = [None] * len(gathers)
    ready = []
    for number, active in enumerate(plan):
        moves = [move for index in active for move in gathers[index].moves()]
        moves = moves + [(held, flip_core) for index in ready for held in gathers[index].held]
        if number == 0:
            moves.append((facts, cross))
        if number == 1:
            moves = moves + [(part, sibling) for part in packed[0]]
        if number == 3:
            moves.append((visiting, cross))
            moves = moves + [(part, sibling) for layer in packed[1:] for part in layer]
        there = steps.run(*moves)
        for index in active:
            gathers[index].take(there[:3])
            there = there[3:]
        for index in ready:
            swapped[index] = there[:3]
            there = there[3:]
        ready = [index for index in active if gathers[index].step == len(masks)]
        if number == 0:
            facts = jnp.where(home, facts, there[0])
        if number == 1:
            packed[0] = [jnp.where(home, here, far_part) for here, far_part in zip(packed[0], there)]
        if number == 3:
            visiting, there = there[0], there[1:]
            for layer in range(1, local_layers):
                packed[layer] = [jnp.where(home, here, far_part) for here, far_part in zip(packed[layer], there)]
                there = there[3:]
    for layer in range(local_layers):
        dense = None
        for which in range(2):
            gather = gathers[2 * layer + which]
            base = jnp.where(stage == which, 0, middle)
            order = gather.found[0]
            info = jnp.stack(
                [jnp.full((middle,), core, jnp.int32), (jnp.asarray(order, jnp.int32) ^ low) + base]
                + [jnp.asarray([known.index(mask) for mask in order], jnp.int32) for known in gather.found]
            )
            dense = assemble(info, gather.held, swapped[2 * layer + which], rows, count, dense)
        weights[layer] = tuple(dense) + tuple(packed[layer])
    start = jnp.where(home, inputs, visiting).astype(jnp.float32).reshape(tokens, model_width)
    valid = jnp.arange(seq_len)[None, :] < facts[0][:, None]
    end_grad = jnp.where(home, cotangent, visiting).astype(jnp.float32)
    end_grad = jnp.where(stage == 1, end_grad * valid[..., None].astype(jnp.float32), 0.0)
    end_grad = end_grad.reshape(tokens, model_width)
    tables = rotary_tables(seq_len)

    def stage_forward(residual):
        kept = []
        for layer in range(local_layers):
            residual, kept_state = layer_forward(residual, weights[layer], tables, facts)
            kept.append(kept_state)
        return residual, kept

    boundary, _ = stage_forward(start)
    boundary = boundary.astype(jnp.bfloat16)
    forward_pairs = [(index, index + middle) for index in range(middle)]
    received = lax.ppermute(boundary, "dp", forward_pairs)
    entry = jnp.where(stage == 0, start, received.astype(jnp.float32))
    final, kept = stage_forward(entry)
    final = final.astype(jnp.bfloat16)

    gradient = end_grad
    late = [None] * local_layers
    for layer in reversed(range(local_layers)):
        gradient, late[layer] = layer_backward(gradient, kept[layer], weights[layer], tables, facts)
    sent = gradient.astype(jnp.bfloat16)
    came_back = lax.ppermute(sent, "dp", [(after, before) for before, after in forward_pairs])
    steps = Steps()
    late_slabs = scatter_section(late, 1, core, low, count, masks, steps)

    gradient = jnp.where(stage == 0, came_back.astype(jnp.float32), 0.0)
    blocks, slabs = [None] * local_layers, [None] * local_layers
    for layer in reversed(range(local_layers)):
        gradient, blocks[layer] = layer_backward(gradient, kept[layer], weights[layer], tables, facts)
        if layer:
            slabs[layer] = scatter_section([blocks[layer]], 0, core, low, count, masks, steps)

    first = Spread(late_slabs, 1, masks, count, stage)
    second = Spread(sum(slabs[1:], []), 0, masks, count, stage)
    third = Scatter([blocks[0]], 0, core, low, count, masks)
    there = steps.run(*third.moves(), *first.moves(), *second.moves())
    there = third.take(there)
    second.take(first.take(there))
    for step in range(len(masks)):
        there = steps.run(*third.moves())
        third.take(there)
    third = Spread(third.slabs, 0, masks, count, stage)
    for step in range(len(masks) + 2):
        groups = [first, second, third] if step else [third, first, second]
        groups = [group for group in groups if not group.done()]
        there = steps.run(*[move for group in groups for move in group.moves()])
        for group in groups:
            there = group.take(there)
    placed = place_section(1, core, low, masks, first, None, local_layers)
    old = placed[1:]
    upper_placed = place_section(0, core, low, masks, second, old, local_layers - 1)
    lower_placed = place_section(0, core, low, masks, third, placed[:1], 1)
    blocks = lower_placed + upper_placed

    out_pairs = [(count + index + middle, index + middle) for index in range(middle)]
    out_pairs = out_pairs + [(index + middle, count + index) for index in range(middle)]
    visiting = both_axes(jnp.where(core == 0, final, received), out_pairs)
    section_out = jnp.where(home, jnp.where(stage == 0, boundary, final), visiting)
    section_out = section_out.reshape(1, rows_dev, seq_len, model_width)
    grad_pairs = [(index, count + index) for index in range(middle)]
    grad_pairs = grad_pairs + [(count + index, index + middle) for index in range(middle)]
    visiting = both_axes(jnp.where(core == 0, came_back, gradient.astype(jnp.bfloat16)), grad_pairs)
    section_grad = jnp.where(
        home, jnp.where(stage == 0, gradient, sent.astype(jnp.float32)), visiting.astype(jnp.float32)
    )
    section_grad = section_grad.reshape(1, rows_dev, seq_len, model_width)

    lane = jnp.arange(128)
    counted = (domain[:, None] == lane[None, :]) | (lane == DOMAINS)[None, :]
    counts = jnp.sum(jnp.where(counted, lengths.astype(jnp.float32)[:, None], 0.0), axis=0, keepdims=True)
    counts = tie(counts, final)
    for mask in masks + [middle]:
        counts = counts + flip_place(counts, mask)
    counts = jnp.maximum(counts, 1.0) * model_width
    rate = peak_rate * (steps_since_reset[0].astype(jnp.float32) + 1.0) / WARM
    *outputs, rms = finish(place, rate, blocks, counts, trained, frozen)
    return (section_out, section_grad, *outputs, rms[:, :, : DOMAINS + 1])


def solution(mesh):
    across = P("dp", None, None)
    copied = P("section", None, None)
    split = P("section", "dp", None)
    wide = P("section", "dp", None, None)
    return jax.shard_map(
        shards,
        mesh=mesh,
        in_specs=(across, across, P("dp"), P("dp"), P()) + (split,) * 4 + (copied,) * 10,
        out_specs=(wide, wide) + (copied,) * 10 + (split,) * 4 + (copied,),
        check_vma=False,
    )
```

time: 1380 us -> 1050 us (0.76)
  matrix products: 306 us -> 0 us
  Pallas kernels: 47.7 us -> 353 us
  other arithmetic: 347 us -> 86.5 us
  local copies, waits for them, and re-layouts: 120 us -> 37.5 us
  waiting for transfers between devices: 282 us -> 337 us
  starting transfers between devices: 250 us -> 220 us
    pallas_call x0 -> x20, Pallas kernels: none -> 305 us  [the longest x4 72.4 us: attention_backward(): kernel_call(attention_backward_kernel, 'attention_backward', groups, [who...]
    dot_general x150 -> x0, matrix products: 300 us -> none  [the longest x16 77.4 us: adapter_forward(): jnp.dot(saved_activations, dense_matmul, preferred_element_type=jnp.float32)]
    convert_element_type x58 -> x34, other arithmetic: 95.9 us -> 8.8 us  [the longest x31 8.66 us: total_of(): (first.astype(jnp.float32) + second.astype(jnp.float32)).astype(jnp.bfloa...]
    select_n x103 -> x22, other arithmetic: 104 us -> 20.5 us  [the longest x6 10.2 us: shards(): jnp.where(home, here, far_part)]
    ppermute x124 -> x67, starting transfers between devices: 162 us -> 83.8 us  [flip_place(): lax.ppermute(value, 'dp', [(place, place ^ mask) for place in range(count)])]
    ppermute x4 -> x45, starting transfers between devices: 11 us -> 85.8 us  [run(): self.ended = tuple((send(value) for value, (_, send) in zip(values, moves)))]
    ppermute x4 -> x45, waiting for transfers between devices: 0.01 us -> 70.7 us  [run(): self.ended = tuple((send(value) for value, (_, send) in zip(values, moves)))]
    ppermute x124 -> x67, waiting for transfers between devices: 251 us -> 181 us  [flip_place(): lax.ppermute(value, 'dp', [(place, place ^ mask) for place in range(count)])]
  transfers between devices with their start and end apart: 174 -> 146, of which waited for: 53 -> 50; matrix products, arithmetic and copies ran while one was open for 22% -> 8% of each run, Pallas kernels for 3% -> 18%
where the time goes in v2:
time: 1050 us; the launch traced here: 1040 us
  Pallas kernels  353 us (34%)
  waiting for transfers between devices  337 us (32%)
  starting transfers between devices  220 us (21%)
  other arithmetic  86.5 us (8%)
  local copies, waits for them, and re-layouts  37.5 us (4%)
    ppermute x67, waiting for transfers between devices, flip_place(): lax.ppermute(value, 'dp', [(place, place ^ mask) for place in range(count)])  181 us
    ppermute x45, starting transfers between devices, run(): self.ended = tuple((send(value) for value, (_, send) in zip(values, moves)))  85.8 us
    ppermute x67, starting transfers between devices, flip_place(): lax.ppermute(value, 'dp', [(place, place ^ mask) for place in range(count)])  83.8 us
    pallas_call x4, Pallas kernels, attention_backward(): kernel_call(attention_backward_kernel, 'attention_backward', groups, [who...  72.4 us
    ppermute x45, waiting for transfers between devices, run(): self.ended = tuple((send(value) for value, (_, send) in zip(values, moves)))  70.7 us
    pallas_call x4, Pallas kernels, feed_backward(): kernel_call(feed_backward_kernel, 'feed_backward', hidden // BLOCK, [whol...  67.5 us
    pallas_call x4, Pallas kernels, feed_forward(): kernel_call(feed_forward_kernel, 'feed_forward', hidden // BLOCK, [whole(...  63.9 us
    ppermute x20, waiting for transfers between devices, both_axes(): return lax.ppermute(value, ('section', 'dp'), pairs)  58.5 us
  transfers between devices with their start and end apart: 146, of which 50 were waited for; matrix products, arithmetic and copies ran while one was open for 8% of the time, Pallas kernels for 18%

profile of v2, /device:TPU:26, one launch (start us, length us, event | category | flops | bytes accessed | tf_op | source)
XLA Modules:
  0.0 1040.1 jit_solution(18176847842435261064)
XLA Ops:
  59.2 10.5 %collective-permute-done.11 = bf16[2,2,64,1024]{3,2,1,0:T(8,128)(2,1)S(1)} collective-permute-done((bf16[2,2,64,1024]{3,2,1,0:T(8,128)(2,1)S(1)}, bf16[2,2,64,1024]{3,2,1,0:T(8,128)(2,1)S(1)}, u32[]{:S(2)}, u32[]{:S(2)}) %collective-permute-start.11) | collective-permute-done | bytes 524320 | tf_op jit(solution)/shard_map/ppermute | solution.py:36
  71.2 15.4 %collective-permute-done.4 = bf16[6,64,1024]{2,1,0:T(8,128)(2,1)S(1)} collective-permute-done((bf16[6,64,1024]{2,1,0:T(8,128)(2,1)S(1)}, bf16[6,64,1024]{2,1,0:T(8,128)(2,1)S(1)}, u32[]{:S(2)}, u32[]{:S(2)}) %collective-permute-start.4) | collective-permute-done | bytes 786464 | tf_op jit(solution)/shard_map/ppermute | solution.py:27
  92.9 21.7 %collective-permute-done.19 = bf16[1,2,64,1024]{3,2,1,0:T(8,128)(2,1)S(1)} collective-permute-done((bf16[1,2,64,1024]{3,2,1,0:T(8,128)(2,1)S(1)}, bf16[1,2,64,1024]{3,2,1,0:T(8,128)(2,1)S(1)}, u32[]{:S(2)}, u32[]{:S(2)}) %collective-permute-start.19) | collective-permute-done | bytes 262176 | tf_op jit(solution)/shard_map/ppermute | solution.py:36
  134.2 23.8 %collective-permute-done.28 = bf16[6,64,1024]{2,1,0:T(8,128)(2,1)S(1)} collective-permute-done((bf16[6,64,1024]{2,1,0:T(8,128)(2,1)S(1)}, bf16[6,64,1024]{2,1,0:T(8,128)(2,1)S(1)}, u32[]{:S(2)}, u32[]{:S(2)}) %collective-permute-start.28) | collective-permute-done | bytes 786464 | tf_op jit(solution)/shard_map/ppermute | solution.py:27
  195.0 22.4 %collective-permute-done.43 = bf16[1,2,64,1024]{3,2,1,0:T(8,128)(2,1)S(1)} collective-permute-done((bf16[1,2,64,1024]{3,2,1,0:T(8,128)(2,1)S(1)}, bf16[1,2,64,1024]{3,2,1,0:T(8,128)(2,1)S(1)}, u32[]{:S(2)}, u32[]{:S(2)}) %collective-permute-start.43) | collective-permute-done | bytes 262176 | tf_op jit(solution)/shard_map/ppermute | solution.py:36
  248.8 19.4 %collective-permute-done.48 = bf16[2,2,64,1024]{3,2,1,0:T(8,128)(2,1)S(1)} collective-permute-done((bf16[2,2,64,1024]{3,2,1,0:T(8,128)(2,1)}, bf16[2,2,64,1024]{3,2,1,0:T(8,128)(2,1)S(1)}, u32[]{:S(2)}, u32[]{:S(2)}) %collective-permute-start.48) | collective-permute-done | bytes 524320 | tf_op jit(solution)/shard_map/ppermute | solution.py:36
  286.5 19.4 %collective-permute-done.53 = bf16[4,2,64,1024]{3,2,1,0:T(8,128)(2,1)S(1)} collective-permute-done((bf16[4,2,64,1024]{3,2,1,0:T(8,128)(2,1)S(1)}, bf16[4,2,64,1024]{3,2,1,0:T(8,128)(2,1)S(1)}, u32[]{:S(2)}, u32[]{:S(2)}) %collective-permute-start.53) | collective-permute-done | bytes 1048608 | tf_op jit(solution)/shard_map/ppermute | solution.py:36
  308.6 12.0 %assemble.4 = (bf16[1024,3072]{1,0:T(8,128)(2,1)}, bf16[1024,1024]{1,0:T(8,128)(2,1)}, bf16[1024,4096]{1,0:T(8,128)(2,1)}, bf16[4096,1024]{1,0:T(8,128)(2,1)}) custom-call(s32[5,8]{1,0:T(8,128)} %stack.185.info_ref, bf16[8,2,64,1024]{3,2,1,0:T(8,128)(2,1)} %copy-done.58, bf16[8,2,64,1024]{3,2,1,0:T(8,128)(2,1)} %copy-done.59, ...), custom_call_target="tpu_custom_call" | custom-call | bytes 25165824 | tf_op jit(solution)/shard_map/assemble/pallas_call | solution.py:107
  333.1 11.9 %assemble.5 = (bf16[1024,3072]{1,0:T(8,128)(2,1)}, bf16[1024,1024]{1,0:T(8,128)(2,1)}, bf16[1024,4096]{1,0:T(8,128)(2,1)}, bf16[4096,1024]{1,0:T(8,128)(2,1)}) custom-call(s32[5,8]{1,0:T(8,128)} %stack.180.info_ref, bf16[8,2,64,1024]{3,2,1,0:T(8,128)(2,1)} %pad_maximum_fusion.5.refs_0_, ...), custom_call_target="tpu_custom_call", output_to_operand_aliasing={{0}: (7, {}), {1}: (8, {}), {2}: (9, {}), {3}: (10, {})} | custom-call | bytes 25165824 | tf_op jit(solution)/shard_map/assemble/pallas_call | solution.py:107
  344.9 14.4 %attention_forward.4 = (bf16[256,1024]{1,0:T(8,128)(2,1)}, bf16[256,1024]{1,0:T(8,128)(2,1)}, bf16[256,1024]{1,0:T(8,128)(2,1)}, bf16[256,1024]{1,0:T(8,128)(2,1...) custom-call(s32[2,2]{1,0:T(2,128)S(1)} %broadcast_select_fusion.17.facts_ref, ...), custom_call_target="tpu_custom_call" | custom-call | flops 2147483648 | bytes 13631488 | tf_op jit(solution)/shard_map/attention_forward/pallas_call | solution.py:551
  359.4 15.9 %feed_forward.4 = (bf16[256,4096]{1,0:T(8,128)(2,1)}, bf16[256,4096]{1,0:T(8,128)(2,1)}, bf16[256,128]{1,0:T(8,128)(2,1)}, bf16[256,128]{1,0:T(8,128)(2,1)}, f32[256,1024]{1,0:T(8,128)S(1)}, /*index=5*/f32[8,128]{1,0:T(8,128)}) custom-call(s32[2,2]{1,0:T(2,128)S(1)} %broadcast_select_fusion.17.facts_ref, f32[256,1024]{1,0:T(8,128)S(1)} %bitcast_convert_fusion.x_ref, ...), custom_call_target="tpu_custom_call" | custom-call | flops 4294967296 | bytes 24117248 | tf_op jit(solution)/shard_map/feed_forward/pallas_call | solution.py:634
  376.3 11.9 %assemble.6 = (bf16[1024,3072]{1,0:T(8,128)(2,1)}, bf16[1024,1024]{1,0:T(8,128)(2,1)}, bf16[1024,4096]{1,0:T(8,128)(2,1)}, bf16[4096,1024]{1,0:T(8,128)(2,1)}) custom-call(s32[5,8]{1,0:T(8,128)} %stack.185.info_ref, bf16[8,2,64,1024]{3,2,1,0:T(8,128)(2,1)} %pad_maximum_fusion.8.refs_0_, bf16[8,2,64,1024]{3,2,1,0:T(8,128)(2,1)} %pad_maximum_fusion.9.refs_1_, ...), custom_call_target="tpu_custom_call" | custom-call | bytes 25165824 | tf_op jit(solution)/shard_map/assemble/pallas_call | solution.py:107
  388.2 12.0 %assemble.7 = (bf16[1024,3072]{1,0:T(8,128)(2,1)}, bf16[1024,1024]{1,0:T(8,128)(2,1)}, bf16[1024,4096]{1,0:T(8,128)(2,1)}, bf16[4096,1024]{1,0:T(8,128)(2,1)}) custom-call(s32[5,8]{1,0:T(8,128)} %stack.180.info_ref, bf16[8,2,64,1024]{3,2,1,0:T(8,128)(2,1)} %pad_maximum_fusion.11.refs_0_, ...), custom_call_target="tpu_custom_call", output_to_operand_aliasing={{0}: (7, {}), {1}: (8, {}), {2}: (9, {}), {3}: (10, {})} | custom-call | bytes 25165824 | tf_op jit(solution)/shard_map/assemble/pallas_call | solution.py:107
  400.2 14.5 %attention_forward.5 = (bf16[256,1024]{1,0:T(8,128)(2,1)}, bf16[256,1024]{1,0:T(8,128)(2,1)}, bf16[256,1024]{1,0:T(8,128)(2,1)}, bf16[256,1024]{1,0:T(8,128)(2,1...) custom-call(s32[2,2]{1,0:T(2,128)S(1)} %broadcast_select_fusion.17.facts_ref, ...), custom_call_target="tpu_custom_call" | custom-call | flops 2147483648 | bytes 13631488 | tf_op jit(solution)/shard_map/attention_forward/pallas_call | solution.py:551
  414.8 16.0 %feed_forward.5 = (bf16[256,4096]{1,0:T(8,128)(2,1)}, bf16[256,4096]{1,0:T(8,128)(2,1)}, bf16[256,128]{1,0:T(8,128)(2,1)}, bf16[256,128]{1,0:T(8,128)(2,1)}, f32[256,1024]{1,0:T(8,128)S(1)}, /*index=5*/f32[8,128]{1,0:T(8,128)}) custom-call(s32[2,2]{1,0:T(2,128)S(1)} %broadcast_select_fusion.17.facts_ref, f32[256,1024]{1,0:T(8,128)S(1)} %copy-done.14, ...), custom_call_target="tpu_custom_call" | custom-call | flops 4294967296 | bytes 24117248 | tf_op jit(solution)/shard_map/feed_forward/pallas_call | solution.py:634
  432.6 27.0 %collective-permute-done.62 = bf16[256,1024]{1,0:T(8,128)(2,1)S(1)} collective-permute-done((bf16[256,1024]{1,0:T(8,128)(2,1)S(1)}, bf16[256,1024]{1,0:T(8,128)(2,1)S(1)}, u32[]{:S(2)}, u32[]{:S(2)}) %collective-permute-start.62) | collective-permute-done | bytes 524320 | tf_op jit(solution)/shard_map/ppermute | solution.py:1043
  459.9 13.9 %attention_forward.6 = (bf16[256,1024]{1,0:T(8,128)(2,1)S(1)}, bf16[256,1024]{1,0:T(8,128)(2,1)S(1)}, bf16[256,1024]{1,0:T(8,128)(2,1)S(1)}, bf16[256,1024]{1,0:...) custom-call(s32[2,2]{1,0:T(2,128)S(1)} %broadcast_select_fusion.17.facts_ref,, ...), custom_call_target="tpu_custom_call" | custom-call | flops 2147483648 | bytes 13631488 | tf_op jit(solution)/shard_map/attention_forward/pallas_call | solution.py:551
  473.9 16.0 %feed_forward.6 = (bf16[256,4096]{1,0:T(8,128)(2,1)}, bf16[256,4096]{1,0:T(8,128)(2,1)}, bf16[256,128]{1,0:T(8,128)(2,1)S(1)}, bf16[256,128]{1,0:T(8,128)(2,1)S(...) custom-call(s32[2,2]{1,0:T(2,128)S(1)} %broadcast_select_fusion.17.facts_ref, ...), custom_call_target="tpu_custom_call" | custom-call | flops 4294967296 | bytes 24117248 | tf_op jit(solution)/shard_map/feed_forward/pallas_call | solution.py:634
  489.9 14.0 %attention_forward.7 = (bf16[256,1024]{1,0:T(8,128)(2,1)S(1)}, bf16[256,1024]{1,0:T(8,128)(2,1)S(1)}, bf16[256,1024]{1,0:T(8,128)(2,1)S(1)}, bf16[256,1024]{1,0:...) custom-call(s32[2,2]{1,0:T(2,128)S(1)} %broadcast_select_fusion.17.facts_ref,, ...), custom_call_target="tpu_custom_call" | custom-call | flops 2147483648 | bytes 13631488 | tf_op jit(solution)/shard_map/attention_forward/pallas_call | solution.py:551
  503.9 15.9 %feed_forward.7 = (bf16[256,4096]{1,0:T(8,128)(2,1)}, bf16[256,4096]{1,0:T(8,128)(2,1)}, bf16[256,128]{1,0:T(8,128)(2,1)S(1)}, bf16[256,128]{1,0:T(8,128)(2,1)S(...) custom-call(s32[2,2]{1,0:T(2,128)S(1)} %broadcast_select_fusion.17.facts_ref, ...), custom_call_target="tpu_custom_call" | custom-call | flops 4294967296 | bytes 24117248 | tf_op jit(solution)/shard_map/feed_forward/pallas_call | solution.py:634
  520.9 16.7 %feed_backward.4 = (bf16[136,16384]{1,0:T(8,128)(2,1)}, f32[256,1024]{1,0:T(8,128)S(1)}) custom-call(s32[2,2]{1,0:T(2,128)S(1)} %broadcast_select_fusion.17.facts_ref, f32[256,1024]{1,0:T(8,128)S(1)} %bitcast.165, f32[256,1024]{1,0:T(8,128)S(1)} %get-tuple-element.312.x_ref, f32[4,1024]{1,0:T(4,128)S(1)} %broadcast_select_fusion.15.norm_ref, ...), custom_call_target="tpu_custom_call" | custom-call | flops 4294967296 | bytes 25165824 | tf_op jit(solution)/shard_map/feed_backward/pallas_call | solution.py:722
  537.7 18.3 %attention_backward.4 = (bf16[136,16384]{1,0:T(8,128)(2,1)}, f32[256,1024]{1,0:T(8,128)S(1)}) custom-call(s32[2,2]{1,0:T(2,128)S(1)} %broadcast_select_fusion.17.facts_ref, f32[256,1024]{1,0:T(8,128)S(1)} %bitcast.166, f32[256,1024]{1,0:T(8,128)S(1)} %get-tuple-element.320.gx_ref, f32[256,1024]{1,0:T(8,128)} %copy-done.8, ...), custom_call_target="tpu_custom_call", output_to_operand_aliasing={{0}: (22, {})} | custom-call | flops 2147483648 | bytes 16777216 | tf_op jit(solution)/shard_map/attention_backward/pallas_call | solution.py:833
  566.9 17.0 %feed_backward.5 = (bf16[136,16384]{1,0:T(8,128)(2,1)}, f32[256,1024]{1,0:T(8,128)S(1)}) custom-call(s32[2,2]{1,0:T(2,128)S(1)} %broadcast_select_fusion.17.facts_ref, f32[256,1024]{1,0:T(8,128)S(1)} %copy-done.16, f32[256,1024]{1,0:T(8,128)S(1)} %convert_select_fusion.2.x_ref, f32[4,1024]{1,0:T(4,128)S(1)} %broadcast_select_fusion.16.norm_ref, ...), custom_call_target="tpu_custom_call" | custom-call | flops 4294967296 | bytes 25165824 | tf_op jit(solution)/shard_map/feed_backward/pallas_call | solution.py:722
  584.0 18.0 %attention_backward.5 = (bf16[136,16384]{1,0:T(8,128)(2,1)}, f32[256,1024]{1,0:T(8,128)S(1)}) custom-call(s32[2,2]{1,0:T(2,128)S(1)} %broadcast_select_fusion.17.facts_ref, f32[256,1024]{1,0:T(8,128)S(1)} %copy-done.17, f32[256,1024]{1,0:T(8,128)S(1)} %get-tuple-element.334.gx_ref, f32[256,1024]{1,0:T(8,128)} %copy-done.6, ...), custom_call_target="tpu_custom_call", output_to_operand_aliasing={{0}: (22, {})} | custom-call | flops 2147483648 | bytes 16777216 | tf_op jit(solution)/shard_map/attention_backward/pallas_call | solution.py:833
  649.1 16.7 %feed_backward.6 = (bf16[136,16384]{1,0:T(8,128)(2,1)}, f32[256,1024]{1,0:T(8,128)S(1)}) custom-call(s32[2,2]{1,0:T(2,128)S(1)} %broadcast_select_fusion.17.facts_ref, f32[256,1024]{1,0:T(8,128)S(1)} %convert_select_fusion.1.g_ref, f32[256,1024]{1,0:T(8,128)S(1)} %copy-done.9, f32[4,1024]{1,0:T(4,128)S(1)} %broadcast_select_fusion.15.norm_ref, ...), custom_call_target="tpu_custom_call" | custom-call | flops 4294967296 | bytes 25165824 | tf_op jit(solution)/shard_map/feed_backward/pallas_call | solution.py:722
  665.9 18.1 %attention_backward.6 = (bf16[136,16384]{1,0:T(8,128)(2,1)}, f32[256,1024]{1,0:T(8,128)S(1)}) custom-call(s32[2,2]{1,0:T(2,128)S(1)} %broadcast_select_fusion.17.facts_ref, f32[256,1024]{1,0:T(8,128)S(1)} %convert_select_fusion.1.g_ref, f32[256,1024]{1,0:T(8,128)S(1)} %get-tuple-element.343.gx_ref, ...), custom_call_target="tpu_custom_call", output_to_operand_aliasing={{0}: (22, {})} | custom-call | flops 2147483648 | bytes 16777216 | tf_op jit(solution)/shard_map/attention_backward/pallas_call | solution.py:833
  687.6 10.5 %collective-permute-start.72 = (bf16[96,2048]{1,0:T(8,128)(2,1)S(1)}, bf16[96,2048]{1,0:T(8,128)(2,1)S(1)}, u32[]{:S(2)}, u32[]{:S(2)}) collective-permute-start(bf16[96,2048]{1,0:T(8,128)(2,1)S(1)} %constant_dynamic-slice_fusion.23), channel_id=1, source_target_pairs={{8,12},{9,13},{10,14},{11,15},{12,8},{13,9},{14,10},{15,11},{24,28... | collective-permute-start | bytes 1179656 | tf_op jit(solution)/shard_map/ppermute | solution.py:131
  723.0 17.1 %feed_backward.7 = (bf16[136,16384]{1,0:T(8,128)(2,1)}, f32[256,1024]{1,0:T(8,128)S(1)}) custom-call(s32[2,2]{1,0:T(2,128)S(1)} %broadcast_select_fusion.17.facts_ref, f32[256,1024]{1,0:T(8,128)S(1)} %copy-done.11, f32[256,1024]{1,0:T(8,128)S(1)} %copy-done.7, f32[4,1024]{1,0:T(4,128)S(1)} %broadcast_select_fusion.16.norm_ref, ...), custom_call_target="tpu_custom_call" | custom-call | flops 4294967296 | bytes 25165824 | tf_op jit(solution)/shard_map/feed_backward/pallas_call | solution.py:722
  740.1 18.0 %attention_backward.7 = (bf16[136,16384]{1,0:T(8,128)(2,1)}, f32[256,1024]{1,0:T(8,128)S(1)}) custom-call(s32[2,2]{1,0:T(2,128)S(1)} %broadcast_select_fusion.17.facts_ref, f32[256,1024]{1,0:T(8,128)S(1)} %copy-done.12, f32[256,1024]{1,0:T(8,128)S(1)} %get-tuple-element.346.gx_ref, f32[256,1024]{1,0:T(8,128)} %copy-done.6, ...), custom_call_target="tpu_custom_call", output_to_operand_aliasing={{0}: (22, {})} | custom-call | flops 2147483648 | bytes 16777216 | tf_op jit(solution)/shard_map/attention_backward/pallas_call | solution.py:833
  800.4 12.5 %collective-permute-start.107 = (bf16[1,48,1024]{2,1,0:T(8,128)(2,1)S(1)}, bf16[1,48,1024]{2,1,0:T(8,128)(2,1)S(1)}, u32[]{:S(2)}, u32[]{:S(2)}) collective-permute-start(bf16[1,48,1024]{2,1,0:T(8,128)(2,1)S(1)} %select_bitcast_fusion.6), channel_id=1, source_target_pairs={{0,4},{1,5},{2,6},{3,7},{4,0},{5,1},{6,2},{7,3},{8,12},{9,13},{10,... | collective-permute-start | bytes 294920 | tf_op jit(solution)/shard_map/ppermute | solution.py:36
  813.5 37.5 %collective-permute-done.111 = bf16[40,1024]{1,0:T(8,128)(2,1)S(1)} collective-permute-done((bf16[40,1024]{1,0:T(8,128)(2,1)S(1)}, bf16[40,1024]{1,0:T(8,128)(2,1)S(1)}, u32[]{:S(2)}, u32[]{:S(2)}) %collective-permute-start.111) | collective-permute-done | bytes 81952 | tf_op jit(solution)/shard_map/ppermute | solution.py:131
  1021.5 16.9 %finish.1 = (f32[2,1024,128]{2,1,0:T(8,128)}, f32[2,128,3072]{2,1,0:T(8,128)}, f32[2,1024,128]{2,1,0:T(8,128)}, f32[2,128,1024]{2,1,0:T(8,128)}, f32[2,1024,128]...) custom-call(s32[1]{0:T(128)} %bitcast.60.info_ref, ...), custom_call_target="tpu_custom_call" | custom-call | flops 1073741824 | bytes 50331648 | tf_op jit(solution)/shard_map/finish/pallas_call | solution.py:369
  (985 shorter events, 488.3 us)
Async XLA Ops:
  42.8 44.0 %collective-permute-start.14 = (bf16[7168,128]{1,0:T(8,128)(2,1)S(1)}, bf16[7168,128]{1,0:T(8,128)(2,1)S(1)}, u32[]{:S(2)}, u32[]{:S(2)}) collective-permute-start(bf16[7168,128]{1,0:T(8,128)(2,1)S(1)} %copy-done.180), channel_id=1, source_target_pairs={{0,16},{1,17},{2,18},{3,19},{4,20},{5,21},{6,22},{7,23},{24,8},{25... | collective-permute-start | bytes 5505032 | tf_op jit(solution)/shard_map/ppermute | solution.py:27
  44.1 42.8 %collective-permute-start.15 = (bf16[128,9216]{1,0:T(8,128)(2,1)S(1)}, bf16[128,9216]{1,0:T(8,128)(2,1)S(1)}, u32[]{:S(2)}, u32[]{:S(2)}) collective-permute-start(bf16[128,9216]{1,0:T(8,128)(2,1)S(1)} %copy-done.120), channel_id=1, source_target_pairs={{0,16},{1,17},{2,18},{3,19},{4,20},{5,21},{6,22},{7,23},{24,8},{25... | collective-permute-start | bytes 7077896 | tf_op jit(solution)/shard_map/ppermute | solution.py:27
  86.9 36.1 %collective-permute-start.20 = (bf16[4,2,64,1024]{3,2,1,0:T(8,128)(2,1)S(1)}, bf16[4,2,64,1024]{3,2,1,0:T(8,128)(2,1)S(1)}, u32[]{:S(2)}, u32[]{:S(2)}) collective-permute-start(bf16[4,2,64,1024]{3,2,1,0:T(8,128)(2,1)S(1)} %pad_maximum_fusion.19), channel_id=1, source_target_pairs={{0,4},{1,5},{2,6},{3,7},{4,0},{5,1},{6,2},{7,3},{8,12},{9,13},{10,... | collective-permute-start | bytes 3145736 | tf_op jit(solution)/shard_map/ppermute | solution.py:36
  89.1 34.1 %collective-permute-start.21 = (bf16[4,2,64,1024]{3,2,1,0:T(8,128)(2,1)S(1)}, bf16[4,2,64,1024]{3,2,1,0:T(8,128)(2,1)S(1)}, u32[]{:S(2)}, u32[]{:S(2)}) collective-permute-start(bf16[4,2,64,1024]{3,2,1,0:T(8,128)(2,1)S(1)} %pad_maximum_fusion.20), channel_id=1, source_target_pairs={{0,1},{1,0},{2,3},{3,2},{4,5},{5,4},{6,7},{7,6},{8,9},{9,8},{10,11... | collective-permute-start | bytes 3145736 | tf_op jit(solution)/shard_map/ppermute | solution.py:36
  90.6 32.8 %collective-permute-start.22 = (bf16[4,2,64,1024]{3,2,1,0:T(8,128)(2,1)S(1)}, bf16[4,2,64,1024]{3,2,1,0:T(8,128)(2,1)S(1)}, u32[]{:S(2)}, u32[]{:S(2)}) collective-permute-start(bf16[4,2,64,1024]{3,2,1,0:T(8,128)(2,1)S(1)} %pad_maximum_fusion.21), channel_id=1, source_target_pairs={{0,2},{1,3},{2,0},{3,1},{4,6},{5,7},{6,4},{7,5},{8,10},{9,11},{10,... | collective-permute-start | bytes 3145736 | tf_op jit(solution)/shard_map/ppermute | solution.py:36
  121.0 37.1 %collective-permute-start.28 = (bf16[6,64,1024]{2,1,0:T(8,128)(2,1)S(1)}, bf16[6,64,1024]{2,1,0:T(8,128)(2,1)S(1)}, u32[]{:S(2)}, u32[]{:S(2)}) collective-permute-start(bf16[6,64,1024]{2,1,0:T(8,128)(2,1)S(1)} %get-tuple-element.257), channel_id=1, source_target_pairs={{16,8},{17,9},{18,10},{19,11},{20,12},{21,13},{22,14},{23,15},{8,1... | collective-permute-start | bytes 2359304 | tf_op jit(solution)/shard_map/ppermute | solution.py:27
  123.7 40.0 %collective-permute-start.23 = (bf16[2,128,1024]{2,1,0:T(8,128)(2,1)S(1)}, bf16[2,128,1024]{2,1,0:T(8,128)(2,1)S(1)}, u32[]{:S(2)}, u32[]{:S(2)}) collective-permute-start(bf16[2,128,1024]{2,1,0:T(8,128)(2,1)S(1)} %broadcast_select_fusion.13), channel_id=1, source_target_pairs={{16,8},{17,9},{18,10},{19,11},{20,12},{21,13},{22,14},{23,15},{8,1... | collective-permute-start | bytes 1572872 | tf_op jit(solution)/shard_map/ppermute | solution.py:27
  128.2 36.0 %collective-permute-start.24 = (bf16[2,2,64,1024]{3,2,1,0:T(8,128)(2,1)S(1)}, bf16[2,2,64,1024]{3,2,1,0:T(8,128)(2,1)S(1)}, u32[]{:S(2)}, u32[]{:S(2)}) collective-permute-start(bf16[2,2,64,1024]{3,2,1,0:T(8,128)(2,1)S(1)} %pad_maximum_fusion.43), channel_id=1, source_target_pairs={{0,2},{1,3},{2,0},{3,1},{4,6},{5,7},{6,4},{7,5},{8,10},{9,11},{10,... | collective-permute-start | bytes 1572872 | tf_op jit(solution)/shard_map/ppermute | solution.py:36
  128.8 36.0 %collective-permute-start.25 = (bf16[2,2,64,1024]{3,2,1,0:T(8,128)(2,1)S(1)}, bf16[2,2,64,1024]{3,2,1,0:T(8,128)(2,1)S(1)}, u32[]{:S(2)}, u32[]{:S(2)}) collective-permute-start(bf16[2,2,64,1024]{3,2,1,0:T(8,128)(2,1)S(1)} %pad_maximum_fusion.44), channel_id=1, source_target_pairs={{0,4},{1,5},{2,6},{3,7},{4,0},{5,1},{6,2},{7,3},{8,12},{9,13},{10,... | collective-permute-start | bytes 1572872 | tf_op jit(solution)/shard_map/ppermute | solution.py:36
  186.2 40.9 %collective-permute-start.38 = (bf16[4,2,64,1024]{3,2,1,0:T(8,128)(2,1)}, bf16[4,2,64,1024]{3,2,1,0:T(8,128)(2,1)}, u32[]{:S(2)}, u32[]{:S(2)}) collective-permute-start(bf16[4,2,64,1024]{3,2,1,0:T(8,128)(2,1)} %pad_maximum_fusion.22), channel_id=1, source_target_pairs={{0,4},{1,5},{2,6},{3,7},{4,0},{5,1},{6,2},{7,3},{8,12},{9,13},{10,... | collective-permute-start | bytes 3145736 | tf_op jit(solution)/shard_map/ppermute | solution.py:36
  188.2 41.7 %collective-permute-start.39 = (bf16[4,2,64,1024]{3,2,1,0:T(8,128)(2,1)}, bf16[4,2,64,1024]{3,2,1,0:T(8,128)(2,1)S(1)}, u32[]{:S(2)}, u32[]{:S(2)}) collective-permute-start(bf16[4,2,64,1024]{3,2,1,0:T(8,128)(2,1)} %pad_maximum_fusion.23), channel_id=1, source_target_pairs={{0,1},{1,0},{2,3},{3,2},{4,5},{5,4},{6,7},{7,6},{8,9},{9,8},{10,11... | collective-permute-start | bytes 3145736 | tf_op jit(solution)/shard_map/ppermute | solution.py:36
  189.6 41.9 %collective-permute-start.40 = (bf16[4,2,64,1024]{3,2,1,0:T(8,128)(2,1)}, bf16[4,2,64,1024]{3,2,1,0:T(8,128)(2,1)S(1)}, u32[]{:S(2)}, u32[]{:S(2)}) collective-permute-start(bf16[4,2,64,1024]{3,2,1,0:T(8,128)(2,1)} %pad_maximum_fusion.24), channel_id=1, source_target_pairs={{0,2},{1,3},{2,0},{3,1},{4,6},{5,7},{6,4},{7,5},{8,10},{9,11},{10,... | collective-permute-start | bytes 3145736 | tf_op jit(solution)/shard_map/ppermute | solution.py:36
  233.1 35.7 %collective-permute-start.50 = (bf16[4,2,64,1024]{3,2,1,0:T(8,128)(2,1)}, bf16[4,2,64,1024]{3,2,1,0:T(8,128)(2,1)}, u32[]{:S(2)}, u32[]{:S(2)}) collective-permute-start(bf16[4,2,64,1024]{3,2,1,0:T(8,128)(2,1)} %pad_maximum_fusion.25), channel_id=1, source_target_pairs={{0,4},{1,5},{2,6},{3,7},{4,0},{5,1},{6,2},{7,3},{8,12},{9,13},{10,... | collective-permute-start | bytes 3145736 | tf_op jit(solution)/shard_map/ppermute | solution.py:36
  238.1 39.6 %collective-permute-start.51 = (bf16[4,2,64,1024]{3,2,1,0:T(8,128)(2,1)}, bf16[4,2,64,1024]{3,2,1,0:T(8,128)(2,1)S(1)}, u32[]{:S(2)}, u32[]{:S(2)}) collective-permute-start(bf16[4,2,64,1024]{3,2,1,0:T(8,128)(2,1)} %pad_maximum_fusion.26), channel_id=1, source_target_pairs={{0,1},{1,0},{2,3},{3,2},{4,5},{5,4},{6,7},{7,6},{8,9},{9,8},{10,11... | collective-permute-start | bytes 3145736 | tf_op jit(solution)/shard_map/ppermute | solution.py:36
  284.9 38.7 %collective-permute-start.54 = (bf16[4,2,64,1024]{3,2,1,0:T(8,128)(2,1)}, bf16[4,2,64,1024]{3,2,1,0:T(8,128)(2,1)}, u32[]{:S(2)}, u32[]{:S(2)}) collective-permute-start(bf16[4,2,64,1024]{3,2,1,0:T(8,128)(2,1)} %pad_maximum_fusion.29), channel_id=1, source_target_pairs={{0,1},{1,0},{2,3},{3,2},{4,5},{5,4},{6,7},{7,6},{8,9},{9,8},{10,11... | collective-permute-start | bytes 3145736 | tf_op jit(solution)/shard_map/ppermute | solution.py:36
  285.5 41.0 %collective-permute-start.55 = (bf16[4,2,64,1024]{3,2,1,0:T(8,128)(2,1)}, bf16[4,2,64,1024]{3,2,1,0:T(8,128)(2,1)}, u32[]{:S(2)}, u32[]{:S(2)}) collective-permute-start(bf16[4,2,64,1024]{3,2,1,0:T(8,128)(2,1)} %pad_maximum_fusion.30), channel_id=1, source_target_pairs={{0,2},{1,3},{2,0},{3,1},{4,6},{5,7},{6,4},{7,5},{8,10},{9,11},{10,... | collective-permute-start | bytes 3145736 | tf_op jit(solution)/shard_map/ppermute | solution.py:36
  286.0 43.4 %collective-permute-start.56 = (bf16[8,2,64,1024]{3,2,1,0:T(8,128)(2,1)}, bf16[8,2,64,1024]{3,2,1,0:T(8,128)(2,1)}, u32[]{:S(2)}, u32[]{:S(2)}) collective-permute-start(bf16[8,2,64,1024]{3,2,1,0:T(8,128)(2,1)} %pad_maximum_fusion.8.refs_0_), channel_id=1, source_target_pairs={{0,16},{16,0},{1,17},{17,1},{2,18},{18,2},{3,19},{19,3},{4,20},{20... | collective-permute-start | bytes 6291464 | tf_op jit(solution)/shard_map/ppermute | solution.py:40
  286.0 43.4 %collective-permute-start.57 = (bf16[8,2,64,1024]{3,2,1,0:T(8,128)(2,1)}, bf16[8,2,64,1024]{3,2,1,0:T(8,128)(2,1)}, u32[]{:S(2)}, u32[]{:S(2)}) collective-permute-start(bf16[8,2,64,1024]{3,2,1,0:T(8,128)(2,1)} %pad_maximum_fusion.9.refs_1_), channel_id=1, source_target_pairs={{0,16},{16,0},{1,17},{17,1},{2,18},{18,2},{3,19},{19,3},{4,20},{20... | collective-permute-start | bytes 6291464 | tf_op jit(solution)/shard_map/ppermute | solution.py:40
  329.4 58.7 %collective-permute-start.59 = (bf16[8,2,64,1024]{3,2,1,0:T(8,128)(2,1)}, bf16[8,2,64,1024]{3,2,1,0:T(8,128)(2,1)}, u32[]{:S(2)}, u32[]{:S(2)}) collective-permute-start(bf16[8,2,64,1024]{3,2,1,0:T(8,128)(2,1)} %pad_maximum_fusion.11.refs_0_), channel_id=1, source_target_pairs={{0,16},{16,0},{1,17},{17,1},{2,18},{18,2},{3,19},{19,3},{4,20},{20... | collective-permute-start | bytes 6291464 | tf_op jit(solution)/shard_map/ppermute | solution.py:40
  329.5 58.6 %collective-permute-start.60 = (bf16[8,2,64,1024]{3,2,1,0:T(8,128)(2,1)}, bf16[8,2,64,1024]{3,2,1,0:T(8,128)(2,1)}, u32[]{:S(2)}, u32[]{:S(2)}) collective-permute-start(bf16[8,2,64,1024]{3,2,1,0:T(8,128)(2,1)} %pad_maximum_fusion.12.refs_1_), channel_id=1, source_target_pairs={{0,16},{16,0},{1,17},{17,1},{2,18},{18,2},{3,19},{19,3},{4,20},{20... | collective-permute-start | bytes 6291464 | tf_op jit(solution)/shard_map/ppermute | solution.py:40
  330.0 58.1 %collective-permute-start.61 = (bf16[8,2,64,1024]{3,2,1,0:T(8,128)(2,1)}, bf16[8,2,64,1024]{3,2,1,0:T(8,128)(2,1)}, u32[]{:S(2)}, u32[]{:S(2)}) collective-permute-start(bf16[8,2,64,1024]{3,2,1,0:T(8,128)(2,1)} %pad_maximum_fusion.13.refs_2_), channel_id=1, source_target_pairs={{0,16},{16,0},{1,17},{17,1},{2,18},{18,2},{3,19},{19,3},{4,20},{20... | collective-permute-start | bytes 6291464 | tf_op jit(solution)/shard_map/ppermute | solution.py:40
  559.5 51.8 %collective-permute-start.67 = (bf16[136,8192]{1,0:T(8,128)(2,1)}, bf16[136,8192]{1,0:T(8,128)(2,1)}, u32[]{:S(2)}, u32[]{:S(2)}) collective-permute-start(bf16[136,8192]{1,0:T(8,128)(2,1)} %constant_dynamic-slice_fusion.25), channel_id=1, source_target_pairs={{8,24},{9,25},{10,26},{11,27},{12,28},{13,29},{14,30},{15,31},{24,... | collective-permute-start | bytes 6684680 | tf_op jit(solution)/shard_map/ppermute | solution.py:27
  645.3 52.9 %collective-permute-start.73 = (bf16[80,2048]{1,0:T(8,128)(2,1)S(1)}, bf16[80,2048]{1,0:T(8,128)(2,1)S(1)}, u32[]{:S(2)}, u32[]{:S(2)}) collective-permute-start(bf16[80,2048]{1,0:T(8,128)(2,1)S(1)} %constant_dynamic-slice_fusion.22), channel_id=1, source_target_pairs={{8,9},{9,8},{10,11},{11,10},{12,13},{13,12},{14,15},{15,14},{24,25... | collective-permute-start | bytes 983048 | tf_op jit(solution)/shard_map/ppermute | solution.py:131
  719.5 38.6 %collective-permute-start.77 = (bf16[136,8192]{1,0:T(8,128)(2,1)}, bf16[136,8192]{1,0:T(8,128)(2,1)}, u32[]{:S(2)}, u32[]{:S(2)}) collective-permute-start(bf16[136,8192]{1,0:T(8,128)(2,1)} %constant_dynamic-slice_fusion.18), channel_id=1, source_target_pairs={{0,16},{1,17},{2,18},{3,19},{4,20},{5,21},{6,22},{7,23},{16,0},{17... | collective-permute-start | bytes 6684680 | tf_op jit(solution)/shard_map/ppermute | solution.py:27
  796.3 54.7 %collective-permute-start.111 = (bf16[40,1024]{1,0:T(8,128)(2,1)S(1)}, bf16[40,1024]{1,0:T(8,128)(2,1)S(1)}, u32[]{:S(2)}, u32[]{:S(2)}) collective-permute-start(bf16[40,1024]{1,0:T(8,128)(2,1)S(1)} %add_convert_fusion.29), channel_id=1, source_target_pairs={{0,8},{1,9},{2,10},{3,11},{4,12},{5,13},{6,14},{7,15},{16,24},{17,... | collective-permute-start | bytes 245768 | tf_op jit(solution)/shard_map/ppermute | solution.py:131
  797.6 54.7 %collective-permute-start.109 = (bf16[1,40,1024]{2,1,0:T(8,128)(2,1)S(1)}, bf16[1,40,1024]{2,1,0:T(8,128)(2,1)S(1)}, u32[]{:S(2)}, u32[]{:S(2)}) collective-permute-start(bf16[1,40,1024]{2,1,0:T(8,128)(2,1)S(1)} %select_bitcast_fusion.8), channel_id=1, source_target_pairs={{0,2},{1,3},{2,0},{3,1},{4,6},{5,7},{6,4},{7,5},{8,10},{9,11},{10,... | collective-permute-start | bytes 245768 | tf_op jit(solution)/shard_map/ppermute | solution.py:36
  799.1 57.1 %collective-permute-start.103 = (bf16[48,1024]{1,0:T(8,128)(2,1)S(1)}, bf16[48,1024]{1,0:T(8,128)(2,1)S(1)}, u32[]{:S(2)}, u32[]{:S(2)}) collective-permute-start(bf16[48,1024]{1,0:T(8,128)(2,1)S(1)} %add_convert_fusion.26), channel_id=1, source_target_pairs={{0,8},{1,9},{2,10},{3,11},{4,12},{5,13},{6,14},{7,15},{16,24},{17,... | collective-permute-start | bytes 294920 | tf_op jit(solution)/shard_map/ppermute | solution.py:131
  800.4 58.8 %collective-permute-start.107 = (bf16[1,48,1024]{2,1,0:T(8,128)(2,1)S(1)}, bf16[1,48,1024]{2,1,0:T(8,128)(2,1)S(1)}, u32[]{:S(2)}, u32[]{:S(2)}) collective-permute-start(bf16[1,48,1024]{2,1,0:T(8,128)(2,1)S(1)} %select_bitcast_fusion.6), channel_id=1, source_target_pairs={{0,4},{1,5},{2,6},{3,7},{4,0},{5,1},{6,2},{7,3},{8,12},{9,13},{10,... | collective-permute-start | bytes 294920 | tf_op jit(solution)/shard_map/ppermute | solution.py:36
  812.9 46.2 %collective-permute-start.108 = (bf16[1,48,1024]{2,1,0:T(8,128)(2,1)S(1)}, bf16[1,48,1024]{2,1,0:T(8,128)(2,1)S(1)}, u32[]{:S(2)}, u32[]{:S(2)}) collective-permute-start(bf16[1,48,1024]{2,1,0:T(8,128)(2,1)S(1)} %select_bitcast_fusion.5), channel_id=1, source_target_pairs={{0,1},{1,0},{2,3},{3,2},{4,5},{5,4},{6,7},{7,6},{8,9},{9,8},{10,11... | collective-permute-start | bytes 294920 | tf_op jit(solution)/shard_map/ppermute | solution.py:36
  942.2 35.2 %collective-permute-start.133 = (bf16[8,96,1024]{2,1,0:T(8,128)(2,1)}, bf16[8,96,1024]{2,1,0:T(8,128)(2,1)}, u32[]{:S(2)}, u32[]{:S(2)}) collective-permute-start(bf16[8,96,1024]{2,1,0:T(8,128)(2,1)} %pad_maximum_fusion.16.refs_0_), channel_id=1, source_target_pairs={{0,16},{1,17},{2,18},{3,19},{4,20},{5,21},{6,22},{7,23},{8,24},{9,... | collective-permute-start | bytes 4718600 | tf_op jit(solution)/shard_map/ppermute | solution.py:131
  945.5 31.9 %collective-permute-start.134 = (bf16[8,96,1024]{2,1,0:T(8,128)(2,1)}, bf16[8,96,1024]{2,1,0:T(8,128)(2,1)}, u32[]{:S(2)}, u32[]{:S(2)}) collective-permute-start(bf16[8,96,1024]{2,1,0:T(8,128)(2,1)} %pad_maximum_fusion.17.refs_1_), channel_id=1, source_target_pairs={{0,16},{1,17},{2,18},{3,19},{4,20},{5,21},{6,22},{7,23},{8,24},{9,... | collective-permute-start | bytes 4718600 | tf_op jit(solution)/shard_map/ppermute | solution.py:131
  977.5 34.5 %collective-permute-start.141 = (bf16[8,40,1024]{2,1,0:T(8,128)(2,1)}, bf16[8,40,1024]{2,1,0:T(8,128)(2,1)}, u32[]{:S(2)}, u32[]{:S(2)}) collective-permute-start(bf16[8,40,1024]{2,1,0:T(8,128)(2,1)} %pad_maximum_fusion.39.refs_2_), channel_id=1, source_target_pairs={{16,0},{17,1},{18,2},{19,3},{20,4},{21,5},{22,6},{23,7},{24,8},{25... | collective-permute-start | bytes 1966088 | tf_op jit(solution)/shard_map/ppermute | solution.py:131
  (350 other events, 5235.1 us)

commit v3 on v2

--- a/solution.py
+++ b/solution.py
@@ -40,280 +40,305 @@
     return lax.ppermute(value, "section", [(0, 1), (1, 0)])
 
 
-def split_units(matrices):
-    query, output, upper, down = matrices
-    rows = output.shape[0]
-    return [
-        query[:, :WIDE],
-        query[:, WIDE : 2 * WIDE],
-        query[:, 2 * WIDE :],
-        output,
-        upper[:, :WIDE],
-        upper[:, WIDE : 2 * WIDE],
-        upper[:, 2 * WIDE : 3 * WIDE],
-        upper[:, 3 * WIDE :],
-        down[:rows],
-        down[rows : 2 * rows],
-        down[2 * rows : 3 * rows],
-        down[3 * rows :],
-    ]
+def pack_kernel(info_ref, query_ref, output_ref, upper_ref, down_ref, keep_ref, send_ref):
+    rows = output_ref.shape[1]
+
+    def write(first, second):
+        for layer in range(output_ref.shape[0]):
+            first[layer, 0] = query_ref[layer, :, :WIDE]
+            first[layer, 1] = query_ref[layer, :, WIDE : 2 * WIDE]
+            first[layer, 2] = query_ref[layer, :, 2 * WIDE :]
+            first[layer, 3] = output_ref[layer]
+            first[layer, 4] = upper_ref[layer, :, :WIDE]
+            first[layer, 5] = upper_ref[layer, :, WIDE : 2 * WIDE]
+            second[layer, 0] = upper_ref[layer, :, 2 * WIDE : 3 * WIDE]
+            second[layer, 1] = upper_ref[layer, :, 3 * WIDE :]
+            for index in range(4):
+                second[layer, 2 + index] = down_ref[layer, index * rows : (index + 1) * rows]
+
+    @pl.when(info_ref[0] == 0)
+    def _():
+        write(keep_ref, send_ref)
+
+    @pl.when(info_ref[0] != 0)
+    def _():
+        write(send_ref, keep_ref)
+
+
+def pack_halves(core, frozen):
+    layers, rows = frozen[1].shape[:2]
+    shape = jax.ShapeDtypeStruct((layers, HALF_UNITS, rows, WIDE), jnp.bfloat16)
+    vmem = pl.BlockSpec(memory_space=pltpu.VMEM)
+    return pl.pallas_call(
+        pack_kernel,
+        out_shape=[shape, shape],
+        in_specs=[pl.BlockSpec(memory_space=pltpu.SMEM)] + [vmem] * 4,
+        out_specs=[vmem, vmem],
+        compiler_params=pltpu.CompilerParams(vmem_limit_bytes=32 << 20),
+        cost_estimate=pl.CostEstimate(
+            flops=0, bytes_accessed=8 * HALF_UNITS * layers * rows * WIDE, transcendentals=0
+        ),
+        name="pack",
+    )(core.reshape(1), *frozen)
 
 
 def rotations(masks):
     return [[masks[(start + index) % len(masks)] for index in range(len(masks))] for start in range(3)]
 
 
-def assemble_kernel(info_ref, *refs):
-    mine, theirs, outs = refs[:3], refs[3:6], refs[-4:]
-    query_out, output_out, upper_out, down_out = outs
-    rows = output_out.shape[0]
-
-    def write(first, second):
-        query_out[:, :WIDE] = first[0][0, 0]
-        query_out[:, WIDE : 2 * WIDE] = first[0][0, 1]
-        query_out[:, 2 * WIDE :] = first[1][0, 0]
-        output_out[...] = first[1][0, 1]
-        upper_out[:, :WIDE] = first[2][0, 0]
-        upper_out[:, WIDE : 2 * WIDE] = first[2][0, 1]
-        upper_out[:, 2 * WIDE : 3 * WIDE] = second[0][0, 0]
-        upper_out[:, 3 * WIDE :] = second[0][0, 1]
-        down_out[:rows] = second[1][0, 0]
-        down_out[rows : 2 * rows] = second[1][0, 1]
-        down_out[2 * rows : 3 * rows] = second[2][0, 0]
-        down_out[3 * rows :] = second[2][0, 1]
-
-    @pl.when(info_ref[0, 0] == 0)
-    def _():
-        write(mine, theirs)
-
-    @pl.when(info_ref[0, 0] != 0)
-    def _():
-        write(theirs, mine)
-
-
-def assemble(info, mine, theirs, rows, count, into):
-    blocks = mine[0].shape[0]
-
-    def source(part):
-        return pl.BlockSpec((1, 2, rows, WIDE), lambda step, info_ref: (info_ref[2 + part, step], 0, 0, 0))
-
-    def target(height, width):
-        return pl.BlockSpec((height, width), lambda step, info_ref: (info_ref[1, step], 0))
-
+def assemble_kernel(layout, info_ref, mine, theirs, *refs):
+    count = len({layer for layer, _ in layout})
+    outs, token_out, sem = refs[-4 * count - 2 : -2], refs[-2], refs[-1]
+    token_out[...] = jnp.zeros_like(token_out)
+    first_layer = min(layer for layer, _ in layout)
+    rows = mine.shape[2]
+
+    def targets(half_index, layer, part, place):
+        query_out, output_out, upper_out, down_out = outs[4 * (layer - first_layer) : 4 * (layer - first_layer) + 4]
+        at = pl.multiple_of(place * rows, rows)
+        down_at = pl.multiple_of(place * 4 * rows, rows)
+
+        def columns(out, index):
+            return out.at[pl.ds(at, rows), pl.ds(index * WIDE, WIDE)]
+
+        def down(index):
+            return down_out.at[pl.ds(down_at + index * rows, rows)]
+
+        return [
+            [(columns(query_out, 0), columns(query_out, 1)), (columns(query_out, 2), columns(output_out, 0)),
+             (columns(upper_out, 0), columns(upper_out, 1))],
+            [(columns(upper_out, 2), columns(upper_out, 3)), (down(0), down(1)), (down(2), down(3))],
+        ][half_index][part]
+
+    def run(first, second):
+        copies = []
+        for block, (layer, part) in enumerate(layout):
+            for half_index, source in enumerate((first, second)):
+                for unit, target in enumerate(targets(half_index, layer, part, info_ref[1 + block])):
+                    where = sem.at[block, half_index * 2 + unit]
+                    copies.append(pltpu.make_async_copy(source.at[block, unit], target, where))
+                    copies[-1].start()
+        for copy in copies:
+            copy.wait()
+
+    @pl.when(info_ref[0] == 0)
+    def _():
+        run(mine, theirs)
+
+    @pl.when(info_ref[0] != 0)
+    def _():
+        run(theirs, mine)
+
+
+def assemble(info, layout, mine, theirs, count, into):
+    rows = mine.shape[2]
     total = rows * count
-    shapes = [(total, 3 * WIDE), (total, WIDE), (total, 4 * WIDE), (4 * total, WIDE)]
-    extra = [] if into is None else list(into)
-    size = 2 * 2 * UNITS * rows * WIDE * blocks
+    layers = sorted({layer for layer, _ in layout})
+    shapes = [(total, 3 * WIDE), (total, WIDE), (total, 4 * WIDE), (4 * total, WIDE)] * len(layers)
+    extra = [matrix for layer in layers for matrix in (into[layer] or ())]
+    anywhere = pl.BlockSpec(memory_space=pltpu.HBM)
+    aliases, index = {}, 3
+    for position, layer in enumerate(layers):
+        if into[layer]:
+            for matrix in range(4):
+                aliases[index] = 4 * position + matrix
+                index = index + 1
+    made = pl.pallas_call(
+        partial(assemble_kernel, tuple(layout)),
+        out_shape=[jax.ShapeDtypeStruct(shape, jnp.bfloat16) for shape in shapes]
+        + [jax.ShapeDtypeStruct((8, 128), jnp.float32)],
+        in_specs=[pl.BlockSpec(memory_space=pltpu.SMEM)]
+        + [pl.BlockSpec(memory_space=pltpu.VMEM)] * 2
+        + [anywhere] * len(extra),
+        out_specs=[anywhere] * len(shapes) + [pl.BlockSpec(memory_space=pltpu.VMEM)],
+        scratch_shapes=[pltpu.SemaphoreType.DMA((len(layout), 4))],
+        input_output_aliases=aliases,
+        compiler_params=pltpu.CompilerParams(vmem_limit_bytes=60 << 20),
+        cost_estimate=pl.CostEstimate(flops=0, bytes_accessed=12 * mine.size, transcendentals=0),
+        name="assemble",
+    )(info, mine, theirs, *extra)
+    for position, layer in enumerate(layers):
+        into[layer] = made[4 * position : 4 * position + 4]
+    return made[-1]
+
+
+def copy_kernel(plans, *refs):
+    inputs, outs = refs[: -len(plans)], refs[-len(plans) :]
+    for plan, out in zip(plans, outs):
+        at = 0
+        for source, begin, size in plan:
+            out[at : at + size] = inputs[source][begin : begin + size]
+            at = at + size
+
+
+def copy_blocks(arrays, plans, after):
+    tail = arrays[0].shape[1:]
+    vmem = pl.BlockSpec(memory_space=pltpu.VMEM)
+    shapes = [jax.ShapeDtypeStruct((sum(size for _, _, size in plan),) + tail, jnp.bfloat16) for plan in plans]
+    moved = 4 * sum(shape.size for shape in shapes)
     return pl.pallas_call(
-        assemble_kernel,
-        out_shape=[jax.ShapeDtypeStruct(shape, jnp.bfloat16) for shape in shapes],
-        grid_spec=pltpu.PrefetchScalarGridSpec(
-            num_scalar_prefetch=1,
-            grid=(blocks,),
-            in_specs=[source(0), source(1), source(2)] * 2
-            + [pl.BlockSpec(memory_space=pl.ANY)] * len(extra),
-            out_specs=[target(rows, 3 * WIDE), target(rows, WIDE), target(rows, 4 * WIDE), target(4 * rows, WIDE)],
-        ),
-        input_output_aliases={7 + index: index for index in range(len(extra))},
-        cost_estimate=pl.CostEstimate(flops=0, bytes_accessed=size, transcendentals=0),
-        name="assemble",
-    )(info, *mine, *theirs, *extra)
-
-
-class Steps:
-    def __init__(self):
-        self.ended = ()
-
-    def run(self, *moves):
-        values = tuple(value for value, _ in moves)
-        if self.ended:
-            values = tie(values, *self.ended)
-        self.ended = tuple(send(value) for value, (_, send) in zip(values, moves))
-        return list(self.ended)
-
-
-def pick_halves(matrices, stage):
-    units = split_units(matrices)
-    first, second = jnp.stack(units[:HALF_UNITS]), jnp.stack(units[HALF_UNITS:])
-    return jnp.where(stage == 0, first, second), jnp.where(stage == 0, second, first)
+        partial(copy_kernel, tuple(tuple(plan) for plan in plans)),
+        out_shape=shapes,
+        in_specs=[vmem] * len(arrays) + [pl.BlockSpec(memory_space=pl.ANY)] * len(after),
+        out_specs=[vmem] * len(shapes),
+        compiler_params=pltpu.CompilerParams(vmem_limit_bytes=40 << 20),
+        cost_estimate=pl.CostEstimate(flops=0, bytes_accessed=moved, transcendentals=0),
+        name="collect",
+    )(*arrays, *after)
 
 
 class Gather:
-    def __init__(self, block, masks):
-        self.held = [block[2 * part : 2 * part + 2][None] for part in range(3)]
+    def __init__(self, layer, which, block, masks):
+        self.layer, self.which = layer, which
+        block = block.reshape((3, 2) + block.shape[1:])
+        self.block = block
+        self.held = [[(block, part, 1)] for part in range(3)]
         self.found = [[0], [0], [0]]
         self.turns = rotations(masks)
         self.step = 0
 
-    def moves(self):
-        return [
-            (self.held[part], partial(flip_place, mask=self.turns[part][self.step])) for part in range(3)
+
+class Store:
+    def __init__(self):
+        self.arrays = []
+
+    def index(self, array):
+        for position, known in enumerate(self.arrays):
+            if known is array:
+                return position
+        self.arrays.append(array)
+        return len(self.arrays) - 1
+
+
+def gather_step(active, masks, fresh, extra, after):
+    store = Store()
+    plans, lists = [], []
+    for mask in masks:
+        entries = [
+            (gather, part) for gather in active for part in range(3) if gather.turns[part][gather.step] == mask
         ]
-
-    def take(self, there):
-        for part in range(3):
-            self.held[part] = jnp.concatenate([self.held[part], there[part]], 0)
-            mask = self.turns[part][self.step]
-            self.found[part] = self.found[part] + [known ^ mask for known in self.found[part]]
-        self.step = self.step + 1
-        return there[3:]
-
-
-def part_rows(total):
-    first = (total // 3 + 15) // 16 * 16
-    return [(0, first), (first, 2 * first), (2 * first, total)]
-
-
-def side(value, which, axis=1):
-    size = value.shape[axis] // 2
-    return lax.dynamic_slice_in_dim(value, which * size, size, axis)
-
-
-def total_of(first, second):
-    return (first.astype(jnp.float32) + second.astype(jnp.float32)).astype(jnp.bfloat16)
-
-
-class Scatter:
-    def __init__(self, blocks, section, core, low, count, masks):
-        middle = count // 2
-        self.inside = [place for place in range(count) if place // middle == section]
-        self.swap = [(here * count + place, (1 - here) * count + place) for here in range(2) for place in self.inside]
-        self.blocks, self.core, self.low = blocks, core, low
-        self.turns = rotations(masks)
-        self.step = -1
-
-    def moves(self):
-        if self.step < 0:
-            return [(side(block, 1 - self.core), partial(both_axes, pairs=self.swap)) for block in self.blocks]
-        moves = []
-        for slab, turn in zip(self.slabs, self.turns):
-            mask = turn[self.step]
-            pairs = [(place, place ^ mask) for place in self.inside]
-            lower_side = ((self.low & mask) == 0).astype(jnp.int32)
-            moves.append((side(slab, lower_side), partial(lax.ppermute, axis_name="dp", perm=pairs)))
-        return moves
-
-    def take(self, there):
-        if self.step < 0:
-            used = len(self.blocks)
-            halves = [total_of(side(block, self.core), part) for block, part in zip(self.blocks, there)]
-            self.slabs = [
-                jnp.concatenate([part[begin:end] for part in halves], 0)
-                for begin, end in part_rows(halves[0].shape[0])
-            ]
-        else:
-            used = 3
-            for part in range(3):
-                upper_side = ((self.low & self.turns[part][self.step]) != 0).astype(jnp.int32)
-                self.slabs[part] = total_of(side(self.slabs[part], upper_side), there[part])
-        self.step = self.step + 1
-        return there[used:]
-
-
-def scatter_section(blocks, section, core, low, count, masks, steps):
-    scatter = Scatter(blocks, section, core, low, count, masks)
-    for step in range(len(masks) + 1):
-        scatter.take(steps.run(*scatter.moves()))
-    return scatter.slabs
-
-
-class Spread:
-    def __init__(self, slabs, section, masks, count, stage):
-        middle = count // 2
-        self.across = [(place, place ^ middle) for place in range(count) if place // middle == section]
-        self.held, self.section, self.here = slabs, section, stage == section
-        self.turns = [list(reversed(turn)) for turn in rotations(masks)]
-        self.step = -1
-
-    def done(self):
-        return self.step > len(self.turns[0])
-
-    def moves(self):
-        if self.step < 0:
-            return [(slab, partial(lax.ppermute, axis_name="dp", perm=self.across)) for slab in self.held]
-        if self.step == len(self.turns[0]):
-            pairs = [(1 - self.section, self.section)]
-            return [(held, partial(lax.ppermute, axis_name="section", perm=pairs)) for held in self.held]
-        return [(held, partial(flip_place, mask=turn[self.step])) for held, turn in zip(self.held, self.turns)]
-
-    def take(self, there):
-        if self.step < 0:
-            self.held = [jnp.where(self.here, held, part)[None] for held, part in zip(self.held, there)]
-        elif self.step == len(self.turns[0]):
-            self.theirs = there[:3]
-        else:
-            self.held = [jnp.concatenate([held, part], 0) for held, part in zip(self.held, there)]
-        self.step = self.step + 1
-        return there[3:]
-
-
-def place_kernel(section, layers, info_ref, *refs):
-    mine, theirs, olds, outs = refs[:3], refs[3:6], refs[6:-layers], refs[-layers:]
-
-    def write():
-        for source, target in ((mine, section), (theirs, 1 - section)):
-            begin = 0
-            for slab in source:
-                rows = slab.shape[1] // layers
-                for layer in range(layers):
-                    outs[layer][target, begin : begin + rows] = slab[0, layer * rows : (layer + 1) * rows]
-                begin = begin + rows
-
-    if not olds:
-        write()
-    else:
-        pl.when(info_ref[0, 0] == section)(write)
-
-        @pl.when(info_ref[0, 0] != section)
-        def _():
-            for old, out in zip(olds, outs):
-                out[...] = old[...]
-
-
-def place_section(section, core, low, masks, spread, olds, layers):
-    mine, theirs = spread.held, spread.theirs
-    pieces, _, columns = mine[0].shape
-    rows = sum(slab.shape[1] for slab in mine) // layers
-    step = jnp.arange(pieces, dtype=jnp.int32)
-    info = [jnp.full((pieces,), core, jnp.int32), step]
-    for turn in rotations(masks):
-        here = sum(((low & mask) != 0).astype(jnp.int32) << (len(masks) - 1 - index) for index, mask in enumerate(turn))
-        info.append(step ^ here)
-    info = jnp.stack(info)
-
-    def source(part):
-        return pl.BlockSpec((1, mine[part].shape[1], columns), lambda step, info_ref: (info_ref[2 + part, step], 0, 0))
-
-    target = pl.BlockSpec((2, rows, columns), lambda step, info_ref: (0, 0, info_ref[1, step]))
-    shape = jax.ShapeDtypeStruct((2, rows, pieces * columns), jnp.bfloat16)
-    return pl.pallas_call(
-        partial(place_kernel, section, layers),
-        out_shape=[shape] * layers,
-        grid_spec=pltpu.PrefetchScalarGridSpec(
-            num_scalar_prefetch=1,
-            grid=(pieces,),
-            in_specs=[source(0), source(1), source(2)] * 2 + [target] * len(olds or ()),
-            out_specs=[target] * layers,
-        ),
-        cost_estimate=pl.CostEstimate(
-            flops=0, bytes_accessed=8 * rows * pieces * columns * layers, transcendentals=0
-        ),
-        name="place",
-    )(info, *mine, *theirs, *(olds or ()))
+        if entries:
+            plans.append(
+                [
+                    (store.index(array), begin, size)
+                    for gather, part in entries
+                    for array, begin, size in gather.held[part]
+                ]
+            )
+            lists.append((mask, entries))
+    if fresh:
+        plans.append([(store.index(array), begin, size) for array, begin, size, _, _, _ in fresh])
+    after = [value for value in after if all(value is not known for known in store.arrays)]
+    values = list(copy_blocks(store.arrays, plans, after)) + [value for value, _ in extra]
+    there = []
+    for value, (mask, _) in zip(values, lists):
+        there.append(flip_place(value, mask))
+    collected = values[len(lists)] if fresh else None
+    swapped = flip_core(collected) if fresh else None
+    results = [send(value) for value, (_, send) in zip(values[len(plans) :], extra)]
+    came = []
+    for (mask, entries), value in zip(lists, there):
+        begin = 0
+        for gather, part in entries:
+            size = sum(amount for _, _, amount in gather.held[part])
+            known = [place ^ gather.turns[part][gather.step] for place in gather.found[part]]
+            gather.held[part] = gather.held[part] + [(value, begin, size)]
+            gather.found[part] = gather.found[part] + known
+            came.append((value, begin, size, gather, part, known))
+            begin = begin + size
+    for gather in active:
+        gather.step = gather.step + 1
+    return there, came, collected, swapped, results
+
+
+def pieces_by_place(block, pieces):
+    if pieces == block.shape[0]:
+        return block
+    split = pieces // block.shape[0]
+    columns = block.shape[2] // split
+    block = block.reshape(block.shape[0], block.shape[1], split, columns).transpose(0, 2, 1, 3)
+    return block.reshape(pieces, block.shape[2], columns)
+
+
+def places_to_blocks(pieces, blocks):
+    if pieces.shape[0] == blocks:
+        return pieces
+    split = pieces.shape[0] // blocks
+    rows, columns = pieces.shape[1:]
+    return pieces.reshape(blocks, split, rows, columns).transpose(0, 2, 1, 3).reshape(blocks, rows, split * columns)
+
+
+def exchange(value, count):
+    middle = count // 2
+    groups = [[half_index * middle + index for index in range(middle)] for half_index in range(2)]
+    return lax.all_to_all(value, "dp", 0, 0, axis_index_groups=groups)
+
+
+def swap_halves(block, section, core, count):
+    middle = count // 2
+    inside = [place for place in range(count) if place // middle == section]
+    swap = [(here * count + place, (1 - here) * count + place) for here in range(2) for place in inside]
+    size = block.shape[0] // 2
+    there = both_axes(lax.dynamic_slice_in_dim(block, (1 - core) * size, size, 0), swap)
+    here = lax.dynamic_slice_in_dim(block, core * size, size, 0)
+    return (here.astype(jnp.float32) + there.astype(jnp.float32)).astype(jnp.bfloat16)
+
+
+def sum_halves(halves, count):
+    pieces = [pieces_by_place(part, count // 2) for part in halves]
+    pieces = pieces[0] if len(pieces) == 1 else jnp.concatenate(pieces, 1)
+    return jnp.sum(exchange(pieces, count).astype(jnp.float32), axis=0).astype(jnp.bfloat16)
+
+
+def scatter_section(blocks, section, core, count):
+    return sum_halves([swap_halves(block, section, core, count) for block in blocks], count)
+
+
+def cross_section(piece, section, stage, count):
+    middle = count // 2
+    across = [(place, place ^ middle) for place in range(count) if place // middle == section]
+    return jnp.where(stage == section, piece, lax.ppermute(piece, "dp", across))
+
+
+def spread_section(piece, section, count):
+    middle = count // 2
+    spread = exchange(jnp.broadcast_to(piece[None], (middle,) + piece.shape), count)
+    here = places_to_blocks(spread, 8)
+    there = lax.ppermute(here, "section", [(1 - section, section)])
+    return (here, there) if section == 0 else (there, here)
 
 
 def finish_kernel(
-    info_ref, rate_ref, g0_ref, g1_ref, counts_ref, aq_ref, ao_ref, au_ref, ad_ref, bq_ref, bo_ref, bu_ref, bd_ref,
-    wq_ref, wo_ref, wu_ref, wd_ref,
-    gaq, gbq, gao, gbo, gau, gbu, gad, gbd, gain_out, bias_out, fq, fo, fu, fd, rms_out,
+    offsets, info_ref, rate_ref, early0_ref, early1_ref, late0_ref, late1_ref, counts_ref,
+    aq_ref, ao_ref, au_ref, ad_ref, bq_ref, bo_ref, bu_ref, bd_ref, wq_ref, wo_ref, wu_ref, wd_ref, *refs,
 ):
+    gaq, gbq, gao, gbo, gau, gbu, gad, gbd, gain_out, bias_out, fq, fo, fu, fd, rms_out, g_ref, sem = refs[-17:]
     rate = rate_ref[0]
-
-    def run(g_ref):
-        per = g_ref.shape[2] // WIDE
-
+    size, height = early0_ref.shape[0], g_ref.shape[1]
+
+    def fetch(sources, begin):
+        copies = [
+            pltpu.make_async_copy(
+                source.at[:, pl.ds(begin, height)], g_ref.at[pl.ds(index * size, size)], sem.at[index]
+            )
+            for index, source in enumerate(sources)
+        ]
+        for copy in copies:
+            copy.start()
+        for copy in copies:
+            copy.wait()
+
+    @pl.when(info_ref[1] == 0)
+    def _():
+        fetch((early0_ref, early1_ref), offsets[0])
+
+    @pl.when(info_ref[1] != 0)
+    def _():
+        fetch((late0_ref, late1_ref), offsets[1])
+
+    def run():
         def columns(index, begin=0, end=RANK):
-            return g_ref[index // per, begin:end, (index % per) * WIDE : (index % per + 1) * WIDE].astype(jnp.float32)
+            return g_ref[index, begin:end].astype(jnp.float32)
 
         def project(first_at, second_at, a_ref, b_ref, w_ref, ga, gb, folded):
             for index in range(ga.shape[1] // WIDE):
@@ -342,21 +367,15 @@
         sums = jnp.concatenate([sums[:, 128 * index : 128 * (index + 1)] for index in range(3)], 0)
         rms_out[0] = jnp.sqrt(sums / counts_ref[...])
 
-    @pl.when(pl.program_id(0) == 0)
-    def _():
-        run(g0_ref)
-
-    @pl.when(pl.program_id(0) != 0)
-    def _():
-        run(g1_ref)
-
-
-def finish(place, rate, blocks, counts, trained, frozen):
+    run()
+
+
+def finish(place, core, rate, early, late, offsets, layer, counts, trained, frozen, into):
     firsts, seconds = trained[0:8:2], trained[1:8:2]
     layers = firsts[0].shape[0]
 
     def layer_block(value):
-        return pl.BlockSpec((1,) + value.shape[1:], lambda step, *_: (step, 0, 0))
+        return pl.BlockSpec((1,) + value.shape[1:], lambda step, *_: (layer, 0, 0))
 
     shapes = []
     for first, second in zip(firsts, seconds):
@@ -365,21 +384,27 @@
     shapes += [jax.ShapeDtypeStruct((layers, 2, WIDE), jnp.float32)] * 2
     shapes += [jax.ShapeDtypeStruct(matrix.shape, jnp.bfloat16) for matrix in frozen]
     shapes += [jax.ShapeDtypeStruct((layers, 3, 128), jnp.float32)]
-    keep = pl.BlockSpec(blocks[0].shape, lambda step, *_: (0, 0, 0))
+    keep = pl.BlockSpec(memory_space=pl.ANY)
+    extra = [] if into is None else list(into)
     return pl.pallas_call(
-        finish_kernel,
+        partial(finish_kernel, offsets),
         out_shape=shapes,
         grid_spec=pltpu.PrefetchScalarGridSpec(
             num_scalar_prefetch=1,
-            grid=(layers,),
-            in_specs=[pl.BlockSpec(memory_space=pltpu.SMEM), keep, keep, pl.BlockSpec((1, 128), lambda step, *_: (0, 0))]
-            + [layer_block(value) for value in firsts + seconds + frozen],
+            grid=(1,),
+            in_specs=[pl.BlockSpec(memory_space=pltpu.SMEM)]
+            + [keep] * 4
+            + [pl.BlockSpec((1, 128), lambda step, *_: (0, 0))]
+            + [layer_block(value) for value in firsts + seconds + frozen]
+            + [keep] * len(extra),
             out_specs=[layer_block(shape) for shape in shapes],
+            scratch_shapes=[pltpu.VMEM((16, RANK + 8, WIDE), jnp.bfloat16), pltpu.SemaphoreType.DMA((2,))],
         ),
+        input_output_aliases={19 + index: index for index in range(len(extra))},
         compiler_params=pltpu.CompilerParams(vmem_limit_bytes=60 << 20),
-        cost_estimate=pl.CostEstimate(flops=1 << 30, bytes_accessed=48 << 20, transcendentals=0),
+        cost_estimate=pl.CostEstimate(flops=1 << 29, bytes_accessed=24 << 20, transcendentals=0),
         name="finish",
-    )(place.reshape(1), rate.reshape(1), *blocks, counts, *firsts, *seconds, *frozen)
+    )(jnp.stack([place, core]), rate.reshape(1), *early, *late, counts, *firsts, *seconds, *frozen, *extra)
 
 
 def mm(left, right):
@@ -514,6 +539,18 @@
     return pl.BlockSpec((height, width), lambda step, facts_ref: (down, right))
 
 
+def layer_fixed(layer, height, width, down=0, right=0):
+    return pl.BlockSpec((None, height, width), lambda step, facts_ref: (layer, down, right))
+
+
+def layer_columns(layer, height, width, offset=0):
+    return pl.BlockSpec((None, height, width), lambda step, facts_ref: (layer, 0, step + offset))
+
+
+def layer_rows(layer, height, width, offset=0):
+    return pl.BlockSpec((None, height, width), lambda step, facts_ref: (layer, step + offset, 0))
+
+
 def column_block(height, width, offset=0):
     return pl.BlockSpec((height, width), lambda step, facts_ref: (0, step + offset))
 
@@ -546,7 +583,7 @@
     tokens, width = residual.shape
     groups = width // GROUP
     joint, output = weights[0], weights[1]
-    firsts, seconds = weights[4:6]
+    firsts, seconds, _, layer = weights[4:8]
     seq_len = tables.shape[1]
     return kernel_call(
         attention_forward_kernel,
@@ -556,16 +593,16 @@
             whole(tokens, width),
             whole(4, width),
             whole(3, seq_len, 2 * HEAD_DIM),
-            whole(width, RANK),
+            layer_fixed(layer, width, RANK),
             column_block(width, GROUP),
             column_block(width, GROUP, groups),
             column_block(width, GROUP, 2 * groups),
-            column_block(RANK, GROUP),
-            column_block(RANK, GROUP, groups),
-            column_block(RANK, GROUP, 2 * groups),
+            layer_columns(layer, RANK, GROUP),
+            layer_columns(layer, RANK, GROUP, groups),
+            layer_columns(layer, RANK, GROUP, 2 * groups),
             row_block(GROUP, width),
-            row_block(GROUP, RANK, groups),
-            fixed(RANK, width, 0, 3),
+            layer_rows(layer, GROUP, RANK, groups),
+            layer_fixed(layer, RANK, width, 0, 3),
         ],
         [column_block(tokens, GROUP)] * 4 + [whole(tokens, RANK), whole(tokens, RANK), whole(tokens, width)],
         [shaped((tokens, width))] * 4
@@ -629,7 +666,7 @@
 def feed_forward(residual, attended, weights, norms, facts):
     tokens, width = residual.shape
     upper, down = weights[2], weights[3]
-    firsts, seconds = weights[4:6]
+    firsts, seconds, _, layer = weights[4:8]
     hidden = upper.shape[1]
     return kernel_call(
         feed_forward_kernel,
@@ -639,12 +676,12 @@
             whole(tokens, width),
             whole(4, width),
             whole(tokens, width),
-            fixed(width, RANK, 2, 0),
+            layer_fixed(layer, width, RANK, 2, 0),
             column_block(width, BLOCK),
-            column_block(RANK, BLOCK, 4 * width // BLOCK),
+            layer_columns(layer, RANK, BLOCK, 4 * width // BLOCK),
             row_block(BLOCK, width),
-            row_block(BLOCK, RANK, 3 * width // BLOCK),
-            fixed(RANK, width, 0, 8),
+            layer_rows(layer, BLOCK, RANK, 3 * width // BLOCK),
+            layer_fixed(layer, RANK, width, 0, 8),
         ],
         [column_block(tokens, BLOCK)] * 2
         + [whole(tokens, RANK), whole(tokens, RANK), whole(tokens, width), whole(8, 128)],
@@ -666,6 +703,16 @@
     block_out[RANK:, :] = half(jnp.concatenate([row, jnp.zeros((7, row.shape[1]), jnp.float32)], 0))
 
 
+def block_copies(block_out, whole_out, first, sem):
+    width = whole_out.shape[2]
+    copies = []
+    for index in range(block_out.shape[1] // width):
+        source = block_out.at[:, pl.ds(index * width, width)]
+        copies.append(pltpu.make_async_copy(source, whole_out.at[first + index], sem.at[index]))
+        copies[-1].start()
+    return copies
+
+
 def feed_backward_kernel(
     facts_ref, g_ref, x_ref, norm_ref, act_ref, slope_ref, midu_ref, midd_ref, sums_ref, wu_ref, wd_ref, au_ref,
     bu_ref, ad_ref, bd_ref,
@@ -705,18 +752,16 @@
         block_out[:RANK, :width] = half(mm(half(grad_mid.astype(jnp.float32).T), normed))
         grad = gx_out[...] + mm_nt(grad_mid, au_ref[...])
         write_extra(block_out, grad, normal, [sums_ref[index : index + 1] for index in range(3)])
-        gather = pltpu.make_async_copy(
-            block_out, whole_out.at[:, pl.ds(6 * width, block_out.shape[1])], sem
-        )
-        gather.start()
+        gather = block_copies(block_out, whole_out, 6, sem)
         gx_out[...] = g_ref[...] + norm_gradient(grad, normal, scale, norm_ref[1:2])
-        gather.wait()
+        for copy in gather:
+            copy.wait()
 
 
 def feed_backward(gradient, residual, weights, norms, kept, facts):
     tokens, width = residual.shape
     upper, down = weights[2], weights[3]
-    firsts, seconds = weights[4:6]
+    firsts, seconds, _, layer = weights[4:8]
     active, slope, mid_u, mid_d, sums = kept
     hidden = upper.shape[1]
     return kernel_call(
@@ -734,13 +779,13 @@
             whole(8, 128),
             column_block(width, BLOCK),
             row_block(BLOCK, width),
-            fixed(width, RANK, 2, 0),
-            column_block(RANK, BLOCK, 4 * width // BLOCK),
-            row_block(BLOCK, RANK, 3 * width // BLOCK),
-            fixed(RANK, width, 0, 8),
+            layer_fixed(layer, width, RANK, 2, 0),
+            layer_columns(layer, RANK, BLOCK, 4 * width // BLOCK),
+            layer_rows(layer, BLOCK, RANK, 3 * width // BLOCK),
+            layer_fixed(layer, RANK, width, 0, 8),
         ],
         [pl.BlockSpec(memory_space=pl.ANY), whole(tokens, width)],
-        [shaped((RANK + 8, 16 * width)), shaped((tokens, width), jnp.float32)],
+        [shaped((16, RANK + 8, width)), shaped((tokens, width), jnp.float32)],
         [
             pltpu.VMEM((RANK + 8, 2 * width + 2 * hidden), jnp.bfloat16),
             pltpu.VMEM((tokens, width), jnp.bfloat16),
@@ -748,7 +793,7 @@
             pltpu.VMEM((RANK, tokens), jnp.bfloat16),
             pltpu.VMEM((RANK, tokens), jnp.bfloat16),
             pltpu.VMEM((tokens, RANK), jnp.float32),
-            pltpu.SemaphoreType.DMA,
+            pltpu.SemaphoreType.DMA((10,)),
         ],
         2 * tokens * width * hidden * 2,
         4 * width * hidden + 4 * tokens * hidden + 16 * tokens * width,
@@ -816,17 +861,17 @@
         block_out[:RANK, :width] = half(mm(half(grad_mid.astype(jnp.float32).T), normed))
         grad = acc_scr[...] + mm_nt(grad_mid, aq_ref[...])
         write_extra(block_out, grad, normal, [])
-        gather = pltpu.make_async_copy(block_out, whole_out.at[:, pl.ds(0, block_out.shape[1])], sem)
-        gather.start()
+        gather = block_copies(block_out, whole_out, 0, sem)
         gx_out[...] = gx_ref[...] + norm_gradient(grad, normal, scale, norm_ref[0:1])
-        gather.wait()
+        for copy in gather:
+            copy.wait()
 
 
 def attention_backward(gradient, grad_feed, feed_block, residual, weights, norms, tables, kept, facts):
     tokens, width = residual.shape
     groups = width // GROUP
     joint, output = weights[0], weights[1]
-    firsts, seconds = weights[4:6]
+    firsts, seconds, _, layer = weights[4:8]
     queries, keys, values, mixed, mid_q, mid_o = kept
     seq_len = tables.shape[1]
     block = column_block(tokens, GROUP)
@@ -849,17 +894,17 @@
             column_block(width, GROUP),
             column_block(width, GROUP, groups),
             column_block(width, GROUP, 2 * groups),
-            whole(width, RANK),
-            column_block(RANK, GROUP),
-            column_block(RANK, GROUP, groups),
-            column_block(RANK, GROUP, 2 * groups),
+            layer_fixed(layer, width, RANK),
+            layer_columns(layer, RANK, GROUP),
+            layer_columns(layer, RANK, GROUP, groups),
+            layer_columns(layer, RANK, GROUP, 2 * groups),
             row_block(GROUP, width),
-            row_block(GROUP, RANK, groups),
-            fixed(RANK, width, 0, 3),
+            layer_rows(layer, GROUP, RANK, groups),
+            layer_fixed(layer, RANK, width, 0, 3),
             pl.BlockSpec(memory_space=pl.ANY),
         ],
         [pl.BlockSpec(memory_space=pl.ANY), whole(tokens, width)],
-        [shaped((RANK + 8, 16 * width)), shaped((tokens, width), jnp.float32)],
+        [shaped((16, RANK + 8, width)), shaped((tokens, width), jnp.float32)],
         [
             pltpu.VMEM((RANK + 8, 6 * width), jnp.bfloat16),
             pltpu.VMEM((tokens, width), jnp.bfloat16),
@@ -871,7 +916,7 @@
             pltpu.VMEM((tokens, GROUP), jnp.float32),
             pltpu.VMEM((tokens, GROUP), jnp.float32),
             pltpu.VMEM((tokens, GROUP), jnp.bfloat16),
-            pltpu.SemaphoreType.DMA,
+            pltpu.SemaphoreType.DMA((6,)),
         ],
         2 * tokens * width * width * 4,
         2 * 5 * width * width + 24 * tokens * width,
@@ -889,10 +934,12 @@
     return output, (residual, kept_attention, kept_feed + [sums])
 
 
-def layer_backward(gradient, kept, weights, tables, facts):
+def layer_backward(gradient, kept, weights, tables, facts, after=()):
     residual, kept_attention, kept_feed = kept
     norms = weights[6]
     feed_block, grad_feed = feed_backward(gradient, residual, weights, norms, kept_feed, facts)
+    if after:
+        grad_feed = tie(grad_feed, *after)
     block, grad_input = attention_backward(
         gradient, grad_feed, feed_block, residual, weights, norms, tables, kept_attention, facts
     )
@@ -901,10 +948,9 @@
 
 def gather_plan(gathers, turns):
     if (gathers, turns) == (4, 3):
-        return [[0, 2], [0], [0, 1], [1, 2], [1, 3], [2, 3], [3], []]
-    return [
-        [index for index in range(gathers) if index <= step < index + turns] for step in range(gathers + turns)
-    ]
+        return [[0, 2], [0, 2], [0, 1], [2, 1], [1, 3], [3], [3]]
+    order = [0, 2, 1, 3]
+    return [[order[step // turns]] for step in range(gathers * turns)]
 
 
 def shards(
@@ -950,86 +996,75 @@
     local_layers = frozen_query_weight.shape[0]
     rows_dev, seq_len, model_width = inputs.shape
     tokens = rows_dev * seq_len
-    rows = frozen_output_weight.shape[1]
 
     places = [(index // middle, index) for index in range(count)]
     to_sibling = [(here * count + index, (1 - here) * count + index) for here, index in places]
-    to_far = [((1 - here) * count + index, (1 - here) * count + (index ^ middle)) for here, index in places]
     to_cross = [((1 - here) * count + index, here * count + (index ^ middle)) for here, index in places]
-    halves = [pick_halves([matrix[layer] for matrix in frozen], stage) for layer in range(local_layers)]
-    packed = [
-        (
-            jnp.concatenate([factor[layer] for factor in trained[0::2]], 0),
-            jnp.concatenate([factor[layer] for factor in trained[1::2]], 1),
-            jnp.concatenate([layer_norm_gain[layer], layer_norm_bias[layer]], 0),
-        )
-        for layer in range(local_layers)
-    ]
-    sibling, far, cross = [
-        partial(both_axes, pairs=pairs) for pairs in (to_sibling, to_far, to_cross)
-    ]
-    steps = Steps()
-    near = steps.run(*[(other, sibling) for _, other in halves])
-    apart = []
-    for same, other in halves:
-        same, other = tie((same, other), *(near + apart[-1:]))
-        apart.append((far(other), cross(same)))
+    sibling, cross = [partial(both_axes, pairs=pairs) for pairs in (to_sibling, to_cross)]
+
+    same, other = pack_halves(core, frozen)
+    swapped = flip_core(other)
+    own = jnp.where(home, same, swapped)
+    leaving = jnp.where(home, swapped, same)
+    partner = [flip_place(leaving[0], middle)]
+    for layer in range(1, local_layers):
+        partner.append(flip_place(tie(leaving[layer], partner[-1]), middle))
     gathers = []
     for layer in range(local_layers):
-        gathers.append(Gather(jnp.where(home, halves[layer][0], near[layer]), masks))
-        gathers.append(Gather(jnp.where(home, *apart[layer]), masks))
-    plan = gather_plan(len(gathers), len(masks))
+        gathers.append(Gather(layer, 0, own[layer], masks))
+        gathers.append(Gather(layer, 1, partner[layer], masks))
+    plan = gather_plan(len(gathers), len(masks)) + [[]]
+    dense = [None] * local_layers
+    facts = jnp.stack([lengths, domain])
+    norms = jnp.concatenate([layer_norm_gain, layer_norm_bias], 1)
+    facts = jnp.where(home, facts, cross(facts))
+    norms = jnp.where(home, norms, sibling(norms))
+    packed = [
+        jnp.concatenate([factor for factor in trained[0::2]], 1),
+        jnp.concatenate([factor for factor in trained[1::2]], 2),
+    ]
     visiting = jnp.where(stage == 0, cotangent, inputs)
-    facts = jnp.stack([lengths, domain])
-    weights = [None] * local_layers
-    swapped = [None] * len(gathers)
-    ready = []
+    tables = rotary_tables(seq_len)
+    ended, fresh, started, waiting = (), [], set(), []
+    bases = [jnp.where(stage == which, 0, middle) for which in range(2)]
     for number, active in enumerate(plan):
-        moves = [move for index in active for move in gathers[index].moves()]
-        moves = moves + [(held, flip_core) for index in ready for held in gathers[index].held]
-        if number == 0:
-            moves.append((facts, cross))
-        if number == 1:
-            moves = moves + [(part, sibling) for part in packed[0]]
-        if number == 3:
-            moves.append((visiting, cross))
-            moves = moves + [(part, sibling) for layer in packed[1:] for part in layer]
-        there = steps.run(*moves)
         for index in active:
-            gathers[index].take(there[:3])
-            there = there[3:]
-        for index in ready:
-            swapped[index] = there[:3]
-            there = there[3:]
-        ready = [index for index in active if gathers[index].step == len(masks)]
-        if number == 0:
-            facts = jnp.where(home, facts, there[0])
-        if number == 1:
-            packed[0] = [jnp.where(home, here, far_part) for here, far_part in zip(packed[0], there)]
-        if number == 3:
-            visiting, there = there[0], there[1:]
-            for layer in range(1, local_layers):
-                packed[layer] = [jnp.where(home, here, far_part) for here, far_part in zip(packed[layer], there)]
-                there = there[3:]
-    for layer in range(local_layers):
-        dense = None
-        for which in range(2):
-            gather = gathers[2 * layer + which]
-            base = jnp.where(stage == which, 0, middle)
-            order = gather.found[0]
-            info = jnp.stack(
-                [jnp.full((middle,), core, jnp.int32), (jnp.asarray(order, jnp.int32) ^ low) + base]
-                + [jnp.asarray([known.index(mask) for mask in order], jnp.int32) for known in gather.found]
-            )
-            dense = assemble(info, gather.held, swapped[2 * layer + which], rows, count, dense)
-        weights[layer] = tuple(dense) + tuple(packed[layer])
+            if index not in started:
+                started.add(index)
+                gather = gathers[index]
+                fresh = fresh + [(gather.block, part, 1, gather, part, [0]) for part in range(3)]
+        extra = []
+        if number < 2:
+            extra.append((packed[number], sibling))
+        if number == 4:
+            extra.append((visiting, cross))
+        moving = fresh if number >= 2 else []
+        there, came, collected, swapped, results = gather_step(
+            [gathers[index] for index in active], masks, moving, extra, ended
+        )
+        fresh = came if moving else fresh + came
+        if number < 2:
+            packed[number] = jnp.where(home, packed[number], results[0])
+        if number == 4:
+            visiting = results[0]
+        marks = [assemble(*waiting.pop(0), count, dense)] if waiting and number < len(plan) - 1 else []
+        ended = tuple(there) + tuple(results) + tuple(marks)
+        if moving:
+            ended = ended + (swapped,)
+            layout = [(gather.layer, part) for _, _, size, gather, part, _ in moving for _ in range(size)]
+            places_of = [
+                (known ^ low) + bases[gather.which] for _, _, _, gather, _, found in moving for known in found
+            ]
+            info = jnp.stack([core] + places_of)
+            waiting.append((info, layout, collected, swapped))
+    for item in waiting:
+        assemble(*item, count, dense)
+    weights = [tuple(dense[layer]) + (packed[0], packed[1], norms[layer], layer) for layer in range(local_layers)]
     start = jnp.where(home, inputs, visiting).astype(jnp.float32).reshape(tokens, model_width)
     valid = jnp.arange(seq_len)[None, :] < facts[0][:, None]
     end_grad = jnp.where(home, cotangent, visiting).astype(jnp.float32)
     end_grad = jnp.where(stage == 1, end_grad * valid[..., None].astype(jnp.float32), 0.0)
     end_grad = end_grad.reshape(tokens, model_width)
-    tables = rotary_tables(seq_len)
-
     def stage_forward(residual):
         kept = []
         for layer in range(local_layers):
@@ -1051,37 +1086,20 @@
         gradient, late[layer] = layer_backward(gradient, kept[layer], weights[layer], tables, facts)
     sent = gradient.astype(jnp.bfloat16)
     came_back = lax.ppermute(sent, "dp", [(after, before) for before, after in forward_pairs])
-    steps = Steps()
-    late_slabs = scatter_section(late, 1, core, low, count, masks, steps)
+    late_halves = tie([swap_halves(block, 1, core, count) for block in late], came_back)
+    late_piece = sum_halves(late_halves, count)
 
     gradient = jnp.where(stage == 0, came_back.astype(jnp.float32), 0.0)
-    blocks, slabs = [None] * local_layers, [None] * local_layers
+    pieces = [None] * local_layers
+    last = late_piece
     for layer in reversed(range(local_layers)):
-        gradient, blocks[layer] = layer_backward(gradient, kept[layer], weights[layer], tables, facts)
-        if layer:
-            slabs[layer] = scatter_section([blocks[layer]], 0, core, low, count, masks, steps)
-
-    first = Spread(late_slabs, 1, masks, count, stage)
-    second = Spread(sum(slabs[1:], []), 0, masks, count, stage)
-    third = Scatter([blocks[0]], 0, core, low, count, masks)
-    there = steps.run(*third.moves(), *first.moves(), *second.moves())
-    there = third.take(there)
-    second.take(first.take(there))
-    for step in range(len(masks)):
-        there = steps.run(*third.moves())
-        third.take(there)
-    third = Spread(third.slabs, 0, masks, count, stage)
-    for step in range(len(masks) + 2):
-        groups = [first, second, third] if step else [third, first, second]
-        groups = [group for group in groups if not group.done()]
-        there = steps.run(*[move for group in groups for move in group.moves()])
-        for group in groups:
-            there = group.take(there)
-    placed = place_section(1, core, low, masks, first, None, local_layers)
-    old = placed[1:]
-    upper_placed = place_section(0, core, low, masks, second, old, local_layers - 1)
-    lower_placed = place_section(0, core, low, masks, third, placed[:1], 1)
-    blocks = lower_placed + upper_placed
+        gradient, block = layer_backward(gradient, kept[layer], weights[layer], tables, facts)
+        halves = swap_halves(block, 0, core, count)
+        pieces[layer] = last = sum_halves([tie(halves, last)], count)
+    late_piece = cross_section(tie(late_piece, pieces[local_layers - 1]), 1, stage, count)
+    early_piece = cross_section(jnp.concatenate(pieces, 0), 0, stage, count)
+    late_whole = spread_section(tie(late_piece, last), 1, count)
+    early_whole = spread_section(tie(early_piece, late_whole[1]), 0, count)
 
     out_pairs = [(count + index + middle, index + middle) for index in range(middle)]
     out_pairs = out_pairs + [(index + middle, count + index) for index in range(middle)]
@@ -1104,7 +1122,13 @@
         counts = counts + flip_place(counts, mask)
     counts = jnp.maximum(counts, 1.0) * model_width
     rate = peak_rate * (steps_since_reset[0].astype(jnp.float32) + 1.0) / WARM
-    *outputs, rms = finish(place, rate, blocks, counts, trained, frozen)
+    outputs = None
+    for layer in reversed(range(local_layers)):
+        offsets = (layer * (RANK + 8),) * 2
+        outputs = finish(
+            place, core, rate, early_whole, late_whole, offsets, layer, counts, trained, frozen, outputs
+        )
+    *outputs, rms = outputs
     return (section_out, section_grad, *outputs, rms[:, :, : DOMAINS + 1])
 
 

time: 1050 us -> 933 us (0.89)
  starting transfers between devices: 220 us -> 118 us
  other arithmetic: 86.5 us -> 42.7 us
  waiting for transfers between devices: 337 us -> 351 us
  local copies, waits for them, and re-layouts: 37.5 us -> 50.6 us
    all_to_all x0 -> x5, waiting for transfers between devices: none -> 93.5 us  [exchange(): return lax.all_to_all(value, 'dp', 0, 0, axis_index_groups=groups)]
    ppermute x45 -> x4, starting transfers between devices: 85.8 us -> 17.2 us  [the longest x2 12.4 us: cross_section(): return jnp.where(stage == section, piece, lax.ppermute(piece, 'dp', across))]
    ppermute x67 -> x27, starting transfers between devices: 83.8 us -> 25.3 us  [flip_place(): lax.ppermute(value, 'dp', [(place, place ^ mask) for place in range(count)])]
    concatenate x72 -> x3, other arithmetic: 54 us -> 2.77 us  [the longest x1 2.72 us: sum_halves(): pieces = pieces[0] if len(pieces) == 1 else jnp.concatenate(pieces, 1)]
    all_to_all x0 -> x5, starting transfers between devices: none -> 46.2 us  [exchange(): return lax.all_to_all(value, 'dp', 0, 0, axis_index_groups=groups)]
    ppermute x67 -> x27, waiting for transfers between devices: 181 us -> 141 us  [flip_place(): lax.ppermute(value, 'dp', [(place, place ^ mask) for place in range(count)])]
    ppermute x20 -> x11, waiting for transfers between devices: 58.5 us -> 32.6 us  [both_axes(): return lax.ppermute(value, ('section', 'dp'), pairs)]
    ppermute x45 -> x4, waiting for transfers between devices: 70.7 us -> 46.6 us  [the longest x2 46.6 us: cross_section(): return jnp.where(stage == section, piece, lax.ppermute(piece, 'dp', across))]
  transfers between devices with their start and end apart: 146 -> 56, of which waited for: 50 -> 27; matrix products, arithmetic and copies ran while one was open for 8% -> 5% of each run, Pallas kernels for 18% -> 20%
where the time goes in v3:
time: 933 us; the launch traced here: 921 us
  Pallas kernels  356 us (38%)
  waiting for transfers between devices  351 us (38%)
  starting transfers between devices  118 us (13%)
  local copies, waits for them, and re-layouts  50.6 us (5%)
  other arithmetic  42.7 us (5%)
    ppermute x27, waiting for transfers between devices, flip_place(): lax.ppermute(value, 'dp', [(place, place ^ mask) for place in range(count)])  141 us
    all_to_all x5, waiting for transfers between devices, exchange(): return lax.all_to_all(value, 'dp', 0, 0, axis_index_groups=groups)  93.5 us
    pallas_call x4, Pallas kernels, attention_backward(): kernel_call(attention_backward_kernel, 'attention_backward', groups, [who...  73.2 us
    pallas_call x4, Pallas kernels, feed_backward(): kernel_call(feed_backward_kernel, 'feed_backward', hidden // BLOCK, [whol...  66.4 us
    pallas_call x4, Pallas kernels, feed_forward(): kernel_call(feed_forward_kernel, 'feed_forward', hidden // BLOCK, [whole(...  63.5 us
    pallas_call x4, Pallas kernels, attention_forward(): kernel_call(attention_forward_kernel, 'attention_forward', groups, [whole...  55.8 us
    pallas_call x6, Pallas kernels, assemble(): pl.pallas_call(partial(assemble_kernel, tuple(layout)), out_shape=[jax.Sh...  47.8 us
    ppermute x2, waiting for transfers between devices, cross_section(): return jnp.where(stage == section, piece, lax.ppermute(piece, 'dp', across))  46.6 us
  transfers between devices with their start and end apart: 56, of which 27 were waited for; matrix products, arithmetic and copies ran while one was open for 5% of the time, Pallas kernels for 20%

profile of v3, /device:TPU:26, one launch (start us, length us, event | category | flops | bytes accessed | tf_op | source)
XLA Modules:
  0.0 921.4 jit_solution(6246929096805495220)
XLA Ops:
  32.5 11.5 %collective-permute-done.7.refs_4_.refs_1_ = bf16[2,2,64,1024]{3,2,1,0:T(8,128)(2,1)S(1)} collective-permute-done((bf16[2,2,64,1024]{3,2,1,0:T(8,128)(2,1)S(1)}, bf16[2,2,64,1024]{3,2,1,0:T(8,128)(2,1)S(1)}, u32[]{:S(2)}, u32[]{:S(2)}) %collective-permute-start.7) | collective-permute-done | bytes 524320 | tf_op jit(solution)/shard_map/ppermute | solution.py:36
  49.3 36.0 %collective-permute-done.5 = bf16[6,64,1024]{2,1,0:T(8,128)(2,1)S(1)} collective-permute-done((bf16[6,64,1024]{2,1,0:T(8,128)(2,1)S(1)}, bf16[6,64,1024]{2,1,0:T(8,128)(2,1)S(1)}, u32[]{:S(2)}, u32[]{:S(2)}) %collective-permute-start.5) | collective-permute-done | bytes 786464 | tf_op jit(solution)/shard_map/ppermute | solution.py:36
  91.6 29.7 %collective-permute-done.14.refs_10_.refs_1_ = bf16[5,2,64,1024]{3,2,1,0:T(8,128)(2,1)S(1)} collective-permute-done((bf16[5,2,64,1024]{3,2,1,0:T(8,128)(2,1)S(1)}, bf16[5,2,64,1024]{3,2,1,0:T(8,128)(2,1)S(1)}, u32[]{:S(2)}, u32[]{:S(2)}) %collective-permute-start.14) | collective-permute-done | bytes 1310752 | tf_op jit(solution)/shard_map/ppermute | solution.py:36
  132.3 11.7 %assemble.6 = (bf16[1024,3072]{1,0:T(8,128)(2,1)}, bf16[1024,1024]{1,0:T(8,128)(2,1)}, bf16[1024,4096]{1,0:T(8,128)(2,1)}, bf16[4096,1024]{1,0:T(8,128)(2,1)}, b...) custom-call(s32[28]{0:T(128)} %stack.79.info_ref, ...), custom_call_target="tpu_custom_call" | custom-call | bytes 42467328 | tf_op jit(solution)/shard_map/assemble/pallas_call | solution.py:146
  144.0 34.8 %collective-permute-done.6 = bf16[6,64,1024]{2,1,0:T(8,128)(2,1)S(1)} collective-permute-done((bf16[6,64,1024]{2,1,0:T(8,128)(2,1)}, bf16[6,64,1024]{2,1,0:T(8,128)(2,1)S(1)}, u32[]{:S(2)}, u32[]{:S(2)}) %collective-permute-start.6) | collective-permute-done | bytes 786464 | tf_op jit(solution)/shard_map/ppermute | solution.py:36
  204.6 21.3 %collective-permute-done.1.refs_4_ = bf16[2,128,1024]{2,1,0:T(8,128)(2,1)S(1)} collective-permute-done((bf16[2,128,1024]{2,1,0:T(8,128)(2,1)S(1)}, bf16[2,128,1024]{2,1,0:T(8,128)(2,1)S(1)}, u32[]{:S(2)}, u32[]{:S(2)}) %collective-permute-start.1) | collective-permute-done | bytes 524320 | tf_op jit(solution)/shard_map/ppermute | solution.py:27
  270.1 15.1 %collective-permute-done.30.refs_0_ = bf16[4,2,64,1024]{3,2,1,0:T(8,128)(2,1)} collective-permute-done((bf16[4,2,64,1024]{3,2,1,0:T(8,128)(2,1)}, bf16[4,2,64,1024]{3,2,1,0:T(8,128)(2,1)}, u32[]{:S(2)}, u32[]{:S(2)}) %collective-permute-start.30) | collective-permute-done | bytes 1048608 | tf_op jit(solution)/shard_map/ppermute | solution.py:36
  300.3 14.1 %attention_forward.4 = (bf16[256,1024]{1,0:T(8,128)(2,1)}, bf16[256,1024]{1,0:T(8,128)(2,1)}, bf16[256,1024]{1,0:T(8,128)(2,1)}, bf16[256,1024]{1,0:T(8,128)(2,1...) custom-call(s32[2,2]{1,0:T(2,128)S(1)} %broadcast_select_fusion.10.facts_ref, ...), custom_call_target="tpu_custom_call" | custom-call | flops 2147483648 | bytes 13631488 | tf_op jit(solution)/shard_map/attention_forward/pallas_call | solution.py:588
  314.4 16.0 %feed_forward.4 = (bf16[256,4096]{1,0:T(8,128)(2,1)}, bf16[256,4096]{1,0:T(8,128)(2,1)}, bf16[256,128]{1,0:T(8,128)(2,1)}, bf16[256,128]{1,0:T(8,128)(2,1)}, f32[256,1024]{1,0:T(8,128)S(1)}, /*index=5*/f32[8,128]{1,0:T(8,128)}) custom-call(s32[2,2]{1,0:T(2,128)S(1)} %broadcast_select_fusion.10.facts_ref, f32[256,1024]{1,0:T(8,128)S(1)} %bitcast_convert_fusion.x_ref, ...), custom_call_target="tpu_custom_call" | custom-call | flops 4294967296 | bytes 24117248 | tf_op jit(solution)/shard_map/feed_forward/pallas_call | solution.py:671
  341.4 14.1 %attention_forward.5 = (bf16[256,1024]{1,0:T(8,128)(2,1)}, bf16[256,1024]{1,0:T(8,128)(2,1)}, bf16[256,1024]{1,0:T(8,128)(2,1)}, bf16[256,1024]{1,0:T(8,128)(2,1...) custom-call(s32[2,2]{1,0:T(2,128)S(1)} %broadcast_select_fusion.10.facts_ref, ...), custom_call_target="tpu_custom_call" | custom-call | flops 2147483648 | bytes 13631488 | tf_op jit(solution)/shard_map/attention_forward/pallas_call | solution.py:588
  355.4 16.0 %feed_forward.5 = (bf16[256,4096]{1,0:T(8,128)(2,1)}, bf16[256,4096]{1,0:T(8,128)(2,1)}, bf16[256,128]{1,0:T(8,128)(2,1)}, bf16[256,128]{1,0:T(8,128)(2,1)}, f32[256,1024]{1,0:T(8,128)S(1)}, /*index=5*/f32[8,128]{1,0:T(8,128)}) custom-call(s32[2,2]{1,0:T(2,128)S(1)} %broadcast_select_fusion.10.facts_ref, f32[256,1024]{1,0:T(8,128)S(1)} %get-tuple-element.219.x_ref, ...), custom_call_target="tpu_custom_call" | custom-call | flops 4294967296 | bytes 24117248 | tf_op jit(solution)/shard_map/feed_forward/pallas_call | solution.py:671
  373.1 26.8 %collective-permute-done.35 = bf16[256,1024]{1,0:T(8,128)(2,1)S(1)} collective-permute-done((bf16[256,1024]{1,0:T(8,128)(2,1)S(1)}, bf16[256,1024]{1,0:T(8,128)(2,1)S(1)}, u32[]{:S(2)}, u32[]{:S(2)}) %collective-permute-start.35) | collective-permute-done | bytes 524320 | tf_op jit(solution)/shard_map/ppermute | solution.py:1078
  400.2 13.7 %attention_forward.6 = (bf16[256,1024]{1,0:T(8,128)(2,1)S(1)}, bf16[256,1024]{1,0:T(8,128)(2,1)S(1)}, bf16[256,1024]{1,0:T(8,128)(2,1)S(1)}, bf16[256,1024]{1,0:...) custom-call(s32[2,2]{1,0:T(2,128)S(1)} %broadcast_select_fusion.10.facts_ref,, ...), custom_call_target="tpu_custom_call" | custom-call | flops 2147483648 | bytes 13631488 | tf_op jit(solution)/shard_map/attention_forward/pallas_call | solution.py:588
  414.0 15.8 %feed_forward.6 = (bf16[256,4096]{1,0:T(8,128)(2,1)S(1)}, bf16[256,4096]{1,0:T(8,128)(2,1)}, bf16[256,128]{1,0:T(8,128)(2,1)S(1)}, bf16[256,128]{1,0:T(8,128)(2,...) custom-call(s32[2,2]{1,0:T(2,128)S(1)} %broadcast_select_fusion.10.facts_ref, ...), custom_call_target="tpu_custom_call" | custom-call | flops 4294967296 | bytes 24117248 | tf_op jit(solution)/shard_map/feed_forward/pallas_call | solution.py:671
  429.7 14.0 %attention_forward.7 = (bf16[256,1024]{1,0:T(8,128)(2,1)S(1)}, bf16[256,1024]{1,0:T(8,128)(2,1)S(1)}, bf16[256,1024]{1,0:T(8,128)(2,1)S(1)}, bf16[256,1024]{1,0:...) custom-call(s32[2,2]{1,0:T(2,128)S(1)} %broadcast_select_fusion.10.facts_ref,, ...), custom_call_target="tpu_custom_call" | custom-call | flops 2147483648 | bytes 13631488 | tf_op jit(solution)/shard_map/attention_forward/pallas_call | solution.py:588
  443.8 15.7 %feed_forward.7 = (bf16[256,4096]{1,0:T(8,128)(2,1)S(1)}, bf16[256,4096]{1,0:T(8,128)(2,1)}, bf16[256,128]{1,0:T(8,128)(2,1)S(1)}, bf16[256,128]{1,0:T(8,128)(2,...) custom-call(s32[2,2]{1,0:T(2,128)S(1)} %broadcast_select_fusion.10.facts_ref, ...), custom_call_target="tpu_custom_call" | custom-call | flops 4294967296 | bytes 24117248 | tf_op jit(solution)/shard_map/feed_forward/pallas_call | solution.py:671
  460.5 16.7 %feed_backward.4 = (bf16[16,136,1024]{2,1,0:T(8,128)(2,1)}, f32[256,1024]{1,0:T(8,128)S(1)}) custom-call(s32[2,2]{1,0:T(2,128)S(1)} %broadcast_select_fusion.10.facts_ref, f32[256,1024]{1,0:T(8,128)S(1)} %bitcast.51, f32[256,1024]{1,0:T(8,128)S(1)} %get-tuple-element.244.x_ref, f32[4,1024]{1,0:T(4,128)S(1)} %get-tuple-element.365.norm_ref, ...), custom_call_target="tpu_custom_call" | custom-call | flops 4294967296 | bytes 25165824 | tf_op jit(solution)/shard_map/feed_backward/pallas_call | solution.py:767
  477.3 18.6 %attention_backward.4 = (bf16[16,136,1024]{2,1,0:T(8,128)(2,1)}, f32[256,1024]{1,0:T(8,128)S(1)}) custom-call(s32[2,2]{1,0:T(2,128)S(1)} %broadcast_select_fusion.10.facts_ref, f32[256,1024]{1,0:T(8,128)S(1)} %bitcast.52, f32[256,1024]{1,0:T(8,128)S(1)} %get-tuple-element.252.gx_ref, f32[256,1024]{1,0:T(8,128)} %copy-done.2, ...), custom_call_target="tpu_custom_call", output_to_operand_aliasing={{0}: (22, {})} | custom-call | flops 2147483648 | bytes 16777216 | tf_op jit(solution)/shard_map/attention_backward/pallas_call | solution.py:878
  501.1 16.4 %feed_backward.5 = (bf16[16,136,1024]{2,1,0:T(8,128)(2,1)}, f32[256,1024]{1,0:T(8,128)S(1)}) custom-call(s32[2,2]{1,0:T(2,128)S(1)} %broadcast_select_fusion.10.facts_ref, f32[256,1024]{1,0:T(8,128)S(1)} %get-tuple-element.260.g_ref, f32[256,1024]{1,0:T(8,128)S(1)} %convert_select_fusion.2.x_ref, f32[4,1024]{1,0:T(4,128)S(1)} %get-tuple-element.366.norm_ref, ...), custom_call_target="tpu_custom_call" | custom-call | flops 4294967296 | bytes 25165824 | tf_op jit(solution)/shard_map/feed_backward/pallas_call | solution.py:767
  517.6 18.1 %attention_backward.5 = (bf16[16,136,1024]{2,1,0:T(8,128)(2,1)}, f32[256,1024]{1,0:T(8,128)S(1)}) custom-call(s32[2,2]{1,0:T(2,128)S(1)} %broadcast_select_fusion.10.facts_ref, f32[256,1024]{1,0:T(8,128)S(1)} %get-tuple-element.260.g_ref, f32[256,1024]{1,0:T(8,128)S(1)} %get-tuple-element.266.gx_ref, ...), custom_call_target="tpu_custom_call", output_to_operand_aliasing={{0}: (22, {})} | custom-call | flops 2147483648 | bytes 16777216 | tf_op jit(solution)/shard_map/attention_backward/pallas_call | solution.py:878
  567.3 16.5 %feed_backward.6 = (bf16[16,136,1024]{2,1,0:T(8,128)(2,1)}, f32[256,1024]{1,0:T(8,128)S(1)}) custom-call(s32[2,2]{1,0:T(2,128)S(1)} %broadcast_select_fusion.10.facts_ref, f32[256,1024]{1,0:T(8,128)S(1)} %convert_select_fusion.1.g_ref, f32[256,1024]{1,0:T(8,128)S(1)} %copy-done.3, f32[4,1024]{1,0:T(4,128)S(1)} %get-tuple-element.365.norm_ref, ...), custom_call_target="tpu_custom_call" | custom-call | flops 4294967296 | bytes 25165824 | tf_op jit(solution)/shard_map/feed_backward/pallas_call | solution.py:767
  583.9 18.2 %attention_backward.6 = (bf16[16,136,1024]{2,1,0:T(8,128)(2,1)}, f32[256,1024]{1,0:T(8,128)S(1)}) custom-call(s32[2,2]{1,0:T(2,128)S(1)} %broadcast_select_fusion.10.facts_ref, f32[256,1024]{1,0:T(8,128)S(1)} %convert_select_fusion.1.g_ref, f32[256,1024]{1,0:T(8,128)S(1)} %get-tuple-element.275.gx_ref, ...), custom_call_target="tpu_custom_call", output_to_operand_aliasing={{0}: (22, {})} | custom-call | flops 2147483648 | bytes 16777216 | tf_op jit(solution)/shard_map/attention_backward/pallas_call | solution.py:878
  629.1 16.8 %feed_backward.7 = (bf16[16,136,1024]{2,1,0:T(8,128)(2,1)}, f32[256,1024]{1,0:T(8,128)S(1)}) custom-call(s32[2,2]{1,0:T(2,128)S(1)} %broadcast_select_fusion.10.facts_ref, f32[256,1024]{1,0:T(8,128)S(1)} %copy-done.19, f32[256,1024]{1,0:T(8,128)S(1)} %copy-done.1, f32[4,1024]{1,0:T(4,128)S(1)} %get-tuple-element.366.norm_ref, ...), custom_call_target="tpu_custom_call" | custom-call | flops 4294967296 | bytes 25165824 | tf_op jit(solution)/shard_map/feed_backward/pallas_call | solution.py:767
  646.0 18.2 %attention_backward.7 = (bf16[16,136,1024]{2,1,0:T(8,128)(2,1)}, f32[256,1024]{1,0:T(8,128)S(1)}) custom-call(s32[2,2]{1,0:T(2,128)S(1)} %broadcast_select_fusion.10.facts_ref, f32[256,1024]{1,0:T(8,128)S(1)} %copy-done.20, f32[256,1024]{1,0:T(8,128)S(1)} %get-tuple-element.278.gx_ref, f32[256,1024]{1,0:T(8,128)} %copy-done, ...), custom_call_target="tpu_custom_call", output_to_operand_aliasing={{0}: (22, {})} | custom-call | flops 2147483648 | bytes 16777216 | tf_op jit(solution)/shard_map/attention_backward/pallas_call | solution.py:878
  687.8 22.6 %collective-permute-done.44 = bf16[272,1024]{1,0:T(8,128)(2,1)S(1)} collective-permute-done((bf16[272,1024]{1,0:T(8,128)(2,1)S(1)}, bf16[272,1024]{1,0:T(8,128)(2,1)S(1)}, u32[]{:S(2)}, u32[]{:S(2)}) %collective-permute-start.44) | collective-permute-done | bytes 557088 | tf_op jit(solution)/shard_map/ppermute | solution.py:300
  723.6 24.0 %collective-permute-done.43 = bf16[272,1024]{1,0:T(8,128)(2,1)S(1)} collective-permute-done((bf16[272,1024]{1,0:T(8,128)(2,1)S(1)}, bf16[272,1024]{1,0:T(8,128)(2,1)S(1)}, u32[]{:S(2)}, u32[]{:S(2)}) %collective-permute-start.43) | collective-permute-done | bytes 557088 | tf_op jit(solution)/shard_map/ppermute | solution.py:300
  748.6 32.8 %all-to-all-done.3.late1_ref = bf16[8,272,1024]{2,1,0:T(8,128)(2,1)} async-done(((bf16[8,272,1024]{2,1,0:T(8,128)(2,1)}), bf16[8,272,1024]{2,1,0:T(8,128)(2,1)}, u32[]{:S(2)}, u32[]{:S(2)}) %all-to-all-start.3) | async-done | bytes 4456480 | tf_op jit(solution)/shard_map/all_to_all | solution.py:274
  785.0 25.1 %all-to-all-start.4 = ((bf16[8,272,1024]{2,1,0:T(8,128)(2,1)}), bf16[8,272,1024]{2,1,0:T(8,128)(2,1)}, u32[]{:S(2)}, u32[]{:S(2)}) async-start(bf16[8,272,1024]{2,1,0:T(8,128)(2,1)} %broadcast_in_dim.80), calls=%async_computation.4 | async-start | bytes 8912896 | tf_op jit(solution)/shard_map/all_to_all | solution.py:274
  813.6 50.8 %all-to-all-done.4.early0_ref = bf16[8,272,1024]{2,1,0:T(8,128)(2,1)} async-done(((bf16[8,272,1024]{2,1,0:T(8,128)(2,1)}), bf16[8,272,1024]{2,1,0:T(8,128)(2,1)}, u32[]{:S(2)}, u32[]{:S(2)}) %all-to-all-start.4) | async-done | bytes 4456480 | tf_op jit(solution)/shard_map/all_to_all | solution.py:274
  884.7 11.2 %collective-permute-done.38 = bf16[256,1024]{1,0:T(8,128)(2,1)S(1)} collective-permute-done((bf16[256,1024]{1,0:T(8,128)(2,1)S(1)}, bf16[256,1024]{1,0:T(8,128)(2,1)S(1)}, u32[]{:S(2)}, u32[]{:S(2)}) %collective-permute-start.38) | collective-permute-done | bytes 524320 | tf_op jit(solution)/shard_map/ppermute | solution.py:27
  897.2 11.3 %finish.2 = (f32[2,1024,128]{2,1,0:T(8,128)}, f32[2,128,3072]{2,1,0:T(8,128)}, f32[2,1024,128]{2,1,0:T(8,128)}, f32[2,128,1024]{2,1,0:T(8,128)}, f32[2,1024,128]...) custom-call(s32[2]{0:T(128)} %pad_add_fusion.1.info_ref, ...), custom_call_target="tpu_custom_call" | custom-call | flops 536870912 | bytes 25165824 | tf_op jit(solution)/shard_map/finish/pallas_call | solution.py:389
  908.5 11.3 %finish.3 = (f32[2,1024,128]{2,1,0:T(8,128)}, f32[2,128,3072]{2,1,0:T(8,128)}, f32[2,1024,128]{2,1,0:T(8,128)}, f32[2,128,1024]{2,1,0:T(8,128)}, f32[2,1024,128]...) custom-call(s32[2]{0:T(128)} %pad_add_fusion.1.info_ref, ...), custom_call_target="tpu_custom_call", output_to_operand_aliasing={{0}: (19, {}), {1}: (20, {}), {2}: (21, {}), {3}: (22, {}),... | custom-call | flops 536870912 | bytes 25165824 | tf_op jit(solution)/shard_map/finish/pallas_call | solution.py:389
  (338 shorter events, 283.4 us)
Async XLA Ops:
  8.1 37.3 %collective-permute-start.3 = (bf16[2,7168,128]{2,1,0:T(8,128)(2,1)}, bf16[2,7168,128]{2,1,0:T(8,128)(2,1)}, u32[]{:S(2)}, u32[]{:S(2)}) collective-permute-start(bf16[2,7168,128]{2,1,0:T(8,128)(2,1)} %constant_dynamic-update-slice_fusion), channel_id=1, source_target_pairs={{0,16},{1,17},{2,18},{3,19},{4,20},{5,21},{6,22},{7,23},{24,8},{25... | collective-permute-start | bytes 11010056 | tf_op jit(solution)/shard_map/ppermute | solution.py:27
  14.0 72.4 %collective-permute-start.13 = (bf16[2,128,9216]{2,1,0:T(8,128)(2,1)}, bf16[2,128,9216]{2,1,0:T(8,128)(2,1)}, u32[]{:S(2)}, u32[]{:S(2)}) collective-permute-start(bf16[2,128,9216]{2,1,0:T(8,128)(2,1)} %constant_dynamic-update-slice_fusion.4), channel_id=1, source_target_pairs={{0,16},{1,17},{2,18},{3,19},{4,20},{5,21},{6,22},{7,23},{24,8},{25... | collective-permute-start | bytes 14155784 | tf_op jit(solution)/shard_map/ppermute | solution.py:27
  45.6 40.8 %collective-permute-start.10 = (bf16[4,2,64,1024]{3,2,1,0:T(8,128)(2,1)S(1)}, bf16[4,2,64,1024]{3,2,1,0:T(8,128)(2,1)S(1)}, u32[]{:S(2)}, u32[]{:S(2)}) collective-permute-start(bf16[4,2,64,1024]{3,2,1,0:T(8,128)(2,1)S(1)} %get-tuple-element.176), channel_id=1, source_target_pairs={{0,4},{1,5},{2,6},{3,7},{4,0},{5,1},{6,2},{7,3},{8,12},{9,13},{10,... | collective-permute-start | bytes 3145736 | tf_op jit(solution)/shard_map/ppermute | solution.py:36
  47.3 39.2 %collective-permute-start.11 = (bf16[4,2,64,1024]{3,2,1,0:T(8,128)(2,1)S(1)}, bf16[4,2,64,1024]{3,2,1,0:T(8,128)(2,1)S(1)}, u32[]{:S(2)}, u32[]{:S(2)}) collective-permute-start(bf16[4,2,64,1024]{3,2,1,0:T(8,128)(2,1)S(1)} %get-tuple-element.177), channel_id=1, source_target_pairs={{0,1},{1,0},{2,3},{3,2},{4,5},{5,4},{6,7},{7,6},{8,9},{9,8},{10,11... | collective-permute-start | bytes 3145736 | tf_op jit(solution)/shard_map/ppermute | solution.py:36
  47.8 38.6 %collective-permute-start.12 = (bf16[4,2,64,1024]{3,2,1,0:T(8,128)(2,1)S(1)}, bf16[4,2,64,1024]{3,2,1,0:T(8,128)(2,1)S(1)}, u32[]{:S(2)}, u32[]{:S(2)}) collective-permute-start(bf16[4,2,64,1024]{3,2,1,0:T(8,128)(2,1)S(1)} %get-tuple-element.178), channel_id=1, source_target_pairs={{0,2},{1,3},{2,0},{3,1},{4,6},{5,7},{6,4},{7,5},{8,10},{9,11},{10,... | collective-permute-start | bytes 3145736 | tf_op jit(solution)/shard_map/ppermute | solution.py:36
  49.3 36.1 %collective-permute-start.5 = (bf16[6,64,1024]{2,1,0:T(8,128)(2,1)S(1)}, bf16[6,64,1024]{2,1,0:T(8,128)(2,1)S(1)}, u32[]{:S(2)}, u32[]{:S(2)}) collective-permute-start(bf16[6,64,1024]{2,1,0:T(8,128)(2,1)S(1)} %get-tuple-element.363), channel_id=1, source_target_pairs={{0,8},{1,9},{2,10},{3,11},{4,12},{5,13},{6,14},{7,15},{8,0},{9,1},... | collective-permute-start | bytes 2359304 | tf_op jit(solution)/shard_map/ppermute | solution.py:36
  90.0 31.5 %collective-permute-start.17 = (bf16[27,2,64,1024]{3,2,1,0:T(8,128)(2,1)}, bf16[27,2,64,1024]{3,2,1,0:T(8,128)(2,1)}, u32[]{:S(2)}, u32[]{:S(2)}) collective-permute-start(bf16[27,2,64,1024]{3,2,1,0:T(8,128)(2,1)} %get-tuple-element.182.mine), channel_id=1, source_target_pairs={{0,16},{16,0},{1,17},{17,1},{2,18},{18,2},{3,19},{19,3},{4,20},{20... | collective-permute-start | bytes 21233672 | tf_op jit(solution)/shard_map/ppermute | solution.py:40
  90.0 31.2 %collective-permute-start.14 = (bf16[5,2,64,1024]{3,2,1,0:T(8,128)(2,1)S(1)}, bf16[5,2,64,1024]{3,2,1,0:T(8,128)(2,1)S(1)}, u32[]{:S(2)}, u32[]{:S(2)}) collective-permute-start(bf16[5,2,64,1024]{3,2,1,0:T(8,128)(2,1)S(1)} %get-tuple-element.179), channel_id=1, source_target_pairs={{0,2},{1,3},{2,0},{3,1},{4,6},{5,7},{6,4},{7,5},{8,10},{9,11},{10,... | collective-permute-start | bytes 3932168 | tf_op jit(solution)/shard_map/ppermute | solution.py:36
  90.7 30.9 %collective-permute-start.15 = (bf16[5,2,64,1024]{3,2,1,0:T(8,128)(2,1)S(1)}, bf16[5,2,64,1024]{3,2,1,0:T(8,128)(2,1)S(1)}, u32[]{:S(2)}, u32[]{:S(2)}) collective-permute-start(bf16[5,2,64,1024]{3,2,1,0:T(8,128)(2,1)S(1)} %get-tuple-element.180), channel_id=1, source_target_pairs={{0,4},{1,5},{2,6},{3,7},{4,0},{5,1},{6,2},{7,3},{8,12},{9,13},{10,... | collective-permute-start | bytes 3932168 | tf_op jit(solution)/shard_map/ppermute | solution.py:36
  91.0 30.6 %collective-permute-start.16 = (bf16[5,2,64,1024]{3,2,1,0:T(8,128)(2,1)S(1)}, bf16[5,2,64,1024]{3,2,1,0:T(8,128)(2,1)S(1)}, u32[]{:S(2)}, u32[]{:S(2)}) collective-permute-start(bf16[5,2,64,1024]{3,2,1,0:T(8,128)(2,1)S(1)} %get-tuple-element.181), channel_id=1, source_target_pairs={{0,1},{1,0},{2,3},{3,2},{4,5},{5,4},{6,7},{7,6},{8,9},{9,8},{10,11... | collective-permute-start | bytes 3932168 | tf_op jit(solution)/shard_map/ppermute | solution.py:36
  125.8 54.0 %collective-permute-start.21 = (bf16[15,2,64,1024]{3,2,1,0:T(8,128)(2,1)}, bf16[15,2,64,1024]{3,2,1,0:T(8,128)(2,1)}, u32[]{:S(2)}, u32[]{:S(2)}) collective-permute-start(bf16[15,2,64,1024]{3,2,1,0:T(8,128)(2,1)} %get-tuple-element.187.mine), channel_id=1, source_target_pairs={{0,16},{16,0},{1,17},{17,1},{2,18},{18,2},{3,19},{19,3},{4,20},{20... | collective-permute-start | bytes 11796488 | tf_op jit(solution)/shard_map/ppermute | solution.py:40
  125.8 54.0 %collective-permute-start.18 = (bf16[6,2,64,1024]{3,2,1,0:T(8,128)(2,1)}, bf16[6,2,64,1024]{3,2,1,0:T(8,128)(2,1)}, u32[]{:S(2)}, u32[]{:S(2)}) collective-permute-start(bf16[6,2,64,1024]{3,2,1,0:T(8,128)(2,1)} %get-tuple-element.183), channel_id=1, source_target_pairs={{0,4},{1,5},{2,6},{3,7},{4,0},{5,1},{6,2},{7,3},{8,12},{9,13},{10,... | collective-permute-start | bytes 4718600 | tf_op jit(solution)/shard_map/ppermute | solution.py:36
  127.4 52.4 %collective-permute-start.19 = (bf16[6,2,64,1024]{3,2,1,0:T(8,128)(2,1)}, bf16[6,2,64,1024]{3,2,1,0:T(8,128)(2,1)}, u32[]{:S(2)}, u32[]{:S(2)}) collective-permute-start(bf16[6,2,64,1024]{3,2,1,0:T(8,128)(2,1)} %get-tuple-element.184), channel_id=1, source_target_pairs={{0,1},{1,0},{2,3},{3,2},{4,5},{5,4},{6,7},{7,6},{8,9},{9,8},{10,11... | collective-permute-start | bytes 4718600 | tf_op jit(solution)/shard_map/ppermute | solution.py:36
  127.9 51.9 %collective-permute-start.20 = (bf16[6,2,64,1024]{3,2,1,0:T(8,128)(2,1)}, bf16[6,2,64,1024]{3,2,1,0:T(8,128)(2,1)}, u32[]{:S(2)}, u32[]{:S(2)}) collective-permute-start(bf16[6,2,64,1024]{3,2,1,0:T(8,128)(2,1)} %get-tuple-element.185), channel_id=1, source_target_pairs={{0,2},{1,3},{2,0},{3,1},{4,6},{5,7},{6,4},{7,5},{8,10},{9,11},{10,... | collective-permute-start | bytes 4718600 | tf_op jit(solution)/shard_map/ppermute | solution.py:36
  129.3 49.5 %collective-permute-start.6 = (bf16[6,64,1024]{2,1,0:T(8,128)(2,1)}, bf16[6,64,1024]{2,1,0:T(8,128)(2,1)S(1)}, u32[]{:S(2)}, u32[]{:S(2)}) collective-permute-start(bf16[6,64,1024]{2,1,0:T(8,128)(2,1)} %get-tuple-element.172), channel_id=1, source_target_pairs={{0,8},{1,9},{2,10},{3,11},{4,12},{5,13},{6,14},{7,15},{8,0},{9,1},... | collective-permute-start | bytes 2359304 | tf_op jit(solution)/shard_map/ppermute | solution.py:36
  189.3 37.4 %collective-permute-start.25 = (bf16[21,2,64,1024]{3,2,1,0:T(8,128)(2,1)}, bf16[21,2,64,1024]{3,2,1,0:T(8,128)(2,1)}, u32[]{:S(2)}, u32[]{:S(2)}) collective-permute-start(bf16[21,2,64,1024]{3,2,1,0:T(8,128)(2,1)} %get-tuple-element.196.mine), channel_id=1, source_target_pairs={{0,16},{16,0},{1,17},{17,1},{2,18},{18,2},{3,19},{19,3},{4,20},{20... | collective-permute-start | bytes 16515080 | tf_op jit(solution)/shard_map/ppermute | solution.py:40
  189.3 37.4 %collective-permute-start.22 = (bf16[5,2,64,1024]{3,2,1,0:T(8,128)(2,1)}, bf16[5,2,64,1024]{3,2,1,0:T(8,128)(2,1)S(1)}, u32[]{:S(2)}, u32[]{:S(2)}) collective-permute-start(bf16[5,2,64,1024]{3,2,1,0:T(8,128)(2,1)} %get-tuple-element.188), channel_id=1, source_target_pairs={{0,4},{1,5},{2,6},{3,7},{4,0},{5,1},{6,2},{7,3},{8,12},{9,13},{10,... | collective-permute-start | bytes 3932168 | tf_op jit(solution)/shard_map/ppermute | solution.py:36
  191.5 35.3 %collective-permute-start.23 = (bf16[5,2,64,1024]{3,2,1,0:T(8,128)(2,1)}, bf16[5,2,64,1024]{3,2,1,0:T(8,128)(2,1)}, u32[]{:S(2)}, u32[]{:S(2)}) collective-permute-start(bf16[5,2,64,1024]{3,2,1,0:T(8,128)(2,1)} %get-tuple-element.189), channel_id=1, source_target_pairs={{0,1},{1,0},{2,3},{3,2},{4,5},{5,4},{6,7},{7,6},{8,9},{9,8},{10,11... | collective-permute-start | bytes 3932168 | tf_op jit(solution)/shard_map/ppermute | solution.py:36
  192.0 34.7 %collective-permute-start.24 = (bf16[5,2,64,1024]{3,2,1,0:T(8,128)(2,1)}, bf16[5,2,64,1024]{3,2,1,0:T(8,128)(2,1)}, u32[]{:S(2)}, u32[]{:S(2)}) collective-permute-start(bf16[5,2,64,1024]{3,2,1,0:T(8,128)(2,1)} %get-tuple-element.190), channel_id=1, source_target_pairs={{0,2},{1,3},{2,0},{3,1},{4,6},{5,7},{6,4},{7,5},{8,10},{9,11},{10,... | collective-permute-start | bytes 3932168 | tf_op jit(solution)/shard_map/ppermute | solution.py:36
  193.6 32.4 %collective-permute-start.1 = (bf16[2,128,1024]{2,1,0:T(8,128)(2,1)S(1)}, bf16[2,128,1024]{2,1,0:T(8,128)(2,1)S(1)}, u32[]{:S(2)}, u32[]{:S(2)}) collective-permute-start(bf16[2,128,1024]{2,1,0:T(8,128)(2,1)S(1)} %broadcast_select_fusion.7), channel_id=1, source_target_pairs={{16,8},{17,9},{18,10},{19,11},{20,12},{21,13},{22,14},{23,15},{8,1... | collective-permute-start | bytes 1572872 | tf_op jit(solution)/shard_map/ppermute | solution.py:27
  256.1 30.5 %collective-permute-start.33 = (bf16[6,2,64,1024]{3,2,1,0:T(8,128)(2,1)}, bf16[6,2,64,1024]{3,2,1,0:T(8,128)(2,1)S(1)}, u32[]{:S(2)}, u32[]{:S(2)}) collective-permute-start(bf16[6,2,64,1024]{3,2,1,0:T(8,128)(2,1)} %get-tuple-element.228.mine), channel_id=1, source_target_pairs={{0,16},{16,0},{1,17},{17,1},{2,18},{18,2},{3,19},{19,3},{4,20},{20... | collective-permute-start | bytes 4718600 | tf_op jit(solution)/shard_map/ppermute | solution.py:40
  291.1 43.7 %collective-permute-start.34 = (bf16[12,2,64,1024]{3,2,1,0:T(8,128)(2,1)}, bf16[12,2,64,1024]{3,2,1,0:T(8,128)(2,1)}, u32[]{:S(2)}, u32[]{:S(2)}) collective-permute-start(bf16[12,2,64,1024]{3,2,1,0:T(8,128)(2,1)} %collect.15.mine), channel_id=1, source_target_pairs={{0,16},{16,0},{1,17},{17,1},{2,18},{18,2},{3,19},{19,3},{4,20},{20... | collective-permute-start | bytes 9437192 | tf_op jit(solution)/shard_map/ppermute | solution.py:40
  371.6 28.4 %collective-permute-start.35 = (bf16[256,1024]{1,0:T(8,128)(2,1)S(1)}, bf16[256,1024]{1,0:T(8,128)(2,1)S(1)}, u32[]{:S(2)}, u32[]{:S(2)}) collective-permute-start(bf16[256,1024]{1,0:T(8,128)(2,1)S(1)} %convert_element_type.97), channel_id=1, source_target_pairs={{0,8},{1,9},{2,10},{3,11},{4,12},{5,13},{6,14},{7,15},{16,24},{17,... | collective-permute-start | bytes 1572872 | tf_op jit(solution)/shard_map/ppermute | solution.py:1078
  499.1 44.8 %collective-permute-start.42 = (bf16[8,136,1024]{2,1,0:T(8,128)(2,1)}, bf16[8,136,1024]{2,1,0:T(8,128)(2,1)}, u32[]{:S(2)}, u32[]{:S(2)}) collective-permute-start(bf16[8,136,1024]{2,1,0:T(8,128)(2,1)} %constant_dynamic-slice_fusion), channel_id=1, source_target_pairs={{8,24},{9,25},{10,26},{11,27},{12,28},{13,29},{14,30},{15,31},{24,... | collective-permute-start | bytes 6684680 | tf_op jit(solution)/shard_map/ppermute | solution.py:27
  557.3 60.6 %all-to-all-start = ((bf16[8,272,1024]{2,1,0:T(8,128)(2,1)}), bf16[8,272,1024]{2,1,0:T(8,128)(2,1)}, u32[]{:S(2)}, u32[]{:S(2)}) async-start(bf16[8,272,1024]{2,1,0:T(8,128)(2,1)} %pad_maximum_fusion), calls=%async_computation | async-start | bytes 8912896 | tf_op jit(solution)/shard_map/all_to_all | solution.py:274
  622.1 47.4 %all-to-all-start.1 = ((bf16[8,136,1024]{2,1,0:T(8,128)(2,1)}), bf16[8,136,1024]{2,1,0:T(8,128)(2,1)}, u32[]{:S(2)}, u32[]{:S(2)}) async-start(bf16[8,136,1024]{2,1,0:T(8,128)(2,1)} %add_convert_fusion.2), calls=%async_computation.1 | async-start | bytes 4456448 | tf_op jit(solution)/shard_map/all_to_all | solution.py:274
  671.6 39.7 %all-to-all-start.2 = ((bf16[8,136,1024]{2,1,0:T(8,128)(2,1)}), bf16[8,136,1024]{2,1,0:T(8,128)(2,1)}, u32[]{:S(2)}, u32[]{:S(2)}) async-start(bf16[8,136,1024]{2,1,0:T(8,128)(2,1)} %add_convert_fusion.3), calls=%async_computation.2 | async-start | bytes 4456448 | tf_op jit(solution)/shard_map/all_to_all | solution.py:274
  676.7 33.7 %collective-permute-start.44 = (bf16[272,1024]{1,0:T(8,128)(2,1)S(1)}, bf16[272,1024]{1,0:T(8,128)(2,1)S(1)}, u32[]{:S(2)}, u32[]{:S(2)}) collective-permute-start(bf16[272,1024]{1,0:T(8,128)(2,1)S(1)} %copy-done.67), channel_id=1, source_target_pairs={{8,0},{9,1},{10,2},{11,3},{12,4},{13,5},{14,6},{15,7},{24,16},{25,... | collective-permute-start | bytes 1671176 | tf_op jit(solution)/shard_map/ppermute | solution.py:300
  717.2 64.2 %all-to-all-start.3 = ((bf16[8,272,1024]{2,1,0:T(8,128)(2,1)}), bf16[8,272,1024]{2,1,0:T(8,128)(2,1)}, u32[]{:S(2)}, u32[]{:S(2)}) async-start(bf16[8,272,1024]{2,1,0:T(8,128)(2,1)} %broadcast_in_dim.79), calls=%async_computation.3 | async-start | bytes 8912896 | tf_op jit(solution)/shard_map/all_to_all | solution.py:274
  785.0 79.4 %all-to-all-start.4 = ((bf16[8,272,1024]{2,1,0:T(8,128)(2,1)}), bf16[8,272,1024]{2,1,0:T(8,128)(2,1)}, u32[]{:S(2)}, u32[]{:S(2)}) async-start(bf16[8,272,1024]{2,1,0:T(8,128)(2,1)} %broadcast_in_dim.80), calls=%async_computation.4 | async-start | bytes 8912896 | tf_op jit(solution)/shard_map/all_to_all | solution.py:274
  810.1 87.0 %collective-permute-start.46 = (bf16[8,272,1024]{2,1,0:T(8,128)(2,1)}, bf16[8,272,1024]{2,1,0:T(8,128)(2,1)}, u32[]{:S(2)}, u32[]{:S(2)}) collective-permute-start(bf16[8,272,1024]{2,1,0:T(8,128)(2,1)} %all-to-all-done.3.late1_ref), channel_id=1, source_target_pairs={{0,16},{1,17},{2,18},{3,19},{4,20},{5,21},{6,22},{7,23},{8,24},{9,... | collective-permute-start | bytes 13369352 | tf_op jit(solution)/shard_map/ppermute | solution.py:307
  864.4 32.8 %collective-permute-start.45 = (bf16[8,272,1024]{2,1,0:T(8,128)(2,1)}, bf16[8,272,1024]{2,1,0:T(8,128)(2,1)}, u32[]{:S(2)}, u32[]{:S(2)}) collective-permute-start(bf16[8,272,1024]{2,1,0:T(8,128)(2,1)} %all-to-all-done.4.early0_ref), channel_id=1, source_target_pairs={{16,0},{17,1},{18,2},{19,3},{20,4},{21,5},{22,6},{23,7},{24,8},{25... | collective-permute-start | bytes 13369352 | tf_op jit(solution)/shard_map/ppermute | solution.py:307
  (102 other events, 2093.0 us)

commit v4 on v3

--- a/solution.py
+++ b/solution.py
@@ -80,6 +80,42 @@
         ),
         name="pack",
     )(core.reshape(1), *frozen)
+
+
+def pack_adapters_kernel(*refs):
+    sources, (first_out, second_out) = refs[:8], refs[-2:]
+    at = 0
+    for source in sources[0::2]:
+        first_out[:, at : at + source.shape[1]] = source[...]
+        at = at + source.shape[1]
+    at = 0
+    for source in sources[1::2]:
+        second_out[:, :, at : at + source.shape[2]] = source[...]
+        at = at + source.shape[2]
+
+
+def pack_adapters(trained, *after):
+    layers = trained[0].shape[0]
+    height = sum(factor.shape[1] for factor in trained[0::2])
+    width = sum(factor.shape[2] for factor in trained[1::2])
+    shapes = [
+        jax.ShapeDtypeStruct((layers, height, RANK), jnp.bfloat16),
+        jax.ShapeDtypeStruct((layers, RANK, width), jnp.bfloat16),
+    ]
+
+    def layer_block(value):
+        return pl.BlockSpec((1,) + value.shape[1:], lambda step: (step, 0, 0))
+
+    return pl.pallas_call(
+        pack_adapters_kernel,
+        out_shape=shapes,
+        grid=(layers,),
+        in_specs=[layer_block(factor) for factor in trained] + [pl.BlockSpec(memory_space=pl.ANY)] * len(after),
+        out_specs=[layer_block(shape) for shape in shapes],
+        compiler_params=pltpu.CompilerParams(vmem_limit_bytes=30 << 20),
+        cost_estimate=pl.CostEstimate(flops=0, bytes_accessed=4 * RANK * layers * (height + width), transcendentals=0),
+        name="pack_adapters",
+    )(*trained, *after)
 
 
 def rotations(masks):
@@ -309,7 +345,7 @@
 
 
 def finish_kernel(
-    offsets, info_ref, rate_ref, early0_ref, early1_ref, late0_ref, late1_ref, counts_ref,
+    info_ref, rate_ref, early0_ref, early1_ref, late0_ref, late1_ref, counts_ref,
     aq_ref, ao_ref, au_ref, ad_ref, bq_ref, bo_ref, bu_ref, bd_ref, wq_ref, wo_ref, wu_ref, wd_ref, *refs,
 ):
     gaq, gbq, gao, gbo, gau, gbu, gad, gbd, gain_out, bias_out, fq, fo, fu, fd, rms_out, g_ref, sem = refs[-17:]
@@ -330,11 +366,11 @@
 
     @pl.when(info_ref[1] == 0)
     def _():
-        fetch((early0_ref, early1_ref), offsets[0])
+        fetch((early0_ref, early1_ref), pl.program_id(0) * height)
 
     @pl.when(info_ref[1] != 0)
     def _():
-        fetch((late0_ref, late1_ref), offsets[1])
+        fetch((late0_ref, late1_ref), pl.program_id(0) * height)
 
     def run():
         def columns(index, begin=0, end=RANK):
@@ -370,12 +406,12 @@
     run()
 
 
-def finish(place, core, rate, early, late, offsets, layer, counts, trained, frozen, into):
+def finish(place, core, rate, early, late, counts, trained, frozen):
     firsts, seconds = trained[0:8:2], trained[1:8:2]
     layers = firsts[0].shape[0]
 
     def layer_block(value):
-        return pl.BlockSpec((1,) + value.shape[1:], lambda step, *_: (layer, 0, 0))
+        return pl.BlockSpec((1,) + value.shape[1:], lambda step, *_: (step, 0, 0))
 
     shapes = []
     for first, second in zip(firsts, seconds):
@@ -385,26 +421,23 @@
     shapes += [jax.ShapeDtypeStruct(matrix.shape, jnp.bfloat16) for matrix in frozen]
     shapes += [jax.ShapeDtypeStruct((layers, 3, 128), jnp.float32)]
     keep = pl.BlockSpec(memory_space=pl.ANY)
-    extra = [] if into is None else list(into)
     return pl.pallas_call(
-        partial(finish_kernel, offsets),
+        finish_kernel,
         out_shape=shapes,
         grid_spec=pltpu.PrefetchScalarGridSpec(
             num_scalar_prefetch=1,
-            grid=(1,),
+            grid=(layers,),
             in_specs=[pl.BlockSpec(memory_space=pltpu.SMEM)]
             + [keep] * 4
             + [pl.BlockSpec((1, 128), lambda step, *_: (0, 0))]
-            + [layer_block(value) for value in firsts + seconds + frozen]
-            + [keep] * len(extra),
+            + [layer_block(value) for value in firsts + seconds + frozen],
             out_specs=[layer_block(shape) for shape in shapes],
             scratch_shapes=[pltpu.VMEM((16, RANK + 8, WIDE), jnp.bfloat16), pltpu.SemaphoreType.DMA((2,))],
         ),
-        input_output_aliases={19 + index: index for index in range(len(extra))},
         compiler_params=pltpu.CompilerParams(vmem_limit_bytes=60 << 20),
         cost_estimate=pl.CostEstimate(flops=1 << 29, bytes_accessed=24 << 20, transcendentals=0),
         name="finish",
-    )(jnp.stack([place, core]), rate.reshape(1), *early, *late, counts, *firsts, *seconds, *frozen, *extra)
+    )(jnp.stack([place, core]), rate.reshape(1), *early, *late, counts, *firsts, *seconds, *frozen)
 
 
 def mm(left, right):
@@ -491,10 +524,9 @@
 
 def attention_forward_kernel(
     facts_ref, x_ref, norm_ref, table_ref, first_ref, wq_ref, wk_ref, wv_ref, bq_ref, bk_ref, bv_ref,
-    wo_ref, ao_ref, bo_ref,
-    q_out, k_out, v_out, mixed_out, midq_out, mido_out, att_out,
-    a_scr, mid_scr,
+    wo_ref, ao_ref, bo_ref, *refs,
 ):
+    q_out, k_out, v_out, mixed_out, midq_out, mido_out, att_out, a_scr, mid_scr = refs[-9:]
     step = pl.program_id(0)
     seqs = x_ref.shape[0] // table_ref.shape[1]
     seq_len = table_ref.shape[1]
@@ -579,7 +611,7 @@
     return jax.ShapeDtypeStruct(shape, dtype)
 
 
-def attention_forward(residual, weights, norms, tables, facts):
+def attention_forward(residual, weights, norms, tables, facts, after):
     tokens, width = residual.shape
     groups = width // GROUP
     joint, output = weights[0], weights[1]
@@ -603,7 +635,8 @@
             row_block(GROUP, width),
             layer_rows(layer, GROUP, RANK, groups),
             layer_fixed(layer, RANK, width, 0, 3),
-        ],
+        ]
+        + [pl.BlockSpec(memory_space=pl.ANY)] * len(after),
         [column_block(tokens, GROUP)] * 4 + [whole(tokens, RANK), whole(tokens, RANK), whole(tokens, width)],
         [shaped((tokens, width))] * 4
         + [shaped((tokens, RANK)), shaped((tokens, RANK)), shaped((tokens, width), jnp.float32)],
@@ -612,7 +645,7 @@
         2 * 5 * width * width + 12 * tokens * width,
     )(
         facts, residual, norms, tables, firsts, joint, joint, joint, seconds, seconds, seconds, output,
-        firsts, seconds,
+        firsts, seconds, *after,
     )
 
 
@@ -805,10 +838,10 @@
 
 def attention_backward_kernel(
     facts_ref, g_ref, gx_ref, x_ref, norm_ref, table_ref, q_ref, k_ref, v_ref, mixed_ref, midq_ref, mido_ref,
-    wq_ref, wk_ref, wv_ref, aq_ref, bq_ref, bk_ref, bv_ref, wo_ref, ao_ref, bo_ref, feed_block_ref,
-    whole_out, gx_out,
-    block_out, g_scr, gmo_scr, gmot_scr, midqt_scr, gmq_scr, acc_scr, gq_scr, gk_scr, gv_scr, sem,
+    wq_ref, wk_ref, wv_ref, aq_ref, bq_ref, bk_ref, bv_ref, wo_ref, ao_ref, bo_ref, feed_block_ref, *refs,
 ):
+    whole_out, gx_out = refs[-13:-11]
+    block_out, g_scr, gmo_scr, gmot_scr, midqt_scr, gmq_scr, acc_scr, gq_scr, gk_scr, gv_scr, sem = refs[-11:]
     step = pl.program_id(0)
     width = x_ref.shape[1]
     seq_len = table_ref.shape[1]
@@ -867,7 +900,7 @@
             copy.wait()
 
 
-def attention_backward(gradient, grad_feed, feed_block, residual, weights, norms, tables, kept, facts):
+def attention_backward(gradient, grad_feed, feed_block, residual, weights, norms, tables, kept, facts, after):
     tokens, width = residual.shape
     groups = width // GROUP
     joint, output = weights[0], weights[1]
@@ -902,7 +935,8 @@
             layer_rows(layer, GROUP, RANK, groups),
             layer_fixed(layer, RANK, width, 0, 3),
             pl.BlockSpec(memory_space=pl.ANY),
-        ],
+        ]
+        + [pl.BlockSpec(memory_space=pl.ANY)] * len(after),
         [pl.BlockSpec(memory_space=pl.ANY), whole(tokens, width)],
         [shaped((16, RANK + 8, width)), shaped((tokens, width), jnp.float32)],
         [
@@ -923,13 +957,13 @@
         aliases={22: 0},
     )(
         facts, gradient, grad_feed, residual, norms, tables, queries, keys, values, mixed, mid_q, mid_o, joint,
-        joint, joint, firsts, seconds, seconds, seconds, output, firsts, seconds, feed_block,
+        joint, joint, firsts, seconds, seconds, seconds, output, firsts, seconds, feed_block, *after,
     )
 
 
-def layer_forward(residual, weights, tables, facts):
+def layer_forward(residual, weights, tables, facts, after=()):
     norms = weights[6]
-    *kept_attention, attended = attention_forward(residual, weights, norms, tables, facts)
+    *kept_attention, attended = attention_forward(residual, weights, norms, tables, facts, after)
     *kept_feed, output, sums = feed_forward(residual, attended, weights, norms, facts)
     return output, (residual, kept_attention, kept_feed + [sums])
 
@@ -938,10 +972,8 @@
     residual, kept_attention, kept_feed = kept
     norms = weights[6]
     feed_block, grad_feed = feed_backward(gradient, residual, weights, norms, kept_feed, facts)
-    if after:
-        grad_feed = tie(grad_feed, *after)
     block, grad_input = attention_backward(
-        gradient, grad_feed, feed_block, residual, weights, norms, tables, kept_attention, facts
+        gradient, grad_feed, feed_block, residual, weights, norms, tables, kept_attention, facts, after
     )
     return grad_input, block
 
@@ -1003,9 +1035,9 @@
     sibling, cross = [partial(both_axes, pairs=pairs) for pairs in (to_sibling, to_cross)]
 
     same, other = pack_halves(core, frozen)
-    swapped = flip_core(other)
-    own = jnp.where(home, same, swapped)
-    leaving = jnp.where(home, swapped, same)
+    swapped_units = flip_core(other)
+    own = jnp.where(home, same, swapped_units)
+    leaving = jnp.where(home, swapped_units, same)
     partner = [flip_place(leaving[0], middle)]
     for layer in range(1, local_layers):
         partner.append(flip_place(tie(leaving[layer], partner[-1]), middle))
@@ -1019,23 +1051,26 @@
     norms = jnp.concatenate([layer_norm_gain, layer_norm_bias], 1)
     facts = jnp.where(home, facts, cross(facts))
     norms = jnp.where(home, norms, sibling(norms))
-    packed = [
-        jnp.concatenate([factor for factor in trained[0::2]], 1),
-        jnp.concatenate([factor for factor in trained[1::2]], 2),
-    ]
     visiting = jnp.where(stage == 0, cotangent, inputs)
     tables = rotary_tables(seq_len)
     ended, fresh, started, waiting = (), [], set(), []
     bases = [jnp.where(stage == which, 0, middle) for which in range(2)]
     for number, active in enumerate(plan):
+        if number == len(plan) - 1:
+            start = jnp.where(home, inputs, visiting).astype(jnp.float32).reshape(tokens, model_width)
+            while waiting and min(layer for layer, _ in waiting[0][1]) == 0:
+                assemble(*waiting.pop(0), count, dense)
+            first_weights = tuple(dense[0]) + (packed[0], packed[1], norms[0], 0)
+            boundary, _ = layer_forward(start, first_weights, tables, facts)
+            ended = ended + (boundary,)
         for index in active:
             if index not in started:
                 started.add(index)
                 gather = gathers[index]
                 fresh = fresh + [(gather.block, part, 1, gather, part, [0]) for part in range(3)]
         extra = []
-        if number < 2:
-            extra.append((packed[number], sibling))
+        if number in (1, 2):
+            extra.append((packed[number - 1], sibling))
         if number == 4:
             extra.append((visiting, cross))
         moving = fresh if number >= 2 else []
@@ -1043,12 +1078,16 @@
             [gathers[index] for index in active], masks, moving, extra, ended
         )
         fresh = came if moving else fresh + came
-        if number < 2:
-            packed[number] = jnp.where(home, packed[number], results[0])
+        if number == 0:
+            packed = list(pack_adapters(trained, swapped_units))
+        if number in (1, 2):
+            packed[number - 1] = jnp.where(home, packed[number - 1], results[0])
         if number == 4:
             visiting = results[0]
         marks = [assemble(*waiting.pop(0), count, dense)] if waiting and number < len(plan) - 1 else []
         ended = tuple(there) + tuple(results) + tuple(marks)
+        if number == 3:
+            ended = ended + tuple(packed)
         if moving:
             ended = ended + (swapped,)
             layout = [(gather.layer, part) for _, _, size, gather, part, _ in moving for _ in range(size)]
@@ -1060,24 +1099,30 @@
     for item in waiting:
         assemble(*item, count, dense)
     weights = [tuple(dense[layer]) + (packed[0], packed[1], norms[layer], layer) for layer in range(local_layers)]
-    start = jnp.where(home, inputs, visiting).astype(jnp.float32).reshape(tokens, model_width)
     valid = jnp.arange(seq_len)[None, :] < facts[0][:, None]
     end_grad = jnp.where(home, cotangent, visiting).astype(jnp.float32)
     end_grad = jnp.where(stage == 1, end_grad * valid[..., None].astype(jnp.float32), 0.0)
     end_grad = end_grad.reshape(tokens, model_width)
-    def stage_forward(residual):
+    def stage_forward(residual, after):
         kept = []
         for layer in range(local_layers):
-            residual, kept_state = layer_forward(residual, weights[layer], tables, facts)
+            residual, kept_state = layer_forward(residual, weights[layer], tables, facts, after if layer == 0 else ())
             kept.append(kept_state)
         return residual, kept
 
-    boundary, _ = stage_forward(start)
+    for layer in range(1, local_layers):
+        boundary, _ = layer_forward(boundary, weights[layer], tables, facts)
     boundary = boundary.astype(jnp.bfloat16)
     forward_pairs = [(index, index + middle) for index in range(middle)]
     received = lax.ppermute(boundary, "dp", forward_pairs)
+    lane = jnp.arange(128)
+    counted = (domain[:, None] == lane[None, :]) | (lane == DOMAINS)[None, :]
+    counts = jnp.sum(jnp.where(counted, lengths.astype(jnp.float32)[:, None], 0.0), axis=0, keepdims=True)
+    for mask in masks + [middle]:
+        counts = counts + flip_place(counts, mask)
+    counts = jnp.maximum(counts, 1.0) * model_width
     entry = jnp.where(stage == 0, start, received.astype(jnp.float32))
-    final, kept = stage_forward(entry)
+    final, kept = stage_forward(entry, (counts,))
     final = final.astype(jnp.bfloat16)
 
     gradient = end_grad
@@ -1090,22 +1135,29 @@
     late_piece = sum_halves(late_halves, count)
 
     gradient = jnp.where(stage == 0, came_back.astype(jnp.float32), 0.0)
-    pieces = [None] * local_layers
-    last = late_piece
-    for layer in reversed(range(local_layers)):
-        gradient, block = layer_backward(gradient, kept[layer], weights[layer], tables, facts)
-        halves = swap_halves(block, 0, core, count)
-        pieces[layer] = last = sum_halves([tie(halves, last)], count)
-    late_piece = cross_section(tie(late_piece, pieces[local_layers - 1]), 1, stage, count)
-    early_piece = cross_section(jnp.concatenate(pieces, 0), 0, stage, count)
-    late_whole = spread_section(tie(late_piece, last), 1, count)
-    early_whole = spread_section(tie(early_piece, late_whole[1]), 0, count)
-
     out_pairs = [(count + index + middle, index + middle) for index in range(middle)]
     out_pairs = out_pairs + [(index + middle, count + index) for index in range(middle)]
     visiting = both_axes(jnp.where(core == 0, final, received), out_pairs)
     section_out = jnp.where(home, jnp.where(stage == 0, boundary, final), visiting)
     section_out = section_out.reshape(1, rows_dev, seq_len, model_width)
+    pieces = [None] * local_layers
+    after = ()
+    for layer in reversed(range(local_layers)):
+        gradient, block = layer_backward(gradient, kept[layer], weights[layer], tables, facts, after)
+        halves = swap_halves(block, 0, core, count)
+        if layer == local_layers - 1:
+            pieces[layer] = sum_halves([tie(halves, late_piece)], count)
+            late_piece = cross_section(late_piece, 1, stage, count)
+            after = (late_piece,)
+        else:
+            if layer == 0:
+                late_whole = spread_section(tie(late_piece, pieces[local_layers - 1]), 1, count)
+                halves = tie(halves, late_whole[1])
+            pieces[layer] = sum_halves([halves], count)
+            after = ()
+    early_piece = cross_section(jnp.concatenate(pieces, 0), 0, stage, count)
+    early_whole = spread_section(early_piece, 0, count)
+
     grad_pairs = [(index, count + index) for index in range(middle)]
     grad_pairs = grad_pairs + [(count + index, index + middle) for index in range(middle)]
     visiting = both_axes(jnp.where(core == 0, came_back, gradient.astype(jnp.bfloat16)), grad_pairs)
@@ -1114,20 +1166,8 @@
     )
     section_grad = section_grad.reshape(1, rows_dev, seq_len, model_width)
 
-    lane = jnp.arange(128)
-    counted = (domain[:, None] == lane[None, :]) | (lane == DOMAINS)[None, :]
-    counts = jnp.sum(jnp.where(counted, lengths.astype(jnp.float32)[:, None], 0.0), axis=0, keepdims=True)
-    counts = tie(counts, final)
-    for mask in masks + [middle]:
-        counts = counts + flip_place(counts, mask)
-    counts = jnp.maximum(counts, 1.0) * model_width
     rate = peak_rate * (steps_since_reset[0].astype(jnp.float32) + 1.0) / WARM
-    outputs = None
-    for layer in reversed(range(local_layers)):
-        offsets = (layer * (RANK + 8),) * 2
-        outputs = finish(
-            place, core, rate, early_whole, late_whole, offsets, layer, counts, trained, frozen, outputs
-        )
+    outputs = finish(place, core, rate, early_whole, late_whole, counts, trained, frozen)
     *outputs, rms = outputs
     return (section_out, section_grad, *outputs, rms[:, :, : DOMAINS + 1])
 

time: 933 us -> 899 us (0.964)
  waiting for transfers between devices: 351 us -> 309 us
  blocking collectives: 0 us -> 31.4 us
  starting transfers between devices: 118 us -> 96.8 us
    ppermute x27, waiting for transfers between devices: 141 us -> 97.8 us  [flip_place(): lax.ppermute(value, 'dp', [(place, place ^ mask) for place in range(count)])]
    all_to_all x0 -> x1, blocking collectives: none -> 31.4 us  [exchange(): return lax.all_to_all(value, 'dp', 0, 0, axis_index_groups=groups)]
    all_to_all x5 -> x4, starting transfers between devices: 46.2 us -> 20.9 us  [exchange(): return lax.all_to_all(value, 'dp', 0, 0, axis_index_groups=groups)]
    all_to_all x5 -> x4, waiting for transfers between devices: 93.5 us -> 72.9 us  [exchange(): return lax.all_to_all(value, 'dp', 0, 0, axis_index_groups=groups)]
    ppermute x11, waiting for transfers between devices: 32.6 us -> 47.2 us  [both_axes(): return lax.ppermute(value, ('section', 'dp'), pairs)]
    ppermute x2, waiting for transfers between devices: 46.6 us -> 58.7 us  [cross_section(): return jnp.where(stage == section, piece, lax.ppermute(piece, 'dp', across))]
    unnamed x163 -> x159, local copies, waits for them, and re-layouts: 25.3 us -> 28.7 us
  transfers between devices with their start and end apart: 56 -> 55, of which waited for: 27 -> 25; matrix products, arithmetic and copies ran while one was open for 5% -> 4% of each run, Pallas kernels for 20% -> 25%
where the time goes in v4:
time: 899 us; the launch traced here: 888 us
  Pallas kernels  361 us (40%)
  waiting for transfers between devices  309 us (34%)
  starting transfers between devices  96.8 us (11%)
  local copies, waits for them, and re-layouts  49.7 us (6%)
  other arithmetic  37 us (4%)
  blocking collectives  31.4 us (3%)
    ppermute x27, waiting for transfers between devices, flip_place(): lax.ppermute(value, 'dp', [(place, place ^ mask) for place in range(count)])  97.8 us
    pallas_call x4, Pallas kernels, attention_backward(): kernel_call(attention_backward_kernel, 'attention_backward', groups, [who...  73.1 us
    all_to_all x4, waiting for transfers between devices, exchange(): return lax.all_to_all(value, 'dp', 0, 0, axis_index_groups=groups)  72.9 us
    pallas_call x4, Pallas kernels, feed_backward(): kernel_call(feed_backward_kernel, 'feed_backward', hidden // BLOCK, [whol...  65.9 us
    pallas_call x4, Pallas kernels, feed_forward(): kernel_call(feed_forward_kernel, 'feed_forward', hidden // BLOCK, [whole(...  63.2 us
    ppermute x2, waiting for transfers between devices, cross_section(): return jnp.where(stage == section, piece, lax.ppermute(piece, 'dp', across))  58.7 us
    pallas_call x4, Pallas kernels, attention_forward(): kernel_call(attention_forward_kernel, 'attention_forward', groups, [whole...  55.8 us
    pallas_call x6, Pallas kernels, assemble(): pl.pallas_call(partial(assemble_kernel, tuple(layout)), out_shape=[jax.Sh...  48 us
  transfers between devices with their start and end apart: 55, of which 25 were waited for; matrix products, arithmetic and copies ran while one was open for 4% of the time, Pallas kernels for 25%

profile of v4, /device:TPU:26, one launch (start us, length us, event | category | flops | bytes accessed | tf_op | source)
XLA Modules:
  0.0 887.7 jit_solution(719668898765857530)
XLA Ops:
  26.4 10.3 %collective-permute-done.7.refs_4_.refs_1_ = bf16[2,2,64,1024]{3,2,1,0:T(8,128)(2,1)S(1)} collective-permute-done((bf16[2,2,64,1024]{3,2,1,0:T(8,128)(2,1)S(1)}, bf16[2,2,64,1024]{3,2,1,0:T(8,128)(2,1)S(1)}, u32[]{:S(2)}, u32[]{:S(2)}) %collective-permute-start.7) | collective-permute-done | bytes 524320 | tf_op jit(solution)/shard_map/ppermute | solution.py:36
  44.0 37.1 %collective-permute-done.5 = bf16[6,64,1024]{2,1,0:T(8,128)(2,1)S(1)} collective-permute-done((bf16[6,64,1024]{2,1,0:T(8,128)(2,1)S(1)}, bf16[6,64,1024]{2,1,0:T(8,128)(2,1)S(1)}, u32[]{:S(2)}, u32[]{:S(2)}) %collective-permute-start.5) | collective-permute-done | bytes 786464 | tf_op jit(solution)/shard_map/ppermute | solution.py:36
  91.0 14.7 %collective-permute-done.16.refs_11_ = bf16[2,128,9216]{2,1,0:T(8,128)(2,1)} collective-permute-done((bf16[2,128,9216]{2,1,0:T(8,128)(2,1)}, bf16[2,128,9216]{2,1,0:T(8,128)(2,1)}, u32[]{:S(2)}, u32[]{:S(2)}) %collective-permute-start.16) | collective-permute-done | bytes 4718624 | tf_op jit(solution)/shard_map/ppermute | solution.py:27
  107.9 10.5 %collective-permute-done.13.refs_10_.refs_1_ = bf16[5,2,64,1024]{3,2,1,0:T(8,128)(2,1)} collective-permute-done((bf16[5,2,64,1024]{3,2,1,0:T(8,128)(2,1)}, bf16[5,2,64,1024]{3,2,1,0:T(8,128)(2,1)}, u32[]{:S(2)}, u32[]{:S(2)}) %collective-permute-start.13) | collective-permute-done | bytes 1310752 | tf_op jit(solution)/shard_map/ppermute | solution.py:36
  118.4 13.5 %collective-permute-done.14.refs_4_ = bf16[5,2,64,1024]{3,2,1,0:T(8,128)(2,1)} collective-permute-done((bf16[5,2,64,1024]{3,2,1,0:T(8,128)(2,1)}, bf16[5,2,64,1024]{3,2,1,0:T(8,128)(2,1)}, u32[]{:S(2)}, u32[]{:S(2)}) %collective-permute-start.14) | collective-permute-done | bytes 1310752 | tf_op jit(solution)/shard_map/ppermute | solution.py:36
  157.4 11.8 %assemble.6 = (bf16[1024,3072]{1,0:T(8,128)(2,1)}, bf16[1024,1024]{1,0:T(8,128)(2,1)}, bf16[1024,4096]{1,0:T(8,128)(2,1)}, bf16[4096,1024]{1,0:T(8,128)(2,1)}, b...) custom-call(s32[28]{0:T(128)} %stack.76.info_ref, ...), custom_call_target="tpu_custom_call" | custom-call | bytes 42467328 | tf_op jit(solution)/shard_map/assemble/pallas_call | solution.py:182
  169.2 17.3 %collective-permute-done.18.refs_2_ = bf16[6,2,64,1024]{3,2,1,0:T(8,128)(2,1)} collective-permute-done((bf16[6,2,64,1024]{3,2,1,0:T(8,128)(2,1)}, bf16[6,2,64,1024]{3,2,1,0:T(8,128)(2,1)}, u32[]{:S(2)}, u32[]{:S(2)}) %collective-permute-start.18) | collective-permute-done | bytes 1572896 | tf_op jit(solution)/shard_map/ppermute | solution.py:36
  212.7 19.0 %collective-permute-done.1.refs_4_ = bf16[2,128,1024]{2,1,0:T(8,128)(2,1)S(1)} collective-permute-done((bf16[2,128,1024]{2,1,0:T(8,128)(2,1)S(1)}, bf16[2,128,1024]{2,1,0:T(8,128)(2,1)S(1)}, u32[]{:S(2)}, u32[]{:S(2)}) %collective-permute-start.1) | collective-permute-done | bytes 524320 | tf_op jit(solution)/shard_map/ppermute | solution.py:27
  277.5 14.1 %attention_forward.4 = (bf16[256,1024]{1,0:T(8,128)(2,1)}, bf16[256,1024]{1,0:T(8,128)(2,1)}, bf16[256,1024]{1,0:T(8,128)(2,1)}, bf16[256,1024]{1,0:T(8,128)(2,1...) custom-call(s32[2,2]{1,0:T(2,128)S(1)} %broadcast_select_fusion.10.facts_ref, ...), custom_call_target="tpu_custom_call" | custom-call | flops 2147483648 | bytes 13631488 | tf_op jit(solution)/shard_map/attention_forward/pallas_call | solution.py:620
  291.6 16.0 %feed_forward.4 = (bf16[256,4096]{1,0:T(8,128)(2,1)}, bf16[256,4096]{1,0:T(8,128)(2,1)}, bf16[256,128]{1,0:T(8,128)(2,1)}, bf16[256,128]{1,0:T(8,128)(2,1)}, f32[256,1024]{1,0:T(8,128)S(1)}, /*index=5*/f32[8,128]{1,0:T(8,128)}) custom-call(s32[2,2]{1,0:T(2,128)S(1)} %broadcast_select_fusion.10.facts_ref, f32[256,1024]{1,0:T(8,128)S(1)} %bitcast_convert_fusion.x_ref, ...), custom_call_target="tpu_custom_call" | custom-call | flops 4294967296 | bytes 24117248 | tf_op jit(solution)/shard_map/feed_forward/pallas_call | solution.py:704
  335.0 14.1 %attention_forward.5 = (bf16[256,1024]{1,0:T(8,128)(2,1)}, bf16[256,1024]{1,0:T(8,128)(2,1)}, bf16[256,1024]{1,0:T(8,128)(2,1)}, bf16[256,1024]{1,0:T(8,128)(2,1...) custom-call(s32[2,2]{1,0:T(2,128)S(1)} %broadcast_select_fusion.10.facts_ref, ...), custom_call_target="tpu_custom_call" | custom-call | flops 2147483648 | bytes 13631488 | tf_op jit(solution)/shard_map/attention_forward/pallas_call | solution.py:620
  349.0 15.9 %feed_forward.5 = (bf16[256,4096]{1,0:T(8,128)(2,1)}, bf16[256,4096]{1,0:T(8,128)(2,1)}, bf16[256,128]{1,0:T(8,128)(2,1)}, bf16[256,128]{1,0:T(8,128)(2,1)}, f32[256,1024]{1,0:T(8,128)S(1)}, /*index=5*/f32[8,128]{1,0:T(8,128)}) custom-call(s32[2,2]{1,0:T(2,128)S(1)} %broadcast_select_fusion.10.facts_ref, f32[256,1024]{1,0:T(8,128)S(1)} %get-tuple-element.205.refs_5_.x_ref, ...), custom_call_target="tpu_custom_call" | custom-call | flops 4294967296 | bytes 24117248 | tf_op jit(solution)/shard_map/feed_forward/pallas_call | solution.py:704
  366.7 23.3 %collective-permute-done.35 = bf16[256,1024]{1,0:T(8,128)(2,1)S(1)} collective-permute-done((bf16[256,1024]{1,0:T(8,128)(2,1)S(1)}, bf16[256,1024]{1,0:T(8,128)(2,1)S(1)}, u32[]{:S(2)}, u32[]{:S(2)}) %collective-permute-start.35) | collective-permute-done | bytes 524320 | tf_op jit(solution)/shard_map/ppermute | solution.py:1117
  391.0 13.7 %attention_forward.6 = (bf16[256,1024]{1,0:T(8,128)(2,1)S(1)}, bf16[256,1024]{1,0:T(8,128)(2,1)S(1)}, bf16[256,1024]{1,0:T(8,128)(2,1)S(1)}, bf16[256,1024]{1,0:...) custom-call(s32[2,2]{1,0:T(2,128)S(1)} %broadcast_select_fusion.10.facts_ref,, ...), custom_call_target="tpu_custom_call" | custom-call | flops 2147483648 | bytes 13631488 | tf_op jit(solution)/shard_map/attention_forward/pallas_call | solution.py:620
  404.8 15.6 %feed_forward.6 = (bf16[256,4096]{1,0:T(8,128)(2,1)S(1)}, bf16[256,4096]{1,0:T(8,128)(2,1)}, bf16[256,128]{1,0:T(8,128)(2,1)S(1)}, bf16[256,128]{1,0:T(8,128)(2,...) custom-call(s32[2,2]{1,0:T(2,128)S(1)} %broadcast_select_fusion.10.facts_ref, ...), custom_call_target="tpu_custom_call" | custom-call | flops 4294967296 | bytes 24117248 | tf_op jit(solution)/shard_map/feed_forward/pallas_call | solution.py:704
  420.4 14.0 %attention_forward.7 = (bf16[256,1024]{1,0:T(8,128)(2,1)S(1)}, bf16[256,1024]{1,0:T(8,128)(2,1)S(1)}, bf16[256,1024]{1,0:T(8,128)(2,1)S(1)}, bf16[256,1024]{1,0:...) custom-call(s32[2,2]{1,0:T(2,128)S(1)} %broadcast_select_fusion.10.facts_ref,, ...), custom_call_target="tpu_custom_call" | custom-call | flops 2147483648 | bytes 13631488 | tf_op jit(solution)/shard_map/attention_forward/pallas_call | solution.py:620
  434.4 15.7 %feed_forward.7 = (bf16[256,4096]{1,0:T(8,128)(2,1)S(1)}, bf16[256,4096]{1,0:T(8,128)(2,1)}, bf16[256,128]{1,0:T(8,128)(2,1)S(1)}, bf16[256,128]{1,0:T(8,128)(2,...) custom-call(s32[2,2]{1,0:T(2,128)S(1)} %broadcast_select_fusion.10.facts_ref, ...), custom_call_target="tpu_custom_call" | custom-call | flops 4294967296 | bytes 24117248 | tf_op jit(solution)/shard_map/feed_forward/pallas_call | solution.py:704
  451.1 16.5 %feed_backward.4 = (bf16[16,136,1024]{2,1,0:T(8,128)(2,1)}, f32[256,1024]{1,0:T(8,128)S(1)}) custom-call(s32[2,2]{1,0:T(2,128)S(1)} %broadcast_select_fusion.10.facts_ref, f32[256,1024]{1,0:T(8,128)S(1)} %bitcast.52, f32[256,1024]{1,0:T(8,128)S(1)} %get-tuple-element.230.x_ref, f32[4,1024]{1,0:T(4,128)S(1)} %get-tuple-element.331.norm_ref, ...), custom_call_target="tpu_custom_call" | custom-call | flops 4294967296 | bytes 25165824 | tf_op jit(solution)/shard_map/feed_backward/pallas_call | solution.py:800
  467.7 18.6 %attention_backward.4 = (bf16[16,136,1024]{2,1,0:T(8,128)(2,1)}, f32[256,1024]{1,0:T(8,128)S(1)}) custom-call(s32[2,2]{1,0:T(2,128)S(1)} %broadcast_select_fusion.10.facts_ref, f32[256,1024]{1,0:T(8,128)S(1)} %bitcast.53, f32[256,1024]{1,0:T(8,128)S(1)} %get-tuple-element.238.gx_ref, f32[256,1024]{1,0:T(8,128)} %copy-done.2, ...), custom_call_target="tpu_custom_call", output_to_operand_aliasing={{0}: (22, {})} | custom-call | flops 2147483648 | bytes 16777216 | tf_op jit(solution)/shard_map/attention_backward/pallas_call | solution.py:911
  491.4 16.4 %feed_backward.5 = (bf16[16,136,1024]{2,1,0:T(8,128)(2,1)}, f32[256,1024]{1,0:T(8,128)S(1)}) custom-call(s32[2,2]{1,0:T(2,128)S(1)} %broadcast_select_fusion.10.facts_ref, f32[256,1024]{1,0:T(8,128)S(1)} %get-tuple-element.246.g_ref, f32[256,1024]{1,0:T(8,128)S(1)} %convert_select_fusion.2.x_ref, f32[4,1024]{1,0:T(4,128)S(1)} %get-tuple-element.332.norm_ref, ...), custom_call_target="tpu_custom_call" | custom-call | flops 4294967296 | bytes 25165824 | tf_op jit(solution)/shard_map/feed_backward/pallas_call | solution.py:800
  507.9 18.2 %attention_backward.5 = (bf16[16,136,1024]{2,1,0:T(8,128)(2,1)}, f32[256,1024]{1,0:T(8,128)S(1)}) custom-call(s32[2,2]{1,0:T(2,128)S(1)} %broadcast_select_fusion.10.facts_ref, f32[256,1024]{1,0:T(8,128)S(1)} %get-tuple-element.246.g_ref, f32[256,1024]{1,0:T(8,128)S(1)} %get-tuple-element.252.gx_ref, ...), custom_call_target="tpu_custom_call", output_to_operand_aliasing={{0}: (22, {})} | custom-call | flops 2147483648 | bytes 16777216 | tf_op jit(solution)/shard_map/attention_backward/pallas_call | solution.py:911
  555.5 16.5 %feed_backward.6 = (bf16[16,136,1024]{2,1,0:T(8,128)(2,1)}, f32[256,1024]{1,0:T(8,128)S(1)}) custom-call(s32[2,2]{1,0:T(2,128)S(1)} %broadcast_select_fusion.10.facts_ref, f32[256,1024]{1,0:T(8,128)S(1)} %convert_select_fusion.1.g_ref, f32[256,1024]{1,0:T(8,128)S(1)} %copy-done.3, f32[4,1024]{1,0:T(4,128)S(1)} %get-tuple-element.331.norm_ref, ...), custom_call_target="tpu_custom_call" | custom-call | flops 4294967296 | bytes 25165824 | tf_op jit(solution)/shard_map/feed_backward/pallas_call | solution.py:800
  572.0 18.2 %attention_backward.6 = (bf16[16,136,1024]{2,1,0:T(8,128)(2,1)}, f32[256,1024]{1,0:T(8,128)S(1)}) custom-call(s32[2,2]{1,0:T(2,128)S(1)} %broadcast_select_fusion.10.facts_ref, f32[256,1024]{1,0:T(8,128)S(1)} %convert_select_fusion.1.g_ref, f32[256,1024]{1,0:T(8,128)S(1)} %get-tuple-element.261.gx_ref, ...), custom_call_target="tpu_custom_call", output_to_operand_aliasing={{0}: (22, {})} | custom-call | flops 2147483648 | bytes 16777216 | tf_op jit(solution)/shard_map/attention_backward/pallas_call | solution.py:911
  595.7 12.6 %all-to-all-done = bf16[8,272,1024]{2,1,0:T(8,128)(2,1)} async-done(((bf16[8,272,1024]{2,1,0:T(8,128)(2,1)}), bf16[8,272,1024]{2,1,0:T(8,128)(2,1)}, u32[]{:S(2)}, u32[]{:S(2)}) %all-to-all-start) | async-done | bytes 4456480 | tf_op jit(solution)/shard_map/all_to_all | solution.py:310
  622.1 29.6 %collective-permute-done.44 = bf16[272,1024]{1,0:T(8,128)(2,1)S(1)} collective-permute-done((bf16[272,1024]{1,0:T(8,128)(2,1)S(1)}, bf16[272,1024]{1,0:T(8,128)(2,1)S(1)}, u32[]{:S(2)}, u32[]{:S(2)}) %collective-permute-start.44) | collective-permute-done | bytes 557088 | tf_op jit(solution)/shard_map/ppermute | solution.py:336
  664.1 16.4 %feed_backward.7 = (bf16[16,136,1024]{2,1,0:T(8,128)(2,1)}, f32[256,1024]{1,0:T(8,128)S(1)}) custom-call(s32[2,2]{1,0:T(2,128)S(1)} %broadcast_select_fusion.10.facts_ref, f32[256,1024]{1,0:T(8,128)S(1)} %get-tuple-element.263.g_ref, f32[256,1024]{1,0:T(8,128)S(1)} %copy-done.1, f32[4,1024]{1,0:T(4,128)S(1)} %get-tuple-element.332.norm_ref, ...), custom_call_target="tpu_custom_call" | custom-call | flops 4294967296 | bytes 25165824 | tf_op jit(solution)/shard_map/feed_backward/pallas_call | solution.py:800
  680.6 18.2 %attention_backward.7 = (bf16[16,136,1024]{2,1,0:T(8,128)(2,1)}, f32[256,1024]{1,0:T(8,128)S(1)}) custom-call(s32[2,2]{1,0:T(2,128)S(1)} %broadcast_select_fusion.10.facts_ref, f32[256,1024]{1,0:T(8,128)S(1)} %get-tuple-element.263.g_ref, f32[256,1024]{1,0:T(8,128)S(1)} %get-tuple-element.264.gx_ref, ...), custom_call_target="tpu_custom_call", output_to_operand_aliasing={{0}: (22, {})} | custom-call | flops 2147483648 | bytes 16777216 | tf_op jit(solution)/shard_map/attention_backward/pallas_call | solution.py:911
  713.6 31.4 %all_to_all.25 = bf16[8,136,1024]{2,1,0:T(8,128)(2,1)S(1)} all-to-all(bf16[8,136,1024]{2,1,0:T(8,128)(2,1)} %add_convert_fusion.1), channel_id=1, replica_groups={{0,1,2,3,4,5,6,7},{8,9,10,11,12,13,14,15},{16,17,18,19,20,21,22,23},{24..., dimensions={0} | all-to-all | bytes 4456448 | tf_op jit(solution)/shard_map/all_to_all | solution.py:310
  746.8 29.1 %collective-permute-done.48 = bf16[272,1024]{1,0:T(8,128)(2,1)S(1)} collective-permute-done((bf16[272,1024]{1,0:T(8,128)(2,1)S(1)}, bf16[272,1024]{1,0:T(8,128)(2,1)S(1)}, u32[]{:S(2)}, u32[]{:S(2)}) %collective-permute-start.48) | collective-permute-done | bytes 557088 | tf_op jit(solution)/shard_map/ppermute | solution.py:336
  787.5 51.9 %all-to-all-done.4.early0_ref = bf16[8,272,1024]{2,1,0:T(8,128)(2,1)} async-done(((bf16[8,272,1024]{2,1,0:T(8,128)(2,1)}), bf16[8,272,1024]{2,1,0:T(8,128)(2,1)}, u32[]{:S(2)}, u32[]{:S(2)}) %all-to-all-start.4) | async-done | bytes 4456480 | tf_op jit(solution)/shard_map/all_to_all | solution.py:310
  853.8 10.5 %collective-permute-done.45 = bf16[256,1024]{1,0:T(8,128)(2,1)S(1)} collective-permute-done((bf16[256,1024]{1,0:T(8,128)(2,1)S(1)}, bf16[256,1024]{1,0:T(8,128)(2,1)S(1)}, u32[]{:S(2)}, u32[]{:S(2)}) %collective-permute-start.45) | collective-permute-done | bytes 524320 | tf_op jit(solution)/shard_map/ppermute | solution.py:27
  865.5 20.5 %finish.1 = (f32[2,1024,128]{2,1,0:T(8,128)}, f32[2,128,3072]{2,1,0:T(8,128)}, f32[2,1024,128]{2,1,0:T(8,128)}, f32[2,128,1024]{2,1,0:T(8,128)}, f32[2,1024,128]...) custom-call(s32[2]{0:T(128)} %pad_add_fusion.1.info_ref, ...), custom_call_target="tpu_custom_call" | custom-call | flops 536870912 | bytes 25165824 | tf_op jit(solution)/shard_map/finish/pallas_call | solution.py:424
  (331 shorter events, 283.5 us)
Async XLA Ops:
  20.1 62.0 %collective-permute-start.4 = (bf16[2,7168,128]{2,1,0:T(8,128)(2,1)}, bf16[2,7168,128]{2,1,0:T(8,128)(2,1)}, u32[]{:S(2)}, u32[]{:S(2)}) collective-permute-start(bf16[2,7168,128]{2,1,0:T(8,128)(2,1)} %get-tuple-element.155), channel_id=1, source_target_pairs={{0,16},{1,17},{2,18},{3,19},{4,20},{5,21},{6,22},{7,23},{24,8},{25... | collective-permute-start | bytes 11010056 | tf_op jit(solution)/shard_map/ppermute | solution.py:27
  39.4 42.7 %collective-permute-start.10 = (bf16[4,2,64,1024]{3,2,1,0:T(8,128)(2,1)S(1)}, bf16[4,2,64,1024]{3,2,1,0:T(8,128)(2,1)S(1)}, u32[]{:S(2)}, u32[]{:S(2)}) collective-permute-start(bf16[4,2,64,1024]{3,2,1,0:T(8,128)(2,1)S(1)} %get-tuple-element.161), channel_id=1, source_target_pairs={{0,4},{1,5},{2,6},{3,7},{4,0},{5,1},{6,2},{7,3},{8,12},{9,13},{10,... | collective-permute-start | bytes 3145736 | tf_op jit(solution)/shard_map/ppermute | solution.py:36
  41.0 41.0 %collective-permute-start.11 = (bf16[4,2,64,1024]{3,2,1,0:T(8,128)(2,1)S(1)}, bf16[4,2,64,1024]{3,2,1,0:T(8,128)(2,1)S(1)}, u32[]{:S(2)}, u32[]{:S(2)}) collective-permute-start(bf16[4,2,64,1024]{3,2,1,0:T(8,128)(2,1)S(1)} %get-tuple-element.162), channel_id=1, source_target_pairs={{0,1},{1,0},{2,3},{3,2},{4,5},{5,4},{6,7},{7,6},{8,9},{9,8},{10,11... | collective-permute-start | bytes 3145736 | tf_op jit(solution)/shard_map/ppermute | solution.py:36
  41.6 40.5 %collective-permute-start.12 = (bf16[4,2,64,1024]{3,2,1,0:T(8,128)(2,1)S(1)}, bf16[4,2,64,1024]{3,2,1,0:T(8,128)(2,1)S(1)}, u32[]{:S(2)}, u32[]{:S(2)}) collective-permute-start(bf16[4,2,64,1024]{3,2,1,0:T(8,128)(2,1)S(1)} %get-tuple-element.163), channel_id=1, source_target_pairs={{0,2},{1,3},{2,0},{3,1},{4,6},{5,7},{6,4},{7,5},{8,10},{9,11},{10,... | collective-permute-start | bytes 3145736 | tf_op jit(solution)/shard_map/ppermute | solution.py:36
  43.1 38.1 %collective-permute-start.5 = (bf16[6,64,1024]{2,1,0:T(8,128)(2,1)S(1)}, bf16[6,64,1024]{2,1,0:T(8,128)(2,1)S(1)}, u32[]{:S(2)}, u32[]{:S(2)}) collective-permute-start(bf16[6,64,1024]{2,1,0:T(8,128)(2,1)S(1)} %get-tuple-element.329), channel_id=1, source_target_pairs={{0,8},{1,9},{2,10},{3,11},{4,12},{5,13},{6,14},{7,15},{8,0},{9,1},... | collective-permute-start | bytes 2359304 | tf_op jit(solution)/shard_map/ppermute | solution.py:36
  87.2 44.7 %collective-permute-start.17 = (bf16[27,2,64,1024]{3,2,1,0:T(8,128)(2,1)}, bf16[27,2,64,1024]{3,2,1,0:T(8,128)(2,1)}, u32[]{:S(2)}, u32[]{:S(2)}) collective-permute-start(bf16[27,2,64,1024]{3,2,1,0:T(8,128)(2,1)} %get-tuple-element.168.mine), channel_id=1, source_target_pairs={{0,16},{16,0},{1,17},{17,1},{2,18},{18,2},{3,19},{19,3},{4,20},{20... | collective-permute-start | bytes 21233672 | tf_op jit(solution)/shard_map/ppermute | solution.py:40
  88.7 29.7 %collective-permute-start.13 = (bf16[5,2,64,1024]{3,2,1,0:T(8,128)(2,1)}, bf16[5,2,64,1024]{3,2,1,0:T(8,128)(2,1)}, u32[]{:S(2)}, u32[]{:S(2)}) collective-permute-start(bf16[5,2,64,1024]{3,2,1,0:T(8,128)(2,1)} %get-tuple-element.164), channel_id=1, source_target_pairs={{0,2},{1,3},{2,0},{3,1},{4,6},{5,7},{6,4},{7,5},{8,10},{9,11},{10,... | collective-permute-start | bytes 3932168 | tf_op jit(solution)/shard_map/ppermute | solution.py:36
  89.3 42.7 %collective-permute-start.14 = (bf16[5,2,64,1024]{3,2,1,0:T(8,128)(2,1)}, bf16[5,2,64,1024]{3,2,1,0:T(8,128)(2,1)}, u32[]{:S(2)}, u32[]{:S(2)}) collective-permute-start(bf16[5,2,64,1024]{3,2,1,0:T(8,128)(2,1)} %get-tuple-element.165), channel_id=1, source_target_pairs={{0,4},{1,5},{2,6},{3,7},{4,0},{5,1},{6,2},{7,3},{8,12},{9,13},{10,... | collective-permute-start | bytes 3932168 | tf_op jit(solution)/shard_map/ppermute | solution.py:36
  89.3 42.7 %collective-permute-start.15 = (bf16[5,2,64,1024]{3,2,1,0:T(8,128)(2,1)}, bf16[5,2,64,1024]{3,2,1,0:T(8,128)(2,1)}, u32[]{:S(2)}, u32[]{:S(2)}) collective-permute-start(bf16[5,2,64,1024]{3,2,1,0:T(8,128)(2,1)} %get-tuple-element.166), channel_id=1, source_target_pairs={{0,1},{1,0},{2,3},{3,2},{4,5},{5,4},{6,7},{7,6},{8,9},{9,8},{10,11... | collective-permute-start | bytes 3932168 | tf_op jit(solution)/shard_map/ppermute | solution.py:36
  105.7 63.5 %collective-permute-start.6 = (bf16[6,64,1024]{2,1,0:T(8,128)(2,1)}, bf16[6,64,1024]{2,1,0:T(8,128)(2,1)S(1)}, u32[]{:S(2)}, u32[]{:S(2)}) collective-permute-start(bf16[6,64,1024]{2,1,0:T(8,128)(2,1)} %get-tuple-element.157), channel_id=1, source_target_pairs={{0,8},{1,9},{2,10},{3,11},{4,12},{5,13},{6,14},{7,15},{8,0},{9,1},... | collective-permute-start | bytes 2359304 | tf_op jit(solution)/shard_map/ppermute | solution.py:36
  143.6 43.7 %collective-permute-start.21 = (bf16[15,2,64,1024]{3,2,1,0:T(8,128)(2,1)}, bf16[15,2,64,1024]{3,2,1,0:T(8,128)(2,1)}, u32[]{:S(2)}, u32[]{:S(2)}) collective-permute-start(bf16[15,2,64,1024]{3,2,1,0:T(8,128)(2,1)} %get-tuple-element.173.mine), channel_id=1, source_target_pairs={{0,16},{16,0},{1,17},{17,1},{2,18},{18,2},{3,19},{19,3},{4,20},{20... | collective-permute-start | bytes 11796488 | tf_op jit(solution)/shard_map/ppermute | solution.py:40
  149.9 36.6 %collective-permute-start.18 = (bf16[6,2,64,1024]{3,2,1,0:T(8,128)(2,1)}, bf16[6,2,64,1024]{3,2,1,0:T(8,128)(2,1)}, u32[]{:S(2)}, u32[]{:S(2)}) collective-permute-start(bf16[6,2,64,1024]{3,2,1,0:T(8,128)(2,1)} %get-tuple-element.169), channel_id=1, source_target_pairs={{0,4},{1,5},{2,6},{3,7},{4,0},{5,1},{6,2},{7,3},{8,12},{9,13},{10,... | collective-permute-start | bytes 4718600 | tf_op jit(solution)/shard_map/ppermute | solution.py:36
  149.9 36.6 %collective-permute-start.19 = (bf16[6,2,64,1024]{3,2,1,0:T(8,128)(2,1)}, bf16[6,2,64,1024]{3,2,1,0:T(8,128)(2,1)}, u32[]{:S(2)}, u32[]{:S(2)}) collective-permute-start(bf16[6,2,64,1024]{3,2,1,0:T(8,128)(2,1)} %get-tuple-element.170), channel_id=1, source_target_pairs={{0,1},{1,0},{2,3},{3,2},{4,5},{5,4},{6,7},{7,6},{8,9},{9,8},{10,11... | collective-permute-start | bytes 4718600 | tf_op jit(solution)/shard_map/ppermute | solution.py:36
  151.0 36.3 %collective-permute-start.20 = (bf16[6,2,64,1024]{3,2,1,0:T(8,128)(2,1)}, bf16[6,2,64,1024]{3,2,1,0:T(8,128)(2,1)}, u32[]{:S(2)}, u32[]{:S(2)}) collective-permute-start(bf16[6,2,64,1024]{3,2,1,0:T(8,128)(2,1)} %get-tuple-element.171), channel_id=1, source_target_pairs={{0,2},{1,3},{2,0},{3,1},{4,6},{5,7},{6,4},{7,5},{8,10},{9,11},{10,... | collective-permute-start | bytes 4718600 | tf_op jit(solution)/shard_map/ppermute | solution.py:36
  195.4 37.0 %collective-permute-start.25 = (bf16[21,2,64,1024]{3,2,1,0:T(8,128)(2,1)}, bf16[21,2,64,1024]{3,2,1,0:T(8,128)(2,1)}, u32[]{:S(2)}, u32[]{:S(2)}) collective-permute-start(bf16[21,2,64,1024]{3,2,1,0:T(8,128)(2,1)} %get-tuple-element.182.mine), channel_id=1, source_target_pairs={{0,16},{16,0},{1,17},{17,1},{2,18},{18,2},{3,19},{19,3},{4,20},{20... | collective-permute-start | bytes 16515080 | tf_op jit(solution)/shard_map/ppermute | solution.py:40
  195.4 37.0 %collective-permute-start.22 = (bf16[5,2,64,1024]{3,2,1,0:T(8,128)(2,1)}, bf16[5,2,64,1024]{3,2,1,0:T(8,128)(2,1)S(1)}, u32[]{:S(2)}, u32[]{:S(2)}) collective-permute-start(bf16[5,2,64,1024]{3,2,1,0:T(8,128)(2,1)} %get-tuple-element.174), channel_id=1, source_target_pairs={{0,4},{1,5},{2,6},{3,7},{4,0},{5,1},{6,2},{7,3},{8,12},{9,13},{10,... | collective-permute-start | bytes 3932168 | tf_op jit(solution)/shard_map/ppermute | solution.py:36
  197.1 35.3 %collective-permute-start.23 = (bf16[5,2,64,1024]{3,2,1,0:T(8,128)(2,1)}, bf16[5,2,64,1024]{3,2,1,0:T(8,128)(2,1)}, u32[]{:S(2)}, u32[]{:S(2)}) collective-permute-start(bf16[5,2,64,1024]{3,2,1,0:T(8,128)(2,1)} %get-tuple-element.175), channel_id=1, source_target_pairs={{0,1},{1,0},{2,3},{3,2},{4,5},{5,4},{6,7},{7,6},{8,9},{9,8},{10,11... | collective-permute-start | bytes 3932168 | tf_op jit(solution)/shard_map/ppermute | solution.py:36
  198.8 33.6 %collective-permute-start.24 = (bf16[5,2,64,1024]{3,2,1,0:T(8,128)(2,1)}, bf16[5,2,64,1024]{3,2,1,0:T(8,128)(2,1)}, u32[]{:S(2)}, u32[]{:S(2)}) collective-permute-start(bf16[5,2,64,1024]{3,2,1,0:T(8,128)(2,1)} %get-tuple-element.176), channel_id=1, source_target_pairs={{0,2},{1,3},{2,0},{3,1},{4,6},{5,7},{6,4},{7,5},{8,10},{9,11},{10,... | collective-permute-start | bytes 3932168 | tf_op jit(solution)/shard_map/ppermute | solution.py:36
  200.6 31.0 %collective-permute-start.1 = (bf16[2,128,1024]{2,1,0:T(8,128)(2,1)S(1)}, bf16[2,128,1024]{2,1,0:T(8,128)(2,1)S(1)}, u32[]{:S(2)}, u32[]{:S(2)}) collective-permute-start(bf16[2,128,1024]{2,1,0:T(8,128)(2,1)S(1)} %broadcast_select_fusion.7), channel_id=1, source_target_pairs={{16,8},{17,9},{18,10},{19,11},{20,12},{21,13},{22,14},{23,15},{8,1... | collective-permute-start | bytes 1572872 | tf_op jit(solution)/shard_map/ppermute | solution.py:27
  266.2 41.4 %collective-permute-start.33 = (bf16[6,2,64,1024]{3,2,1,0:T(8,128)(2,1)}, bf16[6,2,64,1024]{3,2,1,0:T(8,128)(2,1)}, u32[]{:S(2)}, u32[]{:S(2)}) collective-permute-start(bf16[6,2,64,1024]{3,2,1,0:T(8,128)(2,1)} %get-tuple-element.214.mine), channel_id=1, source_target_pairs={{0,16},{16,0},{1,17},{17,1},{2,18},{18,2},{3,19},{19,3},{4,20},{20... | collective-permute-start | bytes 4718600 | tf_op jit(solution)/shard_map/ppermute | solution.py:40
  267.4 40.2 %collective-permute-start.30 = (bf16[4,2,64,1024]{3,2,1,0:T(8,128)(2,1)}, bf16[4,2,64,1024]{3,2,1,0:T(8,128)(2,1)}, u32[]{:S(2)}, u32[]{:S(2)}) collective-permute-start(bf16[4,2,64,1024]{3,2,1,0:T(8,128)(2,1)} %get-tuple-element.210), channel_id=1, source_target_pairs={{0,1},{1,0},{2,3},{3,2},{4,5},{5,4},{6,7},{7,6},{8,9},{9,8},{10,11... | collective-permute-start | bytes 3145736 | tf_op jit(solution)/shard_map/ppermute | solution.py:36
  269.1 38.4 %collective-permute-start.31 = (bf16[4,2,64,1024]{3,2,1,0:T(8,128)(2,1)}, bf16[4,2,64,1024]{3,2,1,0:T(8,128)(2,1)}, u32[]{:S(2)}, u32[]{:S(2)}) collective-permute-start(bf16[4,2,64,1024]{3,2,1,0:T(8,128)(2,1)} %get-tuple-element.211), channel_id=1, source_target_pairs={{0,2},{1,3},{2,0},{3,1},{4,6},{5,7},{6,4},{7,5},{8,10},{9,11},{10,... | collective-permute-start | bytes 3145736 | tf_op jit(solution)/shard_map/ppermute | solution.py:36
  269.4 38.2 %collective-permute-start.32 = (bf16[4,2,64,1024]{3,2,1,0:T(8,128)(2,1)}, bf16[4,2,64,1024]{3,2,1,0:T(8,128)(2,1)}, u32[]{:S(2)}, u32[]{:S(2)}) collective-permute-start(bf16[4,2,64,1024]{3,2,1,0:T(8,128)(2,1)} %get-tuple-element.212), channel_id=1, source_target_pairs={{0,4},{1,5},{2,6},{3,7},{4,0},{5,1},{6,2},{7,3},{8,12},{9,13},{10,... | collective-permute-start | bytes 3145736 | tf_op jit(solution)/shard_map/ppermute | solution.py:36
  322.1 44.3 %collective-permute-start.39 = (f32[1,128]{1,0:T(1,128)S(1)}, f32[1,128]{1,0:T(1,128)S(1)}, u32[]{:S(2)}, u32[]{:S(2)}) collective-permute-start(f32[1,128]{1,0:T(1,128)S(1)} %add.116), channel_id=1, source_target_pairs={{0,8},{1,9},{2,10},{3,11},{4,12},{5,13},{6,14},{7,15},{8,0},{9,1},... | collective-permute-start | bytes 1544 | tf_op jit(solution)/shard_map/ppermute | solution.py:36
  489.5 44.5 %collective-permute-start.43 = (bf16[8,136,1024]{2,1,0:T(8,128)(2,1)}, bf16[8,136,1024]{2,1,0:T(8,128)(2,1)}, u32[]{:S(2)}, u32[]{:S(2)}) collective-permute-start(bf16[8,136,1024]{2,1,0:T(8,128)(2,1)} %constant_dynamic-slice_fusion.2), channel_id=1, source_target_pairs={{8,24},{9,25},{10,26},{11,27},{12,28},{13,29},{14,30},{15,31},{24,... | collective-permute-start | bytes 6684680 | tf_op jit(solution)/shard_map/ppermute | solution.py:27
  548.1 60.3 %all-to-all-start = ((bf16[8,272,1024]{2,1,0:T(8,128)(2,1)}), bf16[8,272,1024]{2,1,0:T(8,128)(2,1)}, u32[]{:S(2)}, u32[]{:S(2)}) async-start(bf16[8,272,1024]{2,1,0:T(8,128)(2,1)} %pad_maximum_fusion), calls=%async_computation | async-start | bytes 8912896 | tf_op jit(solution)/shard_map/all_to_all | solution.py:310
  611.6 40.1 %all-to-all-start.1 = ((bf16[8,136,1024]{2,1,0:T(8,128)(2,1)}), bf16[8,136,1024]{2,1,0:T(8,128)(2,1)}, u32[]{:S(2)}, u32[]{:S(2)}) async-start(bf16[8,136,1024]{2,1,0:T(8,128)(2,1)} %add_convert_fusion), calls=%async_computation.1 | async-start | bytes 4456448 | tf_op jit(solution)/shard_map/all_to_all | solution.py:310
  617.0 34.6 %collective-permute-start.44 = (bf16[272,1024]{1,0:T(8,128)(2,1)S(1)}, bf16[272,1024]{1,0:T(8,128)(2,1)S(1)}, u32[]{:S(2)}, u32[]{:S(2)}) collective-permute-start(bf16[272,1024]{1,0:T(8,128)(2,1)S(1)} %reduce_sum.46), channel_id=1, source_target_pairs={{8,0},{9,1},{10,2},{11,3},{12,4},{13,5},{14,6},{15,7},{24,16},{25,... | collective-permute-start | bytes 1671176 | tf_op jit(solution)/shard_map/ppermute | solution.py:336
  657.3 56.3 %all-to-all-start.2 = ((bf16[8,272,1024]{2,1,0:T(8,128)(2,1)}), bf16[8,272,1024]{2,1,0:T(8,128)(2,1)}, u32[]{:S(2)}, u32[]{:S(2)}) async-start(bf16[8,272,1024]{2,1,0:T(8,128)(2,1)} %broadcast_in_dim.82), calls=%async_computation.2 | async-start | bytes 8912896 | tf_op jit(solution)/shard_map/all_to_all | solution.py:310
  745.5 30.4 %collective-permute-start.48 = (bf16[272,1024]{1,0:T(8,128)(2,1)S(1)}, bf16[272,1024]{1,0:T(8,128)(2,1)S(1)}, u32[]{:S(2)}, u32[]{:S(2)}) collective-permute-start(bf16[272,1024]{1,0:T(8,128)(2,1)S(1)} %pad_maximum_fusion.1), channel_id=1, source_target_pairs={{0,8},{1,9},{2,10},{3,11},{4,12},{5,13},{6,14},{7,15},{16,24},{17,... | collective-permute-start | bytes 1671176 | tf_op jit(solution)/shard_map/ppermute | solution.py:336
  778.7 60.7 %all-to-all-start.4 = ((bf16[8,272,1024]{2,1,0:T(8,128)(2,1)}), bf16[8,272,1024]{2,1,0:T(8,128)(2,1)}, u32[]{:S(2)}, u32[]{:S(2)}) async-start(bf16[8,272,1024]{2,1,0:T(8,128)(2,1)} %broadcast_in_dim.83), calls=%async_computation.4 | async-start | bytes 8912896 | tf_op jit(solution)/shard_map/all_to_all | solution.py:310
  783.3 82.2 %collective-permute-start.50 = (bf16[8,272,1024]{2,1,0:T(8,128)(2,1)}, bf16[8,272,1024]{2,1,0:T(8,128)(2,1)}, u32[]{:S(2)}, u32[]{:S(2)}) collective-permute-start(bf16[8,272,1024]{2,1,0:T(8,128)(2,1)} %all-to-all-done.2.late1_ref), channel_id=1, source_target_pairs={{0,16},{1,17},{2,18},{3,19},{4,20},{5,21},{6,22},{7,23},{8,24},{9,... | collective-permute-start | bytes 13369352 | tf_op jit(solution)/shard_map/ppermute | solution.py:343
  (102 other events, 1899.3 us)

commit v5 on v4

--- a/solution.py
+++ b/solution.py
@@ -508,18 +508,22 @@
     return jnp.where(low, stacked[:rows], stacked[rows:])
 
 
-def pair_softmax(query_stack, key_pair, limit):
+def pair_mask(seq_len, limit):
+    row = lax.broadcasted_iota(jnp.int32, (2 * seq_len, seq_len), 0) % seq_len
+    column = lax.broadcasted_iota(jnp.int32, (2 * seq_len, seq_len), 1)
+    return (column <= row) & (column < limit)
+
+
+def pair_softmax(query_stack, key_pair, mask):
     scores = mm_nt(query_stack, key_pair) * HEAD_DIM ** (-0.5)
-    seq_len = key_pair.shape[0]
-    row = lax.broadcasted_iota(jnp.int32, scores.shape, 0) % seq_len
-    column = lax.broadcasted_iota(jnp.int32, scores.shape, 1)
-    scores = jnp.where((column <= row) & (column < limit), scores, masked_score)
+    scores = jnp.where(mask, scores, masked_score)
     grown = jnp.exp(scores - jnp.max(scores, axis=-1, keepdims=True))
-    return grown / jnp.sum(grown, axis=-1, keepdims=True)
-
-
-GROUP = 4 * HEAD_DIM
-BLOCK = 512
+    return grown * (1.0 / jnp.sum(grown, axis=-1, keepdims=True))
+
+
+GROUP = 8 * HEAD_DIM
+BLOCK = 1024
+PIECE = 256
 
 
 def attention_forward_kernel(
@@ -547,12 +551,15 @@
     key = mm(normed, wk_ref[...]) + adapter_scale * mm(mid, bk_ref[...])
     k_out[...] = half(turn(key, *tables))
     v_out[...] = half(mm(normed, wv_ref[...]) + adapter_scale * mm(mid, bv_ref[...]))
+    work = []
     for seq in range(seqs):
         rows = slice(seq * seq_len, (seq + 1) * seq_len)
+        mask = pair_mask(seq_len, facts_ref[0, seq])
         for pair in range(GROUP // (2 * HEAD_DIM)):
             lanes = slice(pair * 2 * HEAD_DIM, (pair + 1) * 2 * HEAD_DIM)
-            probability = pair_softmax(stack_heads(q_out[rows, lanes]), k_out[rows, lanes], facts_ref[0, seq])
-            mixed_out[rows, lanes] = half(merge_heads(mm(half(probability), v_out[rows, lanes])))
+            work.append((rows, lanes, pair_softmax(stack_heads(q_out[rows, lanes]), k_out[rows, lanes], mask)))
+    for rows, lanes, probability in work:
+        mixed_out[rows, lanes] = half(merge_heads(mm(half(probability), v_out[rows, lanes])))
     mixed = mixed_out[...]
     att_out[...] += mm(mixed, wo_ref[...])
     mid_scr[...] += mm(mixed, ao_ref[...])
@@ -664,14 +671,17 @@
         x_out[...] = jnp.zeros_like(x_out)
         mid_scr[...] = jnp.zeros_like(mid_scr)
 
-    upper = mm(a_scr[...], wu_ref[...]) + adapter_scale * mm(midu_out[...], bu_ref[...])
-    spread = 0.5 + 0.5 * lax.erf(upper * 0.5**0.5)
-    density = jnp.exp(-0.5 * upper * upper) * (0.5 / jnp.pi) ** 0.5
-    act_out[...] = half(upper * spread)
-    slope_out[...] = half(spread + upper * density)
-    active = act_out[...]
-    x_out[...] += mm(active, wd_ref[...])
-    mid_scr[...] += mm(active, ad_ref[...])
+    normed, mid = a_scr[...], midu_out[...]
+    parts = [slice(begin, begin + PIECE) for begin in range(0, act_out.shape[1], PIECE)]
+    uppers = [mm(normed, wu_ref[:, part]) + adapter_scale * mm(mid, bu_ref[:, part]) for part in parts]
+    for upper, part in zip(uppers, parts):
+        spread = 0.5 + 0.5 * lax.erf(upper * 0.5**0.5)
+        density = jnp.exp(-0.5 * upper * upper) * (0.5 / jnp.pi) ** 0.5
+        active = half(upper * spread)
+        act_out[:, part] = active
+        slope_out[:, part] = half(spread + upper * density)
+        x_out[...] += mm(active, wd_ref[part])
+        mid_scr[...] += mm(active, ad_ref[part])
 
     @pl.when(step == pl.num_programs(0) - 1)
     def _():
@@ -863,20 +873,23 @@
     grad_mixed = half(mm_nt(g_scr[...], wo_ref[...]) + mm_nt(gmo_scr[...], ao_ref[...]))
     first_at = pl.multiple_of(width + step * GROUP, GROUP)
     block_out[:RANK, pl.ds(first_at, GROUP)] = half(mm(gmot_scr[...], mixed_ref[...]))
+    work = []
     for seq in range(seqs):
         rows = slice(seq * seq_len, (seq + 1) * seq_len)
+        mask = pair_mask(seq_len, facts_ref[0, seq])
         for pair in range(GROUP // (2 * HEAD_DIM)):
             lanes = slice(pair * 2 * HEAD_DIM, (pair + 1) * 2 * HEAD_DIM)
             query_stack = stack_heads(q_ref[rows, lanes])
-            key_pair = k_ref[rows, lanes]
-            probability = pair_softmax(query_stack, key_pair, facts_ref[0, seq])
             grad_stack = stack_heads(grad_mixed[rows, lanes])
+            probability = pair_softmax(query_stack, k_ref[rows, lanes], mask)
             grad_prob = mm_nt(grad_stack, v_ref[rows, lanes])
-            gv_scr[rows, lanes] = half(mm_tn(half(probability), grad_stack))
             inner = jnp.sum(probability * grad_prob, axis=-1, keepdims=True)
             grad_scores = half(probability * (grad_prob - inner))
-            gq_scr[rows, lanes] = merge_heads(mm(grad_scores, key_pair)) * scale_factor
-            gk_scr[rows, lanes] = mm_tn(grad_scores, query_stack) * scale_factor
+            work.append((rows, lanes, query_stack, grad_stack, half(probability), grad_scores))
+    for rows, lanes, query_stack, grad_stack, probability, grad_scores in work:
+        gv_scr[rows, lanes] = half(mm_tn(probability, grad_stack))
+        gq_scr[rows, lanes] = merge_heads(mm(grad_scores, k_ref[rows, lanes])) * scale_factor
+        gk_scr[rows, lanes] = mm_tn(grad_scores, query_stack) * scale_factor
     tables = [tile_table(table_ref[index], seqs, GROUP) for index in range(3)]
     joint = (half(turn_back(gq_scr[...], *tables)), half(turn_back(gk_scr[...], *tables)), gv_scr[...])
     mid = midqt_scr[...]

time: 899 us -> 858 us (0.954)
  Pallas kernels: 361 us -> 308 us
  waiting for transfers between devices: 309 us -> 322 us
    pallas_call x4, Pallas kernels: 73.1 us -> 54 us  [attention_backward(): kernel_call(attention_backward_kernel, 'attention_backward', groups, [who...]
    pallas_call x4, Pallas kernels: 55.8 us -> 39 us  [attention_forward(): kernel_call(attention_forward_kernel, 'attention_forward', groups, [whole...]
    all_to_all x4, waiting for transfers between devices: 72.9 us -> 86.3 us  [exchange(): return lax.all_to_all(value, 'dp', 0, 0, axis_index_groups=groups)]
    pallas_call x4, Pallas kernels: 63.2 us -> 53 us  [feed_forward(): kernel_call(feed_forward_kernel, 'feed_forward', hidden // BLOCK, [whole(...]
  transfers between devices with their start and end apart: 55 -> 55, of which waited for: 25 -> 25; matrix products, arithmetic and copies ran while one was open for 4% -> 5% of each run, Pallas kernels for 25% -> 22%
where the time goes in v5:
time: 858 us; the launch traced here: 848 us
  waiting for transfers between devices  322 us (38%)
  Pallas kernels  308 us (36%)
  starting transfers between devices  97.1 us (11%)
  local copies, waits for them, and re-layouts  49.7 us (6%)
  other arithmetic  37 us (4%)
  blocking collectives  31.2 us (4%)
    ppermute x27, waiting for transfers between devices, flip_place(): lax.ppermute(value, 'dp', [(place, place ^ mask) for place in range(count)])  97.9 us
    all_to_all x4, waiting for transfers between devices, exchange(): return lax.all_to_all(value, 'dp', 0, 0, axis_index_groups=groups)  86.3 us
    pallas_call x4, Pallas kernels, feed_backward(): kernel_call(feed_backward_kernel, 'feed_backward', hidden // BLOCK, [whol...  58.5 us
    ppermute x2, waiting for transfers between devices, cross_section(): return jnp.where(stage == section, piece, lax.ppermute(piece, 'dp', across))  58.2 us
    pallas_call x4, Pallas kernels, attention_backward(): kernel_call(attention_backward_kernel, 'attention_backward', groups, [who...  54 us
    pallas_call x4, Pallas kernels, feed_forward(): kernel_call(feed_forward_kernel, 'feed_forward', hidden // BLOCK, [whole(...  53 us
    pallas_call x6, Pallas kernels, assemble(): pl.pallas_call(partial(assemble_kernel, tuple(layout)), out_shape=[jax.Sh...  48.1 us
    ppermute x11, waiting for transfers between devices, both_axes(): return lax.ppermute(value, ('section', 'dp'), pairs)  47.2 us
  transfers between devices with their start and end apart: 55, of which 25 were waited for; matrix products, arithmetic and copies ran while one was open for 5% of the time, Pallas kernels for 22%

profile of v5, /device:TPU:26, one launch (start us, length us, event | category | flops | bytes accessed | tf_op | source)
XLA Modules:
  0.0 847.5 jit_solution(10220414353874830228)
XLA Ops:
  26.4 10.3 %collective-permute-done.7.refs_4_.refs_1_ = bf16[2,2,64,1024]{3,2,1,0:T(8,128)(2,1)S(1)} collective-permute-done((bf16[2,2,64,1024]{3,2,1,0:T(8,128)(2,1)S(1)}, bf16[2,2,64,1024]{3,2,1,0:T(8,128)(2,1)S(1)}, u32[]{:S(2)}, u32[]{:S(2)}) %collective-permute-start.7) | collective-permute-done | bytes 524320 | tf_op jit(solution)/shard_map/ppermute | solution.py:36
  44.0 37.1 %collective-permute-done.5 = bf16[6,64,1024]{2,1,0:T(8,128)(2,1)S(1)} collective-permute-done((bf16[6,64,1024]{2,1,0:T(8,128)(2,1)S(1)}, bf16[6,64,1024]{2,1,0:T(8,128)(2,1)S(1)}, u32[]{:S(2)}, u32[]{:S(2)}) %collective-permute-start.5) | collective-permute-done | bytes 786464 | tf_op jit(solution)/shard_map/ppermute | solution.py:36
  91.0 14.7 %collective-permute-done.16.refs_11_ = bf16[2,128,9216]{2,1,0:T(8,128)(2,1)} collective-permute-done((bf16[2,128,9216]{2,1,0:T(8,128)(2,1)}, bf16[2,128,9216]{2,1,0:T(8,128)(2,1)}, u32[]{:S(2)}, u32[]{:S(2)}) %collective-permute-start.16) | collective-permute-done | bytes 4718624 | tf_op jit(solution)/shard_map/ppermute | solution.py:27
  107.9 10.5 %collective-permute-done.13.refs_10_.refs_1_ = bf16[5,2,64,1024]{3,2,1,0:T(8,128)(2,1)} collective-permute-done((bf16[5,2,64,1024]{3,2,1,0:T(8,128)(2,1)}, bf16[5,2,64,1024]{3,2,1,0:T(8,128)(2,1)}, u32[]{:S(2)}, u32[]{:S(2)}) %collective-permute-start.13) | collective-permute-done | bytes 1310752 | tf_op jit(solution)/shard_map/ppermute | solution.py:36
  118.4 13.5 %collective-permute-done.14.refs_4_ = bf16[5,2,64,1024]{3,2,1,0:T(8,128)(2,1)} collective-permute-done((bf16[5,2,64,1024]{3,2,1,0:T(8,128)(2,1)}, bf16[5,2,64,1024]{3,2,1,0:T(8,128)(2,1)}, u32[]{:S(2)}, u32[]{:S(2)}) %collective-permute-start.14) | collective-permute-done | bytes 1310752 | tf_op jit(solution)/shard_map/ppermute | solution.py:36
  157.4 11.8 %assemble.6 = (bf16[1024,3072]{1,0:T(8,128)(2,1)}, bf16[1024,1024]{1,0:T(8,128)(2,1)}, bf16[1024,4096]{1,0:T(8,128)(2,1)}, bf16[4096,1024]{1,0:T(8,128)(2,1)}, b...) custom-call(s32[28]{0:T(128)} %stack.76.info_ref, ...), custom_call_target="tpu_custom_call" | custom-call | bytes 42467328 | tf_op jit(solution)/shard_map/assemble/pallas_call | solution.py:182
  169.2 17.3 %collective-permute-done.18.refs_2_ = bf16[6,2,64,1024]{3,2,1,0:T(8,128)(2,1)} collective-permute-done((bf16[6,2,64,1024]{3,2,1,0:T(8,128)(2,1)}, bf16[6,2,64,1024]{3,2,1,0:T(8,128)(2,1)}, u32[]{:S(2)}, u32[]{:S(2)}) %collective-permute-start.18) | collective-permute-done | bytes 1572896 | tf_op jit(solution)/shard_map/ppermute | solution.py:36
  212.7 19.0 %collective-permute-done.1.refs_4_ = bf16[2,128,1024]{2,1,0:T(8,128)(2,1)S(1)} collective-permute-done((bf16[2,128,1024]{2,1,0:T(8,128)(2,1)S(1)}, bf16[2,128,1024]{2,1,0:T(8,128)(2,1)S(1)}, u32[]{:S(2)}, u32[]{:S(2)}) %collective-permute-start.1) | collective-permute-done | bytes 524320 | tf_op jit(solution)/shard_map/ppermute | solution.py:27
  251.5 9.7 %assemble.8 = (bf16[1024,3072]{1,0:T(8,128)(2,1)}, bf16[1024,1024]{1,0:T(8,128)(2,1)}, bf16[1024,4096]{1,0:T(8,128)(2,1)}, bf16[4096,1024]{1,0:T(8,128)(2,1)}, b...) custom-call(s32[22]{0:T(128)} %stack.79.info_ref, ...), custom_call_target="tpu_custom_call", output_to_operand_aliasing={{0}: (3, {}), {1}: (4, {}), {2}: (5, {}), {3}: (6, {}), {4}... | custom-call | bytes 33030144 | tf_op jit(solution)/shard_map/assemble/pallas_call | solution.py:182
  277.7 10.0 %attention_forward.4 = (bf16[256,1024]{1,0:T(8,128)(2,1)}, bf16[256,1024]{1,0:T(8,128)(2,1)}, bf16[256,1024]{1,0:T(8,128)(2,1)}, bf16[256,1024]{1,0:T(8,128)(2,1...) custom-call(s32[2,2]{1,0:T(2,128)S(1)} %broadcast_select_fusion.10.facts_ref, ...), custom_call_target="tpu_custom_call" | custom-call | flops 2147483648 | bytes 13631488 | tf_op jit(solution)/shard_map/attention_forward/pallas_call | solution.py:627
  287.7 13.5 %feed_forward.4 = (bf16[256,4096]{1,0:T(8,128)(2,1)}, bf16[256,4096]{1,0:T(8,128)(2,1)}, bf16[256,128]{1,0:T(8,128)(2,1)}, bf16[256,128]{1,0:T(8,128)(2,1)}, f32[256,1024]{1,0:T(8,128)S(1)}, /*index=5*/f32[8,128]{1,0:T(8,128)}) custom-call(s32[2,2]{1,0:T(2,128)S(1)} %broadcast_select_fusion.10.facts_ref, f32[256,1024]{1,0:T(8,128)S(1)} %bitcast_convert_fusion.x_ref, ...), custom_call_target="tpu_custom_call" | custom-call | flops 4294967296 | bytes 24117248 | tf_op jit(solution)/shard_map/feed_forward/pallas_call | solution.py:714
  328.5 10.0 %attention_forward.5 = (bf16[256,1024]{1,0:T(8,128)(2,1)}, bf16[256,1024]{1,0:T(8,128)(2,1)}, bf16[256,1024]{1,0:T(8,128)(2,1)}, bf16[256,1024]{1,0:T(8,128)(2,1...) custom-call(s32[2,2]{1,0:T(2,128)S(1)} %broadcast_select_fusion.10.facts_ref, ...), custom_call_target="tpu_custom_call" | custom-call | flops 2147483648 | bytes 13631488 | tf_op jit(solution)/shard_map/attention_forward/pallas_call | solution.py:627
  338.5 13.4 %feed_forward.5 = (bf16[256,4096]{1,0:T(8,128)(2,1)}, bf16[256,4096]{1,0:T(8,128)(2,1)}, bf16[256,128]{1,0:T(8,128)(2,1)}, bf16[256,128]{1,0:T(8,128)(2,1)}, f32[256,1024]{1,0:T(8,128)S(1)}, /*index=5*/f32[8,128]{1,0:T(8,128)}) custom-call(s32[2,2]{1,0:T(2,128)S(1)} %broadcast_select_fusion.10.facts_ref, f32[256,1024]{1,0:T(8,128)S(1)} %get-tuple-element.205.refs_5_.x_ref, ...), custom_call_target="tpu_custom_call" | custom-call | flops 4294967296 | bytes 24117248 | tf_op jit(solution)/shard_map/feed_forward/pallas_call | solution.py:714
  353.6 23.3 %collective-permute-done.35 = bf16[256,1024]{1,0:T(8,128)(2,1)S(1)} collective-permute-done((bf16[256,1024]{1,0:T(8,128)(2,1)S(1)}, bf16[256,1024]{1,0:T(8,128)(2,1)S(1)}, u32[]{:S(2)}, u32[]{:S(2)}) %collective-permute-start.35) | collective-permute-done | bytes 524320 | tf_op jit(solution)/shard_map/ppermute | solution.py:1130
  387.3 13.0 %feed_forward.6 = (bf16[256,4096]{1,0:T(8,128)(2,1)S(1)}, bf16[256,4096]{1,0:T(8,128)(2,1)}, bf16[256,128]{1,0:T(8,128)(2,1)S(1)}, bf16[256,128]{1,0:T(8,128)(2,...) custom-call(s32[2,2]{1,0:T(2,128)S(1)} %broadcast_select_fusion.10.facts_ref, ...), custom_call_target="tpu_custom_call" | custom-call | flops 4294967296 | bytes 24117248 | tf_op jit(solution)/shard_map/feed_forward/pallas_call | solution.py:714
  410.1 13.1 %feed_forward.7 = (bf16[256,4096]{1,0:T(8,128)(2,1)S(1)}, bf16[256,4096]{1,0:T(8,128)(2,1)}, bf16[256,128]{1,0:T(8,128)(2,1)S(1)}, bf16[256,128]{1,0:T(8,128)(2,...) custom-call(s32[2,2]{1,0:T(2,128)S(1)} %broadcast_select_fusion.10.facts_ref, ...), custom_call_target="tpu_custom_call" | custom-call | flops 4294967296 | bytes 24117248 | tf_op jit(solution)/shard_map/feed_forward/pallas_call | solution.py:714
  424.2 14.7 %feed_backward.4 = (bf16[16,136,1024]{2,1,0:T(8,128)(2,1)}, f32[256,1024]{1,0:T(8,128)S(1)}) custom-call(s32[2,2]{1,0:T(2,128)S(1)} %broadcast_select_fusion.10.facts_ref, f32[256,1024]{1,0:T(8,128)S(1)} %bitcast.52, f32[256,1024]{1,0:T(8,128)S(1)} %get-tuple-element.230.x_ref, f32[4,1024]{1,0:T(4,128)S(1)} %get-tuple-element.331.norm_ref, ...), custom_call_target="tpu_custom_call" | custom-call | flops 4294967296 | bytes 25165824 | tf_op jit(solution)/shard_map/feed_backward/pallas_call | solution.py:810
  438.9 13.5 %attention_backward.4 = (bf16[16,136,1024]{2,1,0:T(8,128)(2,1)}, f32[256,1024]{1,0:T(8,128)S(1)}) custom-call(s32[2,2]{1,0:T(2,128)S(1)} %broadcast_select_fusion.10.facts_ref, f32[256,1024]{1,0:T(8,128)S(1)} %bitcast.53, f32[256,1024]{1,0:T(8,128)S(1)} %get-tuple-element.238.gx_ref, f32[256,1024]{1,0:T(8,128)} %copy-done.2, ...), custom_call_target="tpu_custom_call", output_to_operand_aliasing={{0}: (22, {})} | custom-call | flops 2147483648 | bytes 16777216 | tf_op jit(solution)/shard_map/attention_backward/pallas_call | solution.py:924
  457.6 14.9 %feed_backward.5 = (bf16[16,136,1024]{2,1,0:T(8,128)(2,1)}, f32[256,1024]{1,0:T(8,128)S(1)}) custom-call(s32[2,2]{1,0:T(2,128)S(1)} %broadcast_select_fusion.10.facts_ref, f32[256,1024]{1,0:T(8,128)S(1)} %get-tuple-element.246.g_ref, f32[256,1024]{1,0:T(8,128)S(1)} %convert_select_fusion.2.x_ref, f32[4,1024]{1,0:T(4,128)S(1)} %get-tuple-element.332.norm_ref, ...), custom_call_target="tpu_custom_call" | custom-call | flops 4294967296 | bytes 25165824 | tf_op jit(solution)/shard_map/feed_backward/pallas_call | solution.py:810
  472.5 13.5 %attention_backward.5 = (bf16[16,136,1024]{2,1,0:T(8,128)(2,1)}, f32[256,1024]{1,0:T(8,128)S(1)}) custom-call(s32[2,2]{1,0:T(2,128)S(1)} %broadcast_select_fusion.10.facts_ref, f32[256,1024]{1,0:T(8,128)S(1)} %get-tuple-element.246.g_ref, f32[256,1024]{1,0:T(8,128)S(1)} %get-tuple-element.252.gx_ref, ...), custom_call_target="tpu_custom_call", output_to_operand_aliasing={{0}: (22, {})} | custom-call | flops 2147483648 | bytes 16777216 | tf_op jit(solution)/shard_map/attention_backward/pallas_call | solution.py:924
  515.7 14.5 %feed_backward.6 = (bf16[16,136,1024]{2,1,0:T(8,128)(2,1)}, f32[256,1024]{1,0:T(8,128)S(1)}) custom-call(s32[2,2]{1,0:T(2,128)S(1)} %broadcast_select_fusion.10.facts_ref, f32[256,1024]{1,0:T(8,128)S(1)} %convert_select_fusion.1.g_ref, f32[256,1024]{1,0:T(8,128)S(1)} %copy-done.3, f32[4,1024]{1,0:T(4,128)S(1)} %get-tuple-element.331.norm_ref, ...), custom_call_target="tpu_custom_call" | custom-call | flops 4294967296 | bytes 25165824 | tf_op jit(solution)/shard_map/feed_backward/pallas_call | solution.py:810
  530.2 13.5 %attention_backward.6 = (bf16[16,136,1024]{2,1,0:T(8,128)(2,1)}, f32[256,1024]{1,0:T(8,128)S(1)}) custom-call(s32[2,2]{1,0:T(2,128)S(1)} %broadcast_select_fusion.10.facts_ref, f32[256,1024]{1,0:T(8,128)S(1)} %convert_select_fusion.1.g_ref, f32[256,1024]{1,0:T(8,128)S(1)} %get-tuple-element.261.gx_ref, ...), custom_call_target="tpu_custom_call", output_to_operand_aliasing={{0}: (22, {})} | custom-call | flops 2147483648 | bytes 16777216 | tf_op jit(solution)/shard_map/attention_backward/pallas_call | solution.py:924
  549.0 19.4 %all-to-all-done = bf16[8,272,1024]{2,1,0:T(8,128)(2,1)} async-done(((bf16[8,272,1024]{2,1,0:T(8,128)(2,1)}), bf16[8,272,1024]{2,1,0:T(8,128)(2,1)}, u32[]{:S(2)}, u32[]{:S(2)}) %all-to-all-start) | async-done | bytes 4456480 | tf_op jit(solution)/shard_map/all_to_all | solution.py:310
  582.4 29.3 %collective-permute-done.44 = bf16[272,1024]{1,0:T(8,128)(2,1)S(1)} collective-permute-done((bf16[272,1024]{1,0:T(8,128)(2,1)S(1)}, bf16[272,1024]{1,0:T(8,128)(2,1)S(1)}, u32[]{:S(2)}, u32[]{:S(2)}) %collective-permute-start.44) | collective-permute-done | bytes 557088 | tf_op jit(solution)/shard_map/ppermute | solution.py:336
  624.2 14.5 %feed_backward.7 = (bf16[16,136,1024]{2,1,0:T(8,128)(2,1)}, f32[256,1024]{1,0:T(8,128)S(1)}) custom-call(s32[2,2]{1,0:T(2,128)S(1)} %broadcast_select_fusion.10.facts_ref, f32[256,1024]{1,0:T(8,128)S(1)} %get-tuple-element.263.g_ref, f32[256,1024]{1,0:T(8,128)S(1)} %copy-done.1, f32[4,1024]{1,0:T(4,128)S(1)} %get-tuple-element.332.norm_ref, ...), custom_call_target="tpu_custom_call" | custom-call | flops 4294967296 | bytes 25165824 | tf_op jit(solution)/shard_map/feed_backward/pallas_call | solution.py:810
  638.8 13.5 %attention_backward.7 = (bf16[16,136,1024]{2,1,0:T(8,128)(2,1)}, f32[256,1024]{1,0:T(8,128)S(1)}) custom-call(s32[2,2]{1,0:T(2,128)S(1)} %broadcast_select_fusion.10.facts_ref, f32[256,1024]{1,0:T(8,128)S(1)} %get-tuple-element.263.g_ref, f32[256,1024]{1,0:T(8,128)S(1)} %get-tuple-element.264.gx_ref, ...), custom_call_target="tpu_custom_call", output_to_operand_aliasing={{0}: (22, {})} | custom-call | flops 2147483648 | bytes 16777216 | tf_op jit(solution)/shard_map/attention_backward/pallas_call | solution.py:924
  658.6 15.0 %all-to-all-done.2.late1_ref = bf16[8,272,1024]{2,1,0:T(8,128)(2,1)} async-done(((bf16[8,272,1024]{2,1,0:T(8,128)(2,1)}), bf16[8,272,1024]{2,1,0:T(8,128)(2,1)}, u32[]{:S(2)}, u32[]{:S(2)}) %all-to-all-start.2) | async-done | bytes 4456480 | tf_op jit(solution)/shard_map/all_to_all | solution.py:310
  673.6 31.2 %all_to_all.25 = bf16[8,136,1024]{2,1,0:T(8,128)(2,1)S(1)} all-to-all(bf16[8,136,1024]{2,1,0:T(8,128)(2,1)} %add_convert_fusion.1), channel_id=1, replica_groups={{0,1,2,3,4,5,6,7},{8,9,10,11,12,13,14,15},{16,17,18,19,20,21,22,23},{24..., dimensions={0} | all-to-all | bytes 4456448 | tf_op jit(solution)/shard_map/all_to_all | solution.py:310
  706.8 28.9 %collective-permute-done.48 = bf16[272,1024]{1,0:T(8,128)(2,1)S(1)} collective-permute-done((bf16[272,1024]{1,0:T(8,128)(2,1)S(1)}, bf16[272,1024]{1,0:T(8,128)(2,1)S(1)}, u32[]{:S(2)}, u32[]{:S(2)}) %collective-permute-start.48) | collective-permute-done | bytes 557088 | tf_op jit(solution)/shard_map/ppermute | solution.py:336
  747.3 51.9 %all-to-all-done.4.early0_ref = bf16[8,272,1024]{2,1,0:T(8,128)(2,1)} async-done(((bf16[8,272,1024]{2,1,0:T(8,128)(2,1)}), bf16[8,272,1024]{2,1,0:T(8,128)(2,1)}, u32[]{:S(2)}, u32[]{:S(2)}) %all-to-all-start.4) | async-done | bytes 4456480 | tf_op jit(solution)/shard_map/all_to_all | solution.py:310
  813.6 10.5 %collective-permute-done.45 = bf16[256,1024]{1,0:T(8,128)(2,1)S(1)} collective-permute-done((bf16[256,1024]{1,0:T(8,128)(2,1)S(1)}, bf16[256,1024]{1,0:T(8,128)(2,1)S(1)}, u32[]{:S(2)}, u32[]{:S(2)}) %collective-permute-start.45) | collective-permute-done | bytes 524320 | tf_op jit(solution)/shard_map/ppermute | solution.py:27
  825.4 20.5 %finish.1 = (f32[2,1024,128]{2,1,0:T(8,128)}, f32[2,128,3072]{2,1,0:T(8,128)}, f32[2,1024,128]{2,1,0:T(8,128)}, f32[2,128,1024]{2,1,0:T(8,128)}, f32[2,1024,128]...) custom-call(s32[2]{0:T(128)} %pad_add_fusion.1.info_ref, ...), custom_call_target="tpu_custom_call" | custom-call | flops 536870912 | bytes 25165824 | tf_op jit(solution)/shard_map/finish/pallas_call | solution.py:424
  (331 shorter events, 285.0 us)
Async XLA Ops:
  20.1 62.0 %collective-permute-start.4 = (bf16[2,7168,128]{2,1,0:T(8,128)(2,1)}, bf16[2,7168,128]{2,1,0:T(8,128)(2,1)}, u32[]{:S(2)}, u32[]{:S(2)}) collective-permute-start(bf16[2,7168,128]{2,1,0:T(8,128)(2,1)} %get-tuple-element.155), channel_id=1, source_target_pairs={{0,16},{1,17},{2,18},{3,19},{4,20},{5,21},{6,22},{7,23},{24,8},{25... | collective-permute-start | bytes 11010056 | tf_op jit(solution)/shard_map/ppermute | solution.py:27
  39.4 42.7 %collective-permute-start.10 = (bf16[4,2,64,1024]{3,2,1,0:T(8,128)(2,1)S(1)}, bf16[4,2,64,1024]{3,2,1,0:T(8,128)(2,1)S(1)}, u32[]{:S(2)}, u32[]{:S(2)}) collective-permute-start(bf16[4,2,64,1024]{3,2,1,0:T(8,128)(2,1)S(1)} %get-tuple-element.161), channel_id=1, source_target_pairs={{0,4},{1,5},{2,6},{3,7},{4,0},{5,1},{6,2},{7,3},{8,12},{9,13},{10,... | collective-permute-start | bytes 3145736 | tf_op jit(solution)/shard_map/ppermute | solution.py:36
  41.0 41.0 %collective-permute-start.11 = (bf16[4,2,64,1024]{3,2,1,0:T(8,128)(2,1)S(1)}, bf16[4,2,64,1024]{3,2,1,0:T(8,128)(2,1)S(1)}, u32[]{:S(2)}, u32[]{:S(2)}) collective-permute-start(bf16[4,2,64,1024]{3,2,1,0:T(8,128)(2,1)S(1)} %get-tuple-element.162), channel_id=1, source_target_pairs={{0,1},{1,0},{2,3},{3,2},{4,5},{5,4},{6,7},{7,6},{8,9},{9,8},{10,11... | collective-permute-start | bytes 3145736 | tf_op jit(solution)/shard_map/ppermute | solution.py:36
  41.6 40.5 %collective-permute-start.12 = (bf16[4,2,64,1024]{3,2,1,0:T(8,128)(2,1)S(1)}, bf16[4,2,64,1024]{3,2,1,0:T(8,128)(2,1)S(1)}, u32[]{:S(2)}, u32[]{:S(2)}) collective-permute-start(bf16[4,2,64,1024]{3,2,1,0:T(8,128)(2,1)S(1)} %get-tuple-element.163), channel_id=1, source_target_pairs={{0,2},{1,3},{2,0},{3,1},{4,6},{5,7},{6,4},{7,5},{8,10},{9,11},{10,... | collective-permute-start | bytes 3145736 | tf_op jit(solution)/shard_map/ppermute | solution.py:36
  43.1 38.1 %collective-permute-start.5 = (bf16[6,64,1024]{2,1,0:T(8,128)(2,1)S(1)}, bf16[6,64,1024]{2,1,0:T(8,128)(2,1)S(1)}, u32[]{:S(2)}, u32[]{:S(2)}) collective-permute-start(bf16[6,64,1024]{2,1,0:T(8,128)(2,1)S(1)} %get-tuple-element.329), channel_id=1, source_target_pairs={{0,8},{1,9},{2,10},{3,11},{4,12},{5,13},{6,14},{7,15},{8,0},{9,1},... | collective-permute-start | bytes 2359304 | tf_op jit(solution)/shard_map/ppermute | solution.py:36
  87.2 44.7 %collective-permute-start.17 = (bf16[27,2,64,1024]{3,2,1,0:T(8,128)(2,1)}, bf16[27,2,64,1024]{3,2,1,0:T(8,128)(2,1)}, u32[]{:S(2)}, u32[]{:S(2)}) collective-permute-start(bf16[27,2,64,1024]{3,2,1,0:T(8,128)(2,1)} %get-tuple-element.168.mine), channel_id=1, source_target_pairs={{0,16},{16,0},{1,17},{17,1},{2,18},{18,2},{3,19},{19,3},{4,20},{20... | collective-permute-start | bytes 21233672 | tf_op jit(solution)/shard_map/ppermute | solution.py:40
  88.7 29.7 %collective-permute-start.13 = (bf16[5,2,64,1024]{3,2,1,0:T(8,128)(2,1)}, bf16[5,2,64,1024]{3,2,1,0:T(8,128)(2,1)}, u32[]{:S(2)}, u32[]{:S(2)}) collective-permute-start(bf16[5,2,64,1024]{3,2,1,0:T(8,128)(2,1)} %get-tuple-element.164), channel_id=1, source_target_pairs={{0,2},{1,3},{2,0},{3,1},{4,6},{5,7},{6,4},{7,5},{8,10},{9,11},{10,... | collective-permute-start | bytes 3932168 | tf_op jit(solution)/shard_map/ppermute | solution.py:36
  89.3 42.7 %collective-permute-start.14 = (bf16[5,2,64,1024]{3,2,1,0:T(8,128)(2,1)}, bf16[5,2,64,1024]{3,2,1,0:T(8,128)(2,1)}, u32[]{:S(2)}, u32[]{:S(2)}) collective-permute-start(bf16[5,2,64,1024]{3,2,1,0:T(8,128)(2,1)} %get-tuple-element.165), channel_id=1, source_target_pairs={{0,4},{1,5},{2,6},{3,7},{4,0},{5,1},{6,2},{7,3},{8,12},{9,13},{10,... | collective-permute-start | bytes 3932168 | tf_op jit(solution)/shard_map/ppermute | solution.py:36
  89.3 42.7 %collective-permute-start.15 = (bf16[5,2,64,1024]{3,2,1,0:T(8,128)(2,1)}, bf16[5,2,64,1024]{3,2,1,0:T(8,128)(2,1)}, u32[]{:S(2)}, u32[]{:S(2)}) collective-permute-start(bf16[5,2,64,1024]{3,2,1,0:T(8,128)(2,1)} %get-tuple-element.166), channel_id=1, source_target_pairs={{0,1},{1,0},{2,3},{3,2},{4,5},{5,4},{6,7},{7,6},{8,9},{9,8},{10,11... | collective-permute-start | bytes 3932168 | tf_op jit(solution)/shard_map/ppermute | solution.py:36
  105.7 63.5 %collective-permute-start.6 = (bf16[6,64,1024]{2,1,0:T(8,128)(2,1)}, bf16[6,64,1024]{2,1,0:T(8,128)(2,1)S(1)}, u32[]{:S(2)}, u32[]{:S(2)}) collective-permute-start(bf16[6,64,1024]{2,1,0:T(8,128)(2,1)} %get-tuple-element.157), channel_id=1, source_target_pairs={{0,8},{1,9},{2,10},{3,11},{4,12},{5,13},{6,14},{7,15},{8,0},{9,1},... | collective-permute-start | bytes 2359304 | tf_op jit(solution)/shard_map/ppermute | solution.py:36
  143.6 43.7 %collective-permute-start.21 = (bf16[15,2,64,1024]{3,2,1,0:T(8,128)(2,1)}, bf16[15,2,64,1024]{3,2,1,0:T(8,128)(2,1)}, u32[]{:S(2)}, u32[]{:S(2)}) collective-permute-start(bf16[15,2,64,1024]{3,2,1,0:T(8,128)(2,1)} %get-tuple-element.173.mine), channel_id=1, source_target_pairs={{0,16},{16,0},{1,17},{17,1},{2,18},{18,2},{3,19},{19,3},{4,20},{20... | collective-permute-start | bytes 11796488 | tf_op jit(solution)/shard_map/ppermute | solution.py:40
  149.9 36.6 %collective-permute-start.18 = (bf16[6,2,64,1024]{3,2,1,0:T(8,128)(2,1)}, bf16[6,2,64,1024]{3,2,1,0:T(8,128)(2,1)}, u32[]{:S(2)}, u32[]{:S(2)}) collective-permute-start(bf16[6,2,64,1024]{3,2,1,0:T(8,128)(2,1)} %get-tuple-element.169), channel_id=1, source_target_pairs={{0,4},{1,5},{2,6},{3,7},{4,0},{5,1},{6,2},{7,3},{8,12},{9,13},{10,... | collective-permute-start | bytes 4718600 | tf_op jit(solution)/shard_map/ppermute | solution.py:36
  149.9 36.6 %collective-permute-start.19 = (bf16[6,2,64,1024]{3,2,1,0:T(8,128)(2,1)}, bf16[6,2,64,1024]{3,2,1,0:T(8,128)(2,1)}, u32[]{:S(2)}, u32[]{:S(2)}) collective-permute-start(bf16[6,2,64,1024]{3,2,1,0:T(8,128)(2,1)} %get-tuple-element.170), channel_id=1, source_target_pairs={{0,1},{1,0},{2,3},{3,2},{4,5},{5,4},{6,7},{7,6},{8,9},{9,8},{10,11... | collective-permute-start | bytes 4718600 | tf_op jit(solution)/shard_map/ppermute | solution.py:36
  151.0 36.3 %collective-permute-start.20 = (bf16[6,2,64,1024]{3,2,1,0:T(8,128)(2,1)}, bf16[6,2,64,1024]{3,2,1,0:T(8,128)(2,1)}, u32[]{:S(2)}, u32[]{:S(2)}) collective-permute-start(bf16[6,2,64,1024]{3,2,1,0:T(8,128)(2,1)} %get-tuple-element.171), channel_id=1, source_target_pairs={{0,2},{1,3},{2,0},{3,1},{4,6},{5,7},{6,4},{7,5},{8,10},{9,11},{10,... | collective-permute-start | bytes 4718600 | tf_op jit(solution)/shard_map/ppermute | solution.py:36
  195.4 37.0 %collective-permute-start.25 = (bf16[21,2,64,1024]{3,2,1,0:T(8,128)(2,1)}, bf16[21,2,64,1024]{3,2,1,0:T(8,128)(2,1)}, u32[]{:S(2)}, u32[]{:S(2)}) collective-permute-start(bf16[21,2,64,1024]{3,2,1,0:T(8,128)(2,1)} %get-tuple-element.182.mine), channel_id=1, source_target_pairs={{0,16},{16,0},{1,17},{17,1},{2,18},{18,2},{3,19},{19,3},{4,20},{20... | collective-permute-start | bytes 16515080 | tf_op jit(solution)/shard_map/ppermute | solution.py:40
  195.4 37.0 %collective-permute-start.22 = (bf16[5,2,64,1024]{3,2,1,0:T(8,128)(2,1)}, bf16[5,2,64,1024]{3,2,1,0:T(8,128)(2,1)S(1)}, u32[]{:S(2)}, u32[]{:S(2)}) collective-permute-start(bf16[5,2,64,1024]{3,2,1,0:T(8,128)(2,1)} %get-tuple-element.174), channel_id=1, source_target_pairs={{0,4},{1,5},{2,6},{3,7},{4,0},{5,1},{6,2},{7,3},{8,12},{9,13},{10,... | collective-permute-start | bytes 3932168 | tf_op jit(solution)/shard_map/ppermute | solution.py:36
  197.1 35.3 %collective-permute-start.23 = (bf16[5,2,64,1024]{3,2,1,0:T(8,128)(2,1)}, bf16[5,2,64,1024]{3,2,1,0:T(8,128)(2,1)}, u32[]{:S(2)}, u32[]{:S(2)}) collective-permute-start(bf16[5,2,64,1024]{3,2,1,0:T(8,128)(2,1)} %get-tuple-element.175), channel_id=1, source_target_pairs={{0,1},{1,0},{2,3},{3,2},{4,5},{5,4},{6,7},{7,6},{8,9},{9,8},{10,11... | collective-permute-start | bytes 3932168 | tf_op jit(solution)/shard_map/ppermute | solution.py:36
  198.8 33.6 %collective-permute-start.24 = (bf16[5,2,64,1024]{3,2,1,0:T(8,128)(2,1)}, bf16[5,2,64,1024]{3,2,1,0:T(8,128)(2,1)}, u32[]{:S(2)}, u32[]{:S(2)}) collective-permute-start(bf16[5,2,64,1024]{3,2,1,0:T(8,128)(2,1)} %get-tuple-element.176), channel_id=1, source_target_pairs={{0,2},{1,3},{2,0},{3,1},{4,6},{5,7},{6,4},{7,5},{8,10},{9,11},{10,... | collective-permute-start | bytes 3932168 | tf_op jit(solution)/shard_map/ppermute | solution.py:36
  200.6 31.0 %collective-permute-start.1 = (bf16[2,128,1024]{2,1,0:T(8,128)(2,1)S(1)}, bf16[2,128,1024]{2,1,0:T(8,128)(2,1)S(1)}, u32[]{:S(2)}, u32[]{:S(2)}) collective-permute-start(bf16[2,128,1024]{2,1,0:T(8,128)(2,1)S(1)} %broadcast_select_fusion.7), channel_id=1, source_target_pairs={{16,8},{17,9},{18,10},{19,11},{20,12},{21,13},{22,14},{23,15},{8,1... | collective-permute-start | bytes 1572872 | tf_op jit(solution)/shard_map/ppermute | solution.py:27
  266.2 35.0 %collective-permute-start.33 = (bf16[6,2,64,1024]{3,2,1,0:T(8,128)(2,1)}, bf16[6,2,64,1024]{3,2,1,0:T(8,128)(2,1)}, u32[]{:S(2)}, u32[]{:S(2)}) collective-permute-start(bf16[6,2,64,1024]{3,2,1,0:T(8,128)(2,1)} %get-tuple-element.214.mine), channel_id=1, source_target_pairs={{0,16},{16,0},{1,17},{17,1},{2,18},{18,2},{3,19},{19,3},{4,20},{20... | collective-permute-start | bytes 4718600 | tf_op jit(solution)/shard_map/ppermute | solution.py:40
  267.4 33.8 %collective-permute-start.30 = (bf16[4,2,64,1024]{3,2,1,0:T(8,128)(2,1)}, bf16[4,2,64,1024]{3,2,1,0:T(8,128)(2,1)}, u32[]{:S(2)}, u32[]{:S(2)}) collective-permute-start(bf16[4,2,64,1024]{3,2,1,0:T(8,128)(2,1)} %get-tuple-element.210), channel_id=1, source_target_pairs={{0,1},{1,0},{2,3},{3,2},{4,5},{5,4},{6,7},{7,6},{8,9},{9,8},{10,11... | collective-permute-start | bytes 3145736 | tf_op jit(solution)/shard_map/ppermute | solution.py:36
  269.1 32.0 %collective-permute-start.31 = (bf16[4,2,64,1024]{3,2,1,0:T(8,128)(2,1)}, bf16[4,2,64,1024]{3,2,1,0:T(8,128)(2,1)}, u32[]{:S(2)}, u32[]{:S(2)}) collective-permute-start(bf16[4,2,64,1024]{3,2,1,0:T(8,128)(2,1)} %get-tuple-element.211), channel_id=1, source_target_pairs={{0,2},{1,3},{2,0},{3,1},{4,6},{5,7},{6,4},{7,5},{8,10},{9,11},{10,... | collective-permute-start | bytes 3145736 | tf_op jit(solution)/shard_map/ppermute | solution.py:36
  269.4 31.7 %collective-permute-start.32 = (bf16[4,2,64,1024]{3,2,1,0:T(8,128)(2,1)}, bf16[4,2,64,1024]{3,2,1,0:T(8,128)(2,1)}, u32[]{:S(2)}, u32[]{:S(2)}) collective-permute-start(bf16[4,2,64,1024]{3,2,1,0:T(8,128)(2,1)} %get-tuple-element.212), channel_id=1, source_target_pairs={{0,4},{1,5},{2,6},{3,7},{4,0},{5,1},{6,2},{7,3},{8,12},{9,13},{10,... | collective-permute-start | bytes 3145736 | tf_op jit(solution)/shard_map/ppermute | solution.py:36
  315.7 37.7 %collective-permute-start.39 = (f32[1,128]{1,0:T(1,128)S(1)}, f32[1,128]{1,0:T(1,128)S(1)}, u32[]{:S(2)}, u32[]{:S(2)}) collective-permute-start(f32[1,128]{1,0:T(1,128)S(1)} %add.116), channel_id=1, source_target_pairs={{0,8},{1,9},{2,10},{3,11},{4,12},{5,13},{6,14},{7,15},{8,0},{9,1},... | collective-permute-start | bytes 1544 | tf_op jit(solution)/shard_map/ppermute | solution.py:36
  455.6 38.1 %collective-permute-start.43 = (bf16[8,136,1024]{2,1,0:T(8,128)(2,1)}, bf16[8,136,1024]{2,1,0:T(8,128)(2,1)}, u32[]{:S(2)}, u32[]{:S(2)}) collective-permute-start(bf16[8,136,1024]{2,1,0:T(8,128)(2,1)} %constant_dynamic-slice_fusion.2), channel_id=1, source_target_pairs={{8,24},{9,25},{10,26},{11,27},{12,28},{13,29},{14,30},{15,31},{24,... | collective-permute-start | bytes 6684680 | tf_op jit(solution)/shard_map/ppermute | solution.py:27
  508.1 60.4 %all-to-all-start = ((bf16[8,272,1024]{2,1,0:T(8,128)(2,1)}), bf16[8,272,1024]{2,1,0:T(8,128)(2,1)}, u32[]{:S(2)}, u32[]{:S(2)}) async-start(bf16[8,272,1024]{2,1,0:T(8,128)(2,1)} %pad_maximum_fusion), calls=%async_computation | async-start | bytes 8912896 | tf_op jit(solution)/shard_map/all_to_all | solution.py:310
  571.7 40.1 %all-to-all-start.1 = ((bf16[8,136,1024]{2,1,0:T(8,128)(2,1)}), bf16[8,136,1024]{2,1,0:T(8,128)(2,1)}, u32[]{:S(2)}, u32[]{:S(2)}) async-start(bf16[8,136,1024]{2,1,0:T(8,128)(2,1)} %add_convert_fusion), calls=%async_computation.1 | async-start | bytes 4456448 | tf_op jit(solution)/shard_map/all_to_all | solution.py:310
  577.2 34.6 %collective-permute-start.44 = (bf16[272,1024]{1,0:T(8,128)(2,1)S(1)}, bf16[272,1024]{1,0:T(8,128)(2,1)S(1)}, u32[]{:S(2)}, u32[]{:S(2)}) collective-permute-start(bf16[272,1024]{1,0:T(8,128)(2,1)S(1)} %reduce_sum.46), channel_id=1, source_target_pairs={{8,0},{9,1},{10,2},{11,3},{12,4},{13,5},{14,6},{15,7},{24,16},{25,... | collective-permute-start | bytes 1671176 | tf_op jit(solution)/shard_map/ppermute | solution.py:336
  617.3 56.3 %all-to-all-start.2 = ((bf16[8,272,1024]{2,1,0:T(8,128)(2,1)}), bf16[8,272,1024]{2,1,0:T(8,128)(2,1)}, u32[]{:S(2)}, u32[]{:S(2)}) async-start(bf16[8,272,1024]{2,1,0:T(8,128)(2,1)} %broadcast_in_dim.82), calls=%async_computation.2 | async-start | bytes 8912896 | tf_op jit(solution)/shard_map/all_to_all | solution.py:310
  705.3 30.4 %collective-permute-start.48 = (bf16[272,1024]{1,0:T(8,128)(2,1)S(1)}, bf16[272,1024]{1,0:T(8,128)(2,1)S(1)}, u32[]{:S(2)}, u32[]{:S(2)}) collective-permute-start(bf16[272,1024]{1,0:T(8,128)(2,1)S(1)} %pad_maximum_fusion.1), channel_id=1, source_target_pairs={{0,8},{1,9},{2,10},{3,11},{4,12},{5,13},{6,14},{7,15},{16,24},{17,... | collective-permute-start | bytes 1671176 | tf_op jit(solution)/shard_map/ppermute | solution.py:336
  738.5 60.7 %all-to-all-start.4 = ((bf16[8,272,1024]{2,1,0:T(8,128)(2,1)}), bf16[8,272,1024]{2,1,0:T(8,128)(2,1)}, u32[]{:S(2)}, u32[]{:S(2)}) async-start(bf16[8,272,1024]{2,1,0:T(8,128)(2,1)} %broadcast_in_dim.83), calls=%async_computation.4 | async-start | bytes 8912896 | tf_op jit(solution)/shard_map/all_to_all | solution.py:310
  743.2 82.2 %collective-permute-start.50 = (bf16[8,272,1024]{2,1,0:T(8,128)(2,1)}, bf16[8,272,1024]{2,1,0:T(8,128)(2,1)}, u32[]{:S(2)}, u32[]{:S(2)}) collective-permute-start(bf16[8,272,1024]{2,1,0:T(8,128)(2,1)} %all-to-all-done.2.late1_ref), channel_id=1, source_target_pairs={{0,16},{1,17},{2,18},{3,19},{4,20},{5,21},{6,22},{7,23},{8,24},{9,... | collective-permute-start | bytes 13369352 | tf_op jit(solution)/shard_map/ppermute | solution.py:343
  (102 other events, 1727.6 us)

commit v6 on v5

--- a/solution.py
+++ b/solution.py
@@ -523,6 +523,7 @@
 
 GROUP = 8 * HEAD_DIM
 BLOCK = 1024
+BACK_BLOCK = 2048
 PIECE = 256
 
 
@@ -758,13 +759,13 @@
 
 def feed_backward_kernel(
     facts_ref, g_ref, x_ref, norm_ref, act_ref, slope_ref, midu_ref, midd_ref, sums_ref, wu_ref, wd_ref, au_ref,
-    bu_ref, ad_ref, bd_ref,
+    bu_ref, ad_ref, ad_next_ref, bd_ref,
     whole_out, gx_out,
     block_out, g_scr, gmd_scr, gmdt_scr, midut_scr, gmu_scr, sem,
 ):
     step = pl.program_id(0)
     width = x_ref.shape[1]
-    hidden = pl.num_programs(0) * BLOCK
+    hidden = pl.num_programs(0) * BACK_BLOCK
 
     @pl.when(step == 0)
     def _():
@@ -778,12 +779,12 @@
         middt = half(midd_ref[...].astype(jnp.float32).T)
         block_out[:RANK, pl.ds(width + 2 * hidden, width)] = half(adapter_scale * mm(middt, g_scr[...]))
 
-    grad_act = mm_nt(g_scr[...], wd_ref[...]) + mm_nt(gmd_scr[...], ad_ref[...])
+    grad_act = mm_nt(g_scr[...], wd_ref[...]) + mm_nt(gmd_scr[...], jnp.concatenate([ad_ref[...], ad_next_ref[...]], 0))
     grad_up = half(half(grad_act).astype(jnp.float32) * slope_ref[...].astype(jnp.float32))
-    first_at = pl.multiple_of(width + step * BLOCK, BLOCK)
-    second_at = pl.multiple_of(width + hidden + step * BLOCK, BLOCK)
-    block_out[:RANK, pl.ds(first_at, BLOCK)] = half(mm(gmdt_scr[...], act_ref[...]))
-    block_out[:RANK, pl.ds(second_at, BLOCK)] = half(adapter_scale * mm(midut_scr[...], grad_up))
+    first_at = pl.multiple_of(width + step * BACK_BLOCK, BACK_BLOCK)
+    second_at = pl.multiple_of(width + hidden + step * BACK_BLOCK, BACK_BLOCK)
+    block_out[:RANK, pl.ds(first_at, BACK_BLOCK)] = half(mm(gmdt_scr[...], act_ref[...]))
+    block_out[:RANK, pl.ds(second_at, BACK_BLOCK)] = half(adapter_scale * mm(midut_scr[...], grad_up))
     gmu_scr[...] += mm_nt(grad_up, bu_ref[...])
     gx_out[...] += mm_nt(grad_up, wu_ref[...])
 
@@ -810,21 +811,22 @@
     return kernel_call(
         feed_backward_kernel,
         "feed_backward",
-        hidden // BLOCK,
+        hidden // BACK_BLOCK,
         [
             whole(tokens, width),
             whole(tokens, width),
             whole(4, width),
-            column_block(tokens, BLOCK),
-            column_block(tokens, BLOCK),
+            column_block(tokens, BACK_BLOCK),
+            column_block(tokens, BACK_BLOCK),
             whole(tokens, RANK),
             whole(tokens, RANK),
             whole(8, 128),
-            column_block(width, BLOCK),
-            row_block(BLOCK, width),
+            column_block(width, BACK_BLOCK),
+            row_block(BACK_BLOCK, width),
             layer_fixed(layer, width, RANK, 2, 0),
-            layer_columns(layer, RANK, BLOCK, 4 * width // BLOCK),
-            layer_rows(layer, BLOCK, RANK, 3 * width // BLOCK),
+            layer_columns(layer, RANK, BACK_BLOCK, 4 * width // BACK_BLOCK),
+            pl.BlockSpec((None, BACK_BLOCK // 2, RANK), lambda step, facts_ref: (layer, 2 * step + 3, 0)),
+            pl.BlockSpec((None, BACK_BLOCK // 2, RANK), lambda step, facts_ref: (layer, 2 * step + 4, 0)),
             layer_fixed(layer, RANK, width, 0, 8),
         ],
         [pl.BlockSpec(memory_space=pl.ANY), whole(tokens, width)],
@@ -842,7 +844,7 @@
         4 * width * hidden + 4 * tokens * hidden + 16 * tokens * width,
     )(
         facts, gradient, residual, norms, active, slope, mid_u, mid_d, sums, upper, down, firsts, seconds,
-        firsts, seconds,
+        firsts, firsts, seconds,
     )
 
 

time: 858 us -> 858 us (level)
  no operation moved by 1% of the time
where the time goes in v6:
time: 858 us; the launch traced here: 848 us
  waiting for transfers between devices  322 us (38%)
  Pallas kernels  308 us (36%)
  starting transfers between devices  97.1 us (11%)
  local copies, waits for them, and re-layouts  49.7 us (6%)
  other arithmetic  37 us (4%)
  blocking collectives  31.2 us (4%)
    ppermute x27, waiting for transfers between devices, flip_place(): lax.ppermute(value, 'dp', [(place, place ^ mask) for place in range(count)])  97.9 us
    all_to_all x4, waiting for transfers between devices, exchange(): return lax.all_to_all(value, 'dp', 0, 0, axis_index_groups=groups)  85.9 us
    pallas_call x4, Pallas kernels, feed_backward(): kernel_call(feed_backward_kernel, 'feed_backward', hidden // BACK_BLOCK,...  58.9 us
    ppermute x2, waiting for transfers between devices, cross_section(): return jnp.where(stage == section, piece, lax.ppermute(piece, 'dp', across))  58.4 us
    pallas_call x4, Pallas kernels, attention_backward(): kernel_call(attention_backward_kernel, 'attention_backward', groups, [who...  54 us
    pallas_call x4, Pallas kernels, feed_forward(): kernel_call(feed_forward_kernel, 'feed_forward', hidden // BLOCK, [whole(...  53 us
    pallas_call x6, Pallas kernels, assemble(): pl.pallas_call(partial(assemble_kernel, tuple(layout)), out_shape=[jax.Sh...  48.1 us
    ppermute x11, waiting for transfers between devices, both_axes(): return lax.ppermute(value, ('section', 'dp'), pairs)  47.2 us
  transfers between devices with their start and end apart: 55, of which 25 were waited for; matrix products, arithmetic and copies ran while one was open for 5% of the time, Pallas kernels for 22%

profile of v6, /device:TPU:26, one launch (start us, length us, event | category | flops | bytes accessed | tf_op | source)
XLA Modules:
  0.0 847.8 jit_solution(18408269432003536829)
XLA Ops:
  26.4 10.3 %collective-permute-done.7.refs_4_.refs_1_ = bf16[2,2,64,1024]{3,2,1,0:T(8,128)(2,1)S(1)} collective-permute-done((bf16[2,2,64,1024]{3,2,1,0:T(8,128)(2,1)S(1)}, bf16[2,2,64,1024]{3,2,1,0:T(8,128)(2,1)S(1)}, u32[]{:S(2)}, u32[]{:S(2)}) %collective-permute-start.7) | collective-permute-done | bytes 524320 | tf_op jit(solution)/shard_map/ppermute | solution.py:36
  44.0 37.1 %collective-permute-done.5 = bf16[6,64,1024]{2,1,0:T(8,128)(2,1)S(1)} collective-permute-done((bf16[6,64,1024]{2,1,0:T(8,128)(2,1)S(1)}, bf16[6,64,1024]{2,1,0:T(8,128)(2,1)S(1)}, u32[]{:S(2)}, u32[]{:S(2)}) %collective-permute-start.5) | collective-permute-done | bytes 786464 | tf_op jit(solution)/shard_map/ppermute | solution.py:36
  91.0 14.7 %collective-permute-done.16.refs_11_ = bf16[2,128,9216]{2,1,0:T(8,128)(2,1)} collective-permute-done((bf16[2,128,9216]{2,1,0:T(8,128)(2,1)}, bf16[2,128,9216]{2,1,0:T(8,128)(2,1)}, u32[]{:S(2)}, u32[]{:S(2)}) %collective-permute-start.16) | collective-permute-done | bytes 4718624 | tf_op jit(solution)/shard_map/ppermute | solution.py:27
  107.9 10.5 %collective-permute-done.13.refs_10_.refs_1_ = bf16[5,2,64,1024]{3,2,1,0:T(8,128)(2,1)} collective-permute-done((bf16[5,2,64,1024]{3,2,1,0:T(8,128)(2,1)}, bf16[5,2,64,1024]{3,2,1,0:T(8,128)(2,1)}, u32[]{:S(2)}, u32[]{:S(2)}) %collective-permute-start.13) | collective-permute-done | bytes 1310752 | tf_op jit(solution)/shard_map/ppermute | solution.py:36
  118.4 13.5 %collective-permute-done.14.refs_4_ = bf16[5,2,64,1024]{3,2,1,0:T(8,128)(2,1)} collective-permute-done((bf16[5,2,64,1024]{3,2,1,0:T(8,128)(2,1)}, bf16[5,2,64,1024]{3,2,1,0:T(8,128)(2,1)}, u32[]{:S(2)}, u32[]{:S(2)}) %collective-permute-start.14) | collective-permute-done | bytes 1310752 | tf_op jit(solution)/shard_map/ppermute | solution.py:36
  157.4 11.8 %assemble.6 = (bf16[1024,3072]{1,0:T(8,128)(2,1)}, bf16[1024,1024]{1,0:T(8,128)(2,1)}, bf16[1024,4096]{1,0:T(8,128)(2,1)}, bf16[4096,1024]{1,0:T(8,128)(2,1)}, b...) custom-call(s32[28]{0:T(128)} %stack.76.info_ref, ...), custom_call_target="tpu_custom_call" | custom-call | bytes 42467328 | tf_op jit(solution)/shard_map/assemble/pallas_call | solution.py:182
  169.2 17.3 %collective-permute-done.18.refs_2_ = bf16[6,2,64,1024]{3,2,1,0:T(8,128)(2,1)} collective-permute-done((bf16[6,2,64,1024]{3,2,1,0:T(8,128)(2,1)}, bf16[6,2,64,1024]{3,2,1,0:T(8,128)(2,1)}, u32[]{:S(2)}, u32[]{:S(2)}) %collective-permute-start.18) | collective-permute-done | bytes 1572896 | tf_op jit(solution)/shard_map/ppermute | solution.py:36
  212.7 19.0 %collective-permute-done.1.refs_4_ = bf16[2,128,1024]{2,1,0:T(8,128)(2,1)S(1)} collective-permute-done((bf16[2,128,1024]{2,1,0:T(8,128)(2,1)S(1)}, bf16[2,128,1024]{2,1,0:T(8,128)(2,1)S(1)}, u32[]{:S(2)}, u32[]{:S(2)}) %collective-permute-start.1) | collective-permute-done | bytes 524320 | tf_op jit(solution)/shard_map/ppermute | solution.py:27
  251.5 9.7 %assemble.8 = (bf16[1024,3072]{1,0:T(8,128)(2,1)}, bf16[1024,1024]{1,0:T(8,128)(2,1)}, bf16[1024,4096]{1,0:T(8,128)(2,1)}, bf16[4096,1024]{1,0:T(8,128)(2,1)}, b...) custom-call(s32[22]{0:T(128)} %stack.79.info_ref, ...), custom_call_target="tpu_custom_call", output_to_operand_aliasing={{0}: (3, {}), {1}: (4, {}), {2}: (5, {}), {3}: (6, {}), {4}... | custom-call | bytes 33030144 | tf_op jit(solution)/shard_map/assemble/pallas_call | solution.py:182
  277.7 10.0 %attention_forward.4 = (bf16[256,1024]{1,0:T(8,128)(2,1)}, bf16[256,1024]{1,0:T(8,128)(2,1)}, bf16[256,1024]{1,0:T(8,128)(2,1)}, bf16[256,1024]{1,0:T(8,128)(2,1...) custom-call(s32[2,2]{1,0:T(2,128)S(1)} %broadcast_select_fusion.10.facts_ref, ...), custom_call_target="tpu_custom_call" | custom-call | flops 2147483648 | bytes 13631488 | tf_op jit(solution)/shard_map/attention_forward/pallas_call | solution.py:628
  287.7 13.5 %feed_forward.4 = (bf16[256,4096]{1,0:T(8,128)(2,1)}, bf16[256,4096]{1,0:T(8,128)(2,1)}, bf16[256,128]{1,0:T(8,128)(2,1)}, bf16[256,128]{1,0:T(8,128)(2,1)}, f32[256,1024]{1,0:T(8,128)S(1)}, /*index=5*/f32[8,128]{1,0:T(8,128)}) custom-call(s32[2,2]{1,0:T(2,128)S(1)} %broadcast_select_fusion.10.facts_ref, f32[256,1024]{1,0:T(8,128)S(1)} %bitcast_convert_fusion.x_ref, ...), custom_call_target="tpu_custom_call" | custom-call | flops 4294967296 | bytes 24117248 | tf_op jit(solution)/shard_map/feed_forward/pallas_call | solution.py:715
  328.5 10.0 %attention_forward.5 = (bf16[256,1024]{1,0:T(8,128)(2,1)}, bf16[256,1024]{1,0:T(8,128)(2,1)}, bf16[256,1024]{1,0:T(8,128)(2,1)}, bf16[256,1024]{1,0:T(8,128)(2,1...) custom-call(s32[2,2]{1,0:T(2,128)S(1)} %broadcast_select_fusion.10.facts_ref, ...), custom_call_target="tpu_custom_call" | custom-call | flops 2147483648 | bytes 13631488 | tf_op jit(solution)/shard_map/attention_forward/pallas_call | solution.py:628
  338.5 13.4 %feed_forward.5 = (bf16[256,4096]{1,0:T(8,128)(2,1)}, bf16[256,4096]{1,0:T(8,128)(2,1)}, bf16[256,128]{1,0:T(8,128)(2,1)}, bf16[256,128]{1,0:T(8,128)(2,1)}, f32[256,1024]{1,0:T(8,128)S(1)}, /*index=5*/f32[8,128]{1,0:T(8,128)}) custom-call(s32[2,2]{1,0:T(2,128)S(1)} %broadcast_select_fusion.10.facts_ref, f32[256,1024]{1,0:T(8,128)S(1)} %get-tuple-element.205.refs_5_.x_ref, ...), custom_call_target="tpu_custom_call" | custom-call | flops 4294967296 | bytes 24117248 | tf_op jit(solution)/shard_map/feed_forward/pallas_call | solution.py:715
  353.6 23.3 %collective-permute-done.35 = bf16[256,1024]{1,0:T(8,128)(2,1)S(1)} collective-permute-done((bf16[256,1024]{1,0:T(8,128)(2,1)S(1)}, bf16[256,1024]{1,0:T(8,128)(2,1)S(1)}, u32[]{:S(2)}, u32[]{:S(2)}) %collective-permute-start.35) | collective-permute-done | bytes 524320 | tf_op jit(solution)/shard_map/ppermute | solution.py:1132
  387.3 13.0 %feed_forward.6 = (bf16[256,4096]{1,0:T(8,128)(2,1)S(1)}, bf16[256,4096]{1,0:T(8,128)(2,1)}, bf16[256,128]{1,0:T(8,128)(2,1)S(1)}, bf16[256,128]{1,0:T(8,128)(2,...) custom-call(s32[2,2]{1,0:T(2,128)S(1)} %broadcast_select_fusion.10.facts_ref, ...), custom_call_target="tpu_custom_call" | custom-call | flops 4294967296 | bytes 24117248 | tf_op jit(solution)/shard_map/feed_forward/pallas_call | solution.py:715
  410.1 13.1 %feed_forward.7 = (bf16[256,4096]{1,0:T(8,128)(2,1)S(1)}, bf16[256,4096]{1,0:T(8,128)(2,1)}, bf16[256,128]{1,0:T(8,128)(2,1)S(1)}, bf16[256,128]{1,0:T(8,128)(2,...) custom-call(s32[2,2]{1,0:T(2,128)S(1)} %broadcast_select_fusion.10.facts_ref, ...), custom_call_target="tpu_custom_call" | custom-call | flops 4294967296 | bytes 24117248 | tf_op jit(solution)/shard_map/feed_forward/pallas_call | solution.py:715
  424.2 14.7 %feed_backward.4 = (bf16[16,136,1024]{2,1,0:T(8,128)(2,1)}, f32[256,1024]{1,0:T(8,128)S(1)}) custom-call(s32[2,2]{1,0:T(2,128)S(1)} %broadcast_select_fusion.10.facts_ref, f32[256,1024]{1,0:T(8,128)S(1)} %bitcast.52, f32[256,1024]{1,0:T(8,128)S(1)} %get-tuple-element.230.x_ref, f32[4,1024]{1,0:T(4,128)S(1)} %get-tuple-element.331.norm_ref, ...), custom_call_target="tpu_custom_call" | custom-call | flops 4294967296 | bytes 25165824 | tf_op jit(solution)/shard_map/feed_backward/pallas_call | solution.py:811
  439.0 13.5 %attention_backward.4 = (bf16[16,136,1024]{2,1,0:T(8,128)(2,1)}, f32[256,1024]{1,0:T(8,128)S(1)}) custom-call(s32[2,2]{1,0:T(2,128)S(1)} %broadcast_select_fusion.10.facts_ref, f32[256,1024]{1,0:T(8,128)S(1)} %bitcast.53, f32[256,1024]{1,0:T(8,128)S(1)} %get-tuple-element.238.gx_ref, f32[256,1024]{1,0:T(8,128)} %copy-done.2, ...), custom_call_target="tpu_custom_call", output_to_operand_aliasing={{0}: (22, {})} | custom-call | flops 2147483648 | bytes 16777216 | tf_op jit(solution)/shard_map/attention_backward/pallas_call | solution.py:926
  457.6 15.1 %feed_backward.5 = (bf16[16,136,1024]{2,1,0:T(8,128)(2,1)}, f32[256,1024]{1,0:T(8,128)S(1)}) custom-call(s32[2,2]{1,0:T(2,128)S(1)} %broadcast_select_fusion.10.facts_ref, f32[256,1024]{1,0:T(8,128)S(1)} %get-tuple-element.246.g_ref, f32[256,1024]{1,0:T(8,128)S(1)} %convert_select_fusion.2.x_ref, f32[4,1024]{1,0:T(4,128)S(1)} %get-tuple-element.332.norm_ref, ...), custom_call_target="tpu_custom_call" | custom-call | flops 4294967296 | bytes 25165824 | tf_op jit(solution)/shard_map/feed_backward/pallas_call | solution.py:811
  472.7 13.5 %attention_backward.5 = (bf16[16,136,1024]{2,1,0:T(8,128)(2,1)}, f32[256,1024]{1,0:T(8,128)S(1)}) custom-call(s32[2,2]{1,0:T(2,128)S(1)} %broadcast_select_fusion.10.facts_ref, f32[256,1024]{1,0:T(8,128)S(1)} %get-tuple-element.246.g_ref, f32[256,1024]{1,0:T(8,128)S(1)} %get-tuple-element.252.gx_ref, ...), custom_call_target="tpu_custom_call", output_to_operand_aliasing={{0}: (22, {})} | custom-call | flops 2147483648 | bytes 16777216 | tf_op jit(solution)/shard_map/attention_backward/pallas_call | solution.py:926
  515.9 14.5 %feed_backward.6 = (bf16[16,136,1024]{2,1,0:T(8,128)(2,1)}, f32[256,1024]{1,0:T(8,128)S(1)}) custom-call(s32[2,2]{1,0:T(2,128)S(1)} %broadcast_select_fusion.10.facts_ref, f32[256,1024]{1,0:T(8,128)S(1)} %convert_select_fusion.1.g_ref, f32[256,1024]{1,0:T(8,128)S(1)} %copy-done.3, f32[4,1024]{1,0:T(4,128)S(1)} %get-tuple-element.331.norm_ref, ...), custom_call_target="tpu_custom_call" | custom-call | flops 4294967296 | bytes 25165824 | tf_op jit(solution)/shard_map/feed_backward/pallas_call | solution.py:811
  530.4 13.5 %attention_backward.6 = (bf16[16,136,1024]{2,1,0:T(8,128)(2,1)}, f32[256,1024]{1,0:T(8,128)S(1)}) custom-call(s32[2,2]{1,0:T(2,128)S(1)} %broadcast_select_fusion.10.facts_ref, f32[256,1024]{1,0:T(8,128)S(1)} %convert_select_fusion.1.g_ref, f32[256,1024]{1,0:T(8,128)S(1)} %get-tuple-element.261.gx_ref, ...), custom_call_target="tpu_custom_call", output_to_operand_aliasing={{0}: (22, {})} | custom-call | flops 2147483648 | bytes 16777216 | tf_op jit(solution)/shard_map/attention_backward/pallas_call | solution.py:926
  549.5 19.2 %all-to-all-done = bf16[8,272,1024]{2,1,0:T(8,128)(2,1)} async-done(((bf16[8,272,1024]{2,1,0:T(8,128)(2,1)}), bf16[8,272,1024]{2,1,0:T(8,128)(2,1)}, u32[]{:S(2)}, u32[]{:S(2)}) %all-to-all-start) | async-done | bytes 4456480 | tf_op jit(solution)/shard_map/all_to_all | solution.py:310
  582.4 29.5 %collective-permute-done.44 = bf16[272,1024]{1,0:T(8,128)(2,1)S(1)} collective-permute-done((bf16[272,1024]{1,0:T(8,128)(2,1)S(1)}, bf16[272,1024]{1,0:T(8,128)(2,1)S(1)}, u32[]{:S(2)}, u32[]{:S(2)}) %collective-permute-start.44) | collective-permute-done | bytes 557088 | tf_op jit(solution)/shard_map/ppermute | solution.py:336
  624.4 14.7 %feed_backward.7 = (bf16[16,136,1024]{2,1,0:T(8,128)(2,1)}, f32[256,1024]{1,0:T(8,128)S(1)}) custom-call(s32[2,2]{1,0:T(2,128)S(1)} %broadcast_select_fusion.10.facts_ref, f32[256,1024]{1,0:T(8,128)S(1)} %get-tuple-element.263.g_ref, f32[256,1024]{1,0:T(8,128)S(1)} %copy-done.1, f32[4,1024]{1,0:T(4,128)S(1)} %get-tuple-element.332.norm_ref, ...), custom_call_target="tpu_custom_call" | custom-call | flops 4294967296 | bytes 25165824 | tf_op jit(solution)/shard_map/feed_backward/pallas_call | solution.py:811
  639.1 13.5 %attention_backward.7 = (bf16[16,136,1024]{2,1,0:T(8,128)(2,1)}, f32[256,1024]{1,0:T(8,128)S(1)}) custom-call(s32[2,2]{1,0:T(2,128)S(1)} %broadcast_select_fusion.10.facts_ref, f32[256,1024]{1,0:T(8,128)S(1)} %get-tuple-element.263.g_ref, f32[256,1024]{1,0:T(8,128)S(1)} %get-tuple-element.264.gx_ref, ...), custom_call_target="tpu_custom_call", output_to_operand_aliasing={{0}: (22, {})} | custom-call | flops 2147483648 | bytes 16777216 | tf_op jit(solution)/shard_map/attention_backward/pallas_call | solution.py:926
  659.0 14.8 %all-to-all-done.2.late1_ref = bf16[8,272,1024]{2,1,0:T(8,128)(2,1)} async-done(((bf16[8,272,1024]{2,1,0:T(8,128)(2,1)}), bf16[8,272,1024]{2,1,0:T(8,128)(2,1)}, u32[]{:S(2)}, u32[]{:S(2)}) %all-to-all-start.2) | async-done | bytes 4456480 | tf_op jit(solution)/shard_map/all_to_all | solution.py:310
  673.8 31.2 %all_to_all.25 = bf16[8,136,1024]{2,1,0:T(8,128)(2,1)S(1)} all-to-all(bf16[8,136,1024]{2,1,0:T(8,128)(2,1)} %add_convert_fusion.1), channel_id=1, replica_groups={{0,1,2,3,4,5,6,7},{8,9,10,11,12,13,14,15},{16,17,18,19,20,21,22,23},{24..., dimensions={0} | all-to-all | bytes 4456448 | tf_op jit(solution)/shard_map/all_to_all | solution.py:310
  707.1 28.9 %collective-permute-done.48 = bf16[272,1024]{1,0:T(8,128)(2,1)S(1)} collective-permute-done((bf16[272,1024]{1,0:T(8,128)(2,1)S(1)}, bf16[272,1024]{1,0:T(8,128)(2,1)S(1)}, u32[]{:S(2)}, u32[]{:S(2)}) %collective-permute-start.48) | collective-permute-done | bytes 557088 | tf_op jit(solution)/shard_map/ppermute | solution.py:336
  747.6 51.9 %all-to-all-done.4.early0_ref = bf16[8,272,1024]{2,1,0:T(8,128)(2,1)} async-done(((bf16[8,272,1024]{2,1,0:T(8,128)(2,1)}), bf16[8,272,1024]{2,1,0:T(8,128)(2,1)}, u32[]{:S(2)}, u32[]{:S(2)}) %all-to-all-start.4) | async-done | bytes 4456480 | tf_op jit(solution)/shard_map/all_to_all | solution.py:310
  813.8 10.5 %collective-permute-done.45 = bf16[256,1024]{1,0:T(8,128)(2,1)S(1)} collective-permute-done((bf16[256,1024]{1,0:T(8,128)(2,1)S(1)}, bf16[256,1024]{1,0:T(8,128)(2,1)S(1)}, u32[]{:S(2)}, u32[]{:S(2)}) %collective-permute-start.45) | collective-permute-done | bytes 524320 | tf_op jit(solution)/shard_map/ppermute | solution.py:27
  825.6 20.5 %finish.1 = (f32[2,1024,128]{2,1,0:T(8,128)}, f32[2,128,3072]{2,1,0:T(8,128)}, f32[2,1024,128]{2,1,0:T(8,128)}, f32[2,128,1024]{2,1,0:T(8,128)}, f32[2,1024,128]...) custom-call(s32[2]{0:T(128)} %pad_add_fusion.1.info_ref, ...), custom_call_target="tpu_custom_call" | custom-call | flops 536870912 | bytes 25165824 | tf_op jit(solution)/shard_map/finish/pallas_call | solution.py:424
  (331 shorter events, 285.0 us)
Async XLA Ops:
  20.1 62.0 %collective-permute-start.4 = (bf16[2,7168,128]{2,1,0:T(8,128)(2,1)}, bf16[2,7168,128]{2,1,0:T(8,128)(2,1)}, u32[]{:S(2)}, u32[]{:S(2)}) collective-permute-start(bf16[2,7168,128]{2,1,0:T(8,128)(2,1)} %get-tuple-element.155), channel_id=1, source_target_pairs={{0,16},{1,17},{2,18},{3,19},{4,20},{5,21},{6,22},{7,23},{24,8},{25... | collective-permute-start | bytes 11010056 | tf_op jit(solution)/shard_map/ppermute | solution.py:27
  39.4 42.7 %collective-permute-start.10 = (bf16[4,2,64,1024]{3,2,1,0:T(8,128)(2,1)S(1)}, bf16[4,2,64,1024]{3,2,1,0:T(8,128)(2,1)S(1)}, u32[]{:S(2)}, u32[]{:S(2)}) collective-permute-start(bf16[4,2,64,1024]{3,2,1,0:T(8,128)(2,1)S(1)} %get-tuple-element.161), channel_id=1, source_target_pairs={{0,4},{1,5},{2,6},{3,7},{4,0},{5,1},{6,2},{7,3},{8,12},{9,13},{10,... | collective-permute-start | bytes 3145736 | tf_op jit(solution)/shard_map/ppermute | solution.py:36
  41.0 41.0 %collective-permute-start.11 = (bf16[4,2,64,1024]{3,2,1,0:T(8,128)(2,1)S(1)}, bf16[4,2,64,1024]{3,2,1,0:T(8,128)(2,1)S(1)}, u32[]{:S(2)}, u32[]{:S(2)}) collective-permute-start(bf16[4,2,64,1024]{3,2,1,0:T(8,128)(2,1)S(1)} %get-tuple-element.162), channel_id=1, source_target_pairs={{0,1},{1,0},{2,3},{3,2},{4,5},{5,4},{6,7},{7,6},{8,9},{9,8},{10,11... | collective-permute-start | bytes 3145736 | tf_op jit(solution)/shard_map/ppermute | solution.py:36
  41.6 40.5 %collective-permute-start.12 = (bf16[4,2,64,1024]{3,2,1,0:T(8,128)(2,1)S(1)}, bf16[4,2,64,1024]{3,2,1,0:T(8,128)(2,1)S(1)}, u32[]{:S(2)}, u32[]{:S(2)}) collective-permute-start(bf16[4,2,64,1024]{3,2,1,0:T(8,128)(2,1)S(1)} %get-tuple-element.163), channel_id=1, source_target_pairs={{0,2},{1,3},{2,0},{3,1},{4,6},{5,7},{6,4},{7,5},{8,10},{9,11},{10,... | collective-permute-start | bytes 3145736 | tf_op jit(solution)/shard_map/ppermute | solution.py:36
  43.1 38.1 %collective-permute-start.5 = (bf16[6,64,1024]{2,1,0:T(8,128)(2,1)S(1)}, bf16[6,64,1024]{2,1,0:T(8,128)(2,1)S(1)}, u32[]{:S(2)}, u32[]{:S(2)}) collective-permute-start(bf16[6,64,1024]{2,1,0:T(8,128)(2,1)S(1)} %get-tuple-element.329), channel_id=1, source_target_pairs={{0,8},{1,9},{2,10},{3,11},{4,12},{5,13},{6,14},{7,15},{8,0},{9,1},... | collective-permute-start | bytes 2359304 | tf_op jit(solution)/shard_map/ppermute | solution.py:36
  87.2 44.7 %collective-permute-start.17 = (bf16[27,2,64,1024]{3,2,1,0:T(8,128)(2,1)}, bf16[27,2,64,1024]{3,2,1,0:T(8,128)(2,1)}, u32[]{:S(2)}, u32[]{:S(2)}) collective-permute-start(bf16[27,2,64,1024]{3,2,1,0:T(8,128)(2,1)} %get-tuple-element.168.mine), channel_id=1, source_target_pairs={{0,16},{16,0},{1,17},{17,1},{2,18},{18,2},{3,19},{19,3},{4,20},{20... | collective-permute-start | bytes 21233672 | tf_op jit(solution)/shard_map/ppermute | solution.py:40
  88.7 29.7 %collective-permute-start.13 = (bf16[5,2,64,1024]{3,2,1,0:T(8,128)(2,1)}, bf16[5,2,64,1024]{3,2,1,0:T(8,128)(2,1)}, u32[]{:S(2)}, u32[]{:S(2)}) collective-permute-start(bf16[5,2,64,1024]{3,2,1,0:T(8,128)(2,1)} %get-tuple-element.164), channel_id=1, source_target_pairs={{0,2},{1,3},{2,0},{3,1},{4,6},{5,7},{6,4},{7,5},{8,10},{9,11},{10,... | collective-permute-start | bytes 3932168 | tf_op jit(solution)/shard_map/ppermute | solution.py:36
  89.3 42.7 %collective-permute-start.14 = (bf16[5,2,64,1024]{3,2,1,0:T(8,128)(2,1)}, bf16[5,2,64,1024]{3,2,1,0:T(8,128)(2,1)}, u32[]{:S(2)}, u32[]{:S(2)}) collective-permute-start(bf16[5,2,64,1024]{3,2,1,0:T(8,128)(2,1)} %get-tuple-element.165), channel_id=1, source_target_pairs={{0,4},{1,5},{2,6},{3,7},{4,0},{5,1},{6,2},{7,3},{8,12},{9,13},{10,... | collective-permute-start | bytes 3932168 | tf_op jit(solution)/shard_map/ppermute | solution.py:36
  89.3 42.7 %collective-permute-start.15 = (bf16[5,2,64,1024]{3,2,1,0:T(8,128)(2,1)}, bf16[5,2,64,1024]{3,2,1,0:T(8,128)(2,1)}, u32[]{:S(2)}, u32[]{:S(2)}) collective-permute-start(bf16[5,2,64,1024]{3,2,1,0:T(8,128)(2,1)} %get-tuple-element.166), channel_id=1, source_target_pairs={{0,1},{1,0},{2,3},{3,2},{4,5},{5,4},{6,7},{7,6},{8,9},{9,8},{10,11... | collective-permute-start | bytes 3932168 | tf_op jit(solution)/shard_map/ppermute | solution.py:36
  105.7 63.5 %collective-permute-start.6 = (bf16[6,64,1024]{2,1,0:T(8,128)(2,1)}, bf16[6,64,1024]{2,1,0:T(8,128)(2,1)S(1)}, u32[]{:S(2)}, u32[]{:S(2)}) collective-permute-start(bf16[6,64,1024]{2,1,0:T(8,128)(2,1)} %get-tuple-element.157), channel_id=1, source_target_pairs={{0,8},{1,9},{2,10},{3,11},{4,12},{5,13},{6,14},{7,15},{8,0},{9,1},... | collective-permute-start | bytes 2359304 | tf_op jit(solution)/shard_map/ppermute | solution.py:36
  143.6 43.7 %collective-permute-start.21 = (bf16[15,2,64,1024]{3,2,1,0:T(8,128)(2,1)}, bf16[15,2,64,1024]{3,2,1,0:T(8,128)(2,1)}, u32[]{:S(2)}, u32[]{:S(2)}) collective-permute-start(bf16[15,2,64,1024]{3,2,1,0:T(8,128)(2,1)} %get-tuple-element.173.mine), channel_id=1, source_target_pairs={{0,16},{16,0},{1,17},{17,1},{2,18},{18,2},{3,19},{19,3},{4,20},{20... | collective-permute-start | bytes 11796488 | tf_op jit(solution)/shard_map/ppermute | solution.py:40
  149.9 36.6 %collective-permute-start.18 = (bf16[6,2,64,1024]{3,2,1,0:T(8,128)(2,1)}, bf16[6,2,64,1024]{3,2,1,0:T(8,128)(2,1)}, u32[]{:S(2)}, u32[]{:S(2)}) collective-permute-start(bf16[6,2,64,1024]{3,2,1,0:T(8,128)(2,1)} %get-tuple-element.169), channel_id=1, source_target_pairs={{0,4},{1,5},{2,6},{3,7},{4,0},{5,1},{6,2},{7,3},{8,12},{9,13},{10,... | collective-permute-start | bytes 4718600 | tf_op jit(solution)/shard_map/ppermute | solution.py:36
  149.9 36.6 %collective-permute-start.19 = (bf16[6,2,64,1024]{3,2,1,0:T(8,128)(2,1)}, bf16[6,2,64,1024]{3,2,1,0:T(8,128)(2,1)}, u32[]{:S(2)}, u32[]{:S(2)}) collective-permute-start(bf16[6,2,64,1024]{3,2,1,0:T(8,128)(2,1)} %get-tuple-element.170), channel_id=1, source_target_pairs={{0,1},{1,0},{2,3},{3,2},{4,5},{5,4},{6,7},{7,6},{8,9},{9,8},{10,11... | collective-permute-start | bytes 4718600 | tf_op jit(solution)/shard_map/ppermute | solution.py:36
  151.0 36.3 %collective-permute-start.20 = (bf16[6,2,64,1024]{3,2,1,0:T(8,128)(2,1)}, bf16[6,2,64,1024]{3,2,1,0:T(8,128)(2,1)}, u32[]{:S(2)}, u32[]{:S(2)}) collective-permute-start(bf16[6,2,64,1024]{3,2,1,0:T(8,128)(2,1)} %get-tuple-element.171), channel_id=1, source_target_pairs={{0,2},{1,3},{2,0},{3,1},{4,6},{5,7},{6,4},{7,5},{8,10},{9,11},{10,... | collective-permute-start | bytes 4718600 | tf_op jit(solution)/shard_map/ppermute | solution.py:36
  195.4 37.0 %collective-permute-start.25 = (bf16[21,2,64,1024]{3,2,1,0:T(8,128)(2,1)}, bf16[21,2,64,1024]{3,2,1,0:T(8,128)(2,1)}, u32[]{:S(2)}, u32[]{:S(2)}) collective-permute-start(bf16[21,2,64,1024]{3,2,1,0:T(8,128)(2,1)} %get-tuple-element.182.mine), channel_id=1, source_target_pairs={{0,16},{16,0},{1,17},{17,1},{2,18},{18,2},{3,19},{19,3},{4,20},{20... | collective-permute-start | bytes 16515080 | tf_op jit(solution)/shard_map/ppermute | solution.py:40
  195.4 37.0 %collective-permute-start.22 = (bf16[5,2,64,1024]{3,2,1,0:T(8,128)(2,1)}, bf16[5,2,64,1024]{3,2,1,0:T(8,128)(2,1)S(1)}, u32[]{:S(2)}, u32[]{:S(2)}) collective-permute-start(bf16[5,2,64,1024]{3,2,1,0:T(8,128)(2,1)} %get-tuple-element.174), channel_id=1, source_target_pairs={{0,4},{1,5},{2,6},{3,7},{4,0},{5,1},{6,2},{7,3},{8,12},{9,13},{10,... | collective-permute-start | bytes 3932168 | tf_op jit(solution)/shard_map/ppermute | solution.py:36
  197.1 35.3 %collective-permute-start.23 = (bf16[5,2,64,1024]{3,2,1,0:T(8,128)(2,1)}, bf16[5,2,64,1024]{3,2,1,0:T(8,128)(2,1)}, u32[]{:S(2)}, u32[]{:S(2)}) collective-permute-start(bf16[5,2,64,1024]{3,2,1,0:T(8,128)(2,1)} %get-tuple-element.175), channel_id=1, source_target_pairs={{0,1},{1,0},{2,3},{3,2},{4,5},{5,4},{6,7},{7,6},{8,9},{9,8},{10,11... | collective-permute-start | bytes 3932168 | tf_op jit(solution)/shard_map/ppermute | solution.py:36
  198.8 33.6 %collective-permute-start.24 = (bf16[5,2,64,1024]{3,2,1,0:T(8,128)(2,1)}, bf16[5,2,64,1024]{3,2,1,0:T(8,128)(2,1)}, u32[]{:S(2)}, u32[]{:S(2)}) collective-permute-start(bf16[5,2,64,1024]{3,2,1,0:T(8,128)(2,1)} %get-tuple-element.176), channel_id=1, source_target_pairs={{0,2},{1,3},{2,0},{3,1},{4,6},{5,7},{6,4},{7,5},{8,10},{9,11},{10,... | collective-permute-start | bytes 3932168 | tf_op jit(solution)/shard_map/ppermute | solution.py:36
  200.6 31.0 %collective-permute-start.1 = (bf16[2,128,1024]{2,1,0:T(8,128)(2,1)S(1)}, bf16[2,128,1024]{2,1,0:T(8,128)(2,1)S(1)}, u32[]{:S(2)}, u32[]{:S(2)}) collective-permute-start(bf16[2,128,1024]{2,1,0:T(8,128)(2,1)S(1)} %broadcast_select_fusion.7), channel_id=1, source_target_pairs={{16,8},{17,9},{18,10},{19,11},{20,12},{21,13},{22,14},{23,15},{8,1... | collective-permute-start | bytes 1572872 | tf_op jit(solution)/shard_map/ppermute | solution.py:27
  266.2 35.0 %collective-permute-start.33 = (bf16[6,2,64,1024]{3,2,1,0:T(8,128)(2,1)}, bf16[6,2,64,1024]{3,2,1,0:T(8,128)(2,1)}, u32[]{:S(2)}, u32[]{:S(2)}) collective-permute-start(bf16[6,2,64,1024]{3,2,1,0:T(8,128)(2,1)} %get-tuple-element.214.mine), channel_id=1, source_target_pairs={{0,16},{16,0},{1,17},{17,1},{2,18},{18,2},{3,19},{19,3},{4,20},{20... | collective-permute-start | bytes 4718600 | tf_op jit(solution)/shard_map/ppermute | solution.py:40
  267.4 33.8 %collective-permute-start.30 = (bf16[4,2,64,1024]{3,2,1,0:T(8,128)(2,1)}, bf16[4,2,64,1024]{3,2,1,0:T(8,128)(2,1)}, u32[]{:S(2)}, u32[]{:S(2)}) collective-permute-start(bf16[4,2,64,1024]{3,2,1,0:T(8,128)(2,1)} %get-tuple-element.210), channel_id=1, source_target_pairs={{0,1},{1,0},{2,3},{3,2},{4,5},{5,4},{6,7},{7,6},{8,9},{9,8},{10,11... | collective-permute-start | bytes 3145736 | tf_op jit(solution)/shard_map/ppermute | solution.py:36
  269.1 32.0 %collective-permute-start.31 = (bf16[4,2,64,1024]{3,2,1,0:T(8,128)(2,1)}, bf16[4,2,64,1024]{3,2,1,0:T(8,128)(2,1)}, u32[]{:S(2)}, u32[]{:S(2)}) collective-permute-start(bf16[4,2,64,1024]{3,2,1,0:T(8,128)(2,1)} %get-tuple-element.211), channel_id=1, source_target_pairs={{0,2},{1,3},{2,0},{3,1},{4,6},{5,7},{6,4},{7,5},{8,10},{9,11},{10,... | collective-permute-start | bytes 3145736 | tf_op jit(solution)/shard_map/ppermute | solution.py:36
  269.4 31.7 %collective-permute-start.32 = (bf16[4,2,64,1024]{3,2,1,0:T(8,128)(2,1)}, bf16[4,2,64,1024]{3,2,1,0:T(8,128)(2,1)}, u32[]{:S(2)}, u32[]{:S(2)}) collective-permute-start(bf16[4,2,64,1024]{3,2,1,0:T(8,128)(2,1)} %get-tuple-element.212), channel_id=1, source_target_pairs={{0,4},{1,5},{2,6},{3,7},{4,0},{5,1},{6,2},{7,3},{8,12},{9,13},{10,... | collective-permute-start | bytes 3145736 | tf_op jit(solution)/shard_map/ppermute | solution.py:36
  315.7 37.7 %collective-permute-start.39 = (f32[1,128]{1,0:T(1,128)S(1)}, f32[1,128]{1,0:T(1,128)S(1)}, u32[]{:S(2)}, u32[]{:S(2)}) collective-permute-start(f32[1,128]{1,0:T(1,128)S(1)} %add.116), channel_id=1, source_target_pairs={{0,8},{1,9},{2,10},{3,11},{4,12},{5,13},{6,14},{7,15},{8,0},{9,1},... | collective-permute-start | bytes 1544 | tf_op jit(solution)/shard_map/ppermute | solution.py:36
  455.7 38.2 %collective-permute-start.43 = (bf16[8,136,1024]{2,1,0:T(8,128)(2,1)}, bf16[8,136,1024]{2,1,0:T(8,128)(2,1)}, u32[]{:S(2)}, u32[]{:S(2)}) collective-permute-start(bf16[8,136,1024]{2,1,0:T(8,128)(2,1)} %constant_dynamic-slice_fusion.2), channel_id=1, source_target_pairs={{8,24},{9,25},{10,26},{11,27},{12,28},{13,29},{14,30},{15,31},{24,... | collective-permute-start | bytes 6684680 | tf_op jit(solution)/shard_map/ppermute | solution.py:27
  508.3 60.4 %all-to-all-start = ((bf16[8,272,1024]{2,1,0:T(8,128)(2,1)}), bf16[8,272,1024]{2,1,0:T(8,128)(2,1)}, u32[]{:S(2)}, u32[]{:S(2)}) async-start(bf16[8,272,1024]{2,1,0:T(8,128)(2,1)} %pad_maximum_fusion), calls=%async_computation | async-start | bytes 8912896 | tf_op jit(solution)/shard_map/all_to_all | solution.py:310
  571.9 40.1 %all-to-all-start.1 = ((bf16[8,136,1024]{2,1,0:T(8,128)(2,1)}), bf16[8,136,1024]{2,1,0:T(8,128)(2,1)}, u32[]{:S(2)}, u32[]{:S(2)}) async-start(bf16[8,136,1024]{2,1,0:T(8,128)(2,1)} %add_convert_fusion), calls=%async_computation.1 | async-start | bytes 4456448 | tf_op jit(solution)/shard_map/all_to_all | solution.py:310
  577.4 34.5 %collective-permute-start.44 = (bf16[272,1024]{1,0:T(8,128)(2,1)S(1)}, bf16[272,1024]{1,0:T(8,128)(2,1)S(1)}, u32[]{:S(2)}, u32[]{:S(2)}) collective-permute-start(bf16[272,1024]{1,0:T(8,128)(2,1)S(1)} %reduce_sum.46), channel_id=1, source_target_pairs={{8,0},{9,1},{10,2},{11,3},{12,4},{13,5},{14,6},{15,7},{24,16},{25,... | collective-permute-start | bytes 1671176 | tf_op jit(solution)/shard_map/ppermute | solution.py:336
  617.5 56.3 %all-to-all-start.2 = ((bf16[8,272,1024]{2,1,0:T(8,128)(2,1)}), bf16[8,272,1024]{2,1,0:T(8,128)(2,1)}, u32[]{:S(2)}, u32[]{:S(2)}) async-start(bf16[8,272,1024]{2,1,0:T(8,128)(2,1)} %broadcast_in_dim.82), calls=%async_computation.2 | async-start | bytes 8912896 | tf_op jit(solution)/shard_map/all_to_all | solution.py:310
  705.5 30.4 %collective-permute-start.48 = (bf16[272,1024]{1,0:T(8,128)(2,1)S(1)}, bf16[272,1024]{1,0:T(8,128)(2,1)S(1)}, u32[]{:S(2)}, u32[]{:S(2)}) collective-permute-start(bf16[272,1024]{1,0:T(8,128)(2,1)S(1)} %pad_maximum_fusion.1), channel_id=1, source_target_pairs={{0,8},{1,9},{2,10},{3,11},{4,12},{5,13},{6,14},{7,15},{16,24},{17,... | collective-permute-start | bytes 1671176 | tf_op jit(solution)/shard_map/ppermute | solution.py:336
  738.7 60.7 %all-to-all-start.4 = ((bf16[8,272,1024]{2,1,0:T(8,128)(2,1)}), bf16[8,272,1024]{2,1,0:T(8,128)(2,1)}, u32[]{:S(2)}, u32[]{:S(2)}) async-start(bf16[8,272,1024]{2,1,0:T(8,128)(2,1)} %broadcast_in_dim.83), calls=%async_computation.4 | async-start | bytes 8912896 | tf_op jit(solution)/shard_map/all_to_all | solution.py:310
  743.4 82.2 %collective-permute-start.50 = (bf16[8,272,1024]{2,1,0:T(8,128)(2,1)}, bf16[8,272,1024]{2,1,0:T(8,128)(2,1)}, u32[]{:S(2)}, u32[]{:S(2)}) collective-permute-start(bf16[8,272,1024]{2,1,0:T(8,128)(2,1)} %all-to-all-done.2.late1_ref), channel_id=1, source_target_pairs={{0,16},{1,17},{2,18},{3,19},{4,20},{5,21},{6,22},{7,23},{8,24},{9,... | collective-permute-start | bytes 13369352 | tf_op jit(solution)/shard_map/ppermute | solution.py:343
  (102 other events, 1730.1 us)
